TPU v7x, 32 devices: a whole 2x2x4 slice. The times are simulated.
32 devices in a mesh: dp: 8 (over z, x), zero: 4 (over y, core).
Axes of the slice: x: 2, y: 2, z: 4, core: 2. Of those that a mesh axis runs over, the one named last changes fastest.
Arguments:
- tokens: bfloat16 [64, 1024, 768], P('zero', 'dp'), may hold values from -6 to 6
- loss_sensitivity: bfloat16 [32, 1024, 768], P(('dp', 'zero')), may hold values from -6 to 6
- lengths: int32 [64], replicated, may hold values from 0 to 1024, as said below
- holder_sequence_list: int32 [64], replicated, may hold values from 0 to 63, as said below
- master: float32 [3768320], P('zero')
- moment_one: float32 [3768320], P('zero'), may hold values from -18 to 18
- moment_two: float32 [3768320], P('zero'), may hold values from 1 to 1000
- adam_rates: float32 [2], replicated, may hold values from 0.05 to 0.2
- iteration_tally: int32 [1], replicated, may hold values from 1 to 8
Outputs:
- tokens_out: bfloat16 [64, 1024, 768], P('zero', 'dp')
- grad_tokens: bfloat16 [64, 1024, 768], P('zero', 'dp')
- new_master: float32 [3768320], replicated
- grads: float32 [3768320], P('zero')
- moment_one_out: float32 [3768320], P('zero')
- moment_two_out: float32 [3768320], P('zero')
Inputs may be any that keep to these rules, and one draw needn't show every extreme that they name: A permutation of the sequences. Slot i lies on the device whose index along dp+zero is i // 2, and holder_sequence_list[i] is one of the 64 / 4 sequences of that device's zero index (sequences z * 64 / 4 onward for zero index z). The two sequences of slots 2j and 2j + 1 have lengths summing to exactly 1024; in some pack one of them has 1024 tokens and the other none.
All inputs are finite; a program needn't handle non-finite values.
Results may differ from a plain program's by a relative error of at most 0.002.
The roundings to bfloat16 on the way count: a program that leaves them out, or rounds other values in their place, can miss the bound.
Values may be sent and summed in bfloat16 or wider, within the bound.
No kernel may reach another device: no remote copies, remote signals or barrier semaphores. Data moves between devices by JAX's collectives and lax.ppermute only.
A program may use at most 256 MiB of HBM per device.

v0:
```python
from functools import partial

import jax
import jax.numpy as jnp
from jax import lax
from jax.sharding import PartitionSpec as P

D = 768
HEADS = 24
HEADDIM = 64
STATE = 128
CONV = 4
SPAN = 256
INNER = 1536
XBC = 1792
PROJ = 3352


EXACT_MATMUL = lax.Precision.HIGHEST
EPS_NORM = 1e-05
BETA_ONE = 0.9
BETA_TWO = 0.95
EPS_ADAM = 1e-08


def padded_slot(amount):
    return (amount + 127) // 128 * 128


def unpack(linear_coefficient_list):
    piece_sizes = [D, D * PROJ, CONV * XBC, XBC, HEADS, HEADS, HEADS, INNER, INNER * D]
    pieces = []
    offset = 0
    for amount in piece_sizes:
        pieces.append(linear_coefficient_list[offset : offset + amount])
        offset = offset + padded_slot(amount)
    (
        norm_gain,
        input_weight_t,
        conv_w,
        conv_b,
        dt_bias,
        a_log,
        d_skip,
        gated_gain,
        emitting_matrix,
    ) = pieces
    return (
        norm_gain,
        input_weight_t.reshape(PROJ, D),
        conv_w.reshape(CONV, XBC),
        conv_b,
        dt_bias,
        a_log,
        d_skip,
        gated_gain,
        emitting_matrix.reshape(INNER, D),
    )


def pre_norm(values, gain):
    return values * lax.rsqrt(jnp.mean(values * values, axis=-1, keepdims=True) + EPS_NORM) * gain


def causal_conv(conv_in, conv_w, conv_b, segment):
    seq_len = conv_in.shape[1]
    padded = jnp.pad(conv_in, ((0, 0), (CONV - 1, 0), (0, 0)))
    seg_padded = jnp.pad(segment, ((0, 0), (CONV - 1, 0)), constant_values=-1.0)
    summed = conv_b + jnp.zeros_like(conv_in)
    for offset in range(CONV):
        same_seg = (seg_padded[:, offset : offset + seq_len] == segment).astype(jnp.float32)[
            ..., None
        ]
        summed = summed + conv_w[offset] * (padded[:, offset : offset + seq_len] * same_seg)
    return summed


def span_scan(x_heads, dt_pos, decay_rate, b_rows, c_rows, segment):
    batch_size, seq_len, head_count, head_width = x_heads.shape
    block_count = seq_len // SPAN

    def split_blocks(values):
        shaped = values.reshape((batch_size, block_count, SPAN) + values.shape[2:])
        return jnp.moveaxis(shaped, 1, 0)

    causal = jnp.arange(SPAN)[:, None] >= jnp.arange(SPAN)[None, :]

    def advance(carried_pair, block_in):
        carried, last_seg = carried_pair
        x_blk, dt_blk, b_blk, c_blk, membership_tile = block_in
        dt_cols = jnp.swapaxes(dt_blk, 1, 2)
        cum_blk = jnp.cumsum(dt_cols * decay_rate[None, :, None], axis=2)
        differ = cum_blk[:, :, :, None] - cum_blk[:, :, None, :]
        same_seg = membership_tile[:, :, None] == membership_tile[:, None, :]
        allowed = jnp.logical_and(causal[None], same_seg)[:, None]
        weights_in = jnp.exp(jnp.where(allowed, differ, -jnp.inf))
        gram_blk = jnp.einsum("stn,srn->str", c_blk, b_blk, precision=EXACT_MATMUL)
        mixing = gram_blk[:, None] * weights_in * dt_cols[:, :, None, :]
        inside = jnp.einsum("shtr,srhp->sthp", mixing, x_blk, precision=EXACT_MATMUL)
        from_state = jnp.einsum("stn,shpn->sthp", c_blk, carried, precision=EXACT_MATMUL)
        from_state = from_state * jnp.swapaxes(jnp.exp(cum_blk), 1, 2)[..., None]
        keep_state = (membership_tile == last_seg[:, None]).astype(jnp.float32)
        from_state = from_state * keep_state[:, :, None, None]
        cum_end = cum_blk[:, :, -1]
        end_seg = membership_tile[:, -1]
        in_last = (membership_tile == end_seg[:, None]).astype(jnp.float32)
        carry_weight = jnp.exp(cum_end[:, :, None] - cum_blk) * dt_cols * in_last[:, None, :]
        added_state = jnp.einsum(
            "srn,shr,srhp->shpn", b_blk, carry_weight, x_blk, precision=EXACT_MATMUL
        )
        carry_scale = jnp.exp(cum_end) * (end_seg == last_seg).astype(jnp.float32)[:, None]
        carried = carried * carry_scale[:, :, None, None] + added_state
        return ((carried, end_seg), inside + from_state)

    initial = (
        jnp.zeros((batch_size, head_count, head_width, b_rows.shape[-1]), jnp.float32),
        jnp.zeros((batch_size,), jnp.float32),
    )
    final_pair, outputs = lax.scan(
        jax.checkpoint(advance),
        initial,
        (
            split_blocks(x_heads),
            split_blocks(dt_pos),
            split_blocks(b_rows),
            split_blocks(c_rows),
            split_blocks(segment),
        ),
    )
    return jnp.moveaxis(outputs, 0, 1).reshape(batch_size, seq_len, head_count, head_width)


def mixer_branch(input_projection, conv_w, conv_b, dt_bias, a_log, d_skip, gated_gain, segment):
    batch_size, seq_len = (input_projection.shape[0], input_projection.shape[1])
    gate_z = input_projection[..., :INNER]
    conv_in = input_projection[..., INNER : INNER + XBC]
    dt_raw = input_projection[..., INNER + XBC :]
    conv_out = jax.nn.silu(causal_conv(conv_in, conv_w, conv_b, segment))
    x_heads = conv_out[..., :INNER].reshape(batch_size, seq_len, HEADS, HEADDIM)
    b_rows = conv_out[..., INNER : INNER + STATE]
    c_rows = conv_out[..., INNER + STATE :]
    dt_pos = jax.nn.softplus(dt_raw + dt_bias)
    decay_rate = -jnp.exp(a_log)
    scanned = (
        span_scan(x_heads, dt_pos, decay_rate, b_rows, c_rows, segment) + d_skip[:, None] * x_heads
    )
    gated_out = scanned.reshape(batch_size, seq_len, INNER) * jax.nn.silu(gate_z)
    return (
        gated_out
        * lax.rsqrt(jnp.mean(gated_out * gated_out, axis=-1, keepdims=True) + EPS_NORM)
        * gated_gain
    )


def adam_update(weights, first_moment, second_moment, gradient, adam_rates, iteration_tally):
    steps_f = iteration_tally[0].astype(jnp.float32)
    first_next = BETA_ONE * first_moment + (1.0 - BETA_ONE) * gradient
    second_next = BETA_TWO * second_moment + (1.0 - BETA_TWO) * gradient * gradient
    first_hat = first_next / (1.0 - jnp.power(BETA_ONE, steps_f))
    second_hat = second_next / (1.0 - jnp.power(BETA_TWO, steps_f))
    updated = weights - adam_rates[0] * (
        first_hat / (jnp.sqrt(second_hat) + EPS_ADAM) + adam_rates[1] * weights
    )
    return (updated, first_next, second_next)


def on_device(
    tokens,
    loss_sensitivity,
    lengths,
    holder_sequence_list,
    master,
    moment_one,
    moment_two,
    adam_rates,
    iteration_tally,
):
    group_devices = lax.axis_size("zero")
    data_devices = lax.axis_size("dp")
    zero_index = lax.axis_index("zero")
    dp_index = lax.axis_index("dp")
    pack_count = loss_sensitivity.shape[0]
    slot_count = 2 * pack_count
    seq_len = loss_sensitivity.shape[1]
    model_width = loss_sensitivity.shape[2]
    group_seqs = tokens.shape[0]
    full_weights = lax.all_gather(master.astype(jnp.bfloat16), "zero", axis=0, tiled=True)
    (
        norm_gain,
        input_weight_t,
        conv_w,
        conv_b,
        dt_bias,
        a_log,
        d_skip,
        gated_gain,
        emitting_matrix,
    ) = unpack(full_weights)
    small_f = [
        piece.astype(jnp.float32) for piece in (conv_w, conv_b, dt_bias, a_log, d_skip, gated_gain)
    ]
    norm_gain_f = norm_gain.astype(jnp.float32)
    arranged_order = holder_sequence_list.reshape(data_devices, group_devices, slot_count)
    group_order = lax.dynamic_index_in_dim(arranged_order, zero_index, 1, keepdims=False).reshape(
        -1
    )
    local_ids = group_order - zero_index * group_seqs
    dealt_rows = jnp.take(tokens, local_ids, axis=0)
    local_tok = lax.all_to_all(dealt_rows, "dp", split_axis=0, concat_axis=1, tiled=True)
    my_seqs = lax.dynamic_slice_in_dim(group_order, dp_index * slot_count, slot_count)
    my_lengths = jnp.take(lengths, my_seqs)
    bounds = my_lengths.reshape(pack_count, 2)[:, 0]
    positions = jnp.arange(seq_len, dtype=jnp.int32)
    later_part = positions[None, :] >= bounds[:, None]
    pack_ids = jnp.arange(pack_count, dtype=jnp.int32)[:, None]
    source = jnp.where(
        later_part,
        (2 * pack_ids + 1) * seq_len + positions[None, :] - bounds[:, None],
        2 * pack_ids * seq_len + positions[None, :],
    )
    segment = later_part.astype(jnp.float32)
    slot_rows = local_tok.reshape(slot_count * seq_len, model_width)
    packed_tok = jnp.take(slot_rows, source.reshape(-1), axis=0).reshape(
        pack_count, seq_len, model_width
    )
    place_numbering = jnp.arange(slot_count, dtype=jnp.int32)
    shift_by = jnp.where(place_numbering % 2 == 1, jnp.repeat(bounds, 2), 0)
    within = positions[None, :] + shift_by[:, None]
    unpack_rows = (place_numbering // 2)[:, None] * seq_len + jnp.minimum(within, seq_len - 1)
    slot_live = (positions[None, :] < my_lengths[:, None]).astype(jnp.float32)[..., None]

    def to_slots(values):
        flat_rows = values.reshape(pack_count * seq_len, values.shape[2])
        picked = jnp.take(flat_rows, unpack_rows.reshape(-1), axis=0)
        return picked.reshape(slot_count, seq_len, values.shape[2]) * slot_live

    tokens_f = packed_tok.astype(jnp.float32)
    normalized, norm_pull = jax.vjp(pre_norm, tokens_f, norm_gain_f)
    normalized_rows = normalized.astype(jnp.bfloat16)
    input_projection = jnp.einsum(
        "mgv,bv->mgb", normalized_rows, input_weight_t, preferred_element_type=jnp.float32
    )
    mixer_output, mix_pull = jax.vjp(
        partial(mixer_branch, segment=segment), input_projection, *small_f
    )
    mixer_output_rows = mixer_output.astype(jnp.bfloat16)
    mixer_path = jnp.einsum(
        "ocr,rb->ocb", mixer_output_rows, emitting_matrix, preferred_element_type=jnp.float32
    )
    result = (local_tok.astype(jnp.float32) + to_slots(mixer_path)).astype(jnp.bfloat16)
    cot_f = loss_sensitivity.astype(jnp.float32)
    grad_out_weight = jnp.einsum(
        "uir,uin->rn", mixer_output_rows, loss_sensitivity, preferred_element_type=jnp.float32
    )
    grad_mixed = jnp.einsum(
        "nsa,wa->nsw", loss_sensitivity, emitting_matrix, preferred_element_type=jnp.float32
    )
    grad_proj, grad_conv_w, grad_conv_b, grad_dt_bias, grad_a_log, grad_d_skip, grad_gated = (
        mix_pull(grad_mixed)
    )
    grad_projection_rows = grad_proj.astype(jnp.bfloat16)
    grad_in_weight_t = jnp.einsum(
        "pvr,pvy->ry", grad_projection_rows, normalized_rows, preferred_element_type=jnp.float32
    )
    grad_normed = jnp.einsum(
        "ept,tb->epb", grad_projection_rows, input_weight_t, preferred_element_type=jnp.float32
    )
    grad_tok, grad_norm_gain = norm_pull(grad_normed)
    grad_input = to_slots(cot_f + grad_tok).astype(jnp.bfloat16)
    back_out, back_grad = (
        lax.all_to_all(result, "dp", split_axis=1, concat_axis=0, tiled=True),
        lax.all_to_all(grad_input, "dp", split_axis=1, concat_axis=0, tiled=True),
    )
    restore = jnp.zeros_like(local_ids).at[local_ids].set(jnp.arange(group_seqs, dtype=jnp.int32))
    tokens_out = jnp.take(back_out, restore, axis=0)
    grad_tokens = jnp.take(back_grad, restore, axis=0)
    vector_len = master.shape[0] * group_devices
    used = [
        grad_norm_gain,
        grad_in_weight_t.reshape(-1),
        grad_conv_w.reshape(-1),
        grad_conv_b,
        grad_dt_bias,
        grad_a_log,
        grad_d_skip,
        grad_gated,
        grad_out_weight.reshape(-1),
    ]
    laid = [jnp.pad(piece, (0, padded_slot(piece.shape[0]) - piece.shape[0])) for piece in used]
    used_len = sum((piece.shape[0] for piece in laid))
    flat_grad = jnp.concatenate(laid + [jnp.zeros((vector_len - used_len,), jnp.float32)])
    grad_shard = lax.psum_scatter(flat_grad, "zero", scatter_dimension=0, tiled=True)
    grad_shard = lax.psum(grad_shard, "dp")
    new_shard, first_next, second_next = adam_update(
        master, moment_one, moment_two, grad_shard, adam_rates, iteration_tally
    )
    new_master = lax.all_gather(new_shard, "zero", axis=0, tiled=True)
    return (tokens_out, grad_tokens, new_master, grad_shard, first_next, second_next)


def solution(mesh):
    return jax.shard_map(
        on_device,
        mesh=mesh,
        in_specs=(
            P("zero", "dp", None),
            P(("dp", "zero"), None, None),
            P(),
            P(),
            P("zero"),
            P("zero"),
            P("zero"),
            P(),
            P(),
        ),
        out_specs=(
            P("zero", "dp", None),
            P("zero", "dp", None),
            P(),
            P("zero"),
            P("zero"),
            P("zero"),
        ),
        check_vma=False,
    )
```

profile of v0, /device:TPU:0, one launch (start us, length us, event | category | flops | bytes accessed | tf_op | source)
XLA Modules:
  0.0 1918.3 jit_solution(2939030028046940159)
XLA Ops:
  18.1 7.3 all-to-all-start
  27.2 68.9 %all-to-all-done = bf16[16,128,768]{2,1,0:T(8,128)(2,1)} async-done(((bf16[16,128,768]{2,1,0:T(8,128)(2,1)}), bf16[16,128,768]{2,1,0:T(8,128)(2,1)}, u32[]{:S(2)}, u32[]{:S(2)}) %all-to-all-start) | async-done | bytes 3145760 | tf_op jit(solution)/shard_map/all_to_all | solution.py:209
  113.8 9.7 reshape.1647
  124.2 11.8 convolution_bitcast_fusion.1
  141.5 9.5 fusion.126
  156.0 8.1 reshape.1649
  178.9 254.5 %while.45 = (s32[]{:T(128)}, f32[1,24,64,128]{3,2,1,0:T(8,128)S(1)}, f32[1]{0:T(128)}, f32[4,1,256,24,64]{2,0,4,3,1:T(4,128)}, f32[4,1,24,64,128]{4,3,2,1,0:T(8,...) while((s32[]{:T(128)}, ...), condition=%wide.region_4.6_spmd.clone, body=%wide.region_1.5_spmd.clone.sunk | while | flops 2526444544 | bytes 20096584 | solution.py:119
  183.2 9.3 fusion.244
  198.4 34.7 %dynamic_update_slice.74 = f32[4,1,256,24,64]{2,0,4,3,1:T(4,128)} dynamic-update-slice(f32[4,1,256,24,64]{2,0,4,3,1:T(4,128)} %get-tuple-element.1165, f32[1,1,256,24,64]{2,0,4,3,1:T(1,128)} %copy.373, s32[]{:T(128)} %get-tuple-element.1162, s32[]{:T(128)} %constant.237.clone.1..sunk, s32[]{:T(128)} %constant.237.clone.1..sunk, s32[]{:T(128)} %constant.237.clone.1..sunk, s32[]{:T(128)} %constant.237.clone.1..sunk) | dynamic-update-slice | bytes 3145732 | tf_op jit(solution)/shard_map/jvp()/while/body/jit(dynamic_update_index_in_dim)/dynamic_update_slice | solution.py:119
  246.7 9.3 fusion.244
  261.9 34.7 %dynamic_update_slice.74 = f32[4,1,256,24,64]{2,0,4,3,1:T(4,128)} dynamic-update-slice(f32[4,1,256,24,64]{2,0,4,3,1:T(4,128)} %get-tuple-element.1165, f32[1,1,256,24,64]{2,0,4,3,1:T(1,128)} %copy.373, s32[]{:T(128)} %get-tuple-element.1162, s32[]{:T(128)} %constant.237.clone.1..sunk, s32[]{:T(128)} %constant.237.clone.1..sunk, s32[]{:T(128)} %constant.237.clone.1..sunk, s32[]{:T(128)} %constant.237.clone.1..sunk) | dynamic-update-slice | bytes 3145732 | tf_op jit(solution)/shard_map/jvp()/while/body/jit(dynamic_update_index_in_dim)/dynamic_update_slice | solution.py:119
  310.4 9.3 fusion.244
  325.6 34.7 %dynamic_update_slice.74 = f32[4,1,256,24,64]{2,0,4,3,1:T(4,128)} dynamic-update-slice(f32[4,1,256,24,64]{2,0,4,3,1:T(4,128)} %get-tuple-element.1165, f32[1,1,256,24,64]{2,0,4,3,1:T(1,128)} %copy.373, s32[]{:T(128)} %get-tuple-element.1162, s32[]{:T(128)} %constant.237.clone.1..sunk, s32[]{:T(128)} %constant.237.clone.1..sunk, s32[]{:T(128)} %constant.237.clone.1..sunk, s32[]{:T(128)} %constant.237.clone.1..sunk) | dynamic-update-slice | bytes 3145732 | tf_op jit(solution)/shard_map/jvp()/while/body/jit(dynamic_update_index_in_dim)/dynamic_update_slice | solution.py:119
  374.0 9.3 fusion.244
  389.1 34.7 %dynamic_update_slice.74 = f32[4,1,256,24,64]{2,0,4,3,1:T(4,128)} dynamic-update-slice(f32[4,1,256,24,64]{2,0,4,3,1:T(4,128)} %get-tuple-element.1165, f32[1,1,256,24,64]{2,0,4,3,1:T(1,128)} %copy.373, s32[]{:T(128)} %get-tuple-element.1162, s32[]{:T(128)} %constant.237.clone.1..sunk, s32[]{:T(128)} %constant.237.clone.1..sunk, s32[]{:T(128)} %constant.237.clone.1..sunk, s32[]{:T(128)} %constant.237.clone.1..sunk) | dynamic-update-slice | bytes 3145732 | tf_op jit(solution)/shard_map/jvp()/while/body/jit(dynamic_update_index_in_dim)/dynamic_update_slice | solution.py:119
  433.4 8.3 transpose.177
  441.9 10.5 multiply_reduce_fusion.8
  458.8 7.9 fusion.131
  466.7 16.1 multiply_reduce_fusion.7
  482.9 8.1 reshape.1657
  497.6 514.2 %while.46 = (s32[]{:T(128)}, f32[24]{0:T(128)}, f32[1,24,64,128]{3,2,1,0:T(8,128)}, f32[4,1,256,24,64]{2,0,4,3,1:T(4,128)}, f32[4,1,256,24]{3,2,1,0:T(8,128)}, /...) while((s32[]{:T(128)}, f32[24]{0:T(128)}, ...), condition=%wide.region_21.24_spmd.clone, body=%wide.region_8.23_spmd.clone.sunk | while | flops 5772160000 | bytes 61074916 | solution.py:119
  533.2 11.8 fusion.264
  587.7 34.7 %dynamic_update_slice.78 = f32[4,1,256,24,64]{2,0,4,3,1:T(4,128)} dynamic-update-slice(f32[4,1,256,24,64]{2,0,4,3,1:T(4,128)} %get-tuple-element.1215, f32[1,1,256,24,64]{2,0,4,3,1:T(1,128)} %copy.392, s32[]{:T(128)S(6)} %sub.331, s32[]{:T(128)} %constant.237.clone.1..sunk.1, s32[]{:T(128)} %constant.237.clone.1..sunk.1, s32[]{:T(128)} %constant.237.clone.1..sunk.1, s32[]{:T(128)} %constant.237.clone.1..sunk.1) | dynamic-update-slice | bytes 3145732 | tf_op jit(solution)/shard_map/transpose(jvp())/while/body/jit(dynamic_update_index_in_dim)/dynamic_update_slice | solution.py:119
  661.8 11.8 fusion.264
  716.4 34.7 %dynamic_update_slice.78 = f32[4,1,256,24,64]{2,0,4,3,1:T(4,128)} dynamic-update-slice(f32[4,1,256,24,64]{2,0,4,3,1:T(4,128)} %get-tuple-element.1215, f32[1,1,256,24,64]{2,0,4,3,1:T(1,128)} %copy.392, s32[]{:T(128)S(6)} %sub.331, s32[]{:T(128)} %constant.237.clone.1..sunk.1, s32[]{:T(128)} %constant.237.clone.1..sunk.1, s32[]{:T(128)} %constant.237.clone.1..sunk.1, s32[]{:T(128)} %constant.237.clone.1..sunk.1) | dynamic-update-slice | bytes 3145732 | tf_op jit(solution)/shard_map/transpose(jvp())/while/body/jit(dynamic_update_index_in_dim)/dynamic_update_slice | solution.py:119
  790.6 11.8 fusion.264
  845.2 34.7 %dynamic_update_slice.78 = f32[4,1,256,24,64]{2,0,4,3,1:T(4,128)} dynamic-update-slice(f32[4,1,256,24,64]{2,0,4,3,1:T(4,128)} %get-tuple-element.1215, f32[1,1,256,24,64]{2,0,4,3,1:T(1,128)} %copy.392, s32[]{:T(128)S(6)} %sub.331, s32[]{:T(128)} %constant.237.clone.1..sunk.1, s32[]{:T(128)} %constant.237.clone.1..sunk.1, s32[]{:T(128)} %constant.237.clone.1..sunk.1, s32[]{:T(128)} %constant.237.clone.1..sunk.1) | dynamic-update-slice | bytes 3145732 | tf_op jit(solution)/shard_map/transpose(jvp())/while/body/jit(dynamic_update_index_in_dim)/dynamic_update_slice | solution.py:119
  919.2 11.8 fusion.264
  973.8 34.7 %dynamic_update_slice.78 = f32[4,1,256,24,64]{2,0,4,3,1:T(4,128)} dynamic-update-slice(f32[4,1,256,24,64]{2,0,4,3,1:T(4,128)} %get-tuple-element.1215, f32[1,1,256,24,64]{2,0,4,3,1:T(1,128)} %copy.392, s32[]{:T(128)S(6)} %sub.331, s32[]{:T(128)} %constant.237.clone.1..sunk.1, s32[]{:T(128)} %constant.237.clone.1..sunk.1, s32[]{:T(128)} %constant.237.clone.1..sunk.1, s32[]{:T(128)} %constant.237.clone.1..sunk.1) | dynamic-update-slice | bytes 3145732 | tf_op jit(solution)/shard_map/transpose(jvp())/while/body/jit(dynamic_update_index_in_dim)/dynamic_update_slice | solution.py:119
  1011.8 8.3 transpose.181
  1020.1 8.0 multiply_add_fusion.1
  1028.7 19.7 %multiply_reduce_fusion.5 = (f32[1792]{0:T(1024)S(1)}, f32[1792]{0:T(1024)S(1)}, f32[1792]{0:T(1024)S(1)}, f32[1792]{0:T(1024)S(1)}, f32[1792]{0:T(1024)S(1)}, /*index=5*/f32[1,1024,1792]{1,2,0:T(8,128)S(1)}) fusion(f32[1,1024,1792]{1,2,0:T(8,128)} %copy-done.6, f32[1024]{0:T(1024)S(1)} %bitcast.707, f32[1024]{0:T(1024)S(1)} %bitcast.701, ...), kind=kLoop, calls=%fused_computation.202 | loop fusion | flops 44031232 | bytes 36752384 | tf_op jit(solution)/shard_map/transpose(jvp())/reduce_sum | solution.py:74
  1048.5 10.5 multiply_multiply_fusion.4
  1060.3 15.0 pad_add_fusion
  1075.3 14.6 fusion.150
  1090.0 12.5 fusion.138
  1102.5 7.6 fusion.145
  1110.2 11.1 reshape.1661
  1128.4 87.9 %dynamic-update-slice.1 = f32[3768320]{0:T(1024)} dynamic-update-slice(f32[3768320]{0:T(1024)} %constant_dynamic-update-slice_fusion.6, f32[2574336]{0:T(1024)} %reshape.1661, s32[]{} %constant.327) | dynamic-update-slice | bytes 20594692
  1224.9 41.0 %dynamic-update-slice.8 = f32[3768320]{0:T(1024)} dynamic-update-slice(f32[3768320]{0:T(1024)} %constant_dynamic-update-slice_fusion, f32[1179648]{0:T(1024)} %reshape.1663, s32[]{} %constant.334) | dynamic-update-slice | bytes 9437188
  1269.1 258.3 %all-reduce.26.cloned.1.call-done = f32[3768320]{0:T(1024)} async-done(((f32[3768320]{0:T(1024)}), f32[3768320]{0:T(1024)}) %all-reduce.26.cloned.1.call-update) | async-done | bytes 15073296
  1533.0 145.1 %all-reduce.24.cloned.1.call-done = f32[942080]{0:T(1024)} async-done(((f32[942080]{0:T(1024)}), f32[942080]{0:T(1024)}) %all-reduce.24.cloned.1.call-update) | async-done | bytes 3768336 | tf_op jit(solution)/shard_map/psum | solution.py:293
  1678.1 11.5 multiply_subtract_fusion
  1695.8 9.4 gather_fusion.3
  1709.0 9.4 gather_fusion.5
  1741.2 66.2 %all-to-all-done.1 = bf16[2,1024,768]{2,0,1:T(2,128)(2,1)} async-done(((bf16[2,1024,768]{2,0,1:T(2,128)(2,1)}), bf16[2,1024,768]{2,0,1:T(2,128)(2,1)}, u32[]{:S(2)}, u32[]{:S(2)}) %all-to-all-start.1) | async-done | bytes 3145760 | tf_op jit(solution)/shard_map/all_to_all | solution.py:271
  1816.1 65.8 %all-to-all-done.2 = bf16[2,1024,768]{2,0,1:T(2,128)(2,1)S(1)} async-done(((bf16[2,1024,768]{2,0,1:T(2,128)(2,1)}), bf16[2,1024,768]{2,0,1:T(2,128)(2,1)S(1)}, u32[]{:S(2)}, u32[]{:S(2)}) %all-to-all-start.2) | async-done | bytes 3145760 | tf_op jit(solution)/shard_map/all_to_all | solution.py:272
  1897.5 11.7 copy.460
  (689 shorter events, 547.8 us)
Async XLA Ops:
  7.2 100.3 %all-gather.3.cloned.1.call-start = ((), (), s32[]{:S(2)}) async-start(), calls=%async_computation.3 | async-start | bytes 9420800 | tf_op jit(solution)/shard_map/all_gather | solution.py:187
  18.1 78.1 %all-to-all-start = ((bf16[16,128,768]{2,1,0:T(8,128)(2,1)}), bf16[16,128,768]{2,1,0:T(8,128)(2,1)}, u32[]{:S(2)}, u32[]{:S(2)}) async-start(bf16[16,128,768]{2,1,0:T(8,128)(2,1)} %broadcast_select_fusion.6), calls=%async_computation | async-start | bytes 6291456 | tf_op jit(solution)/shard_map/all_to_all | solution.py:209
  25.4 1502.0 %all-reduce.26.cloned.1.call-start = ((), (), s32[]{:S(2)}) async-start(), calls=%async_computation.6 | async-start | bytes 30146560
  27.1 97.1 %copy-start.60 = (pred[1024]{0:T(1024)(128)(4,1)}, pred[1024]{0:T(1024)(128)(4,1)S(1)}, u32[]{:S(2)}) copy-start(pred[1024]{0:T(1024)(128)(4,1)S(1)} %get-tuple-element.907) | copy-start | bytes 3076
  27.1 114.4 %copy-start.33 = (f32[1024]{0:T(1024)}, f32[1024]{0:T(1024)S(1)}, u32[]{:S(2)}) copy-start(f32[1024]{0:T(1024)S(1)} %get-tuple-element.908) | copy-start | bytes 12292
  27.2 114.3 %copy-start.35 = (f32[1,1024]{1,0:T(1,128)}, f32[1,1024]{1,0:T(1,128)S(1)}, u32[]{:S(2)}) copy-start(f32[1,1024]{1,0:T(1,128)S(1)} %get-tuple-element.896) | copy-start | bytes 12292
  27.2 114.3 %copy-start.37 = (f32[1,1024]{1,0:T(1,128)}, f32[1,1024]{1,0:T(1,128)S(1)}, u32[]{:S(2)}) copy-start(f32[1,1024]{1,0:T(1,128)S(1)} %get-tuple-element.897) | copy-start | bytes 12292
  27.2 114.3 %copy-start.39 = (f32[1,1024]{1,0:T(1,128)}, f32[1,1024]{1,0:T(1,128)S(1)}, u32[]{:S(2)}) copy-start(f32[1,1024]{1,0:T(1,128)S(1)} %get-tuple-element.898) | copy-start | bytes 12292
  106.8 17.4 copy-start.9
  107.5 16.0 copy-start.43
  107.5 16.7 copy-start.50
  441.9 24.8 %copy-start.23 = (f32[1536]{0:T(1024)}, f32[1536]{0:T(1024)S(1)}, u32[]{:S(2)}) copy-start(f32[1536]{0:T(1024)S(1)} %mul.958) | copy-start | bytes 18436
  497.7 14.7 copy-start.41
  577.7 44.8 %copy-start.18 = (f32[256,24]{0,1:T(8,128)S(1)}, f32[256,24]{0,1:T(8,128)}, u32[]{:S(2)}) copy-start(f32[256,24]{0,1:T(8,128)} %copy.390) | copy-start | bytes 73732 | tf_op jit(solution)/shard_map/transpose(jvp())/while
  584.8 39.9 %copy-start.57 = (f32[24]{0:T(128)S(1)}, f32[24]{0:T(128)}, u32[]{:S(2)}) copy-start(f32[24]{0:T(128)} %get-tuple-element.1213) | copy-start | bytes 292 | tf_op jit(solution)/shard_map/transpose(jvp())/while
  584.8 40.4 %copy-start.16 = (f32[4,1,256,128]{3,2,1,0:T(8,128)S(1)}, f32[4,1,256,128]{3,2,1,0:T(8,128)}, u32[]{:S(2)}) copy-start(f32[4,1,256,128]{3,2,1,0:T(8,128)} %copy-done.15) | copy-start | bytes 1572868 | tf_op jit(solution)/shard_map/transpose(jvp())/while
  584.9 40.4 %copy-start.42 = (f32[24]{0:T(128)S(1)}, f32[24]{0:T(128)}, u32[]{:S(2)}) copy-start(f32[24]{0:T(128)} %copy-done.41) | copy-start | bytes 292 | tf_op jit(solution)/shard_map/transpose(jvp())/while
  625.3 15.9 copy-start.41
  706.3 44.8 %copy-start.18 = (f32[256,24]{0,1:T(8,128)S(1)}, f32[256,24]{0,1:T(8,128)}, u32[]{:S(2)}) copy-start(f32[256,24]{0,1:T(8,128)} %copy.390) | copy-start | bytes 73732 | tf_op jit(solution)/shard_map/transpose(jvp())/while
  713.5 39.9 %copy-start.57 = (f32[24]{0:T(128)S(1)}, f32[24]{0:T(128)}, u32[]{:S(2)}) copy-start(f32[24]{0:T(128)} %get-tuple-element.1213) | copy-start | bytes 292 | tf_op jit(solution)/shard_map/transpose(jvp())/while
  713.5 40.4 %copy-start.16 = (f32[4,1,256,128]{3,2,1,0:T(8,128)S(1)}, f32[4,1,256,128]{3,2,1,0:T(8,128)}, u32[]{:S(2)}) copy-start(f32[4,1,256,128]{3,2,1,0:T(8,128)} %copy-done.15) | copy-start | bytes 1572868 | tf_op jit(solution)/shard_map/transpose(jvp())/while
  713.6 40.4 %copy-start.42 = (f32[24]{0:T(128)S(1)}, f32[24]{0:T(128)}, u32[]{:S(2)}) copy-start(f32[24]{0:T(128)} %copy-done.41) | copy-start | bytes 292 | tf_op jit(solution)/shard_map/transpose(jvp())/while
  754.0 15.9 copy-start.41
  835.1 44.8 %copy-start.18 = (f32[256,24]{0,1:T(8,128)S(1)}, f32[256,24]{0,1:T(8,128)}, u32[]{:S(2)}) copy-start(f32[256,24]{0,1:T(8,128)} %copy.390) | copy-start | bytes 73732 | tf_op jit(solution)/shard_map/transpose(jvp())/while
  842.3 39.9 %copy-start.57 = (f32[24]{0:T(128)S(1)}, f32[24]{0:T(128)}, u32[]{:S(2)}) copy-start(f32[24]{0:T(128)} %get-tuple-element.1213) | copy-start | bytes 292 | tf_op jit(solution)/shard_map/transpose(jvp())/while
  842.3 40.4 %copy-start.16 = (f32[4,1,256,128]{3,2,1,0:T(8,128)S(1)}, f32[4,1,256,128]{3,2,1,0:T(8,128)}, u32[]{:S(2)}) copy-start(f32[4,1,256,128]{3,2,1,0:T(8,128)} %copy-done.15) | copy-start | bytes 1572868 | tf_op jit(solution)/shard_map/transpose(jvp())/while
  842.3 40.4 %copy-start.42 = (f32[24]{0:T(128)S(1)}, f32[24]{0:T(128)}, u32[]{:S(2)}) copy-start(f32[24]{0:T(128)} %copy-done.41) | copy-start | bytes 292 | tf_op jit(solution)/shard_map/transpose(jvp())/while
  882.7 15.8 copy-start.41
  963.8 44.8 %copy-start.18 = (f32[256,24]{0,1:T(8,128)S(1)}, f32[256,24]{0,1:T(8,128)}, u32[]{:S(2)}) copy-start(f32[256,24]{0,1:T(8,128)} %copy.390) | copy-start | bytes 73732 | tf_op jit(solution)/shard_map/transpose(jvp())/while
  970.9 39.9 %copy-start.57 = (f32[24]{0:T(128)S(1)}, f32[24]{0:T(128)}, u32[]{:S(2)}) copy-start(f32[24]{0:T(128)} %get-tuple-element.1213) | copy-start | bytes 292 | tf_op jit(solution)/shard_map/transpose(jvp())/while
  971.0 40.4 %copy-start.16 = (f32[4,1,256,128]{3,2,1,0:T(8,128)S(1)}, f32[4,1,256,128]{3,2,1,0:T(8,128)}, u32[]{:S(2)}) copy-start(f32[4,1,256,128]{3,2,1,0:T(8,128)} %copy-done.15) | copy-start | bytes 1572868 | tf_op jit(solution)/shard_map/transpose(jvp())/while
  971.0 40.4 %copy-start.42 = (f32[24]{0:T(128)S(1)}, f32[24]{0:T(128)}, u32[]{:S(2)}) copy-start(f32[24]{0:T(128)} %copy-done.41) | copy-start | bytes 292 | tf_op jit(solution)/shard_map/transpose(jvp())/while
  1028.7 19.7 %copy-start.26 = (f32[1792]{0:T(1024)S(1)}, f32[1792]{0:T(1024)}, u32[]{:S(2)}) copy-start(f32[1792]{0:T(1024)} %copy-done.25) | copy-start | bytes 21508
  1028.7 19.7 %copy-start.28 = (f32[1792]{0:T(1024)S(1)}, f32[1792]{0:T(1024)}, u32[]{:S(2)}) copy-start(f32[1792]{0:T(1024)} %copy-done.27) | copy-start | bytes 21508
  1028.7 19.7 %copy-start.30 = (f32[1792]{0:T(1024)S(1)}, f32[1792]{0:T(1024)}, u32[]{:S(2)}) copy-start(f32[1792]{0:T(1024)} %copy-done.29) | copy-start | bytes 21508
  1028.7 19.7 %copy-start.32 = (f32[1792]{0:T(1024)S(1)}, f32[1792]{0:T(1024)}, u32[]{:S(2)}) copy-start(f32[1792]{0:T(1024)} %copy-done.31) | copy-start | bytes 21508
  1060.3 15.0 copy-start.10
  1060.3 15.0 copy-start.51
  1060.3 15.0 copy-start.53
  1060.3 15.0 copy-start.61
  1128.4 91.9 %copy-start.59 = (f32[24]{0:T(128)S(1)}, f32[24]{0:T(128)}, u32[]{:S(2)}) copy-start(f32[24]{0:T(128)} %get-tuple-element.474) | copy-start | bytes 292
  1128.4 95.2 %copy-start.62 = (f32[1536]{0:T(1024)S(1)}, f32[1536]{0:T(1024)}, u32[]{:S(2)}) copy-start(f32[1536]{0:T(1024)} %get-tuple-element.783) | copy-start | bytes 18436
  1267.2 265.1 %copy-start.65 = (f32[2]{0:T(128)S(1)}, f32[2]{0:T(128)}, u32[]{:S(2)}) copy-start(f32[2]{0:T(128)} %param.24) | copy-start | bytes 28
  1267.3 410.9 %all-reduce.24.cloned.1.call-start = ((), (), s32[]{:S(2)}) async-start(), calls=%async_computation.4 | async-start | bytes 7536640 | tf_op jit(solution)/shard_map/psum | solution.py:293
  1531.6 365.9 %all-gather.5.cloned.1.call-start = ((), (), s32[]{:S(2)}) async-start(), calls=%async_computation.5 | async-start | bytes 18841600 | tf_op jit(solution)/shard_map/all_gather | solution.py:297
  1731.6 75.9 %all-to-all-start.1 = ((bf16[2,1024,768]{2,0,1:T(2,128)(2,1)}), bf16[2,1024,768]{2,0,1:T(2,128)(2,1)}, u32[]{:S(2)}, u32[]{:S(2)}) async-start(bf16[2,1024,768]{2,0,1:T(2,128)(2,1)} %copy.241), calls=%async_computation.1 | async-start | bytes 6291456 | tf_op jit(solution)/shard_map/all_to_all | solution.py:271
  1736.3 74.8 %copy-start.56 = (s32[8,2]{1,0:T(8,128)S(1)}, s32[8,2]{1,0:T(8,128)}, u32[]{:S(2)}) copy-start(s32[8,2]{1,0:T(8,128)} %get-tuple-element.789) | copy-start | bytes 196
  1807.4 74.5 %all-to-all-start.2 = ((bf16[2,1024,768]{2,0,1:T(2,128)(2,1)}), bf16[2,1024,768]{2,0,1:T(2,128)(2,1)S(1)}, u32[]{:S(2)}, u32[]{:S(2)}) async-start(bf16[2,1024,768]{2,0,1:T(2,128)(2,1)} %copy.255), calls=%async_computation.2 | async-start | bytes 6291456 | tf_op jit(solution)/shard_map/all_to_all | solution.py:272
  (60 other events, 475.6 us)
Sparse Core Ops, SparseCore 0:
  11.0 56.1 all-gather.2
  1267.4 259.9 all-reduce.25
  1532.1 145.9 all-reduce.23
  1689.8 95.2 all-gather.4
where the time goes:
time: 1950 us; the launch traced here: 1920 us
  local copies, waits for them, and re-layouts  772 us (40%)
  waiting for transfers between devices  604 us (31%)
  matrix products  276 us (14%)
  other arithmetic  221 us (11%)
    dynamic_update_slice x28, local copies, waits for them, and re-layouts, span_scan(): lax.scan(jax.checkpoint(advance), initial, (split_blocks(x_heads), split_...  324 us
    unnamed x5, waiting for transfers between devices  258 us
    unnamed x130, local copies, waits for them, and re-layouts  167 us
    psum x1, waiting for transfers between devices, on_device(): grad_shard = lax.psum(grad_shard, 'dp')  145 us
    dot_general x12, matrix products, advance(): jnp.einsum('shtr,srhp->sthp', mixing, x_blk, precision=EXACT_MATMUL)  113 us
    all_to_all x1, waiting for transfers between devices, on_device(): lax.all_to_all(dealt_rows, 'dp', split_axis=0, concat_axis=1, tiled=True)  68.9 us
    all_to_all x1, waiting for transfers between devices, on_device(): lax.all_to_all(result, 'dp', split_axis=1, concat_axis=0, tiled=True)  66.2 us
    all_to_all x1, waiting for transfers between devices, on_device(): lax.all_to_all(grad_input, 'dp', split_axis=1, concat_axis=0, tiled=True)  65.8 us
  transfers between devices with their start and end apart: 7, of which 5 were waited for; matrix products, arithmetic and copies ran while one was open for 5% of the time, Pallas kernels for 0%

commit v1 on v0

v1 whole, which is shorter than its diff:
```python
import jax
import jax.numpy as jnp
from jax import lax
from jax.experimental import pallas as pl
from jax.experimental.pallas import tpu as pltpu
from jax.sharding import PartitionSpec as P

D = 768
HEADS = 24
HEADDIM = 64
STATE = 128
CONV = 4
INNER = 1536
XBC = 1792
PROJ = 3352
Q = 128
LATE = PROJ - INNER
WINDOW = 1024
PAIRS = HEADS // 2
EPS_NORM = 1e-05
NEG = -1e30
F32 = jnp.float32
BF16 = jnp.bfloat16


def dot(a, b):
    return lax.dot_general(a, b, (((1,), (0,)), ((), ())), preferred_element_type=F32)


def dot_nt(a, b):
    return lax.dot_general(a, b, (((1,), (1,)), ((), ())), preferred_element_type=F32)


def split2(v):
    hi = v.astype(BF16)
    return hi, (v - hi.astype(F32)).astype(BF16)


def split3(v):
    hi = v.astype(BF16)
    rest = v - hi.astype(F32)
    mid = rest.astype(BF16)
    return hi, mid, (rest - mid.astype(F32)).astype(BF16)


def wide_left(v):
    hi, lo = split2(v)
    return jnp.concatenate([hi, lo, hi], axis=1)


def tall_right(v):
    hi, lo = split2(v)
    return jnp.concatenate([hi, hi, lo], axis=0)


def exact_left(v):
    return jnp.concatenate(split3(v), axis=1)


def sigmoid(v):
    return 1.0 / (1.0 + jnp.exp(-v))


def softplus(v):
    return jnp.maximum(v, 0.0) + jnp.log1p(jnp.exp(-jnp.abs(v)))


def iota(shape, dim):
    return lax.broadcasted_iota(jnp.int32, shape, dim)


def expand(v, e_ref):
    hi, lo = split2(v)
    return dot(jnp.concatenate([hi, lo], axis=1), e_ref[...])


def head_sum(v, et_ref):
    hi, lo = split2(v)
    return dot(hi, et_ref[...]) + dot(lo, et_ref[...])


def chunk_masks(t0, bound):
    rows = t0 + iota((Q, 1), 0)
    rr = t0 + iota((Q, Q), 0)
    cc = t0 + iota((Q, Q), 1)
    return rows, rr, cc


def conv_rows(ext_ref, w_ref, b_ref, rows, bound):
    total = b_ref[...] + w_ref[3:4, :] * ext_ref[8 : 8 + Q, :]
    for back in (1, 2, 3):
        ok = jnp.logical_or(rows - back >= bound, rows < bound).astype(F32)
        total = total + w_ref[3 - back : 4 - back, :] * (ext_ref[8 - back : 8 - back + Q, :] * ok)
    return total


def decay_parts(dt_raw, dtb_ref, alog_ref, rr, cc):
    dt_in = dt_raw + dtb_ref[...]
    dt_pos = softplus(dt_in)
    rate = -jnp.exp(alog_ref[...])
    step = dt_pos * rate
    tri = (cc <= rr).astype(F32).astype(BF16)
    s_hi, s_mid, s_lo = split3(step)
    cum = dot(tri, s_hi) + dot(tri, s_mid) + dot(tri, s_lo)
    return dt_in, dt_pos, rate, cum


def forward_kernel(
    bound_ref, z_ref, proj_ref, gm_ref, e_ref, et_ref, convw_ref, convb_ref, dtb_ref, alog_ref,
    skip_ref, gain_ref,
    pair_ref, dy_ref, through_ref, state_ref, ggain_ref,
    ext_ref, dt_ref, carry_ref, xd_ref, acc_ref, cumt_ref,
):
    step = pl.program_id(0)
    bound = bound_ref[0]
    t0 = step * Q

    @pl.when(step == 0)
    def _():
        ext_ref[0:8, :] = jnp.zeros((8, XBC), F32)
        carry_ref[...] = jnp.zeros_like(carry_ref)
        dt_ref[...] = jnp.zeros_like(dt_ref)
        ggain_ref[...] = jnp.zeros_like(ggain_ref)

    rows, rr, cc = chunk_masks(t0, bound)
    ext_ref[8 : 8 + Q, :] = proj_ref[:, :XBC]
    pre = conv_rows(ext_ref, convw_ref, convb_ref, rows, bound)
    ext_ref[0:8, :] = ext_ref[Q : Q + 8, :]
    conv_out = pre * sigmoid(pre)
    x = conv_out[:, :INNER]
    b_rows = conv_out[:, INNER : INNER + STATE]
    c_rows = conv_out[:, INNER + STATE :]
    dt_ref[:, 0:HEADS] = proj_ref[:, XBC:LATE]
    _, dt_pos, _, cum = decay_parts(dt_ref[...], dtb_ref, alog_ref, rr, cc)
    cum_end = cum[Q - 1 : Q, :]
    keep = jnp.logical_or(rows < bound, bound < t0).astype(F32)
    in_last = jnp.logical_or(rows >= bound, bound > t0 + Q - 1).astype(F32)
    whole = jnp.logical_or(bound < t0, bound > t0 + Q - 1).astype(F32)
    from_start = jnp.exp(cum) * keep
    to_end = jnp.exp(cum_end - cum) * in_last
    carry_scale = jnp.exp(cum_end) * whole
    allowed = jnp.logical_and(cc <= rr, (cc >= bound) == (rr >= bound))
    cumt_ref[...] = cum.T

    state = carry_ref[...]
    state_ref[0] = state
    xd = x * expand(dt_pos, e_ref)
    xd_ref[...] = xd
    acc = dot(wide_left(c_rows), tall_right(state)) * expand(from_start, e_ref)
    acc_ref[...] = acc + skip_ref[...] * x
    b_t = b_rows.T
    scale_all = expand(jnp.broadcast_to(carry_scale, (Q, Q)), e_ref)
    carry_ref[...] = state * scale_all + dot(
        wide_left(b_t), tall_right(xd * expand(to_end, e_ref))
    )
    gram = dot(wide_left(c_rows), tall_right(b_t))
    first = iota((Q, Q), 1) < HEADDIM
    for pair in range(PAIRS):
        parts = []
        for head in (2 * pair, 2 * pair + 1):
            differ = cum[:, head : head + 1] - cumt_ref[head : head + 1, :]
            parts.append(gram * jnp.exp(jnp.where(allowed, differ, NEG)))
        left = jnp.concatenate(split2(jnp.concatenate(parts, axis=1)), axis=0)
        lanes = slice(pair * 128, pair * 128 + 128)
        xp = xd_ref[:, lanes]
        diag = jnp.concatenate([jnp.where(first, xp, 0.0), jnp.where(first, 0.0, xp)], axis=0)
        out = dot(left, jnp.concatenate(split2(diag), axis=1))
        acc_ref[:, lanes] += out[:Q, :128] + (out[:Q, 128:] + out[Q:, :128])
    scanned = acc_ref[...]
    z = z_ref[...]
    sig_z = sigmoid(z)
    silu_z = z * sig_z
    gated = scanned * silu_z
    ginv = lax.rsqrt(jnp.mean(gated * gated, axis=1, keepdims=True) + EPS_NORM)
    mhat = gated * ginv
    pair_ref[1] = (mhat * gain_ref[...]).astype(BF16)
    gm = gm_ref[...]
    ggain_ref[...] += jnp.sum(mhat * gm, axis=0, keepdims=True)
    gmg = gm * gain_ref[...]
    ggated = ginv * (gmg - mhat * jnp.mean(mhat * gmg, axis=1, keepdims=True))
    dy = ggated * silu_z
    dy_ref[...] = dy
    pair_ref[0] = (ggated * scanned * (sig_z * (1.0 + z * (1.0 - sig_z)))).astype(BF16)
    through_ref[...] = head_sum(dy * (scanned - skip_ref[...] * x), et_ref)


def const_spec(shape):
    return pl.BlockSpec(shape, lambda *_: (0,) * len(shape))


def run_forward(z, proj, gm, bound, e2, et, params):
    n = proj.shape[0]
    steps = n // Q
    return pl.pallas_call(
        forward_kernel,
        grid=(steps,),
        in_specs=[
            pl.BlockSpec(memory_space=pltpu.SMEM),
            pl.BlockSpec((Q, INNER), lambda i: (i, 0)),
            pl.BlockSpec((Q, LATE), lambda i: (i, 0)),
            pl.BlockSpec((Q, INNER), lambda i: (i, 0)),
            const_spec((256, INNER)), const_spec((INNER, 128)),
            const_spec((8, XBC)), const_spec((1, XBC)), const_spec((1, 128)),
            const_spec((1, 128)), const_spec((1, INNER)), const_spec((1, INNER)),
        ],
        out_specs=[
            pl.BlockSpec((2, Q, INNER), lambda i: (0, i, 0)),
            pl.BlockSpec((Q, INNER), lambda i: (i, 0)),
            pl.BlockSpec((Q, 128), lambda i: (i, 0)),
            pl.BlockSpec((1, STATE, INNER), lambda i: (i, 0, 0)),
            const_spec((1, INNER)),
        ],
        out_shape=[
            jax.ShapeDtypeStruct((2, n, INNER), BF16),
            jax.ShapeDtypeStruct((n, INNER), F32),
            jax.ShapeDtypeStruct((n, 128), F32),
            jax.ShapeDtypeStruct((steps, STATE, INNER), F32),
            jax.ShapeDtypeStruct((1, INNER), F32),
        ],
        scratch_shapes=[
            pltpu.VMEM((Q + 8, XBC), F32),
            pltpu.VMEM((Q, 128), F32),
            pltpu.VMEM((STATE, INNER), F32),
            pltpu.VMEM((Q, INNER), F32),
            pltpu.VMEM((Q, INNER), F32),
            pltpu.VMEM((128, Q), F32),
        ],
        compiler_params=pltpu.CompilerParams(
            dimension_semantics=("arbitrary",), vmem_limit_bytes=48 * 2**20),
        cost_estimate=pl.CostEstimate(
            flops=30 * 10**9, bytes_accessed=40 * 2**20, transcendentals=10**7),
    )(bound, z, proj, gm, e2, et, *params)


def backward_kernel(
    bound_ref, proj_ref, before_ref, dy_ref, through_ref, state_ref,
    e_ref, et_ref, convw_ref, convb_ref, dtb_ref, alog_ref, skip_ref,
    gp_ref, window_ref, small_ref,
    gskip_ref, gsmall_ref, ext_ref, dt_ref, lam_ref, dsum_ref, xd_ref, g_ref, gnext_ref, cumt_ref,
):
    step = pl.program_id(0)
    steps = pl.num_programs(0)
    bound = bound_ref[0]
    t0 = (steps - 1 - step) * Q

    @pl.when(step == 0)
    def _():
        lam_ref[...] = jnp.zeros_like(lam_ref)
        dsum_ref[...] = jnp.zeros_like(dsum_ref)
        dt_ref[...] = jnp.zeros_like(dt_ref)
        gnext_ref[Q : Q + 8, :] = jnp.zeros((8, XBC), F32)
        gskip_ref[...] = jnp.zeros_like(gskip_ref)
        small_ref[...] = jnp.zeros_like(small_ref)
        gsmall_ref[...] = jnp.zeros_like(gsmall_ref)

    rows, rr, cc = chunk_masks(t0, bound)
    dy = dy_ref[...]
    first_chunk = (t0 > 0).astype(F32)
    ext_ref[0:8, :] = before_ref[:, :XBC] * first_chunk
    ext_ref[8 : 8 + Q, :] = proj_ref[:, :XBC]
    pre = conv_rows(ext_ref, convw_ref, convb_ref, rows, bound)
    sig_pre = sigmoid(pre)
    conv_out = pre * sig_pre
    x = conv_out[:, :INNER]
    b_rows = conv_out[:, INNER : INNER + STATE]
    c_rows = conv_out[:, INNER + STATE :]
    dt_ref[:, 0:HEADS] = proj_ref[:, XBC:LATE]
    dt_in, dt_pos, rate, cum = decay_parts(dt_ref[...], dtb_ref, alog_ref, rr, cc)
    cum_end = cum[Q - 1 : Q, :]
    keep = jnp.logical_or(rows < bound, bound < t0).astype(F32)
    in_last = jnp.logical_or(rows >= bound, bound > t0 + Q - 1).astype(F32)
    whole = jnp.logical_or(bound < t0, bound > t0 + Q - 1).astype(F32)
    from_start = jnp.exp(cum) * keep
    to_end = jnp.exp(cum_end - cum) * in_last
    carry_scale = jnp.exp(cum_end) * whole
    allowed_t = jnp.logical_and(rr <= cc, (cc >= bound) == (rr >= bound))
    cumt_ref[...] = cum.T
    c_t = c_rows.T
    gram_t = dot(wide_left(b_rows), tall_right(c_t))
    dt_all = expand(dt_pos, e_ref)
    end_all = expand(to_end, e_ref)
    xd = x * dt_all
    xd_ref[...] = xd
    skip = skip_ref[...]
    gskip_ref[...] += jnp.sum(dy * x, axis=0, keepdims=True)
    lam = lam_ref[...]
    lam_hi, lam_lo = split2(lam)
    g_ref[...] = (
        dot(wide_left(b_rows), jnp.concatenate([lam_hi, lam_hi, lam_lo], axis=0)) * end_all
    )
    xw_hi, xw_lo = split2(xd * end_all)
    grad_b = dot_nt(xw_hi, lam_hi) + (dot_nt(xw_hi, lam_lo) + dot_nt(xw_lo, lam_hi))
    state = state_ref[0]
    st_hi, st_lo = split2(state)
    dye = dy * expand(from_start, e_ref)
    dye_hi, dye_lo = split2(dye)
    grad_c = dot_nt(dye_hi, st_hi) + (dot_nt(dye_hi, st_lo) + dot_nt(dye_lo, st_hi))
    scale_all = expand(jnp.broadcast_to(carry_scale, (Q, Q)), e_ref)
    lam_new = lam * scale_all + dot(
        wide_left(c_t), jnp.concatenate([dye_hi, dye_hi, dye_lo], axis=0)
    )
    lam_ref[...] = lam_new
    ended = dsum_ref[0:1, :]
    first = iota((Q, Q), 1) < HEADDIM
    first_row = iota((Q, Q), 0) < HEADDIM
    gram_grad = jnp.zeros((Q, Q), F32)
    for pair in range(PAIRS):
        lanes = slice(pair * 128, pair * 128 + 128)
        weights = []
        for head in (2 * pair, 2 * pair + 1):
            differ = cumt_ref[head : head + 1, :] - cum[:, head : head + 1]
            weights.append(jnp.exp(jnp.where(allowed_t, differ, NEG)))
        left = jnp.concatenate([gram_t * weights[0], gram_t * weights[1]], axis=1)
        left = jnp.concatenate(split2(left), axis=0)
        dyp = dy_ref[:, lanes]
        diag = jnp.concatenate([jnp.where(first, dyp, 0.0), jnp.where(first, 0.0, dyp)], axis=0)
        out = dot(left, jnp.concatenate(split2(diag), axis=1))
        g_ref[:, lanes] += out[:Q, :128] + (out[:Q, 128:] + out[Q:, :128])
        dyt = dyp.T
        right = jnp.concatenate(
            [jnp.where(first_row, dyt, 0.0), jnp.where(first_row, 0.0, dyt)], axis=1)
        outer = dot(wide_left(xd_ref[:, lanes]), tall_right(right))
        gram_grad = gram_grad + (outer[:, :128] * weights[0] + outer[:, 128:] * weights[1])
    g = g_ref[...]
    grad_x = dt_all * g + skip * dy
    direct = head_sum(x * g, et_ref)
    balance = through_ref[...] - dt_pos * direct
    keep_t = allowed_t.astype(F32).astype(BF16)
    b_hi, b_mid, b_lo = split3(balance)
    grad_step = dot(keep_t, b_hi) + dot(keep_t, b_mid) + dot(keep_t, b_lo) + in_last * ended
    dsum_ref[...] = head_sum(
        jnp.broadcast_to(jnp.sum(lam_new * state, axis=0, keepdims=True), (8, INNER)), et_ref)
    grad_dt = (direct + rate * grad_step) * sigmoid(dt_in)
    gsmall_ref[0:1, :] += jnp.sum(grad_dt, axis=0, keepdims=True)
    gsmall_ref[1:2, :] += rate * jnp.sum(dt_pos * grad_step, axis=0, keepdims=True)
    gp_ref[:, XBC:LATE] = grad_dt[:, 0:HEADS].astype(BF16)
    grad_c = grad_c + dot(wide_left(gram_grad.T), tall_right(b_rows))
    grad_b = grad_b + dot(wide_left(gram_grad), tall_right(c_rows))
    slope = sig_pre * (1.0 + pre * (1.0 - sig_pre))
    gnext_ref[0:Q, :INNER] = grad_x * slope[:, :INNER]
    gnext_ref[0:Q, INNER : INNER + STATE] = grad_b * slope[:, INNER : INNER + STATE]
    gnext_ref[0:Q, INNER + STATE :] = grad_c * slope[:, INNER + STATE :]
    gcp = gnext_ref[0:Q, :]
    small_ref[4:5, :] += jnp.sum(gcp, axis=0, keepdims=True)
    small_ref[3:4, :] += jnp.sum(gcp * ext_ref[8 : 8 + Q, :], axis=0, keepdims=True)
    total = convw_ref[3:4, :] * gcp
    for back in (1, 2, 3):
        ok = jnp.logical_or(rows - back >= bound, rows < bound).astype(F32)
        small_ref[3 - back : 4 - back, :] += jnp.sum(
            gcp * (ext_ref[8 - back : 8 - back + Q, :] * ok), axis=0, keepdims=True)
        okn = jnp.logical_or(rows >= bound, rows + back < bound).astype(F32)
        total = total + convw_ref[3 - back : 4 - back, :] * (gnext_ref[back : back + Q, :] * okn)
    total = total.astype(BF16)
    gp_ref[:, :XBC] = total
    window_ref[0] = total[:, :WINDOW]
    window_ref[1] = total[:, XBC - WINDOW :]
    gnext_ref[Q : Q + 8, :] = gnext_ref[0:8, :]

    @pl.when(step == steps - 1)
    def _():
        skips = head_sum(jnp.broadcast_to(gskip_ref[...], (8, INNER)), et_ref)
        small_ref[6:7, D : D + 128] = gsmall_ref[0:1, :]
        small_ref[6:7, D + 128 : D + 256] = gsmall_ref[1:2, :]
        small_ref[6:7, D + 256 : D + 384] = skips[0:1, :]


def run_backward(proj, dy, through, states, bound, e2, et, params):
    n = proj.shape[0]
    steps = n // Q

    def rev(i):
        return (steps - 1 - i, 0)

    return pl.pallas_call(
        backward_kernel,
        grid=(steps,),
        in_specs=[
            pl.BlockSpec(memory_space=pltpu.SMEM),
            pl.BlockSpec((Q, LATE), rev),
            pl.BlockSpec((8, LATE), lambda i: (jnp.maximum((steps - 1 - i) * (Q // 8) - 1, 0), 0)),
            pl.BlockSpec((Q, INNER), rev),
            pl.BlockSpec((Q, 128), rev),
            pl.BlockSpec((1, STATE, INNER), lambda i: (steps - 1 - i, 0, 0)),
            const_spec((256, INNER)), const_spec((INNER, 128)),
            const_spec((8, XBC)), const_spec((1, XBC)), const_spec((1, 128)),
            const_spec((1, 128)), const_spec((1, INNER)),
        ],
        out_specs=[
            pl.BlockSpec((Q, LATE), rev),
            pl.BlockSpec((2, Q, WINDOW), lambda i: (0, steps - 1 - i, 0)),
            const_spec((8, XBC)),
        ],
        out_shape=[
            jax.ShapeDtypeStruct((n, LATE), BF16),
            jax.ShapeDtypeStruct((2, n, WINDOW), BF16),
            jax.ShapeDtypeStruct((8, XBC), F32),
        ],
        scratch_shapes=[
            pltpu.VMEM((1, INNER), F32),
            pltpu.VMEM((8, 128), F32),
            pltpu.VMEM((Q + 8, XBC), F32),
            pltpu.VMEM((Q, 128), F32),
            pltpu.VMEM((STATE, INNER), F32),
            pltpu.VMEM((8, 128), F32),
            pltpu.VMEM((Q, INNER), F32),
            pltpu.VMEM((Q, INNER), F32),
            pltpu.VMEM((Q + 8, XBC), F32),
            pltpu.VMEM((128, Q), F32),
        ],
        compiler_params=pltpu.CompilerParams(
            dimension_semantics=("arbitrary",), vmem_limit_bytes=48 * 2**20),
        cost_estimate=pl.CostEstimate(
            flops=50 * 10**9, bytes_accessed=50 * 2**20, transcendentals=2 * 10**7),
    )(bound, proj, proj, dy, through, states, e2, et, *params[:5])


BETA_ONE = 0.9
BETA_TWO = 0.95
EPS_ADAM = 1e-08
LANES = 128
NORM_ROWS = D // LANES
IN_ROWS = PROJ * D // LANES
CONVW_ROWS = CONV * XBC // LANES
CONVB_ROWS = XBC // LANES
GAIN_ROWS = INNER // LANES
OUT_ROWS = INNER * D // LANES
DT_ROWS = HEADS * D // LANES
SMALL_ROWS = DT_ROWS + CONVW_ROWS + CONVB_ROWS + 3 + GAIN_ROWS
OUT_START = NORM_ROWS + IN_ROWS + SMALL_ROWS - DT_ROWS
LATE_START = NORM_ROWS + INNER * NORM_ROWS
LEAD = 896
STAGE_ROWS = 16264
ADAM_BLOCKS = 10
F16_TOP = 30000.0


PREP_STEPS = 7
IN_BLOCK = 512
OUT_BLOCK = 256
SMALL_START = NORM_ROWS + IN_ROWS


def prepare_kernel(
    flat_ref,
    in_ref, out_ref, norm_ref, convw_ref, convb_ref, dtb_ref, alog_ref, skip_ref, gain_ref,
    e_ref, et_ref,
    stage_ref,
):
    step = pl.program_id(0)

    @pl.when(step == 0)
    def _():
        rows = flat_ref[0:16, :].astype(F32)
        for lane in range(NORM_ROWS):
            norm_ref[:, lane * LANES : lane * LANES + LANES] = rows[lane : lane + 1, :]
        low = SMALL_START // 16 * 16
        stage_ref[0:112, :] = flat_ref[low : low + 112, :].astype(F32)
        at = SMALL_START - low
        convw_ref[...] = jnp.zeros_like(convw_ref)
        for tap in range(CONV):
            for lane in range(CONVB_ROWS):
                convw_ref[tap : tap + 1, lane * LANES : lane * LANES + LANES] = stage_ref[
                    at : at + 1, :]
                at += 1
        for lane in range(CONVB_ROWS):
            convb_ref[:, lane * LANES : lane * LANES + LANES] = stage_ref[at : at + 1, :]
            at += 1
        heads = iota((1, LANES), 1) < HEADS
        dtb_ref[...] = jnp.where(heads, stage_ref[at : at + 1, :], 0.0)
        alog_ref[...] = jnp.where(heads, stage_ref[at + 1 : at + 2, :], 0.0)
        skips = jnp.where(heads, stage_ref[at + 2 : at + 3, :], 0.0)
        at += 3
        for lane in range(GAIN_ROWS):
            gain_ref[:, lane * LANES : lane * LANES + LANES] = stage_ref[at : at + 1, :]
            at += 1
        one = (iota((128, INNER), 1) // HEADDIM == iota((128, INNER), 0)).astype(F32).astype(BF16)
        e_ref[0:128, :] = one
        e_ref[128:256, :] = one
        et_ref[...] = (
            iota((INNER, 128), 0) // HEADDIM == iota((INNER, 128), 1)).astype(F32).astype(BF16)
        skip_ref[...] = dot(jnp.broadcast_to(skips, (16, LANES)).astype(BF16), one)[0:1, :]

    def block(start, offset, rows, dest_ref):
        size = rows * NORM_ROWS + 16
        at = pl.multiple_of(start + step * (rows * NORM_ROWS), 16)
        stage_ref[0:size, :] = flat_ref[pl.ds(at, size), :].astype(F32)
        for lane in range(NORM_ROWS):
            dest_ref[:, lane * LANES : lane * LANES + LANES] = stage_ref[
                pl.ds(offset + lane, rows, stride=NORM_ROWS), :].astype(BF16)

    block(0, NORM_ROWS, IN_BLOCK, in_ref)

    @pl.when(step < INNER // OUT_BLOCK)
    def _():
        low = OUT_START // 16 * 16
        block(low, OUT_START - low, OUT_BLOCK, out_ref)


def run_prepare(flat):
    vector = lambda n: jax.ShapeDtypeStruct((1, n), F32)
    return pl.pallas_call(
        prepare_kernel,
        grid=(PREP_STEPS,),
        in_specs=[const_spec(flat.shape)],
        out_specs=[
            pl.BlockSpec((IN_BLOCK, D), lambda i: (i, 0)),
            pl.BlockSpec((OUT_BLOCK, D), lambda i: (jnp.minimum(i, INNER // OUT_BLOCK - 1), 0)),
            const_spec((1, D)), const_spec((8, XBC)), const_spec((1, XBC)), const_spec((1, 128)),
            const_spec((1, 128)), const_spec((1, INNER)), const_spec((1, INNER)),
            const_spec((256, INNER)), const_spec((INNER, 128)),
        ],
        out_shape=[
            jax.ShapeDtypeStruct((PROJ, D), BF16), jax.ShapeDtypeStruct((INNER, D), BF16),
            vector(D), jax.ShapeDtypeStruct((8, XBC), F32), vector(XBC), vector(128), vector(128),
            vector(INNER), vector(INNER),
            jax.ShapeDtypeStruct((256, INNER), BF16), jax.ShapeDtypeStruct((INNER, 128), BF16),
        ],
        scratch_shapes=[pltpu.VMEM((IN_BLOCK * NORM_ROWS + 16, LANES), F32)],
        compiler_params=pltpu.CompilerParams(
            dimension_semantics=("arbitrary",), vmem_limit_bytes=40 * 2**20),
        cost_estimate=pl.CostEstimate(
            flops=10**9, bytes_accessed=16 * 2**20, transcendentals=0),
    )(flat)


def adam_kernel(
    who_ref, rate_ref, early_ref, early_other_ref, late_ref, late_other_ref, small_ref,
    weight_ref, first_ref, second_ref,
    grad_ref, first_out_ref, second_out_ref, ratio_ref,
    stage_ref,
):
    step = pl.program_id(0)
    upper = who_ref[0]
    mine = who_ref[1]
    block = weight_ref.shape[0]
    half = 2 * block * ADAM_BLOCKS

    @pl.when(step == 0)
    def _():
        early_at = LEAD + jnp.where(upper == 1, OUT_START - half, NORM_ROWS)
        window = LATE_START + (XBC - WINDOW) * NORM_ROWS
        late_at = LEAD + jnp.where(upper == 1, window - half, LATE_START)
        for source_ref, at, which in (
            (late_ref, late_at, mine), (late_other_ref, late_at, 1 - mine),
            (early_ref, early_at, mine), (early_other_ref, early_at, 1 - mine),
        ):
            size = source_ref.shape[0]
            start = at + which * (size * NORM_ROWS)
            for lane in range(NORM_ROWS):
                stage_ref[pl.ds(start + lane, size, stride=NORM_ROWS), :] = source_ref[
                    :, lane * LANES : lane * LANES + LANES]

        @pl.when(upper == 0)
        def _():
            for lane in range(NORM_ROWS):
                stage_ref[LEAD + lane : LEAD + lane + 1, :] = small_ref[
                    6:7, lane * LANES : lane * LANES + LANES]

        @pl.when(upper == 1)
        def _():
            at = LEAD + OUT_START - half - SMALL_ROWS
            for lane in range(NORM_ROWS):
                stage_ref[pl.ds(at + lane, HEADS, stride=NORM_ROWS), :] = small_ref[
                    8 : 8 + HEADS, lane * LANES : lane * LANES + LANES]
            at += DT_ROWS
            places = [(k, j) for k in range(CONV + 1) for j in range(CONVB_ROWS)]
            places += [(6, NORM_ROWS + j) for j in range(3)]
            places += [(5, j) for j in range(GAIN_ROWS)]
            for number, (line, lane) in enumerate(places):
                stage_ref[at + number : at + number + 1, :] = small_ref[
                    line : line + 1, lane * LANES : lane * LANES + LANES]
            at = LEAD + OUT_START + OUT_ROWS - half
            stage_ref[at : LEAD + half, :] = jnp.zeros((LEAD + half - at, LANES), F32)

    @pl.when(step > 0)
    def _():
        at = LEAD + mine * (half // 2) + (step - 1) * block
        grad = stage_ref[pl.ds(pl.multiple_of(at, 8), block), :]
        grad_ref[...] = grad
        first = BETA_ONE * first_ref[...] + (1.0 - BETA_ONE) * grad
        second = BETA_TWO * second_ref[...] + (1.0 - BETA_TWO) * grad * grad
        first_out_ref[...] = first
        second_out_ref[...] = second
        ratio_ref[...] = (first * rate_ref[0]) / (jnp.sqrt(second * rate_ref[1]) + EPS_ADAM)


def run_adam(who, rates, early, early_other, late, late_other, small, weight, first, second):
    rows = weight.shape[0]
    block = rows // ADAM_BLOCKS

    def at(i):
        return (jnp.maximum(i - 1, 0), 0)

    spec = pl.BlockSpec((block, LANES), at)
    out = jax.ShapeDtypeStruct((rows, LANES), F32)
    return pl.pallas_call(
        adam_kernel,
        grid=(ADAM_BLOCKS + 1,),
        in_specs=[
            pl.BlockSpec(memory_space=pltpu.SMEM), pl.BlockSpec(memory_space=pltpu.SMEM),
            const_spec(early.shape), const_spec(early.shape),
            const_spec(late.shape), const_spec(late.shape), const_spec(small.shape),
            spec, spec, spec,
        ],
        out_specs=[spec, spec, spec, spec],
        out_shape=[out, out, out, out],
        scratch_shapes=[pltpu.VMEM((STAGE_ROWS, LANES), F32)],
        compiler_params=pltpu.CompilerParams(
            dimension_semantics=("arbitrary",), vmem_limit_bytes=48 * 2**20),
        cost_estimate=pl.CostEstimate(
            flops=10**8, bytes_accessed=36 * 2**20, transcendentals=10**6),
    )(who, rates, early, early_other, late, late_other, small, weight, first, second)


def swap(values, axis, bit):
    size = lax.axis_size(axis)
    return lax.ppermute(values, axis, [(i, i ^ bit) for i in range(size)])


def top_block(values):
    return jnp.broadcast_to(jnp.max(jnp.abs(values)), (8, LANES))


def to_wire(values, top):
    return (values * (F16_TOP / jnp.maximum(top[0, 0], 1e-30))).astype(jnp.float16)


def from_wire(values, top):
    return values.astype(F32) * (top[0, 0] * (1.0 / F16_TOP))


def halve(values, top, axis, bit):
    side = (lax.axis_index(axis) // bit) % 2
    keep = lax.dynamic_index_in_dim(values, side, 0, keepdims=False)
    send = lax.dynamic_index_in_dim(values, 1 - side, 0, keepdims=False)
    got = swap(to_wire(send, top), axis, bit)
    got_top = swap(top, axis, bit)
    return keep + from_wire(got, got_top), top + got_top


def data_bits():
    return [1 << k for k in range(lax.axis_size("dp").bit_length() - 1)]


def halve_data(values, top, bit):
    rows = values.shape[0] // 2
    return halve(values.reshape(2, rows, D), top, "dp", bit)


def double_data(wire, bit):
    side = (lax.axis_index("dp") // bit) % 2
    got = swap(wire, "dp", bit)
    return jnp.where(side == 0, jnp.concatenate([wire, got]), jnp.concatenate([got, wire]))


def dot_tn(a, b):
    return lax.dot_general(a, b, (((0,), (0,)), ((), ())), preferred_element_type=F32)


def pick_rows(index, rows):
    chosen = index[:, None] == jnp.arange(rows.shape[0], dtype=jnp.int32)[None, :]
    return dot(chosen.astype(BF16), rows).astype(BF16)


def on_device(
    tokens, loss_sensitivity, lengths, holder_sequence_list, master, moment_one, moment_two,
    adam_rates, iteration_tally,
):
    group_devices = lax.axis_size("zero")
    data_devices = lax.axis_size("dp")
    zero_index = lax.axis_index("zero")
    dp_index = lax.axis_index("dp")
    seq_len = loss_sensitivity.shape[1]
    group_seqs = tokens.shape[0]
    span = tokens.shape[1]
    slots = group_seqs // data_devices
    shard_rows = master.shape[0] // LANES
    tie = lax.optimization_barrier

    own = master.reshape(shard_rows, LANES)
    flat = lax.all_gather(own.astype(BF16), "zero", axis=0, tiled=True)

    arranged = holder_sequence_list.reshape(data_devices, group_devices, slots)
    group_order = lax.dynamic_index_in_dim(arranged, zero_index, 1, keepdims=False).reshape(-1)
    local_ids = group_order - zero_index * group_seqs
    dealt = tokens.at[local_ids].get(mode="promise_in_bounds")
    local_tok = lax.all_to_all(dealt, "dp", split_axis=0, concat_axis=0, tiled=True)
    my_seqs = lax.dynamic_slice_in_dim(group_order, dp_index * slots, slots)
    bound = lengths[my_seqs[0]]
    positions = jnp.arange(seq_len, dtype=jnp.int32)

    in_w, out_w, norm_gain, *params, e2, et = run_prepare(flat)
    cot = loss_sensitivity[0]
    gm = dot_nt(cot, out_w)
    local_tok, in_w, gm = tie((local_tok, in_w, gm))
    own_late, _ = tie((own, flat[:8]))
    whole_master = lax.all_gather(own_late, "zero", axis=0, tiled=True)

    def place(slot, at):
        return (at // span) * (slots * span) + slot * span + at % span

    source = jnp.where(positions < bound, place(0, positions), place(1, positions - bound))
    packed = pick_rows(source, local_tok.reshape(slots * seq_len, D))
    blocks = jnp.arange(data_devices, dtype=jnp.int32)[:, None, None] * span
    within = blocks + jnp.arange(span, dtype=jnp.int32)[None, None, :]
    within = within + jnp.arange(slots, dtype=jnp.int32)[None, :, None] * bound
    unpack_rows = jnp.minimum(within, seq_len - 1).reshape(-1)

    def spread(rows):
        return pick_rows(unpack_rows, rows).reshape(data_devices * slots, span, D)

    def send_back(picked):
        return lax.all_to_all(picked, "dp", split_axis=0, concat_axis=0, tiled=True)

    restore = jnp.zeros_like(local_ids).at[local_ids].set(
        jnp.arange(group_seqs, dtype=jnp.int32))
    mine = lax.dynamic_slice_in_dim(lengths, zero_index * group_seqs, group_seqs)
    at = dp_index * span + jnp.arange(span, dtype=jnp.int32)
    live = (at[None, :] < mine[:, None])[:, :, None]

    bound_arr = bound.reshape(1)
    tok = packed.astype(F32)
    rinv = lax.rsqrt(jnp.mean(tok * tok, axis=1, keepdims=True) + EPS_NORM)
    nhat = tok * rinv
    normed = (nhat * norm_gain).astype(BF16)
    proj_z = dot_nt(normed, in_w[:INNER])
    proj = dot_nt(normed, in_w[INNER:])
    pair, dy, through, states, ggain = run_forward(proj_z, proj, gm, bound_arr, e2, et, params)
    result = (tok + dot(pair[1], out_w)).astype(BF16)
    picked = spread(result)
    picked, pair = tie((picked, pair))
    back_out = send_back(picked)
    early = lax.dot_general(
        pair, jnp.stack([normed, cot]), (((1,), (1,)), ((0,), (0,))), preferred_element_type=F32)
    early = jnp.swapaxes(early.reshape(2, 2, INNER // 2, D), 0, 1)
    early, early_top = halve(early, top_block(early), "zero", 1)
    part_normed = dot(pair[0], in_w[:INNER])
    early, early_top, part_normed, dy = tie((early, early_top, part_normed, dy))
    early, early_top = halve(early, early_top, "zero", 2)
    gp, window, small8 = run_backward(proj, dy, through, states, bound_arr, e2, et, params)
    gp, window, back_out, early, early_top, whole_master = tie(
        (gp, window, back_out, early, early_top, whole_master))

    bits = data_bits()
    late = lax.dot_general(
        window, jnp.stack([normed, normed]), (((1,), (1,)), ((0,), (0,))),
        preferred_element_type=F32)
    late, gp = tie((late, gp))
    late = jnp.swapaxes(late.reshape(2, 2, WINDOW // 2, D), 0, 1)
    late, late_top = halve(late, top_block(late), "zero", 1)
    early, early_top = halve_data(early, early_top, bits[0])
    grad_normed = part_normed + dot(gp, in_w[INNER:])
    late, late_top, early, early_top, grad_normed = tie(
        (late, late_top, early, early_top, grad_normed))
    late, late_top = halve(late, late_top, "zero", 2)
    for bit in bits[1:-1]:
        early, early_top = halve_data(early, early_top, bit)
    gng = grad_normed * norm_gain
    grad_norm_gain = jnp.sum(nhat * grad_normed, axis=0, keepdims=True)
    grad_tok = cot.astype(F32) + rinv * (gng - nhat * jnp.mean(nhat * gng, axis=1, keepdims=True))
    grad_tok = grad_tok.astype(BF16)
    small8 = small8 + jnp.pad(ggain, ((5, 2), (0, XBC - INNER)))
    small8 = small8 + jnp.pad(grad_norm_gain, ((6, 1), (0, XBC - D)))
    small = jnp.concatenate([
        small8, jnp.pad(dot_tn(gp[:, XBC:], normed), ((0, 0), (0, XBC - D)))])
    late, late_top, early, early_top, small, grad_tok = tie(
        (late, late_top, early, early_top, small, grad_tok))
    late, late_top = halve_data(late, late_top, bits[0])
    early, early_top = halve_data(early, early_top, bits[-1])
    early = to_wire(early, early_top)
    small = small + swap(small, "dp", bits[0])
    picked_grad = spread(grad_tok)
    late, late_top, early, small, picked_grad = tie((late, late_top, early, small, picked_grad))
    for bit in bits[1:-1]:
        late, late_top = halve_data(late, late_top, bit)
        small = small + swap(small, "dp", bit)
        early = double_data(early, bits[-1]) if bit == bits[1] else early
    back_rows = back_out.at[restore].get(mode="promise_in_bounds")
    late, late_top, early, small, back_rows = tie((late, late_top, early, small, back_rows))
    late, late_top = halve_data(late, late_top, bits[-1])
    late = to_wire(late, late_top)
    for bit in reversed(bits[1:-1]):
        early = double_data(early, bit)
    small = small + swap(small, "dp", bits[-1])
    tokens_out = jnp.where(live, back_rows, tokens)
    late, early, small, tokens_out = tie((late, early, small, tokens_out))
    late = double_data(late, bits[-1])
    early = from_wire(double_data(early, bits[0]), early_top)
    small = small + swap(small, "zero", 1)
    late, early, small = tie((late, early, small))
    for bit in reversed(bits[1:-1]):
        late = double_data(late, bit)
    early_other = swap(early, "zero", 1)
    small = small + swap(small, "zero", 2)
    late, early_other, small = tie((late, early_other, small))
    late = from_wire(double_data(late, bits[0]), late_top)
    late, picked_grad = tie((late, picked_grad))
    late_other = swap(late, "zero", 1)
    back_grad = send_back(picked_grad)
    grad_tokens = jnp.where(
        live, back_grad.at[restore].get(mode="promise_in_bounds"), jnp.zeros((), BF16))

    steps_f = iteration_tally[0].astype(F32)
    rates = jnp.stack([
        1.0 / (1.0 - jnp.power(BETA_ONE, steps_f)), 1.0 / (1.0 - jnp.power(BETA_TWO, steps_f))])
    who = jnp.stack([zero_index // 2, zero_index % 2]).astype(jnp.int32)
    grad_shard, first_next, second_next, ratio = run_adam(
        who, rates, early, early_other, late, late_other, small,
        own, moment_one.reshape(shard_rows, LANES), moment_two.reshape(shard_rows, LANES))
    ratios = lax.all_gather(ratio.astype(jnp.float16), "zero", axis=0, tiled=True).astype(F32)
    new_master = whole_master - adam_rates[0] * (ratios + adam_rates[1] * whole_master)
    return (
        tokens_out, grad_tokens, new_master.reshape(-1), grad_shard.reshape(-1),
        first_next.reshape(-1), second_next.reshape(-1))


def solution(mesh):
    return jax.shard_map(
        on_device,
        mesh=mesh,
        in_specs=(
            P("zero", "dp", None), P(("dp", "zero"), None, None), P(), P(),
            P("zero"), P("zero"), P("zero"), P(), P(),
        ),
        out_specs=(
            P("zero", "dp", None), P("zero", "dp", None), P(), P("zero"), P("zero"), P("zero"),
        ),
        check_vma=False,
    )
```

time: 1950 us -> 517 us (0.27); the launches traced: 1920 us -> 508 us
  local copies, waits for them, and re-layouts: 772 us -> 36.7 us
  waiting for transfers between devices: 604 us -> 103 us
  matrix products: 276 us -> 73.2 us
  other arithmetic: 221 us -> 65.1 us
  Pallas kernels: 0 us -> 106 us
  blocking collectives: 0 us -> 45.6 us
  starting transfers between devices: 16 us -> 46.7 us
    dynamic_update_slice x28 -> x0, local copies, waits for them, and re-layouts: 324 us -> none  [span_scan(): lax.scan(jax.checkpoint(advance), initial, (split_blocks(x_heads), split_...]
    unnamed x5 -> x2, waiting for transfers between devices: 258 us -> 0.71 us
    dot_general x62 -> x11, matrix products: 276 us -> 73.2 us  [the longest x5 33.9 us: dot(): lax.dot_general(a, b, (((1,), (0,)), ((), ())), preferred_element_type=F32)]
    all_to_all x3, waiting for transfers between devices: 201 us -> 13.5 us  [the longest x1 9.89 us: on_device(): lax.all_to_all(dealt, 'dp', split_axis=0, concat_axis=0, tiled=True)]
    unnamed x130 -> x57, local copies, waits for them, and re-layouts: 167 us -> 10.7 us
    psum x1 -> x0, waiting for transfers between devices: 145 us -> none  [on_device(): grad_shard = lax.psum(grad_shard, 'dp')]
    pallas_call x0 -> x4, Pallas kernels: none -> 106 us  [the longest x1 48.7 us: run_backward(): pl.pallas_call(backward_kernel, grid=(steps,), in_specs=[pl.BlockSpec(mem...]
    reduce_sum x10 -> x1, other arithmetic: 49.4 us -> 0.96 us  [on_device(): jnp.mean(nhat * gng, axis=1, keepdims=True)]
  transfers between devices with their start and end apart: 7 -> 38, of which waited for: 5 -> 13; matrix products, arithmetic and copies ran while one was open for 5% -> 30% of each run, Pallas kernels for 0% -> 21%
where the time goes in v1:
time: 517 us; the launch traced here: 508 us
  Pallas kernels  106 us (21%)
  waiting for transfers between devices  103 us (20%)
  matrix products  73.2 us (14%)
  other arithmetic  65.1 us (13%)
  starting transfers between devices  46.7 us (9%)
  blocking collectives  45.6 us (9%)
  local copies, waits for them, and re-layouts  36.7 us (7%)
  between operations  32.1 us (6%)
    pallas_call x1, Pallas kernels, run_backward(): pl.pallas_call(backward_kernel, grid=(steps,), in_specs=[pl.BlockSpec(mem...  48.7 us
    ppermute x33, waiting for transfers between devices, swap(): return lax.ppermute(values, axis, [(i, i ^ bit) for i in range(size)])  48.2 us
    all_gather x1, blocking collectives, on_device(): lax.all_gather(ratio.astype(jnp.float16), 'zero', axis=0, tiled=True)  45.6 us
    all_gather x1, waiting for transfers between devices, on_device(): flat = lax.all_gather(own.astype(BF16), 'zero', axis=0, tiled=True)  40.5 us
    pallas_call x1, Pallas kernels, run_forward(): pl.pallas_call(forward_kernel, grid=(steps,), in_specs=[pl.BlockSpec(memo...  35 us
    dot_general x5, matrix products, dot(): lax.dot_general(a, b, (((1,), (0,)), ((), ())), preferred_element_type=F32)  33.9 us
    ppermute x33, starting transfers between devices, swap(): return lax.ppermute(values, axis, [(i, i ^ bit) for i in range(size)])  30.4 us
    dot_general x3, matrix products, dot_nt(): lax.dot_general(a, b, (((1,), (1,)), ((), ())), preferred_element_type=F32)  16 us
  transfers between devices with their start and end apart: 38, of which 13 were waited for; matrix products, arithmetic and copies ran while one was open for 30% of the time, Pallas kernels for 21%

profile of v1, /device:TPU:0, one launch (start us, length us, event | category | flops | bytes accessed | tf_op | source)
XLA Modules:
  0.0 507.9 jit_solution(11225207686939890339)
XLA Ops:
  7.2 3.5 bitcast_convert_fusion
  12.6 2.4 gather_fusion
  15.0 7.4 %all-to-all-start = ((bf16[16,128,768]{2,1,0:T(8,128)(2,1)}), bf16[16,128,768]{2,1,0:T(8,128)(2,1)}, u32[]{:S(2)}, u32[]{:S(2)}) async-start(bf16[16,128,768]{2,1,0:T(8,128)(2,1)} %gather_fusion), calls=%async_computation | async-start | bytes 6291456 | tf_op jit(solution)/shard_map/all_to_all | solution.py:687
  26.6 40.5 %all-gather.4.cloned.1.call-done.flat_ref = bf16[29440,128]{1,0:T(8,128)(2,1)} async-done(((bf16[7360,128]{1,0:T(8,128)(2,1)}), bf16[29440,128]{1,0:T(8,128)(2,1)}) %all-gather.4.cloned.1.call-update) | async-done | bytes 7536656 | tf_op jit(solution)/shard_map/all_gather | solution.py:681
  67.0 7.1 %shard_map.136 = (bf16[3352,768]{1,0:T(8,128)(2,1)S(1)}, bf16[1536,768]{1,0:T(8,128)(2,1)S(1)}, f32[1,768]{1,0:T(1,128)S(1)}, f32[8,1792]{1,0:T(8,128)S(1)}, f32...) custom-call(bf16[29440,128]{1,0:T(8,128)(2,1)} %all-gather.4.cloned., ...), custom_call_target="tpu_custom_call" | custom-call | flops 1000000000 | bytes 16777216 | tf_op jit(solution)/shard_map/pallas_call | solution.py:501
  74.2 2.6 copy-done
  78.4 4.9 fusion.42.gm_ref
  83.3 9.9 %all-to-all-done = bf16[16,128,768]{2,1,0:T(8,128)(2,1)} async-done(((bf16[16,128,768]{2,1,0:T(8,128)(2,1)}), bf16[16,128,768]{2,1,0:T(8,128)(2,1)}, u32[]{:S(2)}, u32[]{:S(2)}) %all-to-all-start) | async-done | bytes 3145760 | tf_op jit(solution)/shard_map/all_to_all | solution.py:687
  93.3 5.9 %fusion.21 = (f32[1024]{0:T(1024)S(1)}, bf16[1024,768]{0,1:T(8,128)(2,1)S(1)}) fusion(bf16[2048,768]{1,0:T(8,128)(2,1)} %bitcast.5, s32[1024]{0:T(1024)S(1)} %fusion.66), kind=kOutput, calls=%fused_computation.37 | convolution fusion | flops 3226467328 | bytes 4726784 | tf_op jit(solution)/shard_map/dot_general | solution.py:27
  99.2 5.0 fusion.37.z_ref
  104.2 6.1 %fusion.33.proj_ref.before_ref = f32[1024,1816]{1,0:T(8,128)} fusion(bf16[3352,768]{1,0:T(8,128)(2,1)S(1)} %bitcast.129, bf16[1024,768]{0,1:T(8,128)(2,1)S(1)} %get-tuple-element.159, f32[768]{0:T(1024)S(1)} %reduce.4, f32[1024]{0:T(1024)S(1)} %add_rsqrt_fusion), kind=kOutput, calls=%fused_computation.53 | convolution fusion | flops 2859466752 | bytes 11808768 | tf_op jit(solution)/shard_map/dot_general | solution.py:31
  110.3 35.0 %shard_map.137 = (bf16[2,1024,1536]{2,1,0:T(8,128)(2,1)}, f32[1024,1536]{1,0:T(8,128)}, f32[1024,128]{1,0:T(8,128)S(1)}, f32[8,128,1536]{2,1,0:T(8,128)}, f32[1,1536]{1,0:T(1,128)S(1)}) custom-call(s32[1]{0:T(128)} %dynamic_slice.77.bound_ref, f32[1024,1536]{1,0:T(8,128)} %fusion.37.z_ref, f32[1024,1816]{1,0:T(8,128)} %fusion.33.proj_ref.before_ref, ...), custom_call_target="tpu_custom_call" | custom-call | flops 30000001024 | bytes 41943040 | tf_op jit(solution)/shard_map/pallas_call | solution.py:194
  145.3 10.6 %fusion.10 = bf16[2048,768]{1,0:T(8,128)(2,1)} fusion(s32[2048]{0:T(1024)S(1)} %bitcast.148, bf16[1024,768]{0,1:T(8,128)(2,1)} %copy-done.10, bf16[1536,768]{1,0:T(8,128)(2,1)S(1)} %get-tuple-element.80, bf16[2,1024,1536]{2,1,0:T(8,128)(2,1)} %get-tuple-element.94), kind=kOutput, calls=%fused_computation.26 | convolution fusion | flops 5643173888 | bytes 10231808 | tf_op jit(solution)/shard_map/dot_general | solution.py:27
  157.8 12.7 %fusion.12 = f32[2,1536,768]{2,1,0:T(8,128)} fusion(bf16[2,1024,1536]{2,1,0:T(8,128)(2,1)} %get-tuple-element.94, bf16[1,1024,768]{1,2,0:T(8,128)(2,1)S(1)} %fusion.83, bf16[1,1024,768]{1,2,0:T(8,128)(2,1)S(1)} %copy-done.16), kind=kOutput, calls=%fused_computation.28 | convolution fusion | flops 4833411072 | bytes 18874368 | tf_op jit(solution)/shard_map/dot_general | solution.py:733
  170.5 4.9 abs_reduce_fusion
  176.1 4.2 fusion.35
  182.3 6.9 %fusion.25 = f32[1024,768]{1,0:T(8,128)} fusion(bf16[2,1024,1536]{2,1,0:T(8,128)(2,1)} %get-tuple-element.94, bf16[3352,768]{1,0:T(8,128)(2,1)} %copy-done), kind=kOutput, calls=%fused_computation.42 | convolution fusion | flops 2415919104 | bytes 8650752 | tf_op jit(solution)/shard_map/dot_general | solution.py:27
  189.2 4.4 all-to-all-start.1
  195.5 2.8 bitcast_add_fusion
  203.2 48.7 %shard_map.138 = (bf16[1024,1816]{1,0:T(8,128)(2,1)S(1)}, bf16[2,1024,1024]{2,1,0:T(8,128)(2,1)}, f32[8,1792]{1,0:T(8,128)S(1)}) custom-call(s32[1]{0:T(128)} %dynamic_slice.77.bound_ref, f32[1024,1816]{1,0:T(8,128)} %fusion.33.proj_ref.before_ref, f32[1024,1816]{1,0:T(8,128)} %fusion.33.proj_ref.before_ref, f32[1024,1536]{1,0:T(8,128)} %get-tuple-element.96.dy_ref, ...), custom_call_target="tpu_custom_call" | custom-call | flops 49999998976 | bytes 52428800 | tf_op jit(solution)/shard_map/pallas_call | solution.py:374
  253.8 2.5 copy.35
  257.5 3.7 bitcast_add_fusion.2
  261.2 3.6 all-to-all-done.1
  266.8 10.0 %fusion.13 = f32[2,1024,768]{2,1,0:T(8,128)} fusion(bf16[2,1024,1024]{2,1,0:T(8,128)(2,1)} %get-tuple-element.104, bf16[1,1024,768]{1,2,0:T(8,128)(2,1)} %copy-done.22), kind=kOutput, calls=%fused_computation.29 | convolution fusion | flops 3222798336 | bytes 12058624 | tf_op jit(solution)/shard_map/dot_general | solution.py:745
  279.0 3.8 abs_reduce_fusion.1
  283.5 2.3 fusion.40
  286.6 5.4 %fusion.31 = f32[1024,768]{0,1:T(8,128)S(1)} fusion(bf16[1024,1816]{1,0:T(8,128)(2,1)S(1)} %copy-done.8, bf16[3352,768]{1,0:T(8,128)(2,1)} %copy-done), kind=kOutput, calls=%fused_computation.51 | convolution fusion | flops 2856321024 | bytes 9654272 | tf_op jit(solution)/shard_map/dot_general | solution.py:27
  298.2 2.4 bitcast_add_fusion.1
  305.1 2.1 collective-permute-start.10
  312.1 2.2 collective-permute-done.10
  314.4 13.0 %collective-permute-done.8 = f16[512,768]{1,0:T(8,128)(2,1)S(1)} collective-permute-done((f16[512,768]{1,0:T(8,128)(2,1)S(1)}, f16[512,768]{1,0:T(8,128)(2,1)S(1)}, u32[]{:S(2)}, u32[]{:S(2)}) %collective-permute-start.8) | collective-permute-done | bytes 786464 | tf_op jit(solution)/shard_map/ppermute | solution.py:617
  331.2 2.7 collective-permute-start.14
  335.3 5.2 %fusion.11 = bf16[2048,768]{1,0:T(8,128)(2,1)} fusion(bf16[1024,768]{0,1:T(8,128)(2,1)S(1)} %fusion.20, s32[2048]{0:T(1024)S(1)} %bitcast.149), kind=kOutput, calls=%fused_computation.27 | convolution fusion | flops 3224895488 | bytes 4726784 | tf_op jit(solution)/shard_map/dot_general | solution.py:27
  345.6 3.0 collective-permute-done.16
  353.4 4.4 gather_fusion.1
  364.4 2.0 collective-permute-start.22
  371.2 3.3 broadcast_select_fusion.1
  376.9 3.9 collective-permute-done.21
  383.9 5.7 %collective-permute-done.25 = f16[64,768]{1,0:T(8,128)(2,1)S(1)} collective-permute-done((f16[64,768]{1,0:T(8,128)(2,1)S(1)}, f16[64,768]{1,0:T(8,128)(2,1)S(1)}, u32[]{:S(2)}, u32[]{:S(2)}) %collective-permute-start.25) | collective-permute-done | bytes 98336 | tf_op jit(solution)/shard_map/ppermute | solution.py:617
  389.7 3.6 collective-permute-done.26
  394.5 6.6 %collective-permute-done.28 = f16[128,768]{1,0:T(8,128)(2,1)S(1)} collective-permute-done((f16[128,768]{1,0:T(8,128)(2,1)S(1)}, f16[128,768]{1,0:T(8,128)(2,1)S(1)}, u32[]{:S(2)}, u32[]{:S(2)}) %collective-permute-start.28) | collective-permute-done | bytes 196640 | tf_op jit(solution)/shard_map/ppermute | solution.py:617
  405.6 8.0 %collective-permute-done.31 = f16[256,768]{1,0:T(8,128)(2,1)S(1)} collective-permute-done((f16[256,768]{1,0:T(8,128)(2,1)S(1)}, f16[256,768]{1,0:T(8,128)(2,1)S(1)}, u32[]{:S(2)}, u32[]{:S(2)}) %collective-permute-start.31) | collective-permute-done | bytes 393248 | tf_op jit(solution)/shard_map/ppermute | solution.py:617
  416.7 4.4 all-to-all-start.2
  421.1 14.8 %shard_map.139 = (f32[7360,128]{1,0:T(8,128)}, f32[7360,128]{1,0:T(8,128)}, f32[7360,128]{1,0:T(8,128)}, f32[7360,128]{1,0:T(8,128)}) custom-call(s32[2]{0:T(128)S(1)} %pad_add_fusion.1.who_ref, f32[2]{0:T(128)S(1)} %pad_maximum_fusion.4.rate_ref, f32[768,768]{1,0:T(8,128)S(1)} %convert_multiply_fusion.2.early_ref, f32[768,768]{1,0:T(8,128)} %copy-done.19, ...), custom_call_target="tpu_custom_call" | custom-call | flops 100000000 | bytes 37748736 | tf_op jit(solution)/shard_map/pallas_call | solution.py:596
  436.0 2.3 convert_element_type.192
  438.3 45.6 %all-gather.7 = f16[29440,128]{1,0:T(8,128)(2,1)S(1)} all-gather(f16[7360,128]{1,0:T(8,128)(2,1)S(1)} %convert_element_type.192), channel_id=1, replica_groups=mesh['dp'=8,'zero'=4] {'zero'}, dimensions={0}, use_global_device_ids=true | all-gather | bytes 9420800 | tf_op jit(solution)/shard_map/all_gather | solution.py:810
  483.9 12.4 %subtract_bitcast_fusion = f32[3768320]{0:T(1024)} fusion(f32[29440,128]{1,0:T(8,128)} %all-gather.6.cloned.1.call-done, f16[29440,128]{1,0:T(8,128)(2,1)S(1)} %all-gather.7, f32[]{:T(128)} %bitcast.67, f32[]{:T(128)} %bitcast.62), kind=kLoop, calls=%fused_computation.4 | loop fusion | flops 18841600 | bytes 37683208 | tf_op jit(solution)/shard_map/reshape | solution.py:813
  496.3 2.6 gather_fusion.2
  (211 shorter events, 68.7 us)
Async XLA Ops:
  7.2 59.9 %all-gather.4.cloned.1.call-start = ((), (), s32[]{:S(2)}) async-start(), calls=%async_computation.3 | async-start | bytes 9420800 | tf_op jit(solution)/shard_map/all_gather | solution.py:681
  10.7 254.1 %all-gather.6.cloned.1.call-start = ((), (), s32[]{:S(2)}) async-start(), calls=%async_computation.4 | async-start | bytes 18841600 | tf_op jit(solution)/shard_map/all_gather | solution.py:697
  15.0 7.6 %copy-start.20 = (bf16[1,1024,768]{2,1,0:T(8,128)(2,1)S(1)}, bf16[1,1024,768]{2,1,0:T(8,128)(2,1)}, u32[]{:S(2)}) copy-start(bf16[1,1024,768]{2,1,0:T(8,128)(2,1)} %param.10) | copy-start | bytes 4718596
  15.0 78.2 %all-to-all-start = ((bf16[16,128,768]{2,1,0:T(8,128)(2,1)}), bf16[16,128,768]{2,1,0:T(8,128)(2,1)}, u32[]{:S(2)}, u32[]{:S(2)}) async-start(bf16[16,128,768]{2,1,0:T(8,128)(2,1)} %gather_fusion), calls=%async_computation | async-start | bytes 6291456 | tf_op jit(solution)/shard_map/all_to_all | solution.py:687
  67.0 11.4 %copy-start.21 = (bf16[1,1024,768]{2,1,0:T(8,128)(2,1)S(1)}, bf16[1,1024,768]{2,1,0:T(8,128)(2,1)}, u32[]{:S(2)}) copy-start(bf16[1,1024,768]{2,1,0:T(8,128)(2,1)} %param.10) | copy-start | bytes 4718596
  78.4 20.8 %slice-start = ((s8[5148672]{0:T(1024)(128)(4,1)}), s8[954368]{0:T(1024)(128)(4,1)S(1)}, s32[]{:S(2)}) async-start(s8[5148672]{0:T(1024)(128)(4,1)} %bitcast.128), calls=%async_computation.5 | async-start | bytes 1908736
  104.2 6.1 %copy-start.2 = (bf16[256,1536]{1,0:T(8,128)(2,1)S(1)}, bf16[256,1536]{1,0:T(8,128)(2,1)}, u32[]{:S(2)}) copy-start(bf16[256,1536]{1,0:T(8,128)(2,1)} %copy-done.1) | copy-start | bytes 2359300
  104.2 6.1 %copy-start.5 = (bf16[1536,128]{1,0:T(8,128)(2,1)S(1)}, bf16[1536,128]{1,0:T(8,128)(2,1)}, u32[]{:S(2)}) copy-start(bf16[1536,128]{1,0:T(8,128)(2,1)} %copy-done.4) | copy-start | bytes 1179652
  157.8 12.7 %copy-start.22 = (bf16[1,1024,768]{1,2,0:T(8,128)(2,1)}, bf16[1,1024,768]{1,2,0:T(8,128)(2,1)S(1)}, u32[]{:S(2)}) copy-start(bf16[1,1024,768]{1,2,0:T(8,128)(2,1)S(1)} %fusion.83) | copy-start | bytes 4718596
  180.3 15.2 %collective-permute-start = (f16[2,768,768]{2,1,0:T(8,128)(2,1)}, f16[2,768,768]{2,1,0:T(8,128)(2,1)S(1)}, u32[]{:S(2)}, u32[]{:S(2)}) collective-permute-start(f16[2,768,768]{2,1,0:T(8,128)(2,1)} %fusion.35), channel_id=1, source_target_pairs={{0,1},{1,0},{2,3},{3,2},{4,5},{5,4},{6,7},{7,6},{8,9},{9,8},{10,11... | collective-permute-start | bytes 7077896 | tf_op jit(solution)/shard_map/ppermute | solution.py:617
  181.8 11.9 %collective-permute-start.1 = (f32[8,128]{1,0:T(8,128)S(1)}, f32[8,128]{1,0:T(8,128)S(1)}, u32[]{:S(2)}, u32[]{:S(2)}) collective-permute-start(f32[8,128]{1,0:T(8,128)S(1)} %broadcast_in_dim.19), channel_id=1, source_target_pairs={{0,1},{1,0},{2,3},{3,2},{4,5},{5,4},{6,7},{7,6},{8,9},{9,8},{10,11... | collective-permute-start | bytes 12296 | tf_op jit(solution)/shard_map/ppermute | solution.py:617
  189.2 75.6 %all-to-all-start.1 = ((bf16[16,128,768]{2,1,0:T(8,128)(2,1)}), bf16[16,128,768]{2,1,0:T(8,128)(2,1)}, u32[]{:S(2)}, u32[]{:S(2)}) async-start(bf16[16,128,768]{2,1,0:T(8,128)(2,1)} %bitcast.143), calls=%async_computation.1 | async-start | bytes 6291456 | tf_op jit(solution)/shard_map/all_to_all | solution.py:713
  198.4 58.0 %collective-permute-start.3 = (f32[8,128]{1,0:T(8,128)S(1)}, f32[8,128]{1,0:T(8,128)S(1)}, u32[]{:S(2)}, u32[]{:S(2)}) collective-permute-start(f32[8,128]{1,0:T(8,128)S(1)} %broadcast_add_fusion.1), channel_id=1, source_target_pairs={{0,2},{1,3},{2,0},{3,1},{4,6},{5,7},{6,4},{7,5},{8,10},{9,11},{10,... | collective-permute-start | bytes 12296 | tf_op jit(solution)/shard_map/ppermute | solution.py:617
  202.5 55.0 %collective-permute-start.2 = (f16[768,768]{1,0:T(8,128)(2,1)}, f16[768,768]{1,0:T(8,128)(2,1)}, u32[]{:S(2)}, u32[]{:S(2)}) collective-permute-start(f16[768,768]{1,0:T(8,128)(2,1)} %fusion.44), channel_id=1, source_target_pairs={{0,2},{1,3},{2,0},{3,1},{4,6},{5,7},{6,4},{7,5},{8,10},{9,11},{10,... | collective-permute-start | bytes 3538952 | tf_op jit(solution)/shard_map/ppermute | solution.py:617
  264.8 29.1 %collective-permute-start.7 = (f32[8,128]{1,0:T(8,128)S(1)}, f32[8,128]{1,0:T(8,128)S(1)}, u32[]{:S(2)}, u32[]{:S(2)}) collective-permute-start(f32[8,128]{1,0:T(8,128)S(1)} %add.349), channel_id=1, source_target_pairs={{0,4},{4,0},{8,12},{12,8},{16,20},{20,16},{24,28},{28,24},{1,5},{5... | collective-permute-start | bytes 12296 | tf_op jit(solution)/shard_map/ppermute | solution.py:617
  266.8 10.7 %copy-start.14 = (f32[768,768]{1,0:T(8,128)S(1)}, f32[768,768]{1,0:T(8,128)}, u32[]{:S(2)}) copy-start(f32[768,768]{1,0:T(8,128)} %bitcast_add_fusion.2) | copy-start | bytes 7077892
  278.5 18.5 %collective-permute-start.6 = (f16[384,768]{1,0:T(8,128)(2,1)}, f16[384,768]{1,0:T(8,128)(2,1)}, u32[]{:S(2)}, u32[]{:S(2)}) collective-permute-start(f16[384,768]{1,0:T(8,128)(2,1)} %fusion.46), channel_id=1, source_target_pairs={{0,4},{4,0},{8,12},{12,8},{16,20},{20,16},{24,28},{28,24},{1,5},{5... | collective-permute-start | bytes 1769480 | tf_op jit(solution)/shard_map/ppermute | solution.py:617
  285.9 6.8 %copy-start.11 = (bf16[1024,768]{0,1:T(8,128)(2,1)S(1)}, bf16[1024,768]{0,1:T(8,128)(2,1)}, u32[]{:S(2)}) copy-start(bf16[1024,768]{0,1:T(8,128)(2,1)} %copy-done.10) | copy-start | bytes 4718596
  285.9 12.4 %collective-permute-start.4 = (f16[2,512,768]{2,1,0:T(8,128)(2,1)S(1)}, f16[2,512,768]{2,1,0:T(8,128)(2,1)S(1)}, u32[]{:S(2)}, u32[]{:S(2)}) collective-permute-start(f16[2,512,768]{2,1,0:T(8,128)(2,1)S(1)} %fusion.40), channel_id=1, source_target_pairs={{0,1},{1,0},{2,3},{3,2},{4,5},{5,4},{6,7},{7,6},{8,9},{9,8},{10,11... | collective-permute-start | bytes 4718600 | tf_op jit(solution)/shard_map/ppermute | solution.py:617
  292.6 2.6 collective-permute-start.5
  300.6 9.1 %collective-permute-start.11 = (f32[8,128]{1,0:T(8,128)S(1)}, f32[8,128]{1,0:T(8,128)S(1)}, u32[]{:S(2)}, u32[]{:S(2)}) collective-permute-start(f32[8,128]{1,0:T(8,128)S(1)} %add.356), channel_id=1, source_target_pairs={{0,8},{4,12},{8,0},{12,4},{16,24},{20,28},{24,16},{28,20},{1,9},{5... | collective-permute-start | bytes 12296 | tf_op jit(solution)/shard_map/ppermute | solution.py:617
  301.2 9.7 %collective-permute-start.9 = (f32[8,128]{1,0:T(8,128)S(1)}, f32[8,128]{1,0:T(8,128)S(1)}, u32[]{:S(2)}, u32[]{:S(2)}) collective-permute-start(f32[8,128]{1,0:T(8,128)S(1)} %broadcast_add_fusion), channel_id=1, source_target_pairs={{0,2},{1,3},{2,0},{3,1},{4,6},{5,7},{6,4},{7,5},{8,10},{9,11},{10,... | collective-permute-start | bytes 12296 | tf_op jit(solution)/shard_map/ppermute | solution.py:617
  305.1 9.2 %collective-permute-start.10 = (f16[192,768]{1,0:T(8,128)(2,1)S(1)}, f16[192,768]{1,0:T(8,128)(2,1)S(1)}, u32[]{:S(2)}, u32[]{:S(2)}) collective-permute-start(f16[192,768]{1,0:T(8,128)(2,1)S(1)} %fusion.48), channel_id=1, source_target_pairs={{0,8},{4,12},{8,0},{12,4},{16,24},{20,28},{24,16},{28,20},{1,9},{5... | collective-permute-start | bytes 884744 | tf_op jit(solution)/shard_map/ppermute | solution.py:617
  308.0 19.4 %collective-permute-start.8 = (f16[512,768]{1,0:T(8,128)(2,1)S(1)}, f16[512,768]{1,0:T(8,128)(2,1)S(1)}, u32[]{:S(2)}, u32[]{:S(2)}) collective-permute-start(f16[512,768]{1,0:T(8,128)(2,1)S(1)} %fusion.45), channel_id=1, source_target_pairs={{0,2},{1,3},{2,0},{3,1},{4,6},{5,7},{6,4},{7,5},{8,10},{9,11},{10,... | collective-permute-start | bytes 2359304 | tf_op jit(solution)/shard_map/ppermute | solution.py:617
  327.7 14.3 %collective-permute-start.15 = (f32[8,128]{1,0:T(8,128)S(1)}, f32[8,128]{1,0:T(8,128)S(1)}, u32[]{:S(2)}, u32[]{:S(2)}) collective-permute-start(f32[8,128]{1,0:T(8,128)S(1)} %add.364), channel_id=1, source_target_pairs={{0,16},{4,20},{8,24},{12,28},{16,0},{20,4},{24,8},{28,12},{1,17},{... | collective-permute-start | bytes 12296 | tf_op jit(solution)/shard_map/ppermute | solution.py:617
  329.3 15.0 %collective-permute-start.13 = (f32[8,128]{1,0:T(8,128)S(1)}, f32[8,128]{1,0:T(8,128)S(1)}, u32[]{:S(2)}, u32[]{:S(2)}) collective-permute-start(f32[8,128]{1,0:T(8,128)S(1)} %add.359), channel_id=1, source_target_pairs={{0,4},{4,0},{8,12},{12,8},{16,20},{20,16},{24,28},{28,24},{1,5},{5... | collective-permute-start | bytes 12296 | tf_op jit(solution)/shard_map/ppermute | solution.py:617
  331.2 14.4 %collective-permute-start.14 = (f16[96,768]{1,0:T(8,128)(2,1)S(1)}, f16[96,768]{1,0:T(8,128)(2,1)S(1)}, u32[]{:S(2)}, u32[]{:S(2)}) collective-permute-start(f16[96,768]{1,0:T(8,128)(2,1)S(1)} %fusion.56), channel_id=1, source_target_pairs={{0,16},{4,20},{8,24},{12,28},{16,0},{20,4},{24,8},{28,12},{1,17},{... | collective-permute-start | bytes 442376 | tf_op jit(solution)/shard_map/ppermute | solution.py:617
  334.7 13.9 %collective-permute-start.12 = (f16[256,768]{1,0:T(8,128)(2,1)S(1)}, f16[256,768]{1,0:T(8,128)(2,1)S(1)}, u32[]{:S(2)}, u32[]{:S(2)}) collective-permute-start(f16[256,768]{1,0:T(8,128)(2,1)S(1)} %fusion.47), channel_id=1, source_target_pairs={{0,4},{4,0},{8,12},{12,8},{16,20},{20,16},{24,28},{28,24},{1,5},{5... | collective-permute-start | bytes 1179656 | tf_op jit(solution)/shard_map/ppermute | solution.py:617
  340.5 8.1 %collective-permute-start.16 = (f32[32,1792]{1,0:T(8,128)S(1)}, f32[32,1792]{1,0:T(8,128)S(1)}, u32[]{:S(2)}, u32[]{:S(2)}) collective-permute-start(f32[32,1792]{1,0:T(8,128)S(1)} %select_maximum_fusion), channel_id=1, source_target_pairs={{0,4},{4,0},{8,12},{12,8},{16,20},{20,16},{24,28},{28,24},{1,5},{5... | collective-permute-start | bytes 688136 | tf_op jit(solution)/shard_map/ppermute | solution.py:617
  348.8 10.5 %collective-permute-start.18 = (f32[8,128]{1,0:T(8,128)S(1)}, f32[8,128]{1,0:T(8,128)S(1)}, u32[]{:S(2)}, u32[]{:S(2)}) collective-permute-start(f32[8,128]{1,0:T(8,128)S(1)} %add.369), channel_id=1, source_target_pairs={{0,8},{4,12},{8,0},{12,4},{16,24},{20,28},{24,16},{28,20},{1,9},{5... | collective-permute-start | bytes 12296 | tf_op jit(solution)/shard_map/ppermute | solution.py:617
  350.0 10.5 %collective-permute-start.19 = (f16[96,768]{1,0:T(8,128)(2,1)S(1)}, f16[96,768]{1,0:T(8,128)(2,1)}, u32[]{:S(2)}, u32[]{:S(2)}) collective-permute-start(f16[96,768]{1,0:T(8,128)(2,1)S(1)} %fusion.50), channel_id=1, source_target_pairs={{0,16},{4,20},{8,24},{12,28},{16,0},{20,4},{24,8},{28,12},{1,17},{... | collective-permute-start | bytes 442376 | tf_op jit(solution)/shard_map/ppermute | solution.py:617
  352.8 8.8 %collective-permute-start.17 = (f16[128,768]{1,0:T(8,128)(2,1)}, f16[128,768]{1,0:T(8,128)(2,1)}, u32[]{:S(2)}, u32[]{:S(2)}) collective-permute-start(f16[128,768]{1,0:T(8,128)(2,1)} %fusion.53), channel_id=1, source_target_pairs={{0,8},{4,12},{8,0},{12,4},{16,24},{20,28},{24,16},{28,20},{1,9},{5... | collective-permute-start | bytes 589832 | tf_op jit(solution)/shard_map/ppermute | solution.py:617
  353.4 17.8 %copy-start.13 = (bf16[16,128,768]{2,1,0:T(8,128)(2,1)S(1)}, bf16[16,128,768]{2,1,0:T(8,128)(2,1)}, u32[]{:S(2)}) copy-start(bf16[16,128,768]{2,1,0:T(8,128)(2,1)} %param.9) | copy-start | bytes 9437188
  357.9 6.5 %collective-permute-start.20 = (f32[32,1792]{1,0:T(8,128)S(1)}, f32[32,1792]{1,0:T(8,128)S(1)}, u32[]{:S(2)}, u32[]{:S(2)}) collective-permute-start(f32[32,1792]{1,0:T(8,128)S(1)} %add.375), channel_id=1, source_target_pairs={{0,8},{4,12},{8,0},{12,4},{16,24},{20,28},{24,16},{28,20},{1,9},{5... | collective-permute-start | bytes 688136 | tf_op jit(solution)/shard_map/ppermute | solution.py:617
  364.4 10.1 %collective-permute-start.22 = (f32[8,128]{1,0:T(8,128)S(1)}, f32[8,128]{1,0:T(8,128)S(1)}, u32[]{:S(2)}, u32[]{:S(2)}) collective-permute-start(f32[8,128]{1,0:T(8,128)S(1)} %add.377), channel_id=1, source_target_pairs={{0,16},{4,20},{8,24},{12,28},{16,0},{20,4},{24,8},{28,12},{1,17},{... | collective-permute-start | bytes 12296 | tf_op jit(solution)/shard_map/ppermute | solution.py:617
  366.9 13.9 %collective-permute-start.24 = (f32[32,1792]{1,0:T(8,128)S(1)}, f32[32,1792]{1,0:T(8,128)S(1)}, u32[]{:S(2)}, u32[]{:S(2)}) collective-permute-start(f32[32,1792]{1,0:T(8,128)S(1)} %add.378), channel_id=1, source_target_pairs={{0,16},{4,20},{8,24},{12,28},{16,0},{20,4},{24,8},{28,12},{1,17},{... | collective-permute-start | bytes 688136 | tf_op jit(solution)/shard_map/ppermute | solution.py:617
  367.9 13.0 %collective-permute-start.23 = (f16[192,768]{1,0:T(8,128)(2,1)S(1)}, f16[192,768]{1,0:T(8,128)(2,1)S(1)}, u32[]{:S(2)}, u32[]{:S(2)}) collective-permute-start(f16[192,768]{1,0:T(8,128)(2,1)S(1)} %maximum_select_fusion.4), channel_id=1, source_target_pairs={{0,8},{4,12},{8,0},{12,4},{16,24},{20,28},{24,16},{28,20},{1,9},{5... | collective-permute-start | bytes 884744 | tf_op jit(solution)/shard_map/ppermute | solution.py:617
  369.6 11.2 %collective-permute-start.21 = (f16[64,768]{1,0:T(8,128)(2,1)S(1)}, f16[64,768]{1,0:T(8,128)(2,1)S(1)}, u32[]{:S(2)}, u32[]{:S(2)}) collective-permute-start(f16[64,768]{1,0:T(8,128)(2,1)S(1)} %fusion.57), channel_id=1, source_target_pairs={{0,16},{4,20},{8,24},{12,28},{16,0},{20,4},{24,8},{28,12},{1,17},{... | collective-permute-start | bytes 294920 | tf_op jit(solution)/shard_map/ppermute | solution.py:617
  381.2 12.1 %collective-permute-start.26 = (f16[384,768]{1,0:T(8,128)(2,1)S(1)}, f16[384,768]{1,0:T(8,128)(2,1)S(1)}, u32[]{:S(2)}, u32[]{:S(2)}) collective-permute-start(f16[384,768]{1,0:T(8,128)(2,1)S(1)} %maximum_select_fusion.2), channel_id=1, source_target_pairs={{0,4},{4,0},{8,12},{12,8},{16,20},{20,16},{24,28},{28,24},{1,5},{5... | collective-permute-start | bytes 1769480 | tf_op jit(solution)/shard_map/ppermute | solution.py:617
  381.2 8.4 %collective-permute-start.27 = (f32[32,1792]{1,0:T(8,128)S(1)}, f32[32,1792]{1,0:T(8,128)S(1)}, u32[]{:S(2)}, u32[]{:S(2)}) collective-permute-start(f32[32,1792]{1,0:T(8,128)S(1)} %add.382), channel_id=1, source_target_pairs={{0,1},{1,0},{2,3},{3,2},{4,5},{5,4},{6,7},{7,6},{8,9},{9,8},{10,11... | collective-permute-start | bytes 688136 | tf_op jit(solution)/shard_map/ppermute | solution.py:617
  381.3 8.2 %collective-permute-start.25 = (f16[64,768]{1,0:T(8,128)(2,1)S(1)}, f16[64,768]{1,0:T(8,128)(2,1)S(1)}, u32[]{:S(2)}, u32[]{:S(2)}) collective-permute-start(f16[64,768]{1,0:T(8,128)(2,1)S(1)} %fusion.55), channel_id=1, source_target_pairs={{0,16},{4,20},{8,24},{12,28},{16,0},{20,4},{24,8},{28,12},{1,17},{... | collective-permute-start | bytes 294920 | tf_op jit(solution)/shard_map/ppermute | solution.py:617
  393.2 22.8 %copy-start.23 = (f32[2]{0:T(128)S(1)}, f32[2]{0:T(128)}, u32[]{:S(2)}) copy-start(f32[2]{0:T(128)} %param.16) | copy-start | bytes 28
  393.7 8.1 %collective-permute-start.29 = (f32[768,768]{1,0:T(8,128)S(1)}, f32[768,768]{1,0:T(8,128)S(1)}, u32[]{:S(2)}, u32[]{:S(2)}) collective-permute-start(f32[768,768]{1,0:T(8,128)S(1)} %convert_multiply_fusion.2.early_ref), channel_id=1, source_target_pairs={{0,1},{1,0},{2,3},{3,2},{4,5},{5,4},{6,7},{7,6},{8,9},{9,8},{10,11... | collective-permute-start | bytes 7077896 | tf_op jit(solution)/shard_map/ppermute | solution.py:617
  393.8 7.3 %collective-permute-start.28 = (f16[128,768]{1,0:T(8,128)(2,1)S(1)}, f16[128,768]{1,0:T(8,128)(2,1)S(1)}, u32[]{:S(2)}, u32[]{:S(2)}) collective-permute-start(f16[128,768]{1,0:T(8,128)(2,1)S(1)} %maximum_select_fusion.5), channel_id=1, source_target_pairs={{0,8},{4,12},{8,0},{12,4},{16,24},{20,28},{24,16},{28,20},{1,9},{5... | collective-permute-start | bytes 589832 | tf_op jit(solution)/shard_map/ppermute | solution.py:617
  394.1 7.7 %collective-permute-start.30 = (f32[32,1792]{1,0:T(8,128)S(1)}, f32[32,1792]{1,0:T(8,128)S(1)}, u32[]{:S(2)}, u32[]{:S(2)}) collective-permute-start(f32[32,1792]{1,0:T(8,128)S(1)} %add.386), channel_id=1, source_target_pairs={{0,2},{1,3},{2,0},{3,1},{4,6},{5,7},{6,4},{7,5},{8,10},{9,11},{10,... | collective-permute-start | bytes 688136 | tf_op jit(solution)/shard_map/ppermute | solution.py:617
  403.3 10.4 %collective-permute-start.31 = (f16[256,768]{1,0:T(8,128)(2,1)S(1)}, f16[256,768]{1,0:T(8,128)(2,1)S(1)}, u32[]{:S(2)}, u32[]{:S(2)}) collective-permute-start(f16[256,768]{1,0:T(8,128)(2,1)S(1)} %maximum_select_fusion.3), channel_id=1, source_target_pairs={{0,4},{4,0},{8,12},{12,8},{16,20},{20,16},{24,28},{28,24},{1,5},{5... | collective-permute-start | bytes 1179656 | tf_op jit(solution)/shard_map/ppermute | solution.py:617
  415.1 6.0 %collective-permute-start.32 = (f32[512,768]{1,0:T(8,128)}, f32[512,768]{1,0:T(8,128)}, u32[]{:S(2)}, u32[]{:S(2)}) collective-permute-start(f32[512,768]{1,0:T(8,128)} %convert_multiply_fusion.3.late_ref), channel_id=1, source_target_pairs={{0,1},{1,0},{2,3},{3,2},{4,5},{5,4},{6,7},{7,6},{8,9},{9,8},{10,11... | collective-permute-start | bytes 4718600 | tf_op jit(solution)/shard_map/ppermute | solution.py:617
  416.7 79.7 %all-to-all-start.2 = ((bf16[16,128,768]{2,1,0:T(8,128)(2,1)}), bf16[16,128,768]{2,1,0:T(8,128)(2,1)}, u32[]{:S(2)}, u32[]{:S(2)}) async-start(bf16[16,128,768]{2,1,0:T(8,128)(2,1)} %bitcast.142), calls=%async_computation.2 | async-start | bytes 6291456 | tf_op jit(solution)/shard_map/all_to_all | solution.py:713
  (18 other events, 55.0 us)
Sparse Core Ops, SparseCore 0:
  10.9 56.1 all-gather.3
  68.6 96.2 all-gather.5

commit v2 on v1

--- a/solution.py
+++ b/solution.py
@@ -108,7 +108,7 @@
 def forward_kernel(
     bound_ref, z_ref, proj_ref, gm_ref, e_ref, et_ref, convw_ref, convb_ref, dtb_ref, alog_ref,
     skip_ref, gain_ref,
-    pair_ref, dy_ref, through_ref, state_ref, ggain_ref,
+    pair_ref, dy_ref, through_ref, state_ref, ggain_ref, zmax_ref,
     ext_ref, dt_ref, carry_ref, xd_ref, acc_ref, cumt_ref,
 ):
     step = pl.program_id(0)
@@ -121,6 +121,7 @@
         carry_ref[...] = jnp.zeros_like(carry_ref)
         dt_ref[...] = jnp.zeros_like(dt_ref)
         ggain_ref[...] = jnp.zeros_like(ggain_ref)
+        zmax_ref[...] = jnp.zeros_like(zmax_ref)
 
     rows, rr, cc = chunk_masks(t0, bound)
     ext_ref[8 : 8 + Q, :] = proj_ref[:, :XBC]
@@ -180,7 +181,9 @@
     ggated = ginv * (gmg - mhat * jnp.mean(mhat * gmg, axis=1, keepdims=True))
     dy = ggated * silu_z
     dy_ref[...] = dy
-    pair_ref[0] = (ggated * scanned * (sig_z * (1.0 + z * (1.0 - sig_z)))).astype(BF16)
+    grad_z = ggated * scanned * (sig_z * (1.0 + z * (1.0 - sig_z)))
+    zmax_ref[...] = jnp.maximum(zmax_ref[...], jnp.max(jnp.abs(grad_z), axis=0, keepdims=True))
+    pair_ref[0] = grad_z.astype(BF16)
     through_ref[...] = head_sum(dy * (scanned - skip_ref[...] * x), et_ref)
 
 
@@ -208,13 +211,14 @@
             pl.BlockSpec((Q, INNER), lambda i: (i, 0)),
             pl.BlockSpec((Q, 128), lambda i: (i, 0)),
             pl.BlockSpec((1, STATE, INNER), lambda i: (i, 0, 0)),
-            const_spec((1, INNER)),
+            const_spec((1, INNER)), const_spec((1, INNER)),
         ],
         out_shape=[
             jax.ShapeDtypeStruct((2, n, INNER), BF16),
             jax.ShapeDtypeStruct((n, INNER), F32),
             jax.ShapeDtypeStruct((n, 128), F32),
             jax.ShapeDtypeStruct((steps, STATE, INNER), F32),
+            jax.ShapeDtypeStruct((1, INNER), F32),
             jax.ShapeDtypeStruct((1, INNER), F32),
         ],
         scratch_shapes=[
@@ -350,6 +354,8 @@
             gcp * (ext_ref[8 - back : 8 - back + Q, :] * ok), axis=0, keepdims=True)
         okn = jnp.logical_or(rows >= bound, rows + back < bound).astype(F32)
         total = total + convw_ref[3 - back : 4 - back, :] * (gnext_ref[back : back + Q, :] * okn)
+    small_ref[7:8, :] = jnp.maximum(
+        small_ref[7:8, :], jnp.max(jnp.abs(total), axis=0, keepdims=True))
     total = total.astype(BF16)
     gp_ref[:, :XBC] = total
     window_ref[0] = total[:, :WINDOW]
@@ -432,6 +438,7 @@
 STAGE_ROWS = 16264
 ADAM_BLOCKS = 10
 F16_TOP = 30000.0
+MARK = 16
 
 
 PREP_STEPS = 7
@@ -525,14 +532,14 @@
 
 def adam_kernel(
     who_ref, rate_ref, early_ref, early_other_ref, late_ref, late_other_ref, small_ref,
-    weight_ref, first_ref, second_ref,
-    grad_ref, first_out_ref, second_out_ref, ratio_ref,
+    first_ref, second_ref,
+    grad_ref, ratio_ref,
     stage_ref,
 ):
     step = pl.program_id(0)
     upper = who_ref[0]
     mine = who_ref[1]
-    block = weight_ref.shape[0]
+    block = first_ref.shape[0]
     half = 2 * block * ADAM_BLOCKS
 
     @pl.when(step == 0)
@@ -579,13 +586,11 @@
         grad_ref[...] = grad
         first = BETA_ONE * first_ref[...] + (1.0 - BETA_ONE) * grad
         second = BETA_TWO * second_ref[...] + (1.0 - BETA_TWO) * grad * grad
-        first_out_ref[...] = first
-        second_out_ref[...] = second
         ratio_ref[...] = (first * rate_ref[0]) / (jnp.sqrt(second * rate_ref[1]) + EPS_ADAM)
 
 
-def run_adam(who, rates, early, early_other, late, late_other, small, weight, first, second):
-    rows = weight.shape[0]
+def run_adam(who, rates, early, early_other, late, late_other, small, first, second):
+    rows = first.shape[0]
     block = rows // ADAM_BLOCKS
 
     def at(i):
@@ -600,16 +605,16 @@
             pl.BlockSpec(memory_space=pltpu.SMEM), pl.BlockSpec(memory_space=pltpu.SMEM),
             const_spec(early.shape), const_spec(early.shape),
             const_spec(late.shape), const_spec(late.shape), const_spec(small.shape),
-            spec, spec, spec,
-        ],
-        out_specs=[spec, spec, spec, spec],
-        out_shape=[out, out, out, out],
+            spec, spec,
+        ],
+        out_specs=[spec, spec],
+        out_shape=[out, out],
         scratch_shapes=[pltpu.VMEM((STAGE_ROWS, LANES), F32)],
         compiler_params=pltpu.CompilerParams(
             dimension_semantics=("arbitrary",), vmem_limit_bytes=48 * 2**20),
         cost_estimate=pl.CostEstimate(
-            flops=10**8, bytes_accessed=36 * 2**20, transcendentals=10**6),
-    )(who, rates, early, early_other, late, late_other, small, weight, first, second)
+            flops=10**8, bytes_accessed=24 * 2**20, transcendentals=10**6),
+    )(who, rates, early, early_other, late, late_other, small, first, second)
 
 
 def swap(values, axis, bit):
@@ -617,34 +622,47 @@
     return lax.ppermute(values, axis, [(i, i ^ bit) for i in range(size)])
 
 
-def top_block(values):
-    return jnp.broadcast_to(jnp.max(jnp.abs(values)), (8, LANES))
-
-
-def to_wire(values, top):
-    return (values * (F16_TOP / jnp.maximum(top[0, 0], 1e-30))).astype(jnp.float16)
-
-
-def from_wire(values, top):
-    return values.astype(F32) * (top[0, 0] * (1.0 / F16_TOP))
-
-
-def halve(values, top, axis, bit):
+def power_for(bound):
+    bound = jnp.maximum(bound, 1e-30).reshape(1, 1)
+    return jnp.clip(jnp.floor(jnp.log2(F16_TOP / bound)), -126.0, 120.0)
+
+
+def values_scaled(values, power):
+    return values * jnp.exp2(power)
+
+
+def to_wire(values, power):
+    return values_scaled(values, power).astype(jnp.float16)
+
+
+def from_wire(values, power):
+    return values.astype(F32) * jnp.exp2(-power)
+
+
+def halve(values, power, axis, bit):
     side = (lax.axis_index(axis) // bit) % 2
-    keep = lax.dynamic_index_in_dim(values, side, 0, keepdims=False)
-    send = lax.dynamic_index_in_dim(values, 1 - side, 0, keepdims=False)
-    got = swap(to_wire(send, top), axis, bit)
-    got_top = swap(top, axis, bit)
-    return keep + from_wire(got, got_top), top + got_top
+    rows = values.shape[-2] // 2
+    mark = min(MARK, rows)
+    dim = values.ndim - 2
+    keep = lax.dynamic_slice_in_dim(values, side * rows, rows, dim)
+    send = lax.dynamic_slice_in_dim(values, (1 - side) * (rows - mark), rows + mark, dim)
+    line = lax.broadcasted_iota(jnp.int32, send.shape, dim)
+    marked = jnp.where(side == 1, line >= rows, line < mark)
+    wire = jnp.where(marked, power, values_scaled(send, power)).astype(jnp.float16)
+    got = swap(wire, axis, bit)
+    got_power = lax.dynamic_slice_in_dim(got, (1 - side) * rows, 1, dim)
+    got_power = got_power.reshape(-1, D)[0:1, 0:1].astype(F32)
+    body = lax.dynamic_slice_in_dim(got, side * mark, rows, dim)
+    sum_bound = F16_TOP * (jnp.exp2(-power) + jnp.exp2(-got_power))
+    return keep + from_wire(body, got_power), power_for(sum_bound)
+
+
+def halve_data(values, power, bit):
+    return halve(values, power, "dp", bit)
 
 
 def data_bits():
     return [1 << k for k in range(lax.axis_size("dp").bit_length() - 1)]
-
-
-def halve_data(values, top, bit):
-    rows = values.shape[0] // 2
-    return halve(values.reshape(2, rows, D), top, "dp", bit)
 
 
 def double_data(wire, bit):
@@ -692,7 +710,8 @@
     in_w, out_w, norm_gain, *params, e2, et = run_prepare(flat)
     cot = loss_sensitivity[0]
     gm = dot_nt(cot, out_w)
-    local_tok, in_w, gm = tie((local_tok, in_w, gm))
+    cot_top = jnp.max(jnp.abs(cot)).astype(F32)
+    local_tok, in_w, gm, cot_top = tie((local_tok, in_w, gm, cot_top))
     own_late, _ = tie((own, flat[:8]))
     whole_master = lax.all_gather(own_late, "zero", axis=0, tiled=True)
 
@@ -725,90 +744,120 @@
     normed = (nhat * norm_gain).astype(BF16)
     proj_z = dot_nt(normed, in_w[:INNER])
     proj = dot_nt(normed, in_w[INNER:])
-    pair, dy, through, states, ggain = run_forward(proj_z, proj, gm, bound_arr, e2, et, params)
+    pair, dy, through, states, ggain, zmax = run_forward(
+        proj_z, proj, gm, bound_arr, e2, et, params)
     result = (tok + dot(pair[1], out_w)).astype(BF16)
     picked = spread(result)
     picked, pair = tie((picked, pair))
     back_out = send_back(picked)
+    root = float(seq_len) ** 0.5
+    normed_norm = root * float(D) ** 0.5 * 1.02 * jnp.max(jnp.abs(norm_gain))
+    mixed_norm = root * float(INNER) ** 0.5 * 1.02 * jnp.max(jnp.abs(params[5]))
+    early_power = power_for(jnp.maximum(
+        1.02 * root * jnp.max(zmax) * normed_norm, root * cot_top * mixed_norm))
     early = lax.dot_general(
         pair, jnp.stack([normed, cot]), (((1,), (1,)), ((0,), (0,))), preferred_element_type=F32)
-    early = jnp.swapaxes(early.reshape(2, 2, INNER // 2, D), 0, 1)
-    early, early_top = halve(early, top_block(early), "zero", 1)
+    early, early_power = halve(early, early_power, "zero", 1)
+    early = early.reshape(INNER, D)
     part_normed = dot(pair[0], in_w[:INNER])
-    early, early_top, part_normed, dy = tie((early, early_top, part_normed, dy))
-    early, early_top = halve(early, early_top, "zero", 2)
+    early, early_power, part_normed, dy = tie((early, early_power, part_normed, dy))
+    early, early_power = halve(early, early_power, "zero", 2)
     gp, window, small8 = run_backward(proj, dy, through, states, bound_arr, e2, et, params)
-    gp, window, back_out, early, early_top, whole_master = tie(
-        (gp, window, back_out, early, early_top, whole_master))
+    gp, window, back_out, early, early_power, whole_master = tie(
+        (gp, window, back_out, early, early_power, whole_master))
 
     bits = data_bits()
     late = lax.dot_general(
         window, jnp.stack([normed, normed]), (((1,), (1,)), ((0,), (0,))),
         preferred_element_type=F32)
     late, gp = tie((late, gp))
-    late = jnp.swapaxes(late.reshape(2, 2, WINDOW // 2, D), 0, 1)
-    late, late_top = halve(late, top_block(late), "zero", 1)
-    early, early_top = halve_data(early, early_top, bits[0])
+    late_power = power_for(1.02 * root * jnp.max(small8[7:8]) * normed_norm)
+    late, late_power = halve(late, late_power, "zero", 1)
+    late = late.reshape(WINDOW, D)
+    early, early_power = halve_data(early, early_power, bits[0])
     grad_normed = part_normed + dot(gp, in_w[INNER:])
-    late, late_top, early, early_top, grad_normed = tie(
-        (late, late_top, early, early_top, grad_normed))
-    late, late_top = halve(late, late_top, "zero", 2)
+    late, late_power, early, early_power, grad_normed = tie(
+        (late, late_power, early, early_power, grad_normed))
+    late, late_power = halve(late, late_power, "zero", 2)
     for bit in bits[1:-1]:
-        early, early_top = halve_data(early, early_top, bit)
+        early, early_power = halve_data(early, early_power, bit)
     gng = grad_normed * norm_gain
     grad_norm_gain = jnp.sum(nhat * grad_normed, axis=0, keepdims=True)
     grad_tok = cot.astype(F32) + rinv * (gng - nhat * jnp.mean(nhat * gng, axis=1, keepdims=True))
     grad_tok = grad_tok.astype(BF16)
-    small8 = small8 + jnp.pad(ggain, ((5, 2), (0, XBC - INNER)))
-    small8 = small8 + jnp.pad(grad_norm_gain, ((6, 1), (0, XBC - D)))
+    line = iota((8, 1), 0)
+    small8 = jnp.where(line == 5, jnp.pad(ggain, ((0, 0), (0, XBC - INNER))), small8)
+    small8 = small8 + jnp.where(line == 6, jnp.pad(grad_norm_gain, ((0, 0), (0, XBC - D))), 0.0)
     small = jnp.concatenate([
         small8, jnp.pad(dot_tn(gp[:, XBC:], normed), ((0, 0), (0, XBC - D)))])
-    late, late_top, early, early_top, small, grad_tok = tie(
-        (late, late_top, early, early_top, small, grad_tok))
-    late, late_top = halve_data(late, late_top, bits[0])
-    early, early_top = halve_data(early, early_top, bits[-1])
-    early = to_wire(early, early_top)
+    late, late_power, early, early_power, small, grad_tok = tie(
+        (late, late_power, early, early_power, small, grad_tok))
     small = small + swap(small, "dp", bits[0])
+    late, late_power = halve_data(late, late_power, bits[0])
+    early, early_power = halve_data(early, early_power, bits[-1])
+    early = to_wire(early, early_power)
     picked_grad = spread(grad_tok)
-    late, late_top, early, small, picked_grad = tie((late, late_top, early, small, picked_grad))
+    late, late_power, early, picked_grad, small = tie(
+        (late, late_power, early, picked_grad, small))
     for bit in bits[1:-1]:
-        late, late_top = halve_data(late, late_top, bit)
+        late, late_power = halve_data(late, late_power, bit)
         small = small + swap(small, "dp", bit)
         early = double_data(early, bits[-1]) if bit == bits[1] else early
-    back_rows = back_out.at[restore].get(mode="promise_in_bounds")
-    late, late_top, early, small, back_rows = tie((late, late_top, early, small, back_rows))
-    late, late_top = halve_data(late, late_top, bits[-1])
-    late = to_wire(late, late_top)
+    late, late_power, early, small = tie((late, late_power, early, small))
+    late, late_power = halve_data(late, late_power, bits[-1])
+    small = small + swap(small, "dp", bits[-1])
+    late = to_wire(late, late_power)
     for bit in reversed(bits[1:-1]):
         early = double_data(early, bit)
-    small = small + swap(small, "dp", bits[-1])
-    tokens_out = jnp.where(live, back_rows, tokens)
-    late, early, small, tokens_out = tie((late, early, small, tokens_out))
+    late, early, small = tie((late, early, small))
     late = double_data(late, bits[-1])
-    early = from_wire(double_data(early, bits[0]), early_top)
     small = small + swap(small, "zero", 1)
+    early = from_wire(double_data(early, bits[0]), early_power)
     late, early, small = tie((late, early, small))
     for bit in reversed(bits[1:-1]):
         late = double_data(late, bit)
+    small = small + swap(small, "zero", 2)
     early_other = swap(early, "zero", 1)
-    small = small + swap(small, "zero", 2)
-    late, early_other, small = tie((late, early_other, small))
-    late = from_wire(double_data(late, bits[0]), late_top)
-    late, picked_grad = tie((late, picked_grad))
+    late, early_other, picked_grad, small = tie((late, early_other, picked_grad, small))
+    back_grad = send_back(picked_grad)
+    late = from_wire(double_data(late, bits[0]), late_power)
     late_other = swap(late, "zero", 1)
-    back_grad = send_back(picked_grad)
-    grad_tokens = jnp.where(
-        live, back_grad.at[restore].get(mode="promise_in_bounds"), jnp.zeros((), BF16))
 
     steps_f = iteration_tally[0].astype(F32)
     rates = jnp.stack([
         1.0 / (1.0 - jnp.power(BETA_ONE, steps_f)), 1.0 / (1.0 - jnp.power(BETA_TWO, steps_f))])
     who = jnp.stack([zero_index // 2, zero_index % 2]).astype(jnp.int32)
-    grad_shard, first_next, second_next, ratio = run_adam(
-        who, rates, early, early_other, late, late_other, small,
-        own, moment_one.reshape(shard_rows, LANES), moment_two.reshape(shard_rows, LANES))
-    ratios = lax.all_gather(ratio.astype(jnp.float16), "zero", axis=0, tiled=True).astype(F32)
-    new_master = whole_master - adam_rates[0] * (ratios + adam_rates[1] * whole_master)
+    first = moment_one.reshape(shard_rows, LANES)
+    second = moment_two.reshape(shard_rows, LANES)
+    grad_shard, ratio = run_adam(
+        who, rates, early, early_other, late, late_other, small, first, second)
+    mine = ratio.astype(jnp.float16)
+    mine, grad_shard, back_out = tie((mine, grad_shard, back_out))
+    core = swap(mine, "zero", 1)
+    across = swap(mine, "zero", 2)
+    first_next = BETA_ONE * first + (1.0 - BETA_ONE) * grad_shard
+    second_next = BETA_TWO * second + (1.0 - BETA_TWO) * grad_shard * grad_shard
+    back_rows = back_out.at[restore].get(mode="promise_in_bounds")
+    tokens_out = jnp.where(live, back_rows, tokens)
+    new_master = jnp.zeros((group_devices, shard_rows, LANES), F32)
+    whole_master = whole_master.reshape(group_devices, shard_rows, LANES)
+
+    def put(new_master, piece, offset):
+        shard = zero_index ^ offset
+        old = lax.dynamic_index_in_dim(whole_master, shard, 0, keepdims=False)
+        new = old - adam_rates[0] * (piece.astype(F32) + adam_rates[1] * old)
+        return lax.dynamic_update_index_in_dim(new_master, new, shard, 0)
+
+    new_master = put(put(new_master, mine, 0), core, 1)
+    across, new_master, tokens_out, first_next, second_next = tie(
+        (across, new_master, tokens_out, first_next, second_next))
+    across_core = swap(across, "zero", 1)
+    new_master = put(new_master, across, 2)
+    across_core, new_master = tie((across_core, new_master))
+    new_master = put(new_master, across_core, 3)
+    back_grad, new_master = tie((back_grad, new_master))
+    grad_tokens = jnp.where(
+        live, back_grad.at[restore].get(mode="promise_in_bounds"), jnp.zeros((), BF16))
     return (
         tokens_out, grad_tokens, new_master.reshape(-1), grad_shard.reshape(-1),
         first_next.reshape(-1), second_next.reshape(-1))

time: 517 us -> 514 us (level)
  blocking collectives: 45.6 us -> 0 us
  waiting for transfers between devices: 103 us -> 136 us
  other arithmetic: 65.1 us -> 73.2 us
    all_gather x1 -> x0, blocking collectives: 45.6 us -> none  [on_device(): lax.all_gather(ratio.astype(jnp.float16), 'zero', axis=0, tiled=True)]
    ppermute x33 -> x26, waiting for transfers between devices: 48.2 us -> 81.9 us  [swap(): return lax.ppermute(values, axis, [(i, i ^ bit) for i in range(size)])]
    dynamic_update_slice x0 -> x4, other arithmetic: none -> 19.6 us  [put(): return lax.dynamic_update_index_in_dim(new_master, new, shard, 0)]
    reshape x1 -> x0, other arithmetic: 12.4 us -> none  [on_device(): new_master.reshape(-1)]
    all_to_all x2, starting transfers between devices: 8.89 us -> 18.3 us  [send_back(): return lax.all_to_all(picked, 'dp', split_axis=0, concat_axis=0, tiled=True)]
    slice x21 -> x3, local copies, waits for them, and re-layouts: 10.9 us -> 1.64 us  [the longest x2 1.03 us: halve(): got_power = got_power.reshape(-1, D)[0:1, 0:1].astype(F32)]
    broadcast_in_dim x2 -> x1, local copies, waits for them, and re-layouts: 1.27 us -> 7.55 us  [on_device(): new_master = jnp.zeros((group_devices, shard_rows, LANES), F32)]
    ppermute x33 -> x26, starting transfers between devices: 30.4 us -> 24.3 us  [swap(): return lax.ppermute(values, axis, [(i, i ^ bit) for i in range(size)])]
  transfers between devices with their start and end apart: 38 -> 31, of which waited for: 13 -> 19; matrix products, arithmetic and copies ran while one was open for 30% -> 29% of each run, Pallas kernels for 21% -> 21%
where the time goes in v2:
time: 514 us; the launch traced here: 505 us
  waiting for transfers between devices  136 us (26%)
  Pallas kernels  105 us (20%)
  other arithmetic  73.2 us (14%)
  matrix products  70.5 us (14%)
  starting transfers between devices  50.1 us (10%)
  local copies, waits for them, and re-layouts  41.4 us (8%)
  between operations  29.1 us (6%)
    ppermute x26, waiting for transfers between devices, swap(): return lax.ppermute(values, axis, [(i, i ^ bit) for i in range(size)])  81.9 us
    pallas_call x1, Pallas kernels, run_backward(): pl.pallas_call(backward_kernel, grid=(steps,), in_specs=[pl.BlockSpec(mem...  49.4 us
    all_gather x1, waiting for transfers between devices, on_device(): flat = lax.all_gather(own.astype(BF16), 'zero', axis=0, tiled=True)  39.9 us
    pallas_call x1, Pallas kernels, run_forward(): pl.pallas_call(forward_kernel, grid=(steps,), in_specs=[pl.BlockSpec(memo...  35.9 us
    dot_general x5, matrix products, dot(): lax.dot_general(a, b, (((1,), (0,)), ((), ())), preferred_element_type=F32)  35.3 us
    ppermute x26, starting transfers between devices, swap(): return lax.ppermute(values, axis, [(i, i ^ bit) for i in range(size)])  24.3 us
    dynamic_update_slice x4, other arithmetic, put(): return lax.dynamic_update_index_in_dim(new_master, new, shard, 0)  19.6 us
    all_to_all x2, starting transfers between devices, send_back(): return lax.all_to_all(picked, 'dp', split_axis=0, concat_axis=0, tiled=True)  18.3 us
  transfers between devices with their start and end apart: 31, of which 19 were waited for; matrix products, arithmetic and copies ran while one was open for 29% of the time, Pallas kernels for 21%

profile of v2, /device:TPU:0, one launch (start us, length us, event | category | flops | bytes accessed | tf_op | source)
XLA Modules:
  0.0 505.2 jit_solution(5193802615683075458)
XLA Ops:
  7.2 3.5 bitcast_convert_fusion
  15.0 7.4 %all-to-all-start = ((bf16[16,128,768]{2,1,0:T(8,128)(2,1)}), bf16[16,128,768]{2,1,0:T(8,128)(2,1)}, u32[]{:S(2)}, u32[]{:S(2)}) async-start(bf16[16,128,768]{2,1,0:T(8,128)(2,1)} %gather_fusion), calls=%async_computation | async-start | bytes 6291456 | tf_op jit(solution)/shard_map/all_to_all | solution.py:705
  27.1 39.9 %all-gather.3.cloned.1.call-done.flat_ref = bf16[29440,128]{1,0:T(8,128)(2,1)} async-done(((bf16[7360,128]{1,0:T(8,128)(2,1)}), bf16[29440,128]{1,0:T(8,128)(2,1)}) %all-gather.3.cloned.1.call-update) | async-done | bytes 7536656 | tf_op jit(solution)/shard_map/all_gather | solution.py:699
  67.0 7.1 %shard_map.136 = (bf16[3352,768]{1,0:T(8,128)(2,1)S(1)}, bf16[1536,768]{1,0:T(8,128)(2,1)S(1)}, f32[1,768]{1,0:T(1,128)S(1)}, f32[8,1792]{1,0:T(8,128)S(1)}, f32...) custom-call(bf16[29440,128]{1,0:T(8,128)(2,1)} %all-gather.3.cloned., ...), custom_call_target="tpu_custom_call" | custom-call | flops 1000000000 | bytes 16777216 | tf_op jit(solution)/shard_map/pallas_call | solution.py:508
  74.2 2.6 copy-done
  77.5 4.7 fusion.52.gm_ref
  82.2 11.0 %all-to-all-done = bf16[16,128,768]{2,1,0:T(8,128)(2,1)} async-done(((bf16[16,128,768]{2,1,0:T(8,128)(2,1)}), bf16[16,128,768]{2,1,0:T(8,128)(2,1)}, u32[]{:S(2)}, u32[]{:S(2)}) %all-to-all-start) | async-done | bytes 3145760 | tf_op jit(solution)/shard_map/all_to_all | solution.py:705
  93.8 5.9 %fusion.30 = (f32[1024]{0:T(1024)S(1)}, bf16[1024,768]{0,1:T(8,128)(2,1)S(1)}) fusion(bf16[2048,768]{1,0:T(8,128)(2,1)} %bitcast.7, s32[1024]{0:T(1024)S(1)} %fusion.65), kind=kOutput, calls=%fused_computation.58 | convolution fusion | flops 3226467328 | bytes 4726784 | tf_op jit(solution)/shard_map/dot_general | solution.py:27
  99.8 5.0 fusion.45.z_ref
  104.8 6.1 %fusion.42.proj_ref.before_ref = f32[1024,1816]{1,0:T(8,128)} fusion(bf16[3352,768]{1,0:T(8,128)(2,1)S(1)} %copy-done.1, bf16[1024,768]{0,1:T(8,128)(2,1)S(1)} %get-tuple-element.181, f32[768]{0:T(1024)S(1)} %get-tuple-element.175, f32[1024]{0:T(1024)S(1)} %add_rsqrt_fusion), kind=kOutput, calls=%fused_computation.73 | convolution fusion | flops 2859466752 | bytes 11808768 | tf_op jit(solution)/shard_map/dot_general | solution.py:31
  110.9 35.9 %shard_map.137 = (bf16[2,1024,1536]{2,1,0:T(8,128)(2,1)}, f32[1024,1536]{1,0:T(8,128)}, f32[1024,128]{1,0:T(8,128)S(1)}, f32[8,128,1536]{2,1,0:T(8,128)}, f32[1,1536]{1,0:T(1,128)S(1)}, /*index=5*/f32[1,1536]{1,0:T(1,128)S(1)}) custom-call(s32[1]{0:T(128)} %dynamic_slice.148.bound_ref, f32[1024,1536]{1,0:T(8,128)} %fusion.45.z_ref, ...), custom_call_target="tpu_custom_call" | custom-call | flops 30000001024 | bytes 41943040 | tf_op jit(solution)/shard_map/pallas_call | solution.py:197
  147.6 10.5 %fusion.19 = bf16[2048,768]{1,0:T(8,128)(2,1)} fusion(s32[2048]{0:T(1024)S(1)} %bitcast.168, bf16[1024,768]{0,1:T(8,128)(2,1)} %copy-done.14, bf16[1536,768]{1,0:T(8,128)(2,1)S(1)} %get-tuple-element.89, bf16[2,1024,1536]{2,1,0:T(8,128)(2,1)} %get-tuple-element.103), kind=kOutput, calls=%fused_computation.46 | convolution fusion | flops 5643173888 | bytes 10231808 | tf_op jit(solution)/shard_map/dot_general | solution.py:27
  163.3 9.8 %fusion.21 = f32[2,1536,768]{2,1,0:T(8,128)S(1)} fusion(bf16[2,1024,1536]{2,1,0:T(8,128)(2,1)} %get-tuple-element.103, bf16[1,1024,768]{1,2,0:T(8,128)(2,1)S(1)} %fusion.88, bf16[1,1024,768]{1,2,0:T(8,128)(2,1)S(1)} %copy-done.13), kind=kOutput, calls=%fused_computation.49 | convolution fusion | flops 4833411072 | bytes 18874368 | tf_op jit(solution)/shard_map/dot_general | solution.py:758
  173.1 3.7 copy-done.18
  179.0 13.2 %all-to-all-start.1 = ((bf16[16,128,768]{2,1,0:T(8,128)(2,1)}), bf16[16,128,768]{2,1,0:T(8,128)(2,1)}, u32[]{:S(2)}, u32[]{:S(2)}) async-start(bf16[16,128,768]{2,1,0:T(8,128)(2,1)} %bitcast.167), calls=%async_computation.1 | async-start | bytes 6291456 | tf_op jit(solution)/shard_map/all_to_all | solution.py:732
  192.2 6.9 %fusion.34 = f32[1024,768]{1,0:T(8,128)} fusion(bf16[2,1024,1536]{2,1,0:T(8,128)(2,1)} %get-tuple-element.103, bf16[3352,768]{1,0:T(8,128)(2,1)} %copy-done), kind=kOutput, calls=%fused_computation.62 | convolution fusion | flops 2415919104 | bytes 8650752 | tf_op jit(solution)/shard_map/dot_general | solution.py:27
  201.1 3.6 multiply_add_fusion
  207.8 49.4 %shard_map.138 = (bf16[1024,1816]{1,0:T(8,128)(2,1)S(1)}, bf16[2,1024,1024]{2,1,0:T(8,128)(2,1)}, f32[8,1792]{1,0:T(8,128)S(1)}) custom-call(s32[1]{0:T(128)} %dynamic_slice.148.bound_ref, f32[1024,1816]{1,0:T(8,128)} %fusion.42.proj_ref.before_ref, f32[1024,1816]{1,0:T(8,128)} %fusion.42.proj_ref.before_ref, f32[1024,1536]{1,0:T(8,128)} %get-tuple-element.107.dy_ref, ...), custom_call_target="tpu_custom_call" | custom-call | flops 49999998976 | bytes 52428800 | tf_op jit(solution)/shard_map/pallas_call | solution.py:380
  263.1 3.6 multiply_add_fusion.3
  266.7 7.4 %fusion.22 = f32[2,1024,768]{2,1,0:T(8,128)S(1)} fusion(bf16[2,1024,1024]{2,1,0:T(8,128)(2,1)} %get-tuple-element.115, bf16[1,1024,768]{1,2,0:T(8,128)(2,1)} %copy-done.23), kind=kOutput, calls=%fused_computation.50 | convolution fusion | flops 3222798336 | bytes 12058624 | tf_op jit(solution)/shard_map/dot_general | solution.py:770
  274.1 2.7 copy-done.19
  278.7 3.8 copy.35
  288.3 6.5 %fusion.47 = f32[1024,768]{0,1:T(8,128)S(1)} fusion(f32[1024,768]{0,1:T(8,128)} %copy.35, bf16[1024,1816]{1,0:T(8,128)(2,1)S(1)} %copy-done.6, bf16[3352,768]{1,0:T(8,128)(2,1)} %copy-done), kind=kOutput, calls=%fused_computation.81 | convolution fusion | flops 2857107456 | bytes 12800000 | tf_op jit(solution)/shard_map/dot_general | solution.py:27
  294.8 5.4 %collective-permute-done.3 = f16[400,768]{1,0:T(8,128)(2,1)S(1)} collective-permute-done((f16[400,768]{1,0:T(8,128)(2,1)S(1)}, f16[400,768]{1,0:T(8,128)(2,1)S(1)}, u32[]{:S(2)}, u32[]{:S(2)}) %collective-permute-start.3) | collective-permute-done | bytes 614432 | tf_op jit(solution)/shard_map/ppermute | solution.py:622
  311.5 4.5 collective-permute-done.5
  317.3 11.0 %collective-permute-done.4 = f16[528,768]{1,0:T(8,128)(2,1)S(1)} collective-permute-done((f16[528,768]{1,0:T(8,128)(2,1)S(1)}, f16[528,768]{1,0:T(8,128)(2,1)S(1)}, u32[]{:S(2)}, u32[]{:S(2)}) %collective-permute-start.4) | collective-permute-done | bytes 811040 | tf_op jit(solution)/shard_map/ppermute | solution.py:622
  334.7 5.4 %fusion.20 = bf16[2048,768]{1,0:T(8,128)(2,1)} fusion(bf16[1024,768]{0,1:T(8,128)(2,1)S(1)} %fusion.29, s32[2048]{0:T(1024)S(1)} %bitcast.169), kind=kOutput, calls=%fused_computation.47 | convolution fusion | flops 3224895488 | bytes 4726784 | tf_op jit(solution)/shard_map/dot_general | solution.py:27
  341.9 2.9 collective-permute-done.6
  350.7 3.1 collective-permute-done.10
  353.9 3.9 collective-permute-done.9
  364.5 11.0 %collective-permute-done.12 = f16[80,768]{1,0:T(8,128)(2,1)S(1)} collective-permute-done((f16[80,768]{1,0:T(8,128)(2,1)S(1)}, f16[80,768]{1,0:T(8,128)(2,1)S(1)}, u32[]{:S(2)}, u32[]{:S(2)}) %collective-permute-start.12) | collective-permute-done | bytes 122912 | tf_op jit(solution)/shard_map/ppermute | solution.py:622
  380.3 8.0 %collective-permute-done.15 = f16[64,768]{1,0:T(8,128)(2,1)S(1)} collective-permute-done((f16[64,768]{1,0:T(8,128)(2,1)S(1)}, f16[64,768]{1,0:T(8,128)(2,1)S(1)}, u32[]{:S(2)}, u32[]{:S(2)}) %collective-permute-start.15) | collective-permute-done | bytes 98336 | tf_op jit(solution)/shard_map/ppermute | solution.py:622
  388.4 3.8 collective-permute-done.16
  393.8 6.3 %collective-permute-done.18 = f16[128,768]{1,0:T(8,128)(2,1)S(1)} collective-permute-done((f16[128,768]{1,0:T(8,128)(2,1)S(1)}, f16[128,768]{1,0:T(8,128)(2,1)S(1)}, u32[]{:S(2)}, u32[]{:S(2)}) %collective-permute-start.18) | collective-permute-done | bytes 196640 | tf_op jit(solution)/shard_map/ppermute | solution.py:622
  403.7 9.1 %collective-permute-done.21 = f16[256,768]{1,0:T(8,128)(2,1)S(1)} collective-permute-done((f16[256,768]{1,0:T(8,128)(2,1)S(1)}, f16[256,768]{1,0:T(8,128)(2,1)S(1)}, u32[]{:S(2)}, u32[]{:S(2)}) %collective-permute-start.21) | collective-permute-done | bytes 393248 | tf_op jit(solution)/shard_map/ppermute | solution.py:622
  416.7 5.1 %all-to-all-start.2 = ((bf16[16,128,768]{2,1,0:T(8,128)(2,1)}), bf16[16,128,768]{2,1,0:T(8,128)(2,1)}, u32[]{:S(2)}, u32[]{:S(2)}) async-start(bf16[16,128,768]{2,1,0:T(8,128)(2,1)} %bitcast.166), calls=%async_computation.2 | async-start | bytes 6291456 | tf_op jit(solution)/shard_map/all_to_all | solution.py:732
  421.9 12.7 %shard_map.139 = (f32[7360,128]{1,0:T(8,128)}, f32[7360,128]{1,0:T(8,128)}) custom-call(s32[2]{0:T(128)S(1)} %pad_add_fusion.who_ref, f32[2]{0:T(128)S(1)} %pad_maximum_fusion.4.rate_ref, f32[768,768]{1,0:T(8,128)S(1)} %convert_multiply_fusion.2.early_ref, f32[768,768]{1,0:T(8,128)} %copy-done.20, f32[512,768]{1,0:T(8,128)} %convert_multiply_fusion.3.late_ref, ...), custom_call_target="tpu_custom_call" | custom-call | flops 100000000 | bytes 25165824 | tf_op jit(solution)/shard_map/pallas_call | solution.py:601
  434.6 3.8 convert_element_type.205
  439.8 6.4 %fusion.10 = (f32[7360,128]{1,0:T(8,128)}, f32[7360,128]{1,0:T(8,128)}) fusion(f32[7360,128]{1,0:T(8,128)} %get-tuple-element.159, f32[942080]{0:T(1024)S(1)} %copy-done.11, f32[942080]{0:T(1024)S(1)} %copy-done.10), kind=kLoop, calls=%fused_computation.22 | loop fusion | flops 6594560 | bytes 18841600 | tf_op jit(solution)/shard_map/add | solution.py:839
  446.2 4.5 gather_fusion.1
  450.6 4.3 broadcast_select_fusion.1
  455.0 7.6 %broadcast_in_dim.221 = f32[4,7360,128]{2,1,0:T(8,128)} broadcast(f32[]{:T(128)} %constant.301.clone.1), dimensions={} | broadcast | bytes 15073284 | tf_op jit(solution)/shard_map/broadcast_in_dim | solution.py:842
  462.6 5.3 %bitcast_dynamic-update-slice_fusion.3 = f32[4,7360,128]{2,1,0:T(8,128)} fusion(f32[4,7360,128]{2,1,0:T(8,128)} %broadcast_in_dim.221, s32[]{:T(128)S(6)} %select_n.475, f16[7360,128]{1,0:T(8,128)(2,1)} %convert_element_type.205, f32[4,7360,128]{2,1,0:T(8,128)S(1)} %bitcast.151, f32[]{:T(128)} %bitcast.53, f32[]{:T(128)} %bitcast.52), kind=kLoop, calls=%fused_computation.38 | loop fusion | flops 4710400 | bytes 9421828 | tf_op jit(solution)/shard_map/jit(dynamic_update_index_in_dim)/dynamic_update_slice | solution.py:849
  467.8 5.3 %bitcast_dynamic-update-slice_fusion.2 = f32[4,7360,128]{2,1,0:T(8,128)} fusion(f32[4,7360,128]{2,1,0:T(8,128)} %bitcast_dynamic-update-slice_fusion.3, s32[]{:T(128)S(6)} %select_n.571, f16[7360,128]{1,0:T(8,128)(2,1)} %collective-permute-done.24, f32[4,7360,128]{2,1,0:T(8,128)S(1)} %bitcast.152, f32[]{:T(128)} %bitcast.53, f32[]{:T(128)} %bitcast.52), kind=kLoop, calls=%fused_computation.33 | loop fusion | flops 4710400 | bytes 9421828 | tf_op jit(solution)/shard_map/jit(dynamic_update_index_in_dim)/dynamic_update_slice | solution.py:849
  473.1 9.0 %collective-permute-done.23 = f16[7360,128]{1,0:T(8,128)(2,1)} collective-permute-done((f16[7360,128]{1,0:T(8,128)(2,1)}, f16[7360,128]{1,0:T(8,128)(2,1)}, u32[]{:S(2)}, u32[]{:S(2)}) %collective-permute-start.23) | collective-permute-done | bytes 1884192 | tf_op jit(solution)/shard_map/ppermute | solution.py:622
  482.1 5.3 %bitcast_dynamic-update-slice_fusion.1 = f32[4,7360,128]{2,1,0:T(8,128)} fusion(f32[4,7360,128]{2,1,0:T(8,128)} %bitcast_dynamic-update-slice_fusion.2, s32[]{:T(128)S(6)} %select_n.575, f16[7360,128]{1,0:T(8,128)(2,1)} %collective-permute-done.23, f32[4,7360,128]{2,1,0:T(8,128)S(1)} %bitcast.153, f32[]{:T(128)} %bitcast.53, f32[]{:T(128)} %bitcast.52), kind=kLoop, calls=%fused_computation.28 | loop fusion | flops 4710400 | bytes 9421828 | tf_op jit(solution)/shard_map/jit(dynamic_update_index_in_dim)/dynamic_update_slice | solution.py:849
  487.4 3.7 bitcast_dynamic-update-slice_fusion
  493.3 2.6 gather_fusion.2
  (211 shorter events, 76.0 us)
Async XLA Ops:
  7.2 59.9 %all-gather.3.cloned.1.call-start = ((), (), s32[]{:S(2)}) async-start(), calls=%async_computation.3 | async-start | bytes 9420800 | tf_op jit(solution)/shard_map/all_gather | solution.py:699
  10.7 256.0 %all-gather.5.cloned.1.call-start = ((), (), s32[]{:S(2)}) async-start(), calls=%async_computation.4 | async-start | bytes 18841600 | tf_op jit(solution)/shard_map/all_gather | solution.py:716
  15.0 7.7 %copy-start.21 = (bf16[1,1024,768]{2,1,0:T(8,128)(2,1)S(1)}, bf16[1,1024,768]{2,1,0:T(8,128)(2,1)}, u32[]{:S(2)}) copy-start(bf16[1,1024,768]{2,1,0:T(8,128)(2,1)} %param.10) | copy-start | bytes 4718596
  15.0 78.2 %all-to-all-start = ((bf16[16,128,768]{2,1,0:T(8,128)(2,1)}), bf16[16,128,768]{2,1,0:T(8,128)(2,1)}, u32[]{:S(2)}, u32[]{:S(2)}) async-start(bf16[16,128,768]{2,1,0:T(8,128)(2,1)} %gather_fusion), calls=%async_computation | async-start | bytes 6291456 | tf_op jit(solution)/shard_map/all_to_all | solution.py:705
  67.0 10.5 %copy-start.22 = (bf16[1,1024,768]{2,1,0:T(8,128)(2,1)S(1)}, bf16[1,1024,768]{2,1,0:T(8,128)(2,1)}, u32[]{:S(2)}) copy-start(bf16[1,1024,768]{2,1,0:T(8,128)(2,1)} %param.10) | copy-start | bytes 4718596
  93.8 5.9 %copy-start.1 = (bf16[3352,768]{1,0:T(8,128)(2,1)S(1)}, bf16[3352,768]{1,0:T(8,128)(2,1)}, u32[]{:S(2)}) copy-start(bf16[3352,768]{1,0:T(8,128)(2,1)} %copy-done) | copy-start | bytes 15446020
  104.8 6.1 %copy-start.3 = (bf16[1536,128]{1,0:T(8,128)(2,1)S(1)}, bf16[1536,128]{1,0:T(8,128)(2,1)}, u32[]{:S(2)}) copy-start(bf16[1536,128]{1,0:T(8,128)(2,1)} %copy-done.2) | copy-start | bytes 1179652
  163.3 9.8 %copy-start.23 = (bf16[1,1024,768]{1,2,0:T(8,128)(2,1)}, bf16[1,1024,768]{1,2,0:T(8,128)(2,1)S(1)}, u32[]{:S(2)}) copy-start(bf16[1,1024,768]{1,2,0:T(8,128)(2,1)S(1)} %fusion.88) | copy-start | bytes 4718596
  178.8 20.2 %collective-permute-start = (f16[2,784,768]{2,1,0:T(8,128)(2,1)}, f16[2,784,768]{2,1,0:T(8,128)(2,1)}, u32[]{:S(2)}, u32[]{:S(2)}) collective-permute-start(f16[2,784,768]{2,1,0:T(8,128)(2,1)} %select_convert_fusion), channel_id=1, source_target_pairs={{0,1},{1,0},{2,3},{3,2},{4,5},{5,4},{6,7},{7,6},{8,9},{9,8},{10,11... | collective-permute-start | bytes 7225352 | tf_op jit(solution)/shard_map/ppermute | solution.py:622
  179.0 87.7 %all-to-all-start.1 = ((bf16[16,128,768]{2,1,0:T(8,128)(2,1)}), bf16[16,128,768]{2,1,0:T(8,128)(2,1)}, u32[]{:S(2)}, u32[]{:S(2)}) async-start(bf16[16,128,768]{2,1,0:T(8,128)(2,1)} %bitcast.167), calls=%async_computation.1 | async-start | bytes 6291456 | tf_op jit(solution)/shard_map/all_to_all | solution.py:732
  206.2 55.0 %collective-permute-start.1 = (f16[784,768]{1,0:T(8,128)(2,1)}, f16[784,768]{1,0:T(8,128)(2,1)}, u32[]{:S(2)}, u32[]{:S(2)}) collective-permute-start(f16[784,768]{1,0:T(8,128)(2,1)} %select_convert_fusion.2), channel_id=1, source_target_pairs={{0,2},{1,3},{2,0},{3,1},{4,6},{5,7},{6,4},{7,5},{8,10},{9,11},{10,... | collective-permute-start | bytes 3612680 | tf_op jit(solution)/shard_map/ppermute | solution.py:622
  278.4 23.3 %collective-permute-start.2 = (f16[2,528,768]{2,1,0:T(8,128)(2,1)}, f16[2,528,768]{2,1,0:T(8,128)(2,1)}, u32[]{:S(2)}, u32[]{:S(2)}) collective-permute-start(f16[2,528,768]{2,1,0:T(8,128)(2,1)} %select_convert_fusion.1), channel_id=1, source_target_pairs={{0,1},{1,0},{2,3},{3,2},{4,5},{5,4},{6,7},{7,6},{8,9},{9,8},{10,11... | collective-permute-start | bytes 4866056 | tf_op jit(solution)/shard_map/ppermute | solution.py:622
  282.5 5.8 %copy-start.6 = (bf16[1024,1816]{1,0:T(8,128)(2,1)S(1)}, bf16[1024,1816]{1,0:T(8,128)(2,1)}, u32[]{:S(2)}) copy-start(bf16[1024,1816]{1,0:T(8,128)(2,1)} %copy-done.5) | copy-start | bytes 11157508
  284.2 16.1 %collective-permute-start.3 = (f16[400,768]{1,0:T(8,128)(2,1)S(1)}, f16[400,768]{1,0:T(8,128)(2,1)S(1)}, u32[]{:S(2)}, u32[]{:S(2)}) collective-permute-start(f16[400,768]{1,0:T(8,128)(2,1)S(1)} %select_convert_fusion.4), channel_id=1, source_target_pairs={{0,4},{4,0},{8,12},{12,8},{16,20},{20,16},{24,28},{28,24},{1,5},{5... | collective-permute-start | bytes 1843208 | tf_op jit(solution)/shard_map/ppermute | solution.py:622
  286.0 17.8 %slice-start.4 = ((s8[6291456]{0:T(1024)(128)(4,1)}), s8[4194304]{0:T(1024)(128)(4,1)S(1)}, s32[]{:S(2)}) async-start(s8[6291456]{0:T(1024)(128)(4,1)} %bitcast.161), calls=%async_computation.9 | async-start | bytes 8388608
  288.3 13.3 %copy-start.17 = (f32[768,768]{1,0:T(8,128)S(1)}, f32[768,768]{1,0:T(8,128)}, u32[]{:S(2)}) copy-start(f32[768,768]{1,0:T(8,128)} %multiply_add_fusion.3) | copy-start | bytes 7077892
  288.3 15.5 %slice-start.5 = ((s8[6291456]{0:T(1024)(128)(4,1)}), s8[2097152]{0:T(1024)(128)(4,1)S(1)}, s32[]{:S(2)}) async-start(s8[6291456]{0:T(1024)(128)(4,1)} %bitcast.161), calls=%async_computation.10 | async-start | bytes 4194304
  307.0 9.0 %collective-permute-start.5 = (f16[208,768]{1,0:T(8,128)(2,1)S(1)}, f16[208,768]{1,0:T(8,128)(2,1)S(1)}, u32[]{:S(2)}, u32[]{:S(2)}) collective-permute-start(f16[208,768]{1,0:T(8,128)(2,1)S(1)} %select_convert_fusion.6), channel_id=1, source_target_pairs={{0,8},{4,12},{8,0},{12,4},{16,24},{20,28},{24,16},{28,20},{1,9},{5... | collective-permute-start | bytes 958472 | tf_op jit(solution)/shard_map/ppermute | solution.py:622
  309.1 19.2 %collective-permute-start.4 = (f16[528,768]{1,0:T(8,128)(2,1)S(1)}, f16[528,768]{1,0:T(8,128)(2,1)S(1)}, u32[]{:S(2)}, u32[]{:S(2)}) collective-permute-start(f16[528,768]{1,0:T(8,128)(2,1)S(1)} %select_convert_fusion.3), channel_id=1, source_target_pairs={{0,2},{1,3},{2,0},{3,1},{4,6},{5,7},{6,4},{7,5},{8,10},{9,11},{10,... | collective-permute-start | bytes 2433032 | tf_op jit(solution)/shard_map/ppermute | solution.py:622
  329.8 12.1 %collective-permute-start.8 = (f32[32,1792]{1,0:T(8,128)S(1)}, f32[32,1792]{1,0:T(8,128)S(1)}, u32[]{:S(2)}, u32[]{:S(2)}) collective-permute-start(f32[32,1792]{1,0:T(8,128)S(1)} %select_maximum_fusion), channel_id=1, source_target_pairs={{0,4},{4,0},{8,12},{12,8},{16,20},{20,16},{24,28},{28,24},{1,5},{5... | collective-permute-start | bytes 688136 | tf_op jit(solution)/shard_map/ppermute | solution.py:622
  331.5 8.9 %collective-permute-start.7 = (f16[112,768]{1,0:T(8,128)(2,1)S(1)}, f16[112,768]{1,0:T(8,128)(2,1)S(1)}, u32[]{:S(2)}, u32[]{:S(2)}) collective-permute-start(f16[112,768]{1,0:T(8,128)(2,1)S(1)} %select_convert_fusion.8), channel_id=1, source_target_pairs={{0,16},{4,20},{8,24},{12,28},{16,0},{20,4},{24,8},{28,12},{1,17},{... | collective-permute-start | bytes 516104 | tf_op jit(solution)/shard_map/ppermute | solution.py:622
  334.2 10.6 %collective-permute-start.6 = (f16[272,768]{1,0:T(8,128)(2,1)S(1)}, f16[272,768]{1,0:T(8,128)(2,1)S(1)}, u32[]{:S(2)}, u32[]{:S(2)}) collective-permute-start(f16[272,768]{1,0:T(8,128)(2,1)S(1)} %select_convert_fusion.5), channel_id=1, source_target_pairs={{0,4},{4,0},{8,12},{12,8},{16,20},{20,16},{24,28},{28,24},{1,5},{5... | collective-permute-start | bytes 1253384 | tf_op jit(solution)/shard_map/ppermute | solution.py:622
  346.2 7.6 %collective-permute-start.10 = (f16[96,768]{1,0:T(8,128)(2,1)S(1)}, f16[96,768]{1,0:T(8,128)(2,1)S(1)}, u32[]{:S(2)}, u32[]{:S(2)}) collective-permute-start(f16[96,768]{1,0:T(8,128)(2,1)S(1)} %multiply_convert_fusion), channel_id=1, source_target_pairs={{0,16},{4,20},{8,24},{12,28},{16,0},{20,4},{24,8},{28,12},{1,17},{... | collective-permute-start | bytes 442376 | tf_op jit(solution)/shard_map/ppermute | solution.py:622
  348.6 9.3 %collective-permute-start.9 = (f16[144,768]{1,0:T(8,128)(2,1)S(1)}, f16[144,768]{1,0:T(8,128)(2,1)S(1)}, u32[]{:S(2)}, u32[]{:S(2)}) collective-permute-start(f16[144,768]{1,0:T(8,128)(2,1)S(1)} %select_convert_fusion.7), channel_id=1, source_target_pairs={{0,8},{4,12},{8,0},{12,4},{16,24},{20,28},{24,16},{28,20},{1,9},{5... | collective-permute-start | bytes 663560 | tf_op jit(solution)/shard_map/ppermute | solution.py:622
  349.2 11.9 %collective-permute-start.11 = (f32[32,1792]{1,0:T(8,128)S(1)}, f32[32,1792]{1,0:T(8,128)S(1)}, u32[]{:S(2)}, u32[]{:S(2)}) collective-permute-start(f32[32,1792]{1,0:T(8,128)S(1)} %add.489), channel_id=1, source_target_pairs={{0,8},{4,12},{8,0},{12,4},{16,24},{20,28},{24,16},{28,20},{1,9},{5... | collective-permute-start | bytes 688136 | tf_op jit(solution)/shard_map/ppermute | solution.py:622
  361.1 17.3 %collective-permute-start.13 = (f16[192,768]{1,0:T(8,128)(2,1)S(1)}, f16[192,768]{1,0:T(8,128)(2,1)S(1)}, u32[]{:S(2)}, u32[]{:S(2)}) collective-permute-start(f16[192,768]{1,0:T(8,128)(2,1)S(1)} %maximum_select_fusion.4), channel_id=1, source_target_pairs={{0,8},{4,12},{8,0},{12,4},{16,24},{20,28},{24,16},{28,20},{1,9},{5... | collective-permute-start | bytes 884744 | tf_op jit(solution)/shard_map/ppermute | solution.py:622
  361.4 14.0 %collective-permute-start.12 = (f16[80,768]{1,0:T(8,128)(2,1)S(1)}, f16[80,768]{1,0:T(8,128)(2,1)S(1)}, u32[]{:S(2)}, u32[]{:S(2)}) collective-permute-start(f16[80,768]{1,0:T(8,128)(2,1)S(1)} %select_convert_fusion.9), channel_id=1, source_target_pairs={{0,16},{4,20},{8,24},{12,28},{16,0},{20,4},{24,8},{28,12},{1,17},{... | collective-permute-start | bytes 368648 | tf_op jit(solution)/shard_map/ppermute | solution.py:622
  362.9 15.5 %collective-permute-start.14 = (f32[32,1792]{1,0:T(8,128)S(1)}, f32[32,1792]{1,0:T(8,128)S(1)}, u32[]{:S(2)}, u32[]{:S(2)}) collective-permute-start(f32[32,1792]{1,0:T(8,128)S(1)} %add.496), channel_id=1, source_target_pairs={{0,16},{4,20},{8,24},{12,28},{16,0},{20,4},{24,8},{28,12},{1,17},{... | collective-permute-start | bytes 688136 | tf_op jit(solution)/shard_map/ppermute | solution.py:622
  378.7 13.4 %collective-permute-start.16 = (f16[384,768]{1,0:T(8,128)(2,1)S(1)}, f16[384,768]{1,0:T(8,128)(2,1)S(1)}, u32[]{:S(2)}, u32[]{:S(2)}) collective-permute-start(f16[384,768]{1,0:T(8,128)(2,1)S(1)} %maximum_select_fusion.2), channel_id=1, source_target_pairs={{0,4},{4,0},{8,12},{12,8},{16,20},{20,16},{24,28},{28,24},{1,5},{5... | collective-permute-start | bytes 1769480 | tf_op jit(solution)/shard_map/ppermute | solution.py:622
  380.2 8.1 %collective-permute-start.17 = (f32[32,1792]{1,0:T(8,128)S(1)}, f32[32,1792]{1,0:T(8,128)S(1)}, u32[]{:S(2)}, u32[]{:S(2)}) collective-permute-start(f32[32,1792]{1,0:T(8,128)S(1)} %add.503), channel_id=1, source_target_pairs={{0,1},{1,0},{2,3},{3,2},{4,5},{5,4},{6,7},{7,6},{8,9},{9,8},{10,11... | collective-permute-start | bytes 688136 | tf_op jit(solution)/shard_map/ppermute | solution.py:622
  380.2 8.0 %collective-permute-start.15 = (f16[64,768]{1,0:T(8,128)(2,1)S(1)}, f16[64,768]{1,0:T(8,128)(2,1)S(1)}, u32[]{:S(2)}, u32[]{:S(2)}) collective-permute-start(f16[64,768]{1,0:T(8,128)(2,1)S(1)} %multiply_convert_fusion.1), channel_id=1, source_target_pairs={{0,16},{4,20},{8,24},{12,28},{16,0},{20,4},{24,8},{28,12},{1,17},{... | collective-permute-start | bytes 294920 | tf_op jit(solution)/shard_map/ppermute | solution.py:622
  392.2 23.6 %copy-start.28 = (s32[64]{0:T(128)S(1)}, s32[64]{0:T(128)}, u32[]{:S(2)}) copy-start(s32[64]{0:T(128)} %param.11) | copy-start | bytes 772
  392.2 23.9 %copy-start.24 = (f32[2]{0:T(128)S(1)}, f32[2]{0:T(128)}, u32[]{:S(2)}) copy-start(f32[2]{0:T(128)} %param.16) | copy-start | bytes 28
  392.6 8.1 %collective-permute-start.19 = (f32[768,768]{1,0:T(8,128)S(1)}, f32[768,768]{1,0:T(8,128)S(1)}, u32[]{:S(2)}, u32[]{:S(2)}) collective-permute-start(f32[768,768]{1,0:T(8,128)S(1)} %convert_multiply_fusion.2.early_ref), channel_id=1, source_target_pairs={{0,1},{1,0},{2,3},{3,2},{4,5},{5,4},{6,7},{7,6},{8,9},{9,8},{10,11... | collective-permute-start | bytes 7077896 | tf_op jit(solution)/shard_map/ppermute | solution.py:622
  392.7 7.3 %collective-permute-start.18 = (f16[128,768]{1,0:T(8,128)(2,1)S(1)}, f16[128,768]{1,0:T(8,128)(2,1)S(1)}, u32[]{:S(2)}, u32[]{:S(2)}) collective-permute-start(f16[128,768]{1,0:T(8,128)(2,1)S(1)} %maximum_select_fusion.5), channel_id=1, source_target_pairs={{0,8},{4,12},{8,0},{12,4},{16,24},{20,28},{24,16},{28,20},{1,9},{5... | collective-permute-start | bytes 589832 | tf_op jit(solution)/shard_map/ppermute | solution.py:622
  392.8 7.9 %collective-permute-start.20 = (f32[32,1792]{1,0:T(8,128)S(1)}, f32[32,1792]{1,0:T(8,128)S(1)}, u32[]{:S(2)}, u32[]{:S(2)}) collective-permute-start(f32[32,1792]{1,0:T(8,128)S(1)} %add.504), channel_id=1, source_target_pairs={{0,2},{1,3},{2,0},{3,1},{4,6},{5,7},{6,4},{7,5},{8,10},{9,11},{10,... | collective-permute-start | bytes 688136 | tf_op jit(solution)/shard_map/ppermute | solution.py:622
  402.2 10.6 %collective-permute-start.21 = (f16[256,768]{1,0:T(8,128)(2,1)S(1)}, f16[256,768]{1,0:T(8,128)(2,1)S(1)}, u32[]{:S(2)}, u32[]{:S(2)}) collective-permute-start(f16[256,768]{1,0:T(8,128)(2,1)S(1)} %maximum_select_fusion.3), channel_id=1, source_target_pairs={{0,4},{4,0},{8,12},{12,8},{16,20},{20,16},{24,28},{28,24},{1,5},{5... | collective-permute-start | bytes 1179656 | tf_op jit(solution)/shard_map/ppermute | solution.py:622
  414.2 7.6 %collective-permute-start.22 = (f32[512,768]{1,0:T(8,128)}, f32[512,768]{1,0:T(8,128)}, u32[]{:S(2)}, u32[]{:S(2)}) collective-permute-start(f32[512,768]{1,0:T(8,128)} %convert_multiply_fusion.3.late_ref), channel_id=1, source_target_pairs={{0,1},{1,0},{2,3},{3,2},{4,5},{5,4},{6,7},{7,6},{8,9},{9,8},{10,11... | collective-permute-start | bytes 4718600 | tf_op jit(solution)/shard_map/ppermute | solution.py:622
  416.7 76.6 %all-to-all-start.2 = ((bf16[16,128,768]{2,1,0:T(8,128)(2,1)}), bf16[16,128,768]{2,1,0:T(8,128)(2,1)}, u32[]{:S(2)}, u32[]{:S(2)}) async-start(bf16[16,128,768]{2,1,0:T(8,128)(2,1)} %bitcast.166), calls=%async_computation.2 | async-start | bytes 6291456 | tf_op jit(solution)/shard_map/all_to_all | solution.py:732
  421.9 17.9 %copy-start.11 = (f32[942080]{0:T(1024)S(1)}, f32[942080]{0:T(1024)}, u32[]{:S(2)}) copy-start(f32[942080]{0:T(1024)} %param.15) | copy-start | bytes 11304964
  434.5 5.2 %copy-start.10 = (f32[942080]{0:T(1024)S(1)}, f32[942080]{0:T(1024)}, u32[]{:S(2)}) copy-start(f32[942080]{0:T(1024)} %param.14) | copy-start | bytes 11304964
  438.3 29.5 %collective-permute-start.24 = (f16[7360,128]{1,0:T(8,128)(2,1)}, f16[7360,128]{1,0:T(8,128)(2,1)}, u32[]{:S(2)}, u32[]{:S(2)}) collective-permute-start(f16[7360,128]{1,0:T(8,128)(2,1)} %convert_element_type.205), channel_id=1, source_target_pairs={{0,1},{1,0},{2,3},{3,2},{4,5},{5,4},{6,7},{7,6},{8,9},{9,8},{10,11... | collective-permute-start | bytes 5652488 | tf_op jit(solution)/shard_map/ppermute | solution.py:622
  438.5 43.6 %collective-permute-start.23 = (f16[7360,128]{1,0:T(8,128)(2,1)}, f16[7360,128]{1,0:T(8,128)(2,1)}, u32[]{:S(2)}, u32[]{:S(2)}) collective-permute-start(f16[7360,128]{1,0:T(8,128)(2,1)} %convert_element_type.205), channel_id=1, source_target_pairs={{0,2},{1,3},{2,0},{3,1},{4,6},{5,7},{6,4},{7,5},{8,10},{9,11},{10,... | collective-permute-start | bytes 5652488 | tf_op jit(solution)/shard_map/ppermute | solution.py:622
  446.2 16.4 %slice-start = ((s8[15073280]{0:T(1024)(128)(4,1)}), s8[2490368]{0:T(1024)(128)(4,1)S(1)}, s32[]{:S(2)}) async-start(s8[15073280]{0:T(1024)(128)(4,1)} %bitcast.149), calls=%async_computation.5 | async-start | bytes 4980736
  450.6 11.9 %slice-start.1 = ((s8[15073280]{0:T(1024)(128)(4,1)}), s8[4194304]{0:T(1024)(128)(4,1)S(1)}, s32[]{:S(2)}) async-start(s8[15073280]{0:T(1024)(128)(4,1)} %bitcast.149), calls=%async_computation.6 | async-start | bytes 8388608
  450.6 11.9 %slice-start.2 = ((s8[15073280]{0:T(1024)(128)(4,1)}), s8[4194304]{0:T(1024)(128)(4,1)S(1)}, s32[]{:S(2)}) async-start(s8[15073280]{0:T(1024)(128)(4,1)} %bitcast.149), calls=%async_computation.7 | async-start | bytes 8388608
  455.0 7.6 %slice-start.3 = ((s8[15073280]{0:T(1024)(128)(4,1)}), s8[4194304]{0:T(1024)(128)(4,1)S(1)}, s32[]{:S(2)}) async-start(s8[15073280]{0:T(1024)(128)(4,1)} %bitcast.149), calls=%async_computation.8 | async-start | bytes 8388608
  482.1 5.3 %collective-permute-start.25 = (f16[7360,128]{1,0:T(8,128)(2,1)}, f16[7360,128]{1,0:T(8,128)(2,1)S(1)}, u32[]{:S(2)}, u32[]{:S(2)}) collective-permute-start(f16[7360,128]{1,0:T(8,128)(2,1)} %collective-permute-done.23), channel_id=1, source_target_pairs={{0,1},{1,0},{2,3},{3,2},{4,5},{5,4},{6,7},{7,6},{8,9},{9,8},{10,11... | collective-permute-start | bytes 5652488 | tf_op jit(solution)/shard_map/ppermute | solution.py:622
  (18 other events, 47.7 us)
Sparse Core Ops, SparseCore 0:
  10.9 56.1 all-gather.2
  68.6 96.2 all-gather.4

commit v3 on v2

--- a/solution.py
+++ b/solution.py
@@ -237,10 +237,11 @@
 
 
 def backward_kernel(
-    bound_ref, proj_ref, before_ref, dy_ref, through_ref, state_ref,
+    bound_ref, proj_ref, before_ref, dy_ref, through_ref, state_ref, gz_ref, tok_ref, cot_ref,
+    in_ref, norm_ref, ggain_ref,
     e_ref, et_ref, convw_ref, convb_ref, dtb_ref, alog_ref, skip_ref,
-    gp_ref, window_ref, small_ref,
-    gskip_ref, gsmall_ref, ext_ref, dt_ref, lam_ref, dsum_ref, xd_ref, g_ref, gnext_ref, cumt_ref,
+    window_ref, gtok_ref, small_ref,
+    gskip_ref, gsmall_ref, dtw_ref, ext_ref, dt_ref, lam_ref, dsum_ref, xd_ref, g_ref, gnext_ref, cumt_ref,
 ):
     step = pl.program_id(0)
     steps = pl.num_programs(0)
@@ -255,6 +256,7 @@
         gnext_ref[Q : Q + 8, :] = jnp.zeros((8, XBC), F32)
         gskip_ref[...] = jnp.zeros_like(gskip_ref)
         small_ref[...] = jnp.zeros_like(small_ref)
+        dtw_ref[...] = jnp.zeros_like(dtw_ref)
         gsmall_ref[...] = jnp.zeros_like(gsmall_ref)
 
     rows, rr, cc = chunk_masks(t0, bound)
@@ -337,7 +339,6 @@
     grad_dt = (direct + rate * grad_step) * sigmoid(dt_in)
     gsmall_ref[0:1, :] += jnp.sum(grad_dt, axis=0, keepdims=True)
     gsmall_ref[1:2, :] += rate * jnp.sum(dt_pos * grad_step, axis=0, keepdims=True)
-    gp_ref[:, XBC:LATE] = grad_dt[:, 0:HEADS].astype(BF16)
     grad_c = grad_c + dot(wide_left(gram_grad.T), tall_right(b_rows))
     grad_b = grad_b + dot(wide_left(gram_grad), tall_right(c_rows))
     slope = sig_pre * (1.0 + pre * (1.0 - sig_pre))
@@ -357,20 +358,36 @@
     small_ref[7:8, :] = jnp.maximum(
         small_ref[7:8, :], jnp.max(jnp.abs(total), axis=0, keepdims=True))
     total = total.astype(BF16)
-    gp_ref[:, :XBC] = total
     window_ref[0] = total[:, :WINDOW]
     window_ref[1] = total[:, XBC - WINDOW :]
     gnext_ref[Q : Q + 8, :] = gnext_ref[0:8, :]
+    grad_dt = grad_dt.astype(BF16)
+    grad_normed = (
+        dot(gz_ref[0], in_ref[:INNER, :]) + dot(total, in_ref[INNER : INNER + XBC, :])
+        + dot(grad_dt, in_ref[INNER + XBC : INNER + XBC + 128, :]))
+    tok = tok_ref[...].astype(F32)
+    rinv = lax.rsqrt(jnp.mean(tok * tok, axis=1, keepdims=True) + EPS_NORM)
+    nhat = tok * rinv
+    gain = norm_ref[...]
+    gng = grad_normed * gain
+    gtok_ref[...] = (cot_ref[...].astype(F32) + rinv * (
+        gng - nhat * jnp.mean(nhat * gng, axis=1, keepdims=True))).astype(BF16)
+    small_ref[6:7, :D] += jnp.sum(nhat * grad_normed, axis=0, keepdims=True)
+    dtw_ref[...] += dot(grad_dt.astype(F32).T.astype(BF16), (nhat * gain).astype(BF16))
 
     @pl.when(step == steps - 1)
     def _():
         skips = head_sum(jnp.broadcast_to(gskip_ref[...], (8, INNER)), et_ref)
+        small_ref[5:6, :INNER] = ggain_ref[...]
         small_ref[6:7, D : D + 128] = gsmall_ref[0:1, :]
         small_ref[6:7, D + 128 : D + 256] = gsmall_ref[1:2, :]
         small_ref[6:7, D + 256 : D + 384] = skips[0:1, :]
-
-
-def run_backward(proj, dy, through, states, bound, e2, et, params):
+        small_ref[8 : 8 + HEADS, :D] = dtw_ref[0:HEADS, :]
+
+
+def run_backward(
+    proj, dy, through, states, pair, tok, cot, in_w, norm_gain, ggain, bound, e2, et, params
+):
     n = proj.shape[0]
     steps = n // Q
 
@@ -387,23 +404,27 @@
             pl.BlockSpec((Q, INNER), rev),
             pl.BlockSpec((Q, 128), rev),
             pl.BlockSpec((1, STATE, INNER), lambda i: (steps - 1 - i, 0, 0)),
+            pl.BlockSpec((1, Q, INNER), lambda i: (0, steps - 1 - i, 0)),
+            pl.BlockSpec((Q, D), rev), pl.BlockSpec((Q, D), rev),
+            const_spec(in_w.shape), const_spec((1, D)), const_spec((1, INNER)),
             const_spec((256, INNER)), const_spec((INNER, 128)),
             const_spec((8, XBC)), const_spec((1, XBC)), const_spec((1, 128)),
             const_spec((1, 128)), const_spec((1, INNER)),
         ],
         out_specs=[
-            pl.BlockSpec((Q, LATE), rev),
             pl.BlockSpec((2, Q, WINDOW), lambda i: (0, steps - 1 - i, 0)),
-            const_spec((8, XBC)),
+            pl.BlockSpec((Q, D), rev),
+            const_spec((32, XBC)),
         ],
         out_shape=[
-            jax.ShapeDtypeStruct((n, LATE), BF16),
             jax.ShapeDtypeStruct((2, n, WINDOW), BF16),
-            jax.ShapeDtypeStruct((8, XBC), F32),
+            jax.ShapeDtypeStruct((n, D), BF16),
+            jax.ShapeDtypeStruct((32, XBC), F32),
         ],
         scratch_shapes=[
             pltpu.VMEM((1, INNER), F32),
             pltpu.VMEM((8, 128), F32),
+            pltpu.VMEM((128, D), F32),
             pltpu.VMEM((Q + 8, XBC), F32),
             pltpu.VMEM((Q, 128), F32),
             pltpu.VMEM((STATE, INNER), F32),
@@ -417,7 +438,8 @@
             dimension_semantics=("arbitrary",), vmem_limit_bytes=48 * 2**20),
         cost_estimate=pl.CostEstimate(
             flops=50 * 10**9, bytes_accessed=50 * 2**20, transcendentals=2 * 10**7),
-    )(bound, proj, proj, dy, through, states, e2, et, *params[:5])
+    )(bound, proj, proj, dy, through, states, pair, tok, cot, in_w, norm_gain, ggain,
+      e2, et, *params[:5])
 
 
 BETA_ONE = 0.9
@@ -497,6 +519,11 @@
 
     block(0, NORM_ROWS, IN_BLOCK, in_ref)
 
+    @pl.when(step == PREP_STEPS - 1)
+    def _():
+        used = PROJ - (PREP_STEPS - 1) * IN_BLOCK
+        in_ref[used:, :] = jnp.zeros((IN_BLOCK - used, D), BF16)
+
     @pl.when(step < INNER // OUT_BLOCK)
     def _():
         low = OUT_START // 16 * 16
@@ -517,7 +544,8 @@
             const_spec((256, INNER)), const_spec((INNER, 128)),
         ],
         out_shape=[
-            jax.ShapeDtypeStruct((PROJ, D), BF16), jax.ShapeDtypeStruct((INNER, D), BF16),
+            jax.ShapeDtypeStruct((PREP_STEPS * IN_BLOCK, D), BF16),
+            jax.ShapeDtypeStruct((INNER, D), BF16),
             vector(D), jax.ShapeDtypeStruct((8, XBC), F32), vector(XBC), vector(128), vector(128),
             vector(INNER), vector(INNER),
             jax.ShapeDtypeStruct((256, INNER), BF16), jax.ShapeDtypeStruct((INNER, 128), BF16),
@@ -627,48 +655,73 @@
     return jnp.clip(jnp.floor(jnp.log2(F16_TOP / bound)), -126.0, 120.0)
 
 
-def values_scaled(values, power):
-    return values * jnp.exp2(power)
-
-
 def to_wire(values, power):
-    return values_scaled(values, power).astype(jnp.float16)
+    return (values * jnp.exp2(power)).astype(jnp.float16)
 
 
 def from_wire(values, power):
     return values.astype(F32) * jnp.exp2(-power)
 
 
-def halve(values, power, axis, bit):
-    side = (lax.axis_index(axis) // bit) % 2
-    rows = values.shape[-2] // 2
+def scatter(values, power, axis, bit=1, count=2):
+    place = (lax.axis_index(axis) // bit) % count
+    rows = values.shape[-2] // count
     mark = min(MARK, rows)
     dim = values.ndim - 2
-    keep = lax.dynamic_slice_in_dim(values, side * rows, rows, dim)
-    send = lax.dynamic_slice_in_dim(values, (1 - side) * (rows - mark), rows + mark, dim)
-    line = lax.broadcasted_iota(jnp.int32, send.shape, dim)
-    marked = jnp.where(side == 1, line >= rows, line < mark)
-    wire = jnp.where(marked, power, values_scaled(send, power)).astype(jnp.float16)
-    got = swap(wire, axis, bit)
-    got_power = lax.dynamic_slice_in_dim(got, (1 - side) * rows, 1, dim)
-    got_power = got_power.reshape(-1, D)[0:1, 0:1].astype(F32)
-    body = lax.dynamic_slice_in_dim(got, side * mark, rows, dim)
-    sum_bound = F16_TOP * (jnp.exp2(-power) + jnp.exp2(-got_power))
-    return keep + from_wire(body, got_power), power_for(sum_bound)
-
-
-def halve_data(values, power, bit):
-    return halve(values, power, "dp", bit)
-
-
-def data_bits():
-    return [1 << k for k in range(lax.axis_size("dp").bit_length() - 1)]
-
-
-def double_data(wire, bit):
-    side = (lax.axis_index("dp") // bit) % 2
-    got = swap(wire, "dp", bit)
-    return jnp.where(side == 0, jnp.concatenate([wire, got]), jnp.concatenate([got, wire]))
+    total = lax.dynamic_slice_in_dim(values, place * rows, rows, dim)
+    least = power
+    for offset in range(1, count):
+        to = place ^ offset
+        last = to == count - 1
+        start = to * rows - jnp.where(last, mark, 0)
+        send = lax.dynamic_slice_in_dim(values, start, rows + mark, dim)
+        line = lax.broadcasted_iota(jnp.int32, send.shape, dim)
+        marked = jnp.where(last, line < mark, line >= rows)
+        wire = jnp.where(marked, power, send * jnp.exp2(power)).astype(jnp.float16)
+        got = swap(wire, axis, bit * offset)
+        last = place == count - 1
+        got_power = lax.dynamic_slice_in_dim(got, jnp.where(last, 0, rows), 1, dim)
+        got_power = got_power.reshape(-1, D)[0:1, 0:1].astype(F32)
+        body = lax.dynamic_slice_in_dim(got, jnp.where(last, mark, 0), rows, dim)
+        total = total + from_wire(body, got_power)
+        least = jnp.minimum(least, got_power)
+    return total, least - float(count.bit_length() - 1)
+
+
+def everyones(values, axis, bit=1, count=2):
+    place = (lax.axis_index(axis) // bit) % count
+    pieces = [values] + [swap(values, axis, bit * offset) for offset in range(1, count)]
+    step = 1
+    while step < count:
+        flip = (place // step) % 2 == 1
+        pieces = [
+            jnp.where(flip, pieces[i ^ step], pieces[i]) for i in range(count)]
+        step *= 2
+    return pieces
+
+
+def gather(values, axis, bit=1, count=2):
+    return jnp.concatenate(everyones(values, axis, bit, count))
+
+
+def add_all(values, axis, bit=1, count=2):
+    pieces = everyones(values, axis, bit, count) if count > 2 else [
+        values, swap(values, axis, bit)]
+    total = pieces[0]
+    for piece in pieces[1:]:
+        total = total + piece
+    return total
+
+
+def data_groups():
+    size = lax.axis_size("dp")
+    groups = [(1, 2)]
+    bit = 2
+    while bit < size:
+        count = 4 if bit * 4 <= size else 2
+        groups.append((bit, count))
+        bit *= count
+    return groups
 
 
 def dot_tn(a, b):
@@ -739,11 +792,10 @@
 
     bound_arr = bound.reshape(1)
     tok = packed.astype(F32)
-    rinv = lax.rsqrt(jnp.mean(tok * tok, axis=1, keepdims=True) + EPS_NORM)
-    nhat = tok * rinv
+    nhat = tok * lax.rsqrt(jnp.mean(tok * tok, axis=1, keepdims=True) + EPS_NORM)
     normed = (nhat * norm_gain).astype(BF16)
     proj_z = dot_nt(normed, in_w[:INNER])
-    proj = dot_nt(normed, in_w[INNER:])
+    proj = dot_nt(normed, in_w[INNER:PROJ])
     pair, dy, through, states, ggain, zmax = run_forward(
         proj_z, proj, gm, bound_arr, e2, et, params)
     result = (tok + dot(pair[1], out_w)).astype(BF16)
@@ -757,70 +809,50 @@
         1.02 * root * jnp.max(zmax) * normed_norm, root * cot_top * mixed_norm))
     early = lax.dot_general(
         pair, jnp.stack([normed, cot]), (((1,), (1,)), ((0,), (0,))), preferred_element_type=F32)
-    early, early_power = halve(early, early_power, "zero", 1)
-    early = early.reshape(INNER, D)
-    part_normed = dot(pair[0], in_w[:INNER])
-    early, early_power, part_normed, dy = tie((early, early_power, part_normed, dy))
-    early, early_power = halve(early, early_power, "zero", 2)
-    gp, window, small8 = run_backward(proj, dy, through, states, bound_arr, e2, et, params)
-    gp, window, back_out, early, early_power, whole_master = tie(
-        (gp, window, back_out, early, early_power, whole_master))
-
-    bits = data_bits()
+    early, early_power = scatter(early, early_power, "zero", 1)
+    early, early_power, dy = tie((early.reshape(INNER, D), early_power, dy))
+    early, early_power = scatter(early, early_power, "zero", 2)
+    window, grad_tok, small = run_backward(
+        proj, dy, through, states, pair, packed, cot, in_w, norm_gain, ggain,
+        bound_arr, e2, et, params)
+    window, small, back_out, early, early_power, whole_master = tie(
+        (window, small, back_out, early, early_power, whole_master))
+
+    groups = data_groups()
     late = lax.dot_general(
         window, jnp.stack([normed, normed]), (((1,), (1,)), ((0,), (0,))),
         preferred_element_type=F32)
-    late, gp = tie((late, gp))
-    late_power = power_for(1.02 * root * jnp.max(small8[7:8]) * normed_norm)
-    late, late_power = halve(late, late_power, "zero", 1)
-    late = late.reshape(WINDOW, D)
-    early, early_power = halve_data(early, early_power, bits[0])
-    grad_normed = part_normed + dot(gp, in_w[INNER:])
-    late, late_power, early, early_power, grad_normed = tie(
-        (late, late_power, early, early_power, grad_normed))
-    late, late_power = halve(late, late_power, "zero", 2)
-    for bit in bits[1:-1]:
-        early, early_power = halve_data(early, early_power, bit)
-    gng = grad_normed * norm_gain
-    grad_norm_gain = jnp.sum(nhat * grad_normed, axis=0, keepdims=True)
-    grad_tok = cot.astype(F32) + rinv * (gng - nhat * jnp.mean(nhat * gng, axis=1, keepdims=True))
-    grad_tok = grad_tok.astype(BF16)
-    line = iota((8, 1), 0)
-    small8 = jnp.where(line == 5, jnp.pad(ggain, ((0, 0), (0, XBC - INNER))), small8)
-    small8 = small8 + jnp.where(line == 6, jnp.pad(grad_norm_gain, ((0, 0), (0, XBC - D))), 0.0)
-    small = jnp.concatenate([
-        small8, jnp.pad(dot_tn(gp[:, XBC:], normed), ((0, 0), (0, XBC - D)))])
-    late, late_power, early, early_power, small, grad_tok = tie(
-        (late, late_power, early, early_power, small, grad_tok))
-    small = small + swap(small, "dp", bits[0])
-    late, late_power = halve_data(late, late_power, bits[0])
-    early, early_power = halve_data(early, early_power, bits[-1])
+    late_power = power_for(1.02 * root * jnp.max(small[7:8]) * normed_norm)
+    late, late_power = scatter(late, late_power, "zero", 1)
+    early, early_power = scatter(early, early_power, "dp", *groups[0])
+    small = add_all(small, "zero", 1)
+    late, late_power, early, early_power, small = tie(
+        (late.reshape(WINDOW, D), late_power, early, early_power, small))
+    late, late_power = scatter(late, late_power, "zero", 2)
+    for group in groups[1:]:
+        early, early_power = scatter(early, early_power, "dp", *group)
     early = to_wire(early, early_power)
+    small = add_all(small, "zero", 2)
     picked_grad = spread(grad_tok)
-    late, late_power, early, picked_grad, small = tie(
-        (late, late_power, early, picked_grad, small))
-    for bit in bits[1:-1]:
-        late, late_power = halve_data(late, late_power, bit)
-        small = small + swap(small, "dp", bit)
-        early = double_data(early, bits[-1]) if bit == bits[1] else early
+    late, late_power, early, small, picked_grad = tie(
+        (late, late_power, early, small, picked_grad))
+    late, late_power = scatter(late, late_power, "dp", *groups[0])
+    for group in reversed(groups[1:]):
+        early = gather(early, "dp", *group)
+    small = add_all(small, "dp", *groups[0])
     late, late_power, early, small = tie((late, late_power, early, small))
-    late, late_power = halve_data(late, late_power, bits[-1])
-    small = small + swap(small, "dp", bits[-1])
+    for group in groups[1:]:
+        late, late_power = scatter(late, late_power, "dp", *group)
+        small = add_all(small, "dp", *group)
     late = to_wire(late, late_power)
-    for bit in reversed(bits[1:-1]):
-        early = double_data(early, bit)
+    early = from_wire(gather(early, "dp", *groups[0]), early_power)
     late, early, small = tie((late, early, small))
-    late = double_data(late, bits[-1])
-    small = small + swap(small, "zero", 1)
-    early = from_wire(double_data(early, bits[0]), early_power)
-    late, early, small = tie((late, early, small))
-    for bit in reversed(bits[1:-1]):
-        late = double_data(late, bit)
-    small = small + swap(small, "zero", 2)
+    for group in reversed(groups[1:]):
+        late = gather(late, "dp", *group)
     early_other = swap(early, "zero", 1)
-    late, early_other, picked_grad, small = tie((late, early_other, picked_grad, small))
+    late, early_other, picked_grad = tie((late, early_other, picked_grad))
     back_grad = send_back(picked_grad)
-    late = from_wire(double_data(late, bits[0]), late_power)
+    late = from_wire(gather(late, "dp", *groups[0]), late_power)
     late_other = swap(late, "zero", 1)
 
     steps_f = iteration_tally[0].astype(F32)

time: 514 us -> 501 us (0.975)
  matrix products: 70.5 us -> 52.4 us
  Pallas kernels: 105 us -> 116 us
  between operations: 29.1 us -> 35.5 us
    dot_general x5 -> x3, matrix products: 35.3 us -> 21.4 us  [dot(): lax.dot_general(a, b, (((1,), (0,)), ((), ())), preferred_element_type=F32)]
    pallas_call x1, Pallas kernels: 49.4 us -> 61.6 us  [run_backward(): pl.pallas_call(backward_kernel, grid=(steps,), in_specs=[pl.BlockSpec(mem...]
    ppermute x26 -> x31, starting transfers between devices: 24.3 us -> 33.5 us  [swap(): return lax.ppermute(values, axis, [(i, i ^ bit) for i in range(size)])]
    all_to_all x2, starting transfers between devices: 18.3 us -> 9.5 us  [send_back(): return lax.all_to_all(picked, 'dp', split_axis=0, concat_axis=0, tiled=True)]
    ppermute x26 -> x31, waiting for transfers between devices: 81.9 us -> 76.2 us  [swap(): return lax.ppermute(values, axis, [(i, i ^ bit) for i in range(size)])]
    convert_element_type x21 -> x20, other arithmetic: 13.3 us -> 12.3 us  [the longest x10 6.51 us: scatter(): got_power = got_power.reshape(-1, D)[0:1, 0:1].astype(F32)]
    unnamed x73 -> x52, local copies, waits for them, and re-layouts: 15.7 us -> 15.7 us
  transfers between devices with their start and end apart: 31 -> 36, of which waited for: 19 -> 18; matrix products, arithmetic and copies ran while one was open for 29% -> 24% of each run, Pallas kernels for 21% -> 24%
where the time goes in v3:
time: 501 us; the launch traced here: 493 us
  waiting for transfers between devices  132 us (26%)
  Pallas kernels  116 us (23%)
  other arithmetic  69 us (14%)
  matrix products  52.4 us (10%)
  starting transfers between devices  50.5 us (10%)
  local copies, waits for them, and re-layouts  37.6 us (8%)
  between operations  35.5 us (7%)
    ppermute x31, waiting for transfers between devices, swap(): return lax.ppermute(values, axis, [(i, i ^ bit) for i in range(size)])  76.2 us
    pallas_call x1, Pallas kernels, run_backward(): pl.pallas_call(backward_kernel, grid=(steps,), in_specs=[pl.BlockSpec(mem...  61.6 us
    all_gather x1, waiting for transfers between devices, on_device(): flat = lax.all_gather(own.astype(BF16), 'zero', axis=0, tiled=True)  40.8 us
    pallas_call x1, Pallas kernels, run_forward(): pl.pallas_call(forward_kernel, grid=(steps,), in_specs=[pl.BlockSpec(memo...  36.2 us
    ppermute x31, starting transfers between devices, swap(): return lax.ppermute(values, axis, [(i, i ^ bit) for i in range(size)])  33.5 us
    dot_general x3, matrix products, dot(): lax.dot_general(a, b, (((1,), (0,)), ((), ())), preferred_element_type=F32)  21.4 us
    dynamic_update_slice x4, other arithmetic, put(): return lax.dynamic_update_index_in_dim(new_master, new, shard, 0)  19.6 us
    unnamed x52, local copies, waits for them, and re-layouts  15.7 us
  transfers between devices with their start and end apart: 36, of which 18 were waited for; matrix products, arithmetic and copies ran while one was open for 24% of the time, Pallas kernels for 24%

profile of v3, /device:TPU:0, one launch (start us, length us, event | category | flops | bytes accessed | tf_op | source)
XLA Modules:
  0.0 492.9 jit_solution(7465321533603199181)
XLA Ops:
  7.2 3.5 bitcast_convert_fusion
  15.0 7.4 %all-to-all-start = ((bf16[16,128,768]{2,1,0:T(8,128)(2,1)}), bf16[16,128,768]{2,1,0:T(8,128)(2,1)}, u32[]{:S(2)}, u32[]{:S(2)}) async-start(bf16[16,128,768]{2,1,0:T(8,128)(2,1)} %gather_fusion), calls=%async_computation | async-start | bytes 6291456 | tf_op jit(solution)/shard_map/all_to_all | solution.py:758
  26.3 40.8 %all-gather.3.cloned.1.call-done.flat_ref = bf16[29440,128]{1,0:T(8,128)(2,1)} async-done(((bf16[7360,128]{1,0:T(8,128)(2,1)}), bf16[29440,128]{1,0:T(8,128)(2,1)}) %all-gather.3.cloned.1.call-update) | async-done | bytes 7536656 | tf_op jit(solution)/shard_map/all_gather | solution.py:752
  67.0 6.0 %shard_map.136 = (bf16[3584,768]{1,0:T(8,128)(2,1)S(1)}, bf16[1536,768]{1,0:T(8,128)(2,1)S(1)}, f32[1,768]{1,0:T(1,128)S(1)}, f32[8,1792]{1,0:T(8,128)S(1)}, f32...) custom-call(bf16[29440,128]{1,0:T(8,128)(2,1)} %all-gather.3.cloned., ...), custom_call_target="tpu_custom_call" | custom-call | flops 1000000000 | bytes 16777216 | tf_op jit(solution)/shard_map/pallas_call | solution.py:535
  73.0 2.6 copy-done
  77.0 4.7 fusion.62.gm_ref
  81.7 11.5 %all-to-all-done = bf16[16,128,768]{2,1,0:T(8,128)(2,1)} async-done(((bf16[16,128,768]{2,1,0:T(8,128)(2,1)}), bf16[16,128,768]{2,1,0:T(8,128)(2,1)}, u32[]{:S(2)}, u32[]{:S(2)}) %all-to-all-start) | async-done | bytes 3145760 | tf_op jit(solution)/shard_map/all_to_all | solution.py:758
  93.9 5.8 %fusion.19 = (f32[1024]{0:T(1024)S(1)}, bf16[1024,768]{1,0:T(8,128)(2,1)S(1)}) fusion(bf16[2048,768]{1,0:T(8,128)(2,1)} %bitcast.7, s32[1024]{0:T(1024)S(1)} %fusion.42), kind=kOutput, calls=%fused_computation.47 | convolution fusion | flops 3226467328 | bytes 4726784 | tf_op jit(solution)/shard_map/dot_general | solution.py:27
  99.7 4.6 fusion.30.z_ref
  104.3 5.8 %fusion.28.proj_ref.before_ref = f32[1024,1816]{1,0:T(8,128)} fusion(bf16[3584,768]{1,0:T(8,128)(2,1)S(1)} %copy-done.1, bf16[1024,768]{1,0:T(8,128)(2,1)S(1)} %get-tuple-element.171.tok_ref, f32[768]{0:T(1024)S(1)} %get-tuple-element.147, f32[1024]{0:T(1024)S(1)} %add_rsqrt_fusion), kind=kOutput, calls=%fused_computation.59 | convolution fusion | flops 2859466752 | bytes 11808768 | tf_op jit(solution)/shard_map/dot_general | solution.py:31
  110.1 36.2 %shard_map.137 = (bf16[2,1024,1536]{2,1,0:T(8,128)(2,1)}, f32[1024,1536]{1,0:T(8,128)}, f32[1024,128]{1,0:T(8,128)S(1)}, f32[8,128,1536]{2,1,0:T(8,128)}, f32[1,1536]{1,0:T(1,128)S(1)}, /*index=5*/f32[1,1536]{1,0:T(1,128)S(1)}) custom-call(s32[1]{0:T(128)} %dynamic_slice.160.bound_ref, f32[1024,1536]{1,0:T(8,128)} %fusion.30.z_ref, ...), custom_call_target="tpu_custom_call" | custom-call | flops 30000001024 | bytes 41943040 | tf_op jit(solution)/shard_map/pallas_call | solution.py:197
  150.4 10.5 %fusion.15 = bf16[2048,768]{1,0:T(8,128)(2,1)} fusion(s32[2048]{0:T(1024)S(1)} %bitcast.159, bf16[1024,768]{1,0:T(8,128)(2,1)S(1)} %get-tuple-element.171.tok_ref, bf16[1536,768]{1,0:T(8,128)(2,1)} %copy-done.2, bf16[2,1024,1536]{2,1,0:T(8,128)(2,1)} %get-tuple-element.90.gz_ref), kind=kOutput, calls=%fused_computation.42 | convolution fusion | flops 5643173888 | bytes 10231808 | tf_op jit(solution)/shard_map/dot_general | solution.py:27
  162.3 8.6 %fusion.17 = f32[2,1536,768]{2,1,0:T(8,128)S(1)} fusion(bf16[2,1024,1536]{2,1,0:T(8,128)(2,1)} %get-tuple-element.90.gz_ref, bf16[1,1024,768]{2,1,0:T(8,128)(2,1)S(1)} %fusion.66, bf16[1,1024,768]{2,1,0:T(8,128)(2,1)S(1)} %copy-done.14), kind=kOutput, calls=%fused_computation.45 | convolution fusion | flops 4833411072 | bytes 18874368 | tf_op jit(solution)/shard_map/dot_general | solution.py:810
  170.9 3.7 copy-done.10
  176.7 4.7 all-to-all-start.1
  183.6 3.6 multiply_add_fusion
  189.2 61.6 %shard_map.138 = (bf16[2,1024,1024]{2,1,0:T(8,128)(2,1)}, bf16[1024,768]{1,0:T(8,128)(2,1)S(1)}, f32[32,1792]{1,0:T(8,128)S(1)}) custom-call(s32[1]{0:T(128)} %dynamic_slice.160.bound_ref, f32[1024,1816]{1,0:T(8,128)} %fusion.28.proj_ref.before_ref, f32[1024,1816]{1,0:T(8,128)} %fusion.28.proj_ref.before_ref, f32[1024,1536]{1,0:T(8,128)} %get-tuple-element.94.dy_ref, ...), custom_call_target="tpu_custom_call" | custom-call | flops 49999998976 | bytes 52428800 | tf_op jit(solution)/shard_map/pallas_call | solution.py:397
  256.2 7.2 %fusion.18 = f32[2,1024,768]{2,1,0:T(8,128)S(1)} fusion(bf16[2,1024,1024]{2,1,0:T(8,128)(2,1)} %get-tuple-element.103, bf16[1,1024,768]{2,1,0:T(8,128)(2,1)} %copy-done.15), kind=kOutput, calls=%fused_computation.46 | convolution fusion | flops 3222798336 | bytes 12058624 | tf_op jit(solution)/shard_map/dot_general | solution.py:822
  263.5 2.7 copy-done.11
  271.6 12.9 %collective-permute-done.3 = f16[400,768]{1,0:T(8,128)(2,1)} collective-permute-done((f16[400,768]{1,0:T(8,128)(2,1)S(1)}, f16[400,768]{1,0:T(8,128)(2,1)}, u32[]{:S(2)}, u32[]{:S(2)}) %collective-permute-start.3) | collective-permute-done | bytes 614432 | tf_op jit(solution)/shard_map/ppermute | solution.py:650
  290.2 2.7 multiply_add_fusion.2
  295.5 3.6 collective-permute-start.8
  300.0 5.1 %fusion.16 = bf16[2048,768]{1,0:T(8,128)(2,1)} fusion(bf16[1024,768]{1,0:T(8,128)(2,1)S(1)} %copy-done.4, s32[2048]{0:T(1024)S(1)} %bitcast.160), kind=kOutput, calls=%fused_computation.43 | convolution fusion | flops 3224895488 | bytes 4726784 | tf_op jit(solution)/shard_map/dot_general | solution.py:27
  305.1 4.4 collective-permute-done.6
  319.7 3.6 collective-permute-start.11
  328.3 6.7 %collective-permute-done.12 = f16[96,768]{1,0:T(8,128)(2,1)S(1)} collective-permute-done((f16[96,768]{1,0:T(8,128)(2,1)S(1)}, f16[96,768]{1,0:T(8,128)(2,1)S(1)}, u32[]{:S(2)}, u32[]{:S(2)}) %collective-permute-start.12) | collective-permute-done | bytes 147488 | tf_op jit(solution)/shard_map/ppermute | solution.py:650
  335.3 4.6 collective-permute-done.14
  345.2 2.6 collective-permute-start.16
  348.3 3.3 collective-permute-start.19
  354.5 9.8 %collective-permute-done.16 = f16[80,768]{1,0:T(8,128)(2,1)S(1)} collective-permute-done((f16[80,768]{1,0:T(8,128)(2,1)S(1)}, f16[80,768]{1,0:T(8,128)(2,1)S(1)}, u32[]{:S(2)}, u32[]{:S(2)}) %collective-permute-start.16) | collective-permute-done | bytes 122912 | tf_op jit(solution)/shard_map/ppermute | solution.py:650
  369.7 6.3 %collective-permute-done.20 = f32[32,1792]{1,0:T(8,128)S(1)} collective-permute-done((f32[32,1792]{1,0:T(8,128)S(1)}, f32[32,1792]{1,0:T(8,128)S(1)}, u32[]{:S(2)}, u32[]{:S(2)}) %collective-permute-start.20) | collective-permute-done | bytes 229408 | tf_op jit(solution)/shard_map/ppermute | solution.py:650
  376.7 2.4 collective-permute-start.22
  381.2 3.1 collective-permute-done.22
  384.3 3.7 collective-permute-done.23
  391.2 9.5 %collective-permute-done.26 = f16[256,768]{1,0:T(8,128)(2,1)S(1)} collective-permute-done((f16[256,768]{1,0:T(8,128)(2,1)S(1)}, f16[256,768]{1,0:T(8,128)(2,1)S(1)}, u32[]{:S(2)}, u32[]{:S(2)}) %collective-permute-start.26) | collective-permute-done | bytes 393248 | tf_op jit(solution)/shard_map/ppermute | solution.py:650
  404.7 4.9 all-to-all-start.2
  409.6 12.7 %shard_map.139 = (f32[7360,128]{1,0:T(8,128)}, f32[7360,128]{1,0:T(8,128)}) custom-call(s32[2]{0:T(128)S(1)} %pad_add_fusion.who_ref, f32[2]{0:T(128)S(1)} %pad_maximum_fusion.6.rate_ref, f32[768,768]{1,0:T(8,128)S(1)} %convert_multiply_fusion.2.early_ref, f32[768,768]{1,0:T(8,128)} %copy-done.12, f32[512,768]{1,0:T(8,128)} %convert_multiply_fusion.3.late_ref, ...), custom_call_target="tpu_custom_call" | custom-call | flops 100000000 | bytes 25165824 | tf_op jit(solution)/shard_map/pallas_call | solution.py:629
  422.3 3.7 convert_element_type.215
  426.4 6.2 %fusion.6 = (f32[7360,128]{1,0:T(8,128)}, f32[7360,128]{1,0:T(8,128)}) fusion(f32[7360,128]{1,0:T(8,128)} %get-tuple-element.133, f32[942080]{0:T(1024)S(1)} %copy-done.8, f32[942080]{0:T(1024)S(1)} %copy-done.7), kind=kLoop, calls=%fused_computation.18 | loop fusion | flops 6594560 | bytes 18841600 | tf_op jit(solution)/shard_map/add | solution.py:871
  432.6 4.5 gather_fusion.1
  437.1 4.3 broadcast_select_fusion.1
  441.4 7.6 %broadcast_in_dim.157 = f32[4,7360,128]{2,1,0:T(8,128)} broadcast(f32[]{:T(128)} %constant.340.clone.1), dimensions={} | broadcast | bytes 15073284 | tf_op jit(solution)/shard_map/broadcast_in_dim | solution.py:874
  449.0 5.3 %bitcast_dynamic-update-slice_fusion.3 = f32[4,7360,128]{2,1,0:T(8,128)} fusion(f32[4,7360,128]{2,1,0:T(8,128)} %broadcast_in_dim.157, s32[]{:T(128)S(6)} %select_n.624, f16[7360,128]{1,0:T(8,128)(2,1)} %convert_element_type.215, f32[4,7360,128]{2,1,0:T(8,128)S(1)} %bitcast.143, f32[]{:T(128)} %bitcast.52, f32[]{:T(128)} %bitcast.51), kind=kLoop, calls=%fused_computation.34 | loop fusion | flops 4710400 | bytes 9421828 | tf_op jit(solution)/shard_map/jit(dynamic_update_index_in_dim)/dynamic_update_slice | solution.py:881
  454.3 5.3 %bitcast_dynamic-update-slice_fusion.2 = f32[4,7360,128]{2,1,0:T(8,128)} fusion(f32[4,7360,128]{2,1,0:T(8,128)} %bitcast_dynamic-update-slice_fusion.3, s32[]{:T(128)S(6)} %select_n.751, f16[7360,128]{1,0:T(8,128)(2,1)} %collective-permute-done.29, f32[4,7360,128]{2,1,0:T(8,128)S(1)} %bitcast.144, f32[]{:T(128)} %bitcast.52, f32[]{:T(128)} %bitcast.51), kind=kLoop, calls=%fused_computation.29 | loop fusion | flops 4710400 | bytes 9421828 | tf_op jit(solution)/shard_map/jit(dynamic_update_index_in_dim)/dynamic_update_slice | solution.py:881
  459.6 10.3 %collective-permute-done.28 = f16[7360,128]{1,0:T(8,128)(2,1)} collective-permute-done((f16[7360,128]{1,0:T(8,128)(2,1)}, f16[7360,128]{1,0:T(8,128)(2,1)}, u32[]{:S(2)}, u32[]{:S(2)}) %collective-permute-start.28) | collective-permute-done | bytes 1884192 | tf_op jit(solution)/shard_map/ppermute | solution.py:650
  469.8 5.3 %bitcast_dynamic-update-slice_fusion.1 = f32[4,7360,128]{2,1,0:T(8,128)} fusion(f32[4,7360,128]{2,1,0:T(8,128)} %bitcast_dynamic-update-slice_fusion.2, s32[]{:T(128)S(6)} %select_n.755, f16[7360,128]{1,0:T(8,128)(2,1)} %collective-permute-done.28, f32[4,7360,128]{2,1,0:T(8,128)S(1)} %bitcast.145, f32[]{:T(128)} %bitcast.52, f32[]{:T(128)} %bitcast.51), kind=kLoop, calls=%fused_computation.24 | loop fusion | flops 4710400 | bytes 9421828 | tf_op jit(solution)/shard_map/jit(dynamic_update_index_in_dim)/dynamic_update_slice | solution.py:881
  475.1 3.8 bitcast_dynamic-update-slice_fusion
  481.1 2.6 gather_fusion.2
  (186 shorter events, 65.3 us)
Async XLA Ops:
  7.2 59.9 %all-gather.3.cloned.1.call-start = ((), (), s32[]{:S(2)}) async-start(), calls=%async_computation.3 | async-start | bytes 9420800 | tf_op jit(solution)/shard_map/all_gather | solution.py:752
  10.7 243.4 %all-gather.5.cloned.1.call-start = ((), (), s32[]{:S(2)}) async-start(), calls=%async_computation.4 | async-start | bytes 18841600 | tf_op jit(solution)/shard_map/all_gather | solution.py:769
  15.0 7.6 %copy-start.13 = (bf16[1,1024,768]{2,1,0:T(8,128)(2,1)S(1)}, bf16[1,1024,768]{2,1,0:T(8,128)(2,1)}, u32[]{:S(2)}) copy-start(bf16[1,1024,768]{2,1,0:T(8,128)(2,1)} %param.10) | copy-start | bytes 4718596
  15.0 9.2 %copy-start.19 = (s32[64]{0:T(128)S(1)}, s32[64]{0:T(128)}, u32[]{:S(2)}) copy-start(s32[64]{0:T(128)} %param.11) | copy-start | bytes 772
  15.0 78.2 %all-to-all-start = ((bf16[16,128,768]{2,1,0:T(8,128)(2,1)}), bf16[16,128,768]{2,1,0:T(8,128)(2,1)}, u32[]{:S(2)}, u32[]{:S(2)}) async-start(bf16[16,128,768]{2,1,0:T(8,128)(2,1)} %gather_fusion), calls=%async_computation | async-start | bytes 6291456 | tf_op jit(solution)/shard_map/all_to_all | solution.py:758
  93.9 5.8 %copy-start.1 = (bf16[3584,768]{1,0:T(8,128)(2,1)S(1)}, bf16[3584,768]{1,0:T(8,128)(2,1)}, u32[]{:S(2)}) copy-start(bf16[3584,768]{1,0:T(8,128)(2,1)} %copy-done) | copy-start | bytes 16515076
  162.3 8.7 %copy-start.15 = (bf16[1,1024,768]{2,1,0:T(8,128)(2,1)}, bf16[1,1024,768]{2,1,0:T(8,128)(2,1)S(1)}, u32[]{:S(2)}) copy-start(bf16[1,1024,768]{2,1,0:T(8,128)(2,1)S(1)} %fusion.66) | copy-start | bytes 4718596
  176.7 4.9 %collective-permute-start = (f16[2,784,768]{2,1,0:T(8,128)(2,1)}, f16[2,784,768]{2,1,0:T(8,128)(2,1)}, u32[]{:S(2)}, u32[]{:S(2)}) collective-permute-start(f16[2,784,768]{2,1,0:T(8,128)(2,1)} %select_convert_fusion), channel_id=1, source_target_pairs={{0,1},{1,0},{2,3},{3,2},{4,5},{5,4},{6,7},{7,6},{8,9},{9,8},{10,11... | collective-permute-start | bytes 7225352 | tf_op jit(solution)/shard_map/ppermute | solution.py:650
  176.7 77.5 %all-to-all-start.1 = ((bf16[16,128,768]{2,1,0:T(8,128)(2,1)}), bf16[16,128,768]{2,1,0:T(8,128)(2,1)}, u32[]{:S(2)}, u32[]{:S(2)}) async-start(bf16[16,128,768]{2,1,0:T(8,128)(2,1)} %bitcast.157), calls=%async_computation.1 | async-start | bytes 6291456 | tf_op jit(solution)/shard_map/all_to_all | solution.py:785
  187.6 64.4 %collective-permute-start.1 = (f16[784,768]{1,0:T(8,128)(2,1)S(1)}, f16[784,768]{1,0:T(8,128)(2,1)S(1)}, u32[]{:S(2)}, u32[]{:S(2)}) collective-permute-start(f16[784,768]{1,0:T(8,128)(2,1)S(1)} %select_convert_fusion.2), channel_id=1, source_target_pairs={{0,2},{1,3},{2,0},{3,1},{4,6},{5,7},{6,4},{7,5},{8,10},{9,11},{10,... | collective-permute-start | bytes 3612680 | tf_op jit(solution)/shard_map/ppermute | solution.py:650
  267.7 20.4 %collective-permute-start.2 = (f16[2,528,768]{2,1,0:T(8,128)(2,1)}, f16[2,528,768]{2,1,0:T(8,128)(2,1)}, u32[]{:S(2)}, u32[]{:S(2)}) collective-permute-start(f16[2,528,768]{2,1,0:T(8,128)(2,1)} %select_convert_fusion.1), channel_id=1, source_target_pairs={{0,1},{1,0},{2,3},{3,2},{4,5},{5,4},{6,7},{7,6},{8,9},{9,8},{10,11... | collective-permute-start | bytes 4866056 | tf_op jit(solution)/shard_map/ppermute | solution.py:650
  268.0 16.4 %collective-permute-start.3 = (f16[400,768]{1,0:T(8,128)(2,1)S(1)}, f16[400,768]{1,0:T(8,128)(2,1)}, u32[]{:S(2)}, u32[]{:S(2)}) collective-permute-start(f16[400,768]{1,0:T(8,128)(2,1)S(1)} %select_convert_fusion.4), channel_id=1, source_target_pairs={{0,4},{4,0},{8,12},{12,8},{16,20},{20,16},{24,28},{28,24},{1,5},{5... | collective-permute-start | bytes 1843208 | tf_op jit(solution)/shard_map/ppermute | solution.py:650
  269.8 1.7 collective-permute-start.4
  292.8 7.1 %copy-start.4 = (bf16[1024,768]{1,0:T(8,128)(2,1)S(1)}, bf16[1024,768]{1,0:T(8,128)(2,1)}, u32[]{:S(2)}) copy-start(bf16[1024,768]{1,0:T(8,128)(2,1)} %copy-done.3) | copy-start | bytes 4718596
  292.9 24.4 %collective-permute-start.9 = (f32[32,1792]{1,0:T(8,128)S(1)}, f32[32,1792]{1,0:T(8,128)S(1)}, u32[]{:S(2)}, u32[]{:S(2)}) collective-permute-start(f32[32,1792]{1,0:T(8,128)S(1)} %add.395), channel_id=1, source_target_pairs={{0,2},{1,3},{2,0},{3,1},{4,6},{5,7},{6,4},{7,5},{8,10},{9,11},{10,... | collective-permute-start | bytes 688136 | tf_op jit(solution)/shard_map/ppermute | solution.py:650
  293.9 23.7 %collective-permute-start.5 = (f16[528,768]{1,0:T(8,128)(2,1)S(1)}, f16[528,768]{1,0:T(8,128)(2,1)S(1)}, u32[]{:S(2)}, u32[]{:S(2)}) collective-permute-start(f16[528,768]{1,0:T(8,128)(2,1)S(1)} %select_convert_fusion.3), channel_id=1, source_target_pairs={{0,2},{1,3},{2,0},{3,1},{4,6},{5,7},{6,4},{7,5},{8,10},{9,11},{10,... | collective-permute-start | bytes 2433032 | tf_op jit(solution)/shard_map/ppermute | solution.py:650
  295.5 19.6 %collective-permute-start.8 = (f16[112,768]{1,0:T(8,128)(2,1)S(1)}, f16[112,768]{1,0:T(8,128)(2,1)S(1)}, u32[]{:S(2)}, u32[]{:S(2)}) collective-permute-start(f16[112,768]{1,0:T(8,128)(2,1)S(1)} %get-tuple-element.152), channel_id=1, source_target_pairs={{0,24},{4,28},{8,16},{12,20},{16,8},{20,12},{24,0},{28,4},{1,25},{... | collective-permute-start | bytes 516104 | tf_op jit(solution)/shard_map/ppermute | solution.py:650
  299.2 14.1 %collective-permute-start.7 = (f16[112,768]{1,0:T(8,128)(2,1)S(1)}, f16[112,768]{1,0:T(8,128)(2,1)S(1)}, u32[]{:S(2)}, u32[]{:S(2)}) collective-permute-start(f16[112,768]{1,0:T(8,128)(2,1)S(1)} %get-tuple-element.153), channel_id=1, source_target_pairs={{0,16},{4,20},{8,24},{12,28},{16,0},{20,4},{24,8},{28,12},{1,17},{... | collective-permute-start | bytes 516104 | tf_op jit(solution)/shard_map/ppermute | solution.py:650
  299.2 10.4 %collective-permute-start.6 = (f16[112,768]{1,0:T(8,128)(2,1)S(1)}, f16[112,768]{1,0:T(8,128)(2,1)S(1)}, u32[]{:S(2)}, u32[]{:S(2)}) collective-permute-start(f16[112,768]{1,0:T(8,128)(2,1)S(1)} %get-tuple-element.154), channel_id=1, source_target_pairs={{0,8},{4,12},{8,0},{12,4},{16,24},{20,28},{24,16},{28,20},{1,9},{5... | collective-permute-start | bytes 516104 | tf_op jit(solution)/shard_map/ppermute | solution.py:650
  319.7 8.6 %collective-permute-start.11 = (f16[96,768]{1,0:T(8,128)(2,1)S(1)}, f16[96,768]{1,0:T(8,128)(2,1)S(1)}, u32[]{:S(2)}, u32[]{:S(2)}) collective-permute-start(f16[96,768]{1,0:T(8,128)(2,1)S(1)} %multiply_convert_fusion), channel_id=1, source_target_pairs={{0,24},{4,28},{8,16},{12,20},{16,8},{20,12},{24,0},{28,4},{1,25},{... | collective-permute-start | bytes 442376 | tf_op jit(solution)/shard_map/ppermute | solution.py:650
  323.3 11.7 %collective-permute-start.12 = (f16[96,768]{1,0:T(8,128)(2,1)S(1)}, f16[96,768]{1,0:T(8,128)(2,1)S(1)}, u32[]{:S(2)}, u32[]{:S(2)}) collective-permute-start(f16[96,768]{1,0:T(8,128)(2,1)S(1)} %multiply_convert_fusion), channel_id=1, source_target_pairs={{0,16},{4,20},{8,24},{12,28},{16,0},{20,4},{24,8},{28,12},{1,17},{... | collective-permute-start | bytes 442376 | tf_op jit(solution)/shard_map/ppermute | solution.py:650
  323.3 11.7 %collective-permute-start.13 = (f16[96,768]{1,0:T(8,128)(2,1)S(1)}, f16[96,768]{1,0:T(8,128)(2,1)S(1)}, u32[]{:S(2)}, u32[]{:S(2)}) collective-permute-start(f16[96,768]{1,0:T(8,128)(2,1)S(1)} %multiply_convert_fusion), channel_id=1, source_target_pairs={{0,8},{4,12},{8,0},{12,4},{16,24},{20,28},{24,16},{28,20},{1,9},{5... | collective-permute-start | bytes 442376 | tf_op jit(solution)/shard_map/ppermute | solution.py:650
  325.1 14.9 %collective-permute-start.10 = (f16[272,768]{1,0:T(8,128)(2,1)}, f16[272,768]{1,0:T(8,128)(2,1)}, u32[]{:S(2)}, u32[]{:S(2)}) collective-permute-start(f16[272,768]{1,0:T(8,128)(2,1)} %select_convert_fusion.5), channel_id=1, source_target_pairs={{0,4},{4,0},{8,12},{12,8},{16,20},{20,16},{24,28},{28,24},{1,5},{5... | collective-permute-start | bytes 1253384 | tf_op jit(solution)/shard_map/ppermute | solution.py:650
  326.8 13.1 %collective-permute-start.14 = (f32[32,1792]{1,0:T(8,128)S(1)}, f32[32,1792]{1,0:T(8,128)S(1)}, u32[]{:S(2)}, u32[]{:S(2)}) collective-permute-start(f32[32,1792]{1,0:T(8,128)S(1)} %add.407), channel_id=1, source_target_pairs={{0,4},{4,0},{8,12},{12,8},{16,20},{20,16},{24,28},{28,24},{1,5},{5... | collective-permute-start | bytes 688136 | tf_op jit(solution)/shard_map/ppermute | solution.py:650
  343.8 7.8 %collective-permute-start.15 = (f16[80,768]{1,0:T(8,128)(2,1)S(1)}, f16[80,768]{1,0:T(8,128)(2,1)S(1)}, u32[]{:S(2)}, u32[]{:S(2)}) collective-permute-start(f16[80,768]{1,0:T(8,128)(2,1)S(1)} %get-tuple-element.159), channel_id=1, source_target_pairs={{0,8},{4,12},{8,0},{12,4},{16,24},{20,28},{24,16},{28,20},{1,9},{5... | collective-permute-start | bytes 368648 | tf_op jit(solution)/shard_map/ppermute | solution.py:650
  345.2 19.2 %collective-permute-start.16 = (f16[80,768]{1,0:T(8,128)(2,1)S(1)}, f16[80,768]{1,0:T(8,128)(2,1)S(1)}, u32[]{:S(2)}, u32[]{:S(2)}) collective-permute-start(f16[80,768]{1,0:T(8,128)(2,1)S(1)} %get-tuple-element.158), channel_id=1, source_target_pairs={{0,16},{4,20},{8,24},{12,28},{16,0},{20,4},{24,8},{28,12},{1,17},{... | collective-permute-start | bytes 368648 | tf_op jit(solution)/shard_map/ppermute | solution.py:650
  347.8 19.8 %collective-permute-start.17 = (f16[80,768]{1,0:T(8,128)(2,1)S(1)}, f16[80,768]{1,0:T(8,128)(2,1)S(1)}, u32[]{:S(2)}, u32[]{:S(2)}) collective-permute-start(f16[80,768]{1,0:T(8,128)(2,1)S(1)} %get-tuple-element.157), channel_id=1, source_target_pairs={{0,24},{4,28},{8,16},{12,20},{16,8},{20,12},{24,0},{28,4},{1,25},{... | collective-permute-start | bytes 368648 | tf_op jit(solution)/shard_map/ppermute | solution.py:650
  348.3 21.5 %collective-permute-start.19 = (f32[32,1792]{1,0:T(8,128)S(1)}, f32[32,1792]{1,0:T(8,128)S(1)}, u32[]{:S(2)}, u32[]{:S(2)}) collective-permute-start(f32[32,1792]{1,0:T(8,128)S(1)} %add.413), channel_id=1, source_target_pairs={{0,24},{4,28},{8,16},{12,20},{16,8},{20,12},{24,0},{28,4},{1,25},{... | collective-permute-start | bytes 688136 | tf_op jit(solution)/shard_map/ppermute | solution.py:650
  351.6 24.4 %collective-permute-start.20 = (f32[32,1792]{1,0:T(8,128)S(1)}, f32[32,1792]{1,0:T(8,128)S(1)}, u32[]{:S(2)}, u32[]{:S(2)}) collective-permute-start(f32[32,1792]{1,0:T(8,128)S(1)} %add.413), channel_id=1, source_target_pairs={{0,16},{4,20},{8,24},{12,28},{16,0},{20,4},{24,8},{28,12},{1,17},{... | collective-permute-start | bytes 688136 | tf_op jit(solution)/shard_map/ppermute | solution.py:650
  351.6 24.4 %collective-permute-start.21 = (f32[32,1792]{1,0:T(8,128)S(1)}, f32[32,1792]{1,0:T(8,128)S(1)}, u32[]{:S(2)}, u32[]{:S(2)}) collective-permute-start(f32[32,1792]{1,0:T(8,128)S(1)} %add.413), channel_id=1, source_target_pairs={{0,8},{4,12},{8,0},{12,4},{16,24},{20,28},{24,16},{28,20},{1,9},{5... | collective-permute-start | bytes 688136 | tf_op jit(solution)/shard_map/ppermute | solution.py:650
  364.3 11.8 %collective-permute-start.18 = (f16[384,768]{1,0:T(8,128)(2,1)S(1)}, f16[384,768]{1,0:T(8,128)(2,1)S(1)}, u32[]{:S(2)}, u32[]{:S(2)}) collective-permute-start(f16[384,768]{1,0:T(8,128)(2,1)S(1)} %pad_maximum_fusion.4), channel_id=1, source_target_pairs={{0,4},{4,0},{8,12},{12,8},{16,20},{20,16},{24,28},{28,24},{1,5},{5... | collective-permute-start | bytes 1769480 | tf_op jit(solution)/shard_map/ppermute | solution.py:650
  376.6 27.1 %copy-start.20 = (s32[64]{0:T(128)S(1)}, s32[64]{0:T(128)}, u32[]{:S(2)}) copy-start(s32[64]{0:T(128)} %param.11) | copy-start | bytes 772
  376.7 27.4 %copy-start.16 = (f32[2]{0:T(128)S(1)}, f32[2]{0:T(128)}, u32[]{:S(2)}) copy-start(f32[2]{0:T(128)} %param.16) | copy-start | bytes 28
  376.7 11.6 %collective-permute-start.25 = (f32[768,768]{1,0:T(8,128)S(1)}, f32[768,768]{1,0:T(8,128)S(1)}, u32[]{:S(2)}, u32[]{:S(2)}) collective-permute-start(f32[768,768]{1,0:T(8,128)S(1)} %convert_multiply_fusion.2.early_ref), channel_id=1, source_target_pairs={{0,1},{1,0},{2,3},{3,2},{4,5},{5,4},{6,7},{7,6},{8,9},{9,8},{10,11... | collective-permute-start | bytes 7077896 | tf_op jit(solution)/shard_map/ppermute | solution.py:650
  376.7 7.6 %collective-permute-start.22 = (f16[64,768]{1,0:T(8,128)(2,1)S(1)}, f16[64,768]{1,0:T(8,128)(2,1)S(1)}, u32[]{:S(2)}, u32[]{:S(2)}) collective-permute-start(f16[64,768]{1,0:T(8,128)(2,1)S(1)} %multiply_convert_fusion.1), channel_id=1, source_target_pairs={{0,24},{4,28},{8,16},{12,20},{16,8},{20,12},{24,0},{28,4},{1,25},{... | collective-permute-start | bytes 294920 | tf_op jit(solution)/shard_map/ppermute | solution.py:650
  379.2 8.8 %collective-permute-start.23 = (f16[64,768]{1,0:T(8,128)(2,1)S(1)}, f16[64,768]{1,0:T(8,128)(2,1)S(1)}, u32[]{:S(2)}, u32[]{:S(2)}) collective-permute-start(f16[64,768]{1,0:T(8,128)(2,1)S(1)} %multiply_convert_fusion.1), channel_id=1, source_target_pairs={{0,16},{4,20},{8,24},{12,28},{16,0},{20,4},{24,8},{28,12},{1,17},{... | collective-permute-start | bytes 294920 | tf_op jit(solution)/shard_map/ppermute | solution.py:650
  379.2 8.8 %collective-permute-start.24 = (f16[64,768]{1,0:T(8,128)(2,1)S(1)}, f16[64,768]{1,0:T(8,128)(2,1)S(1)}, u32[]{:S(2)}, u32[]{:S(2)}) collective-permute-start(f16[64,768]{1,0:T(8,128)(2,1)S(1)} %multiply_convert_fusion.1), channel_id=1, source_target_pairs={{0,8},{4,12},{8,0},{12,4},{16,24},{20,28},{24,16},{28,20},{1,9},{5... | collective-permute-start | bytes 294920 | tf_op jit(solution)/shard_map/ppermute | solution.py:650
  389.7 11.1 %collective-permute-start.26 = (f16[256,768]{1,0:T(8,128)(2,1)S(1)}, f16[256,768]{1,0:T(8,128)(2,1)S(1)}, u32[]{:S(2)}, u32[]{:S(2)}) collective-permute-start(f16[256,768]{1,0:T(8,128)(2,1)S(1)} %pad_maximum_fusion.5), channel_id=1, source_target_pairs={{0,4},{4,0},{8,12},{12,8},{16,20},{20,16},{24,28},{28,24},{1,5},{5... | collective-permute-start | bytes 1179656 | tf_op jit(solution)/shard_map/ppermute | solution.py:650
  402.2 7.4 %collective-permute-start.27 = (f32[512,768]{1,0:T(8,128)}, f32[512,768]{1,0:T(8,128)}, u32[]{:S(2)}, u32[]{:S(2)}) collective-permute-start(f32[512,768]{1,0:T(8,128)} %convert_multiply_fusion.3.late_ref), channel_id=1, source_target_pairs={{0,1},{1,0},{2,3},{3,2},{4,5},{5,4},{6,7},{7,6},{8,9},{9,8},{10,11... | collective-permute-start | bytes 4718600 | tf_op jit(solution)/shard_map/ppermute | solution.py:650
  404.7 76.4 %all-to-all-start.2 = ((bf16[16,128,768]{2,1,0:T(8,128)(2,1)}), bf16[16,128,768]{2,1,0:T(8,128)(2,1)}, u32[]{:S(2)}, u32[]{:S(2)}) async-start(bf16[16,128,768]{2,1,0:T(8,128)(2,1)} %bitcast.156), calls=%async_computation.2 | async-start | bytes 6291456 | tf_op jit(solution)/shard_map/all_to_all | solution.py:785
  409.6 16.8 %copy-start.8 = (f32[942080]{0:T(1024)S(1)}, f32[942080]{0:T(1024)}, u32[]{:S(2)}) copy-start(f32[942080]{0:T(1024)} %param.15) | copy-start | bytes 11304964
  426.0 28.3 %collective-permute-start.29 = (f16[7360,128]{1,0:T(8,128)(2,1)}, f16[7360,128]{1,0:T(8,128)(2,1)}, u32[]{:S(2)}, u32[]{:S(2)}) collective-permute-start(f16[7360,128]{1,0:T(8,128)(2,1)} %convert_element_type.215), channel_id=1, source_target_pairs={{0,1},{1,0},{2,3},{3,2},{4,5},{5,4},{6,7},{7,6},{8,9},{9,8},{10,11... | collective-permute-start | bytes 5652488 | tf_op jit(solution)/shard_map/ppermute | solution.py:650
  426.4 43.4 %collective-permute-start.28 = (f16[7360,128]{1,0:T(8,128)(2,1)}, f16[7360,128]{1,0:T(8,128)(2,1)}, u32[]{:S(2)}, u32[]{:S(2)}) collective-permute-start(f16[7360,128]{1,0:T(8,128)(2,1)} %convert_element_type.215), channel_id=1, source_target_pairs={{0,2},{1,3},{2,0},{3,1},{4,6},{5,7},{6,4},{7,5},{8,10},{9,11},{10,... | collective-permute-start | bytes 5652488 | tf_op jit(solution)/shard_map/ppermute | solution.py:650
  432.6 16.4 %slice-start = ((s8[15073280]{0:T(1024)(128)(4,1)}), s8[2490368]{0:T(1024)(128)(4,1)S(1)}, s32[]{:S(2)}) async-start(s8[15073280]{0:T(1024)(128)(4,1)} %bitcast.141), calls=%async_computation.5 | async-start | bytes 4980736
  437.1 11.9 %slice-start.1 = ((s8[15073280]{0:T(1024)(128)(4,1)}), s8[4194304]{0:T(1024)(128)(4,1)S(1)}, s32[]{:S(2)}) async-start(s8[15073280]{0:T(1024)(128)(4,1)} %bitcast.141), calls=%async_computation.6 | async-start | bytes 8388608
  437.1 11.9 %slice-start.2 = ((s8[15073280]{0:T(1024)(128)(4,1)}), s8[4194304]{0:T(1024)(128)(4,1)S(1)}, s32[]{:S(2)}) async-start(s8[15073280]{0:T(1024)(128)(4,1)} %bitcast.141), calls=%async_computation.7 | async-start | bytes 8388608
  441.4 7.6 %slice-start.3 = ((s8[15073280]{0:T(1024)(128)(4,1)}), s8[4194304]{0:T(1024)(128)(4,1)S(1)}, s32[]{:S(2)}) async-start(s8[15073280]{0:T(1024)(128)(4,1)} %bitcast.141), calls=%async_computation.8 | async-start | bytes 8388608
  469.8 5.3 %collective-permute-start.30 = (f16[7360,128]{1,0:T(8,128)(2,1)}, f16[7360,128]{1,0:T(8,128)(2,1)S(1)}, u32[]{:S(2)}, u32[]{:S(2)}) collective-permute-start(f16[7360,128]{1,0:T(8,128)(2,1)} %collective-permute-done.28), channel_id=1, source_target_pairs={{0,1},{1,0},{2,3},{3,2},{4,5},{5,4},{6,7},{7,6},{8,9},{9,8},{10,11... | collective-permute-start | bytes 5652488 | tf_op jit(solution)/shard_map/ppermute | solution.py:650
  (13 other events, 27.3 us)
Sparse Core Ops, SparseCore 0:
  10.9 56.1 all-gather.2
  68.6 96.2 all-gather.4

commit v4 on v3

--- a/solution.py
+++ b/solution.py
@@ -19,6 +19,8 @@
 PAIRS = HEADS // 2
 EPS_NORM = 1e-05
 NEG = -1e30
+F16_TOP = 30000.0
+LOG2E = 1.4426950408889634
 F32 = jnp.float32
 BF16 = jnp.bfloat16
 
@@ -53,12 +55,15 @@
     return jnp.concatenate([hi, hi, lo], axis=0)
 
 
-def exact_left(v):
-    return jnp.concatenate(split3(v), axis=1)
+def split_pair(v, masks):
+    hi, lo = split2(v)
+    return jnp.concatenate([
+        jnp.concatenate([hi * masks[0], lo * masks[0]], axis=1),
+        jnp.concatenate([hi * masks[1], lo * masks[1]], axis=1)], axis=0)
 
 
 def sigmoid(v):
-    return 1.0 / (1.0 + jnp.exp(-v))
+    return lax.logistic(v)
 
 
 def softplus(v):
@@ -77,6 +82,15 @@
 def head_sum(v, et_ref):
     hi, lo = split2(v)
     return dot(hi, et_ref[...]) + dot(lo, et_ref[...])
+
+
+def quarters(out):
+    return out[:Q, :Q] + (out[:Q, Q:] + out[Q:, :Q])
+
+
+def power_for(bound):
+    scale = jnp.log(0.9 * F16_TOP / jnp.maximum(bound, 1e-30)) * LOG2E
+    return jnp.clip(jnp.floor(scale), -126.0, 120.0)
 
 
 def chunk_masks(t0, bound):
@@ -106,10 +120,10 @@
 
 
 def forward_kernel(
-    bound_ref, z_ref, proj_ref, gm_ref, e_ref, et_ref, convw_ref, convb_ref, dtb_ref, alog_ref,
+    bound_ref, cot_ref, z_ref, proj_ref, gm_ref, norm_ref, e_ref, et_ref, convw_ref, convb_ref, dtb_ref, alog_ref,
     skip_ref, gain_ref,
-    pair_ref, dy_ref, through_ref, state_ref, ggain_ref, zmax_ref,
-    ext_ref, dt_ref, carry_ref, xd_ref, acc_ref, cumt_ref,
+    pair_ref, dy_ref, through_ref, state_ref, ggain_ref, power_ref,
+    zmax_ref, ext_ref, dt_ref, carry_ref, xd_ref, acc_ref, cumt_ref,
 ):
     step = pl.program_id(0)
     bound = bound_ref[0]
@@ -141,31 +155,32 @@
     to_end = jnp.exp(cum_end - cum) * in_last
     carry_scale = jnp.exp(cum_end) * whole
     allowed = jnp.logical_and(cc <= rr, (cc >= bound) == (rr >= bound))
-    cumt_ref[...] = cum.T
+    cum2 = cum * LOG2E
+    cumt_ref[...] = cum2.T
 
     state = carry_ref[...]
     state_ref[0] = state
-    xd = x * expand(dt_pos, e_ref)
+    spread = expand(jnp.concatenate(
+        [dt_pos, to_end, from_start, jnp.broadcast_to(carry_scale, (16, 128))], axis=0), e_ref)
+    xd = x * spread[:Q]
     xd_ref[...] = xd
-    acc = dot(wide_left(c_rows), tall_right(state)) * expand(from_start, e_ref)
+    acc = dot(wide_left(c_rows), tall_right(state)) * spread[2 * Q : 3 * Q]
     acc_ref[...] = acc + skip_ref[...] * x
     b_t = b_rows.T
-    scale_all = expand(jnp.broadcast_to(carry_scale, (Q, Q)), e_ref)
-    carry_ref[...] = state * scale_all + dot(
-        wide_left(b_t), tall_right(xd * expand(to_end, e_ref))
-    )
+    carry_ref[...] = state * spread[3 * Q : 3 * Q + 1] + dot(
+        wide_left(b_t), tall_right(xd * spread[Q : 2 * Q]))
     gram = dot(wide_left(c_rows), tall_right(b_t))
     first = iota((Q, Q), 1) < HEADDIM
+    first_b = (first.astype(F32).astype(BF16), 1.0 - first.astype(F32).astype(BF16))
     for pair in range(PAIRS):
         parts = []
         for head in (2 * pair, 2 * pair + 1):
-            differ = cum[:, head : head + 1] - cumt_ref[head : head + 1, :]
-            parts.append(gram * jnp.exp(jnp.where(allowed, differ, NEG)))
+            differ = cum2[:, head : head + 1] - cumt_ref[head : head + 1, :]
+            parts.append(gram * jnp.exp2(jnp.where(allowed, differ, NEG)))
         left = jnp.concatenate(split2(jnp.concatenate(parts, axis=1)), axis=0)
         lanes = slice(pair * 128, pair * 128 + 128)
         xp = xd_ref[:, lanes]
-        diag = jnp.concatenate([jnp.where(first, xp, 0.0), jnp.where(first, 0.0, xp)], axis=0)
-        out = dot(left, jnp.concatenate(split2(diag), axis=1))
+        out = dot(left, split_pair(xp, first_b))
         acc_ref[:, lanes] += out[:Q, :128] + (out[:Q, 128:] + out[Q:, :128])
     scanned = acc_ref[...]
     z = z_ref[...]
@@ -186,22 +201,32 @@
     pair_ref[0] = grad_z.astype(BF16)
     through_ref[...] = head_sum(dy * (scanned - skip_ref[...] * x), et_ref)
 
+    @pl.when(step == pl.num_programs(0) - 1)
+    def _():
+        count = float(Q * pl.num_programs(0))
+        largest = jnp.max(zmax_ref[...], axis=1, keepdims=True)
+        normed = jnp.max(jnp.abs(norm_ref[...]), axis=1, keepdims=True) * (D ** 0.5)
+        mixed = jnp.max(jnp.abs(gain_ref[...]), axis=1, keepdims=True) * (INNER ** 0.5)
+        power_ref[...] = jnp.broadcast_to(power_for(
+            1.05 * count * jnp.maximum(largest * normed, cot_ref[0] * mixed)), (8, 128))
+
 
 def const_spec(shape):
     return pl.BlockSpec(shape, lambda *_: (0,) * len(shape))
 
 
-def run_forward(z, proj, gm, bound, e2, et, params):
+def run_forward(z, proj, gm, bound, cot_top, norm_gain, e2, et, params):
     n = proj.shape[0]
     steps = n // Q
     return pl.pallas_call(
         forward_kernel,
         grid=(steps,),
         in_specs=[
-            pl.BlockSpec(memory_space=pltpu.SMEM),
+            pl.BlockSpec(memory_space=pltpu.SMEM), pl.BlockSpec(memory_space=pltpu.SMEM),
             pl.BlockSpec((Q, INNER), lambda i: (i, 0)),
             pl.BlockSpec((Q, LATE), lambda i: (i, 0)),
             pl.BlockSpec((Q, INNER), lambda i: (i, 0)),
+            const_spec((1, D)),
             const_spec((256, INNER)), const_spec((INNER, 128)),
             const_spec((8, XBC)), const_spec((1, XBC)), const_spec((1, 128)),
             const_spec((1, 128)), const_spec((1, INNER)), const_spec((1, INNER)),
@@ -211,7 +236,7 @@
             pl.BlockSpec((Q, INNER), lambda i: (i, 0)),
             pl.BlockSpec((Q, 128), lambda i: (i, 0)),
             pl.BlockSpec((1, STATE, INNER), lambda i: (i, 0, 0)),
-            const_spec((1, INNER)), const_spec((1, INNER)),
+            const_spec((1, INNER)), const_spec((8, 128)),
         ],
         out_shape=[
             jax.ShapeDtypeStruct((2, n, INNER), BF16),
@@ -219,9 +244,10 @@
             jax.ShapeDtypeStruct((n, 128), F32),
             jax.ShapeDtypeStruct((steps, STATE, INNER), F32),
             jax.ShapeDtypeStruct((1, INNER), F32),
-            jax.ShapeDtypeStruct((1, INNER), F32),
+            jax.ShapeDtypeStruct((8, 128), F32),
         ],
         scratch_shapes=[
+            pltpu.VMEM((1, INNER), F32),
             pltpu.VMEM((Q + 8, XBC), F32),
             pltpu.VMEM((Q, 128), F32),
             pltpu.VMEM((STATE, INNER), F32),
@@ -233,15 +259,15 @@
             dimension_semantics=("arbitrary",), vmem_limit_bytes=48 * 2**20),
         cost_estimate=pl.CostEstimate(
             flops=30 * 10**9, bytes_accessed=40 * 2**20, transcendentals=10**7),
-    )(bound, z, proj, gm, e2, et, *params)
+    )(bound, cot_top, z, proj, gm, norm_gain, e2, et, *params)
 
 
 def backward_kernel(
     bound_ref, proj_ref, before_ref, dy_ref, through_ref, state_ref, gz_ref, tok_ref, cot_ref,
     in_ref, norm_ref, ggain_ref,
     e_ref, et_ref, convw_ref, convb_ref, dtb_ref, alog_ref, skip_ref,
-    window_ref, gtok_ref, small_ref,
-    gskip_ref, gsmall_ref, dtw_ref, ext_ref, dt_ref, lam_ref, dsum_ref, xd_ref, g_ref, gnext_ref, cumt_ref,
+    window_ref, gtok_ref, small_ref, power_ref,
+    total_ref, gskip_ref, gsmall_ref, dtw_ref, gp_ref, ext_ref, dt_ref, lam_ref, dsum_ref, xd_ref, g_ref, gnext_ref, cumt_ref,
 ):
     step = pl.program_id(0)
     steps = pl.num_programs(0)
@@ -255,7 +281,7 @@
         dt_ref[...] = jnp.zeros_like(dt_ref)
         gnext_ref[Q : Q + 8, :] = jnp.zeros((8, XBC), F32)
         gskip_ref[...] = jnp.zeros_like(gskip_ref)
-        small_ref[...] = jnp.zeros_like(small_ref)
+        total_ref[...] = jnp.zeros_like(total_ref)
         dtw_ref[...] = jnp.zeros_like(dtw_ref)
         gsmall_ref[...] = jnp.zeros_like(gsmall_ref)
 
@@ -280,11 +306,14 @@
     to_end = jnp.exp(cum_end - cum) * in_last
     carry_scale = jnp.exp(cum_end) * whole
     allowed_t = jnp.logical_and(rr <= cc, (cc >= bound) == (rr >= bound))
-    cumt_ref[...] = cum.T
+    cum2 = cum * LOG2E
+    cumt_ref[...] = cum2.T
     c_t = c_rows.T
     gram_t = dot(wide_left(b_rows), tall_right(c_t))
-    dt_all = expand(dt_pos, e_ref)
-    end_all = expand(to_end, e_ref)
+    spread = expand(jnp.concatenate(
+        [dt_pos, to_end, from_start, jnp.broadcast_to(carry_scale, (16, 128))], axis=0), e_ref)
+    dt_all = spread[:Q]
+    end_all = spread[Q : 2 * Q]
     xd = x * dt_all
     xd_ref[...] = xd
     skip = skip_ref[...]
@@ -294,48 +323,50 @@
     g_ref[...] = (
         dot(wide_left(b_rows), jnp.concatenate([lam_hi, lam_hi, lam_lo], axis=0)) * end_all
     )
-    xw_hi, xw_lo = split2(xd * end_all)
-    grad_b = dot_nt(xw_hi, lam_hi) + (dot_nt(xw_hi, lam_lo) + dot_nt(xw_lo, lam_hi))
+    grad_b = quarters(dot_nt(
+        jnp.concatenate(split2(xd * end_all), axis=0), jnp.concatenate([lam_hi, lam_lo], axis=0)))
     state = state_ref[0]
-    st_hi, st_lo = split2(state)
-    dye = dy * expand(from_start, e_ref)
-    dye_hi, dye_lo = split2(dye)
-    grad_c = dot_nt(dye_hi, st_hi) + (dot_nt(dye_hi, st_lo) + dot_nt(dye_lo, st_hi))
-    scale_all = expand(jnp.broadcast_to(carry_scale, (Q, Q)), e_ref)
-    lam_new = lam * scale_all + dot(
+    dye_hi, dye_lo = split2(dy * spread[2 * Q : 3 * Q])
+    grad_c = quarters(dot_nt(
+        jnp.concatenate([dye_hi, dye_lo], axis=0), jnp.concatenate(split2(state), axis=0)))
+    lam_new = lam * spread[3 * Q : 3 * Q + 1] + dot(
         wide_left(c_t), jnp.concatenate([dye_hi, dye_hi, dye_lo], axis=0)
     )
     lam_ref[...] = lam_new
     ended = dsum_ref[0:1, :]
     first = iota((Q, Q), 1) < HEADDIM
-    first_row = iota((Q, Q), 0) < HEADDIM
+    first_b = (first.astype(F32).astype(BF16), 1.0 - first.astype(F32).astype(BF16))
+    first_row = (iota((Q, Q), 0) < HEADDIM).astype(F32).astype(BF16)
+    first_row = (first_row, 1.0 - first_row)
     gram_grad = jnp.zeros((Q, Q), F32)
     for pair in range(PAIRS):
         lanes = slice(pair * 128, pair * 128 + 128)
         weights = []
         for head in (2 * pair, 2 * pair + 1):
-            differ = cumt_ref[head : head + 1, :] - cum[:, head : head + 1]
-            weights.append(jnp.exp(jnp.where(allowed_t, differ, NEG)))
+            differ = cumt_ref[head : head + 1, :] - cum2[:, head : head + 1]
+            weights.append(jnp.exp2(jnp.where(allowed_t, differ, NEG)))
         left = jnp.concatenate([gram_t * weights[0], gram_t * weights[1]], axis=1)
         left = jnp.concatenate(split2(left), axis=0)
         dyp = dy_ref[:, lanes]
-        diag = jnp.concatenate([jnp.where(first, dyp, 0.0), jnp.where(first, 0.0, dyp)], axis=0)
-        out = dot(left, jnp.concatenate(split2(diag), axis=1))
+        out = dot(left, split_pair(dyp, first_b))
         g_ref[:, lanes] += out[:Q, :128] + (out[:Q, 128:] + out[Q:, :128])
-        dyt = dyp.T
-        right = jnp.concatenate(
-            [jnp.where(first_row, dyt, 0.0), jnp.where(first_row, 0.0, dyt)], axis=1)
-        outer = dot(wide_left(xd_ref[:, lanes]), tall_right(right))
+        dyt_hi, dyt_lo = split2(dyp.T)
+        right_hi = jnp.concatenate([dyt_hi * first_row[0], dyt_hi * first_row[1]], axis=1)
+        right_lo = jnp.concatenate([dyt_lo * first_row[0], dyt_lo * first_row[1]], axis=1)
+        outer = dot(
+            wide_left(xd_ref[:, lanes]), jnp.concatenate([right_hi, right_hi, right_lo], axis=0))
         gram_grad = gram_grad + (outer[:, :128] * weights[0] + outer[:, 128:] * weights[1])
     g = g_ref[...]
     grad_x = dt_all * g + skip * dy
-    direct = head_sum(x * g, et_ref)
+    sums = dot(jnp.concatenate(
+        split2(x * g) + split2(jnp.broadcast_to(
+            jnp.sum(lam_new * state, axis=0, keepdims=True), (16, INNER))), axis=0), et_ref[...])
+    direct = sums[:Q] + sums[Q : 2 * Q]
     balance = through_ref[...] - dt_pos * direct
     keep_t = allowed_t.astype(F32).astype(BF16)
     b_hi, b_mid, b_lo = split3(balance)
     grad_step = dot(keep_t, b_hi) + dot(keep_t, b_mid) + dot(keep_t, b_lo) + in_last * ended
-    dsum_ref[...] = head_sum(
-        jnp.broadcast_to(jnp.sum(lam_new * state, axis=0, keepdims=True), (8, INNER)), et_ref)
+    dsum_ref[...] = sums[2 * Q : 2 * Q + 8] + sums[2 * Q + 16 : 2 * Q + 24]
     grad_dt = (direct + rate * grad_step) * sigmoid(dt_in)
     gsmall_ref[0:1, :] += jnp.sum(grad_dt, axis=0, keepdims=True)
     gsmall_ref[1:2, :] += rate * jnp.sum(dt_pos * grad_step, axis=0, keepdims=True)
@@ -346,43 +377,65 @@
     gnext_ref[0:Q, INNER : INNER + STATE] = grad_b * slope[:, INNER : INNER + STATE]
     gnext_ref[0:Q, INNER + STATE :] = grad_c * slope[:, INNER + STATE :]
     gcp = gnext_ref[0:Q, :]
-    small_ref[4:5, :] += jnp.sum(gcp, axis=0, keepdims=True)
-    small_ref[3:4, :] += jnp.sum(gcp * ext_ref[8 : 8 + Q, :], axis=0, keepdims=True)
+    total_ref[4:5, :] += jnp.sum(gcp, axis=0, keepdims=True)
+    total_ref[3:4, :] += jnp.sum(gcp * ext_ref[8 : 8 + Q, :], axis=0, keepdims=True)
     total = convw_ref[3:4, :] * gcp
     for back in (1, 2, 3):
         ok = jnp.logical_or(rows - back >= bound, rows < bound).astype(F32)
-        small_ref[3 - back : 4 - back, :] += jnp.sum(
+        total_ref[3 - back : 4 - back, :] += jnp.sum(
             gcp * (ext_ref[8 - back : 8 - back + Q, :] * ok), axis=0, keepdims=True)
         okn = jnp.logical_or(rows >= bound, rows + back < bound).astype(F32)
         total = total + convw_ref[3 - back : 4 - back, :] * (gnext_ref[back : back + Q, :] * okn)
-    small_ref[7:8, :] = jnp.maximum(
-        small_ref[7:8, :], jnp.max(jnp.abs(total), axis=0, keepdims=True))
+    total_ref[7:8, :] = jnp.maximum(
+        total_ref[7:8, :], jnp.max(jnp.abs(total), axis=0, keepdims=True))
     total = total.astype(BF16)
     window_ref[0] = total[:, :WINDOW]
     window_ref[1] = total[:, XBC - WINDOW :]
     gnext_ref[Q : Q + 8, :] = gnext_ref[0:8, :]
-    grad_dt = grad_dt.astype(BF16)
-    grad_normed = (
-        dot(gz_ref[0], in_ref[:INNER, :]) + dot(total, in_ref[INNER : INNER + XBC, :])
-        + dot(grad_dt, in_ref[INNER + XBC : INNER + XBC + 128, :]))
-    tok = tok_ref[...].astype(F32)
-    rinv = lax.rsqrt(jnp.mean(tok * tok, axis=1, keepdims=True) + EPS_NORM)
-    nhat = tok * rinv
-    gain = norm_ref[...]
-    gng = grad_normed * gain
-    gtok_ref[...] = (cot_ref[...].astype(F32) + rinv * (
-        gng - nhat * jnp.mean(nhat * gng, axis=1, keepdims=True))).astype(BF16)
-    small_ref[6:7, :D] += jnp.sum(nhat * grad_normed, axis=0, keepdims=True)
-    dtw_ref[...] += dot(grad_dt.astype(F32).T.astype(BF16), (nhat * gain).astype(BF16))
+    half = (steps - 1 - step) % 2
+    at = pl.multiple_of(half * Q, Q)
+    gp_ref[pl.ds(at, Q), :INNER] = gz_ref[0]
+    gp_ref[pl.ds(at, Q), INNER : INNER + XBC] = total
+    gp_ref[pl.ds(at, Q), INNER + XBC :] = grad_dt.astype(BF16)
+
+    @pl.when(half == 0)
+    def _():
+        grad_normed = dot(gp_ref[...], in_ref[: INNER + XBC + 128, :])
+        tok = tok_ref[...].astype(F32)
+        rinv = lax.rsqrt(jnp.mean(tok * tok, axis=1, keepdims=True) + EPS_NORM)
+        nhat = tok * rinv
+        gain = norm_ref[...]
+        gng = grad_normed * gain
+        gtok_ref[...] = (cot_ref[...].astype(F32) + rinv * (
+            gng - nhat * jnp.mean(nhat * gng, axis=1, keepdims=True))).astype(BF16)
+        total_ref[6:7, :D] += jnp.sum(nhat * grad_normed, axis=0, keepdims=True)
+        normed = (nhat * gain).astype(BF16)
+        gdt = gp_ref[:, INNER + XBC :].astype(F32)
+        dtw_ref[...] += dot(jnp.concatenate(
+            [gdt[:Q].T, gdt[Q:].T], axis=1).astype(BF16), normed)
 
     @pl.when(step == steps - 1)
     def _():
         skips = head_sum(jnp.broadcast_to(gskip_ref[...], (8, INNER)), et_ref)
-        small_ref[5:6, :INNER] = ggain_ref[...]
-        small_ref[6:7, D : D + 128] = gsmall_ref[0:1, :]
-        small_ref[6:7, D + 128 : D + 256] = gsmall_ref[1:2, :]
-        small_ref[6:7, D + 256 : D + 384] = skips[0:1, :]
-        small_ref[8 : 8 + HEADS, :D] = dtw_ref[0:HEADS, :]
+        small_ref[...] = jnp.zeros_like(small_ref)
+        small_ref[0:HEADS, :] = dtw_ref[0:HEADS, :]
+        pieces = [
+            total_ref[k : k + 1, j * 128 : j * 128 + 128]
+            for k in range(CONV + 1) for j in range(XBC // 128)]
+        pieces += [gsmall_ref[0:1, :], gsmall_ref[1:2, :], skips[0:1, :]]
+        pieces += [ggain_ref[:, j * 128 : j * 128 + 128] for j in range(INNER // 128)]
+        lines = D // 128
+        for number, piece in enumerate(pieces):
+            line = HEADS + number // lines
+            at = number % lines * 128
+            small_ref[line : line + 1, at : at + 128] = piece
+        small_ref[40:41, :] = total_ref[6:7, :D]
+        count = float(Q * steps)
+        largest = jnp.max(total_ref[7:8, :], axis=1, keepdims=True)
+        normed = jnp.max(jnp.abs(norm_ref[...]), axis=1, keepdims=True) * (D ** 0.5)
+        others = jnp.max(jnp.max(jnp.abs(small_ref[...]), axis=1, keepdims=True), axis=0, keepdims=True)
+        power_ref[...] = jnp.broadcast_to(power_for(
+            jnp.maximum(1.05 * count * largest * normed, others)), (8, 128))
 
 
 def run_backward(
@@ -393,6 +446,9 @@
 
     def rev(i):
         return (steps - 1 - i, 0)
+
+    def rev_two(i):
+        return ((steps - 1 - i) // 2, 0)
 
     return pl.pallas_call(
         backward_kernel,
@@ -405,7 +461,7 @@
             pl.BlockSpec((Q, 128), rev),
             pl.BlockSpec((1, STATE, INNER), lambda i: (steps - 1 - i, 0, 0)),
             pl.BlockSpec((1, Q, INNER), lambda i: (0, steps - 1 - i, 0)),
-            pl.BlockSpec((Q, D), rev), pl.BlockSpec((Q, D), rev),
+            pl.BlockSpec((2 * Q, D), rev_two), pl.BlockSpec((2 * Q, D), rev_two),
             const_spec(in_w.shape), const_spec((1, D)), const_spec((1, INNER)),
             const_spec((256, INNER)), const_spec((INNER, 128)),
             const_spec((8, XBC)), const_spec((1, XBC)), const_spec((1, 128)),
@@ -413,18 +469,21 @@
         ],
         out_specs=[
             pl.BlockSpec((2, Q, WINDOW), lambda i: (0, steps - 1 - i, 0)),
-            pl.BlockSpec((Q, D), rev),
-            const_spec((32, XBC)),
+            pl.BlockSpec((2 * Q, D), rev_two),
+            const_spec((48, D)), const_spec((8, 128)),
         ],
         out_shape=[
             jax.ShapeDtypeStruct((2, n, WINDOW), BF16),
             jax.ShapeDtypeStruct((n, D), BF16),
-            jax.ShapeDtypeStruct((32, XBC), F32),
+            jax.ShapeDtypeStruct((48, D), F32),
+            jax.ShapeDtypeStruct((8, 128), F32),
         ],
         scratch_shapes=[
+            pltpu.VMEM((8, XBC), F32),
             pltpu.VMEM((1, INNER), F32),
             pltpu.VMEM((8, 128), F32),
             pltpu.VMEM((128, D), F32),
+            pltpu.VMEM((2 * Q, INNER + XBC + 128), BF16),
             pltpu.VMEM((Q + 8, XBC), F32),
             pltpu.VMEM((Q, 128), F32),
             pltpu.VMEM((STATE, INNER), F32),
@@ -459,7 +518,6 @@
 LEAD = 896
 STAGE_ROWS = 16264
 ADAM_BLOCKS = 10
-F16_TOP = 30000.0
 MARK = 16
 
 
@@ -575,35 +633,31 @@
         early_at = LEAD + jnp.where(upper == 1, OUT_START - half, NORM_ROWS)
         window = LATE_START + (XBC - WINDOW) * NORM_ROWS
         late_at = LEAD + jnp.where(upper == 1, window - half, LATE_START)
-        for source_ref, at, which in (
-            (late_ref, late_at, mine), (late_other_ref, late_at, 1 - mine),
-            (early_ref, early_at, mine), (early_other_ref, early_at, 1 - mine),
-        ):
-            size = source_ref.shape[0]
-            start = at + which * (size * NORM_ROWS)
+        def lay(source_ref, start, size):
             for lane in range(NORM_ROWS):
                 stage_ref[pl.ds(start + lane, size, stride=NORM_ROWS), :] = source_ref[
-                    :, lane * LANES : lane * LANES + LANES]
+                    0:size, lane * LANES : lane * LANES + LANES]
+
+        lines = late_ref.shape[0]
+        lay(late_ref, late_at + mine * (lines * NORM_ROWS), lines)
+        lay(late_other_ref, late_at + (1 - mine) * (lines * NORM_ROWS), lines)
+
+        @pl.when(upper == 1)
+        def _():
+            lay(small_ref, LEAD + OUT_START - half - SMALL_ROWS, -(-SMALL_ROWS // NORM_ROWS))
+
+        lines = early_ref.shape[0]
+        lay(early_ref, early_at + mine * (lines * NORM_ROWS), lines)
+        lay(early_other_ref, early_at + (1 - mine) * (lines * NORM_ROWS), lines)
 
         @pl.when(upper == 0)
         def _():
             for lane in range(NORM_ROWS):
                 stage_ref[LEAD + lane : LEAD + lane + 1, :] = small_ref[
-                    6:7, lane * LANES : lane * LANES + LANES]
+                    40:41, lane * LANES : lane * LANES + LANES]
 
         @pl.when(upper == 1)
         def _():
-            at = LEAD + OUT_START - half - SMALL_ROWS
-            for lane in range(NORM_ROWS):
-                stage_ref[pl.ds(at + lane, HEADS, stride=NORM_ROWS), :] = small_ref[
-                    8 : 8 + HEADS, lane * LANES : lane * LANES + LANES]
-            at += DT_ROWS
-            places = [(k, j) for k in range(CONV + 1) for j in range(CONVB_ROWS)]
-            places += [(6, NORM_ROWS + j) for j in range(3)]
-            places += [(5, j) for j in range(GAIN_ROWS)]
-            for number, (line, lane) in enumerate(places):
-                stage_ref[at + number : at + number + 1, :] = small_ref[
-                    line : line + 1, lane * LANES : lane * LANES + LANES]
             at = LEAD + OUT_START + OUT_ROWS - half
             stage_ref[at : LEAD + half, :] = jnp.zeros((LEAD + half - at, LANES), F32)
 
@@ -648,11 +702,6 @@
 def swap(values, axis, bit):
     size = lax.axis_size(axis)
     return lax.ppermute(values, axis, [(i, i ^ bit) for i in range(size)])
-
-
-def power_for(bound):
-    bound = jnp.maximum(bound, 1e-30).reshape(1, 1)
-    return jnp.clip(jnp.floor(jnp.log2(F16_TOP / bound)), -126.0, 120.0)
 
 
 def to_wire(values, power):
@@ -704,13 +753,8 @@
     return jnp.concatenate(everyones(values, axis, bit, count))
 
 
-def add_all(values, axis, bit=1, count=2):
-    pieces = everyones(values, axis, bit, count) if count > 2 else [
-        values, swap(values, axis, bit)]
-    total = pieces[0]
-    for piece in pieces[1:]:
-        total = total + piece
-    return total
+def add_pair(values, axis, bit):
+    return values + swap(values, axis, bit)
 
 
 def data_groups():
@@ -749,12 +793,13 @@
     tie = lax.optimization_barrier
 
     own = master.reshape(shard_rows, LANES)
-    flat = lax.all_gather(own.astype(BF16), "zero", axis=0, tiled=True)
-
     arranged = holder_sequence_list.reshape(data_devices, group_devices, slots)
     group_order = lax.dynamic_index_in_dim(arranged, zero_index, 1, keepdims=False).reshape(-1)
     local_ids = group_order - zero_index * group_seqs
     dealt = tokens.at[local_ids].get(mode="promise_in_bounds")
+    own, dealt = tie((own, dealt))
+    flat = lax.all_gather(own.astype(BF16), "zero", axis=0, tiled=True)
+
     local_tok = lax.all_to_all(dealt, "dp", split_axis=0, concat_axis=0, tiled=True)
     my_seqs = lax.dynamic_slice_in_dim(group_order, dp_index * slots, slots)
     bound = lengths[my_seqs[0]]
@@ -763,7 +808,7 @@
     in_w, out_w, norm_gain, *params, e2, et = run_prepare(flat)
     cot = loss_sensitivity[0]
     gm = dot_nt(cot, out_w)
-    cot_top = jnp.max(jnp.abs(cot)).astype(F32)
+    cot_top = jnp.max(jnp.abs(cot)).astype(F32).reshape(1)
     local_tok, in_w, gm, cot_top = tie((local_tok, in_w, gm, cot_top))
     own_late, _ = tie((own, flat[:8]))
     whole_master = lax.all_gather(own_late, "zero", axis=0, tiled=True)
@@ -796,63 +841,60 @@
     normed = (nhat * norm_gain).astype(BF16)
     proj_z = dot_nt(normed, in_w[:INNER])
     proj = dot_nt(normed, in_w[INNER:PROJ])
-    pair, dy, through, states, ggain, zmax = run_forward(
-        proj_z, proj, gm, bound_arr, e2, et, params)
+    pair, dy, through, states, ggain, early_power = run_forward(
+        proj_z, proj, gm, bound_arr, cot_top, norm_gain, e2, et, params)
     result = (tok + dot(pair[1], out_w)).astype(BF16)
     picked = spread(result)
     picked, pair = tie((picked, pair))
     back_out = send_back(picked)
-    root = float(seq_len) ** 0.5
-    normed_norm = root * float(D) ** 0.5 * 1.02 * jnp.max(jnp.abs(norm_gain))
-    mixed_norm = root * float(INNER) ** 0.5 * 1.02 * jnp.max(jnp.abs(params[5]))
-    early_power = power_for(jnp.maximum(
-        1.02 * root * jnp.max(zmax) * normed_norm, root * cot_top * mixed_norm))
+    early_power = early_power[0:1, 0:1]
     early = lax.dot_general(
         pair, jnp.stack([normed, cot]), (((1,), (1,)), ((0,), (0,))), preferred_element_type=F32)
     early, early_power = scatter(early, early_power, "zero", 1)
     early, early_power, dy = tie((early.reshape(INNER, D), early_power, dy))
     early, early_power = scatter(early, early_power, "zero", 2)
-    window, grad_tok, small = run_backward(
+    window, grad_tok, small, late_power = run_backward(
         proj, dy, through, states, pair, packed, cot, in_w, norm_gain, ggain,
         bound_arr, e2, et, params)
-    window, small, back_out, early, early_power, whole_master = tie(
-        (window, small, back_out, early, early_power, whole_master))
+    window, small, late_power, back_out, early, early_power, whole_master = tie(
+        (window, small, late_power, back_out, early, early_power, whole_master))
 
     groups = data_groups()
     late = lax.dot_general(
         window, jnp.stack([normed, normed]), (((1,), (1,)), ((0,), (0,))),
         preferred_element_type=F32)
-    late_power = power_for(1.02 * root * jnp.max(small[7:8]) * normed_norm)
+    late_power = late_power[0:1, 0:1]
     late, late_power = scatter(late, late_power, "zero", 1)
     early, early_power = scatter(early, early_power, "dp", *groups[0])
-    small = add_all(small, "zero", 1)
+    small = add_pair(small, "zero", 1)
     late, late_power, early, early_power, small = tie(
         (late.reshape(WINDOW, D), late_power, early, early_power, small))
     late, late_power = scatter(late, late_power, "zero", 2)
     for group in groups[1:]:
         early, early_power = scatter(early, early_power, "dp", *group)
     early = to_wire(early, early_power)
-    small = add_all(small, "zero", 2)
+    small = add_pair(small, "zero", 2)
     picked_grad = spread(grad_tok)
-    late, late_power, early, small, picked_grad = tie(
-        (late, late_power, early, small, picked_grad))
+    lines = small.shape[0]
+    late = jnp.concatenate([late, small, jnp.zeros((WINDOW // 8 - lines, D), F32)])
+    late, late_power, early, picked_grad = tie((late, late_power, early, picked_grad))
     late, late_power = scatter(late, late_power, "dp", *groups[0])
     for group in reversed(groups[1:]):
         early = gather(early, "dp", *group)
-    small = add_all(small, "dp", *groups[0])
-    late, late_power, early, small = tie((late, late_power, early, small))
+    late, late_power, early = tie((late, late_power, early))
     for group in groups[1:]:
         late, late_power = scatter(late, late_power, "dp", *group)
-        small = add_all(small, "dp", *group)
     late = to_wire(late, late_power)
     early = from_wire(gather(early, "dp", *groups[0]), early_power)
-    late, early, small = tie((late, early, small))
+    late, early = tie((late, early))
     for group in reversed(groups[1:]):
         late = gather(late, "dp", *group)
     early_other = swap(early, "zero", 1)
     late, early_other, picked_grad = tie((late, early_other, picked_grad))
     back_grad = send_back(picked_grad)
-    late = from_wire(gather(late, "dp", *groups[0]), late_power)
+    wire = gather(late, "dp", *groups[0])
+    late = from_wire(wire[: WINDOW // 2], late_power)
+    small = from_wire(wire[WINDOW // 2 : WINDOW // 2 + lines], late_power)
     late_other = swap(late, "zero", 1)
 
     steps_f = iteration_tally[0].astype(F32)

time: 501 us -> 486 us (0.970)
    ppermute x31 -> x27, waiting for transfers between devices: 76.2 us -> 71.2 us  [swap(): return lax.ppermute(values, axis, [(i, i ^ bit) for i in range(size)])]
    ppermute x31 -> x27, starting transfers between devices: 33.5 us -> 29.2 us  [swap(): return lax.ppermute(values, axis, [(i, i ^ bit) for i in range(size)])]
    unnamed x52 -> x44, local copies, waits for them, and re-layouts: 15.7 us -> 11.8 us
  transfers between devices with their start and end apart: 36 -> 32, of which waited for: 18 -> 17; matrix products, arithmetic and copies ran while one was open for 24% -> 24% of each run, Pallas kernels for 24% -> 23%
where the time goes in v4:
time: 486 us; the launch traced here: 478 us
  waiting for transfers between devices  129 us (27%)
  Pallas kernels  111 us (23%)
  other arithmetic  67.7 us (14%)
  matrix products  52.1 us (11%)
  starting transfers between devices  46 us (9%)
  local copies, waits for them, and re-layouts  37.5 us (8%)
  between operations  34.6 us (7%)
    ppermute x27, waiting for transfers between devices, swap(): return lax.ppermute(values, axis, [(i, i ^ bit) for i in range(size)])  71.2 us
    pallas_call x1, Pallas kernels, run_backward(): pl.pallas_call(backward_kernel, grid=(steps,), in_specs=[pl.BlockSpec(mem...  57.7 us
    all_gather x1, waiting for transfers between devices, on_device(): flat = lax.all_gather(own.astype(BF16), 'zero', axis=0, tiled=True)  44.3 us
    pallas_call x1, Pallas kernels, run_forward(): pl.pallas_call(forward_kernel, grid=(steps,), in_specs=[pl.BlockSpec(memo...  35.1 us
    ppermute x27, starting transfers between devices, swap(): return lax.ppermute(values, axis, [(i, i ^ bit) for i in range(size)])  29.2 us
    dot_general x3, matrix products, dot(): lax.dot_general(a, b, (((1,), (0,)), ((), ())), preferred_element_type=F32)  21.4 us
    dynamic_update_slice x4, other arithmetic, put(): return lax.dynamic_update_index_in_dim(new_master, new, shard, 0)  19.2 us
    dot_general x3, matrix products, dot_nt(): lax.dot_general(a, b, (((1,), (1,)), ((), ())), preferred_element_type=F32)  15 us
  transfers between devices with their start and end apart: 32, of which 17 were waited for; matrix products, arithmetic and copies ran while one was open for 24% of the time, Pallas kernels for 23%

profile of v4, /device:TPU:0, one launch (start us, length us, event | category | flops | bytes accessed | tf_op | source)
XLA Modules:
  0.0 478.2 jit_solution(12489884794295618766)
XLA Ops:
  8.1 4.3 gather_fusion
  12.4 3.5 convert_element_type.168
  16.7 7.4 %all-to-all-start = ((bf16[16,128,768]{2,1,0:T(8,128)(2,1)}), bf16[16,128,768]{2,1,0:T(8,128)(2,1)}, u32[]{:S(2)}, u32[]{:S(2)}) async-start(bf16[16,128,768]{2,1,0:T(8,128)(2,1)} %gather_fusion), calls=%async_computation | async-start | bytes 6291456 | tf_op jit(solution)/shard_map/all_to_all | solution.py:803
  28.0 44.3 %all-gather.3.cloned.1.call-done.flat_ref = bf16[29440,128]{1,0:T(8,128)(2,1)} async-done(((bf16[7360,128]{1,0:T(8,128)(2,1)}), bf16[29440,128]{1,0:T(8,128)(2,1)}) %all-gather.3.cloned.1.call-update) | async-done | bytes 7536656 | tf_op jit(solution)/shard_map/all_gather | solution.py:801
  72.3 6.0 %shard_map.136 = (bf16[3584,768]{1,0:T(8,128)(2,1)S(1)}, bf16[1536,768]{1,0:T(8,128)(2,1)S(1)}, f32[1,768]{1,0:T(1,128)S(1)}, f32[8,1792]{1,0:T(8,128)S(1)}, f32...) custom-call(bf16[29440,128]{1,0:T(8,128)(2,1)} %all-gather.3.cloned., ...), custom_call_target="tpu_custom_call" | custom-call | flops 1000000000 | bytes 16777216 | tf_op jit(solution)/shard_map/pallas_call | solution.py:593
  78.3 2.6 copy-done
  82.2 4.6 convolution_bitcast_fusion.gm_ref
  86.8 8.1 %all-to-all-done = bf16[16,128,768]{2,1,0:T(8,128)(2,1)} async-done(((bf16[16,128,768]{2,1,0:T(8,128)(2,1)}), bf16[16,128,768]{2,1,0:T(8,128)(2,1)}, u32[]{:S(2)}, u32[]{:S(2)}) %all-to-all-start) | async-done | bytes 3145760 | tf_op jit(solution)/shard_map/all_to_all | solution.py:803
  95.0 5.8 %fusion.19 = (f32[1024]{0:T(1024)S(1)}, bf16[1024,768]{1,0:T(8,128)(2,1)S(1)}) fusion(bf16[2048,768]{1,0:T(8,128)(2,1)} %bitcast.9, s32[1024]{0:T(1024)S(1)} %fusion.42), kind=kOutput, calls=%fused_computation.48 | convolution fusion | flops 3226467328 | bytes 4726784 | tf_op jit(solution)/shard_map/dot_general | solution.py:29
  100.8 4.6 fusion.30.z_ref
  105.4 5.8 %fusion.28.proj_ref.before_ref = f32[1024,1816]{1,0:T(8,128)} fusion(bf16[3584,768]{1,0:T(8,128)(2,1)S(1)} %copy-done.1, bf16[1024,768]{1,0:T(8,128)(2,1)S(1)} %get-tuple-element.171.tok_ref, f32[768]{0:T(1024)S(1)} %reduce.2, f32[1024]{0:T(1024)S(1)} %add_rsqrt_fusion), kind=kOutput, calls=%fused_computation.60 | convolution fusion | flops 2859466752 | bytes 11808768 | tf_op jit(solution)/shard_map/dot_general | solution.py:33
  111.2 35.1 %shard_map.137 = (bf16[2,1024,1536]{2,1,0:T(8,128)(2,1)}, f32[1024,1536]{1,0:T(8,128)}, f32[1024,128]{1,0:T(8,128)S(1)}, f32[8,128,1536]{2,1,0:T(8,128)}, f32[1,1536]{1,0:T(1,128)S(1)}, /*index=5*/f32[8,128]{1,0:T(8,128)S(1)}) custom-call(s32[1]{0:T(128)} %dynamic_slice.160.bound_ref, f32[1]{0:T(128)S(6)} %convert.1.cot_ref, f32[1024,1536]{1,0:T(8,128)} %fusion.30.z_ref, ...), custom_call_target="tpu_custom_call" | custom-call | flops 30000001024 | bytes 41943040 | tf_op jit(solution)/shard_map/pallas_call | solution.py:221
  146.3 10.4 %fusion.15 = bf16[2048,768]{1,0:T(8,128)(2,1)} fusion(s32[2048]{0:T(1024)S(1)} %bitcast.163, bf16[1024,768]{1,0:T(8,128)(2,1)S(1)} %get-tuple-element.171.tok_ref, bf16[1536,768]{1,0:T(8,128)(2,1)} %copy-done.2, bf16[2,1024,1536]{2,1,0:T(8,128)(2,1)} %get-tuple-element.94.gz_ref), kind=kOutput, calls=%fused_computation.43 | convolution fusion | flops 5643173888 | bytes 10231808 | tf_op jit(solution)/shard_map/dot_general | solution.py:29
  158.5 8.5 %fusion.17 = f32[2,1536,768]{2,1,0:T(8,128)S(1)} fusion(bf16[2,1024,1536]{2,1,0:T(8,128)(2,1)} %get-tuple-element.94.gz_ref, bf16[1,1024,768]{2,1,0:T(8,128)(2,1)S(1)} %fusion.65, bf16[1,1024,768]{2,1,0:T(8,128)(2,1)S(1)} %copy-done.11), kind=kOutput, calls=%fused_computation.46 | convolution fusion | flops 4833411072 | bytes 18874368 | tf_op jit(solution)/shard_map/dot_general | solution.py:851
  167.0 3.7 copy-done.7
  170.7 2.7 select_convert_fusion
  173.4 4.6 all-to-all-start.1
  181.0 3.6 multiply_add_fusion
  186.7 57.7 %shard_map.138 = (bf16[2,1024,1024]{2,1,0:T(8,128)(2,1)}, bf16[1024,768]{1,0:T(8,128)(2,1)S(1)}, f32[48,768]{1,0:T(8,128)S(1)}, f32[8,128]{1,0:T(8,128)S(1)}) custom-call(s32[1]{0:T(128)} %dynamic_slice.160.bound_ref, f32[1024,1816]{1,0:T(8,128)} %fusion.28.proj_ref.before_ref, f32[1024,1816]{1,0:T(8,128)} %fusion.28.proj_ref.before_ref, ...), custom_call_target="tpu_custom_call" | custom-call | flops 49999998976 | bytes 52428800 | tf_op jit(solution)/shard_map/pallas_call | solution.py:453
  249.7 7.2 %fusion.18 = f32[2,1024,768]{2,1,0:T(8,128)S(1)} fusion(bf16[2,1024,1024]{2,1,0:T(8,128)(2,1)} %get-tuple-element.107, bf16[1,1024,768]{2,1,0:T(8,128)(2,1)} %copy-done.12), kind=kOutput, calls=%fused_computation.47 | convolution fusion | flops 3222798336 | bytes 12058624 | tf_op jit(solution)/shard_map/dot_general | solution.py:863
  265.6 13.0 %collective-permute-done.3 = f16[400,768]{1,0:T(8,128)(2,1)} collective-permute-done((f16[400,768]{1,0:T(8,128)(2,1)S(1)}, f16[400,768]{1,0:T(8,128)(2,1)}, u32[]{:S(2)}, u32[]{:S(2)}) %collective-permute-start.3) | collective-permute-done | bytes 614432 | tf_op jit(solution)/shard_map/ppermute | solution.py:704
  284.9 2.7 multiply_add_fusion.2
  289.8 2.4 collective-permute-start.9
  294.6 5.1 %fusion.16 = bf16[2048,768]{1,0:T(8,128)(2,1)} fusion(bf16[1024,768]{1,0:T(8,128)(2,1)S(1)} %copy-done.4, s32[2048]{0:T(1024)S(1)} %bitcast.164), kind=kOutput, calls=%fused_computation.44 | convolution fusion | flops 3224895488 | bytes 4726784 | tf_op jit(solution)/shard_map/dot_general | solution.py:29
  299.7 11.1 %collective-permute-done.6 = f32[48,768]{1,0:T(8,128)S(1)} collective-permute-done((f32[48,768]{1,0:T(8,128)S(1)}, f32[48,768]{1,0:T(8,128)S(1)}, u32[]{:S(2)}, u32[]{:S(2)}) %collective-permute-start.6) | collective-permute-done | bytes 147488 | tf_op jit(solution)/shard_map/ppermute | solution.py:704
  319.0 2.3 collective-permute-start.11
  327.6 5.3 %collective-permute-done.12 = f16[96,768]{1,0:T(8,128)(2,1)S(1)} collective-permute-done((f16[96,768]{1,0:T(8,128)(2,1)S(1)}, f16[96,768]{1,0:T(8,128)(2,1)S(1)}, u32[]{:S(2)}, u32[]{:S(2)}) %collective-permute-start.12) | collective-permute-done | bytes 147488 | tf_op jit(solution)/shard_map/ppermute | solution.py:704
  333.3 3.1 collective-permute-done.10
  346.3 2.9 collective-permute-done.14
  351.0 2.5 collective-permute-done.15
  359.9 2.6 collective-permute-start.20
  362.5 3.7 collective-permute-done.18
  366.2 5.3 %collective-permute-done.19 = f16[80,768]{1,0:T(8,128)(2,1)S(1)} collective-permute-done((f16[80,768]{1,0:T(8,128)(2,1)S(1)}, f16[80,768]{1,0:T(8,128)(2,1)S(1)}, u32[]{:S(2)}, u32[]{:S(2)}) %collective-permute-start.19) | collective-permute-done | bytes 122912 | tf_op jit(solution)/shard_map/ppermute | solution.py:704
  373.8 12.2 %collective-permute-done.22 = f16[320,768]{1,0:T(8,128)(2,1)S(1)} collective-permute-done((f16[320,768]{1,0:T(8,128)(2,1)S(1)}, f16[320,768]{1,0:T(8,128)(2,1)S(1)}, u32[]{:S(2)}, u32[]{:S(2)}) %collective-permute-start.22) | collective-permute-done | bytes 491552 | tf_op jit(solution)/shard_map/ppermute | solution.py:704
  390.0 4.7 all-to-all-start.2
  394.8 12.7 %shard_map.139 = (f32[7360,128]{1,0:T(8,128)}, f32[7360,128]{1,0:T(8,128)}) custom-call(s32[2]{0:T(128)S(1)} %pad_add_fusion.who_ref, f32[2]{0:T(128)S(1)} %pad_maximum_fusion.7.rate_ref, f32[768,768]{1,0:T(8,128)S(1)} %convert_multiply_fusion.2.early_ref, f32[768,768]{1,0:T(8,128)} %copy-done.9, f32[512,768]{1,0:T(8,128)} %convert_multiply_fusion.3.late_ref, ...), custom_call_target="tpu_custom_call" | custom-call | flops 100000000 | bytes 25165824 | tf_op jit(solution)/shard_map/pallas_call | solution.py:683
  407.5 3.7 convert_element_type.216
  413.3 6.2 %fusion.6 = (f32[7360,128]{1,0:T(8,128)}, f32[7360,128]{1,0:T(8,128)}) fusion(f32[7360,128]{1,0:T(8,128)} %get-tuple-element.135, f32[942080]{0:T(1024)S(1)} %copy-done.6, f32[942080]{0:T(1024)S(1)} %copy-done.5), kind=kLoop, calls=%fused_computation.19 | loop fusion | flops 6594560 | bytes 18841600 | tf_op jit(solution)/shard_map/add | solution.py:913
  419.5 4.5 gather_fusion.1
  424.0 4.3 broadcast_select_fusion.1
  428.3 7.6 %broadcast_in_dim.161 = f32[4,7360,128]{2,1,0:T(8,128)} broadcast(f32[]{:T(128)} %constant.311.clone.1), dimensions={} | broadcast | bytes 15073284 | tf_op jit(solution)/shard_map/broadcast_in_dim | solution.py:916
  435.9 5.2 %bitcast_dynamic-update-slice_fusion.3 = f32[4,7360,128]{2,1,0:T(8,128)} fusion(f32[4,7360,128]{2,1,0:T(8,128)} %broadcast_in_dim.161, s32[]{:T(128)S(6)} %select_n.577, f16[7360,128]{1,0:T(8,128)(2,1)} %convert_element_type.216, f32[4,7360,128]{2,1,0:T(8,128)S(1)} %bitcast.146, f32[]{:T(128)} %bitcast.54, f32[]{:T(128)} %bitcast.53), kind=kLoop, calls=%fused_computation.35 | loop fusion | flops 4710400 | bytes 9421828 | tf_op jit(solution)/shard_map/jit(dynamic_update_index_in_dim)/dynamic_update_slice | solution.py:923
  441.1 5.2 %bitcast_dynamic-update-slice_fusion.2 = f32[4,7360,128]{2,1,0:T(8,128)} fusion(f32[4,7360,128]{2,1,0:T(8,128)} %bitcast_dynamic-update-slice_fusion.3, s32[]{:T(128)S(6)} %select_n.694, f16[7360,128]{1,0:T(8,128)(2,1)} %collective-permute-done.25, f32[4,7360,128]{2,1,0:T(8,128)S(1)} %bitcast.147, f32[]{:T(128)} %bitcast.54, f32[]{:T(128)} %bitcast.53), kind=kLoop, calls=%fused_computation.30 | loop fusion | flops 4710400 | bytes 9421828 | tf_op jit(solution)/shard_map/jit(dynamic_update_index_in_dim)/dynamic_update_slice | solution.py:923
  446.2 8.7 %collective-permute-done.24 = f16[7360,128]{1,0:T(8,128)(2,1)} collective-permute-done((f16[7360,128]{1,0:T(8,128)(2,1)}, f16[7360,128]{1,0:T(8,128)(2,1)}, u32[]{:S(2)}, u32[]{:S(2)}) %collective-permute-start.24) | collective-permute-done | bytes 1884192 | tf_op jit(solution)/shard_map/ppermute | solution.py:704
  455.0 5.2 %bitcast_dynamic-update-slice_fusion.1 = f32[4,7360,128]{2,1,0:T(8,128)} fusion(f32[4,7360,128]{2,1,0:T(8,128)} %bitcast_dynamic-update-slice_fusion.2, s32[]{:T(128)S(6)} %select_n.698, f16[7360,128]{1,0:T(8,128)(2,1)} %collective-permute-done.24, f32[4,7360,128]{2,1,0:T(8,128)S(1)} %bitcast.148, f32[]{:T(128)} %bitcast.54, f32[]{:T(128)} %bitcast.53), kind=kLoop, calls=%fused_computation.25 | loop fusion | flops 4710400 | bytes 9421828 | tf_op jit(solution)/shard_map/jit(dynamic_update_index_in_dim)/dynamic_update_slice | solution.py:923
  460.1 3.6 bitcast_dynamic-update-slice_fusion
  463.8 2.6 all-to-all-done.2
  466.4 2.6 gather_fusion.2
  (171 shorter events, 62.3 us)
Async XLA Ops:
  7.2 65.1 %all-gather.3.cloned.1.call-start = ((), (), s32[]{:S(2)}) async-start(), calls=%async_computation.3 | async-start | bytes 9420800 | tf_op jit(solution)/shard_map/all_gather | solution.py:801
  8.1 4.3 copy-start.14
  16.0 233.7 %all-gather.5.cloned.1.call-start = ((), (), s32[]{:S(2)}) async-start(), calls=%async_computation.4 | async-start | bytes 18841600 | tf_op jit(solution)/shard_map/all_gather | solution.py:814
  16.7 7.7 %copy-start.10 = (bf16[1,1024,768]{2,1,0:T(8,128)(2,1)S(1)}, bf16[1,1024,768]{2,1,0:T(8,128)(2,1)}, u32[]{:S(2)}) copy-start(bf16[1,1024,768]{2,1,0:T(8,128)(2,1)} %param.10) | copy-start | bytes 4718596
  16.7 9.2 %copy-start.15 = (s32[64]{0:T(128)S(1)}, s32[64]{0:T(128)}, u32[]{:S(2)}) copy-start(s32[64]{0:T(128)} %param.11) | copy-start | bytes 772
  16.7 78.2 %all-to-all-start = ((bf16[16,128,768]{2,1,0:T(8,128)(2,1)}), bf16[16,128,768]{2,1,0:T(8,128)(2,1)}, u32[]{:S(2)}, u32[]{:S(2)}) async-start(bf16[16,128,768]{2,1,0:T(8,128)(2,1)} %gather_fusion), calls=%async_computation | async-start | bytes 6291456 | tf_op jit(solution)/shard_map/all_to_all | solution.py:803
  95.0 5.8 %copy-start.1 = (bf16[3584,768]{1,0:T(8,128)(2,1)S(1)}, bf16[3584,768]{1,0:T(8,128)(2,1)}, u32[]{:S(2)}) copy-start(bf16[3584,768]{1,0:T(8,128)(2,1)} %copy-done) | copy-start | bytes 16515076
  158.4 8.5 %copy-start.12 = (bf16[1,1024,768]{2,1,0:T(8,128)(2,1)}, bf16[1,1024,768]{2,1,0:T(8,128)(2,1)S(1)}, u32[]{:S(2)}) copy-start(bf16[1,1024,768]{2,1,0:T(8,128)(2,1)S(1)} %fusion.65) | copy-start | bytes 4718596
  167.0 3.7 copy-start.7
  173.4 4.9 %collective-permute-start = (f16[2,784,768]{2,1,0:T(8,128)(2,1)}, f16[2,784,768]{2,1,0:T(8,128)(2,1)}, u32[]{:S(2)}, u32[]{:S(2)}) collective-permute-start(f16[2,784,768]{2,1,0:T(8,128)(2,1)} %select_convert_fusion), channel_id=1, source_target_pairs={{0,1},{1,0},{2,3},{3,2},{4,5},{5,4},{6,7},{7,6},{8,9},{9,8},{10,11... | collective-permute-start | bytes 7225352 | tf_op jit(solution)/shard_map/ppermute | solution.py:704
  173.4 76.3 %all-to-all-start.1 = ((bf16[16,128,768]{2,1,0:T(8,128)(2,1)}), bf16[16,128,768]{2,1,0:T(8,128)(2,1)}, u32[]{:S(2)}, u32[]{:S(2)}) async-start(bf16[16,128,768]{2,1,0:T(8,128)(2,1)} %bitcast.161), calls=%async_computation.1 | async-start | bytes 6291456 | tf_op jit(solution)/shard_map/all_to_all | solution.py:830
  184.9 60.6 %collective-permute-start.1 = (f16[784,768]{1,0:T(8,128)(2,1)S(1)}, f16[784,768]{1,0:T(8,128)(2,1)S(1)}, u32[]{:S(2)}, u32[]{:S(2)}) collective-permute-start(f16[784,768]{1,0:T(8,128)(2,1)S(1)} %select_convert_fusion.2), channel_id=1, source_target_pairs={{0,2},{1,3},{2,0},{3,1},{4,6},{5,7},{6,4},{7,5},{8,10},{9,11},{10,... | collective-permute-start | bytes 3612680 | tf_op jit(solution)/shard_map/ppermute | solution.py:704
  256.9 2.7 copy-start.8
  261.8 20.4 %collective-permute-start.2 = (f16[2,528,768]{2,1,0:T(8,128)(2,1)}, f16[2,528,768]{2,1,0:T(8,128)(2,1)}, u32[]{:S(2)}, u32[]{:S(2)}) collective-permute-start(f16[2,528,768]{2,1,0:T(8,128)(2,1)} %select_convert_fusion.1), channel_id=1, source_target_pairs={{0,1},{1,0},{2,3},{3,2},{4,5},{5,4},{6,7},{7,6},{8,9},{9,8},{10,11... | collective-permute-start | bytes 4866056 | tf_op jit(solution)/shard_map/ppermute | solution.py:704
  262.1 16.4 %collective-permute-start.3 = (f16[400,768]{1,0:T(8,128)(2,1)S(1)}, f16[400,768]{1,0:T(8,128)(2,1)}, u32[]{:S(2)}, u32[]{:S(2)}) collective-permute-start(f16[400,768]{1,0:T(8,128)(2,1)S(1)} %select_convert_fusion.4), channel_id=1, source_target_pairs={{0,4},{4,0},{8,12},{12,8},{16,20},{20,16},{24,28},{28,24},{1,5},{5... | collective-permute-start | bytes 1843208 | tf_op jit(solution)/shard_map/ppermute | solution.py:704
  263.6 1.9 collective-permute-start.4
  287.5 7.1 %copy-start.4 = (bf16[1024,768]{1,0:T(8,128)(2,1)S(1)}, bf16[1024,768]{1,0:T(8,128)(2,1)}, u32[]{:S(2)}) copy-start(bf16[1024,768]{1,0:T(8,128)(2,1)} %copy-done.3) | copy-start | bytes 4718596
  287.9 28.8 %collective-permute-start.5 = (f16[528,768]{1,0:T(8,128)(2,1)S(1)}, f16[528,768]{1,0:T(8,128)(2,1)S(1)}, u32[]{:S(2)}, u32[]{:S(2)}) collective-permute-start(f16[528,768]{1,0:T(8,128)(2,1)S(1)} %select_convert_fusion.3), channel_id=1, source_target_pairs={{0,2},{1,3},{2,0},{3,1},{4,6},{5,7},{6,4},{7,5},{8,10},{9,11},{10,... | collective-permute-start | bytes 2433032 | tf_op jit(solution)/shard_map/ppermute | solution.py:704
  289.8 24.7 %collective-permute-start.9 = (f16[112,768]{1,0:T(8,128)(2,1)S(1)}, f16[112,768]{1,0:T(8,128)(2,1)S(1)}, u32[]{:S(2)}, u32[]{:S(2)}) collective-permute-start(f16[112,768]{1,0:T(8,128)(2,1)S(1)} %get-tuple-element.152), channel_id=1, source_target_pairs={{0,24},{4,28},{8,16},{12,20},{16,8},{20,12},{24,0},{28,4},{1,25},{... | collective-permute-start | bytes 516104 | tf_op jit(solution)/shard_map/ppermute | solution.py:704
  292.2 20.5 %collective-permute-start.8 = (f16[112,768]{1,0:T(8,128)(2,1)S(1)}, f16[112,768]{1,0:T(8,128)(2,1)S(1)}, u32[]{:S(2)}, u32[]{:S(2)}) collective-permute-start(f16[112,768]{1,0:T(8,128)(2,1)S(1)} %get-tuple-element.153), channel_id=1, source_target_pairs={{0,16},{4,20},{8,24},{12,28},{16,0},{20,4},{24,8},{28,12},{1,17},{... | collective-permute-start | bytes 516104 | tf_op jit(solution)/shard_map/ppermute | solution.py:704
  292.2 18.7 %collective-permute-start.7 = (f16[112,768]{1,0:T(8,128)(2,1)S(1)}, f16[112,768]{1,0:T(8,128)(2,1)S(1)}, u32[]{:S(2)}, u32[]{:S(2)}) collective-permute-start(f16[112,768]{1,0:T(8,128)(2,1)S(1)} %get-tuple-element.154), channel_id=1, source_target_pairs={{0,8},{4,12},{8,0},{12,4},{16,24},{20,28},{24,16},{28,20},{1,9},{5... | collective-permute-start | bytes 516104 | tf_op jit(solution)/shard_map/ppermute | solution.py:704
  294.3 16.6 %collective-permute-start.6 = (f32[48,768]{1,0:T(8,128)S(1)}, f32[48,768]{1,0:T(8,128)S(1)}, u32[]{:S(2)}, u32[]{:S(2)}) collective-permute-start(f32[48,768]{1,0:T(8,128)S(1)} %add.380), channel_id=1, source_target_pairs={{0,2},{1,3},{2,0},{3,1},{4,6},{5,7},{6,4},{7,5},{8,10},{9,11},{10,... | collective-permute-start | bytes 442376 | tf_op jit(solution)/shard_map/ppermute | solution.py:704
  319.0 8.7 %collective-permute-start.11 = (f16[96,768]{1,0:T(8,128)(2,1)S(1)}, f16[96,768]{1,0:T(8,128)(2,1)S(1)}, u32[]{:S(2)}, u32[]{:S(2)}) collective-permute-start(f16[96,768]{1,0:T(8,128)(2,1)S(1)} %multiply_convert_fusion), channel_id=1, source_target_pairs={{0,24},{4,28},{8,16},{12,20},{16,8},{20,12},{24,0},{28,4},{1,25},{... | collective-permute-start | bytes 442376 | tf_op jit(solution)/shard_map/ppermute | solution.py:704
  321.2 11.7 %collective-permute-start.12 = (f16[96,768]{1,0:T(8,128)(2,1)S(1)}, f16[96,768]{1,0:T(8,128)(2,1)S(1)}, u32[]{:S(2)}, u32[]{:S(2)}) collective-permute-start(f16[96,768]{1,0:T(8,128)(2,1)S(1)} %multiply_convert_fusion), channel_id=1, source_target_pairs={{0,16},{4,20},{8,24},{12,28},{16,0},{20,4},{24,8},{28,12},{1,17},{... | collective-permute-start | bytes 442376 | tf_op jit(solution)/shard_map/ppermute | solution.py:704
  321.3 11.7 %collective-permute-start.13 = (f16[96,768]{1,0:T(8,128)(2,1)S(1)}, f16[96,768]{1,0:T(8,128)(2,1)S(1)}, u32[]{:S(2)}, u32[]{:S(2)}) collective-permute-start(f16[96,768]{1,0:T(8,128)(2,1)S(1)} %multiply_convert_fusion), channel_id=1, source_target_pairs={{0,8},{4,12},{8,0},{12,4},{16,24},{20,28},{24,16},{28,20},{1,9},{5... | collective-permute-start | bytes 442376 | tf_op jit(solution)/shard_map/ppermute | solution.py:704
  324.4 12.0 %collective-permute-start.10 = (f16[336,768]{1,0:T(8,128)(2,1)}, f16[336,768]{1,0:T(8,128)(2,1)}, u32[]{:S(2)}, u32[]{:S(2)}) collective-permute-start(f16[336,768]{1,0:T(8,128)(2,1)} %select_convert_fusion.5), channel_id=1, source_target_pairs={{0,4},{4,0},{8,12},{12,8},{16,20},{20,16},{24,28},{28,24},{1,5},{5... | collective-permute-start | bytes 1548296 | tf_op jit(solution)/shard_map/ppermute | solution.py:704
  340.1 17.4 %collective-permute-start.17 = (f16[384,768]{1,0:T(8,128)(2,1)S(1)}, f16[384,768]{1,0:T(8,128)(2,1)S(1)}, u32[]{:S(2)}, u32[]{:S(2)}) collective-permute-start(f16[384,768]{1,0:T(8,128)(2,1)S(1)} %pad_maximum_fusion.5), channel_id=1, source_target_pairs={{0,4},{4,0},{8,12},{12,8},{16,20},{20,16},{24,28},{28,24},{1,5},{5... | collective-permute-start | bytes 1769480 | tf_op jit(solution)/shard_map/ppermute | solution.py:704
  341.8 7.4 %collective-permute-start.14 = (f16[96,768]{1,0:T(8,128)(2,1)S(1)}, f16[96,768]{1,0:T(8,128)(2,1)S(1)}, u32[]{:S(2)}, u32[]{:S(2)}) collective-permute-start(f16[96,768]{1,0:T(8,128)(2,1)S(1)} %get-tuple-element.159), channel_id=1, source_target_pairs={{0,8},{4,12},{8,0},{12,4},{16,24},{20,28},{24,16},{28,20},{1,9},{5... | collective-permute-start | bytes 442376 | tf_op jit(solution)/shard_map/ppermute | solution.py:704
  342.2 11.3 %collective-permute-start.15 = (f16[96,768]{1,0:T(8,128)(2,1)S(1)}, f16[96,768]{1,0:T(8,128)(2,1)S(1)}, u32[]{:S(2)}, u32[]{:S(2)}) collective-permute-start(f16[96,768]{1,0:T(8,128)(2,1)S(1)} %get-tuple-element.158), channel_id=1, source_target_pairs={{0,16},{4,20},{8,24},{12,28},{16,0},{20,4},{24,8},{28,12},{1,17},{... | collective-permute-start | bytes 442376 | tf_op jit(solution)/shard_map/ppermute | solution.py:704
  344.1 11.3 %collective-permute-start.16 = (f16[96,768]{1,0:T(8,128)(2,1)S(1)}, f16[96,768]{1,0:T(8,128)(2,1)S(1)}, u32[]{:S(2)}, u32[]{:S(2)}) collective-permute-start(f16[96,768]{1,0:T(8,128)(2,1)S(1)} %get-tuple-element.157), channel_id=1, source_target_pairs={{0,24},{4,28},{8,16},{12,20},{16,8},{20,12},{24,0},{28,4},{1,25},{... | collective-permute-start | bytes 442376 | tf_op jit(solution)/shard_map/ppermute | solution.py:704
  358.0 31.1 %copy-start.16 = (s32[64]{0:T(128)S(1)}, s32[64]{0:T(128)}, u32[]{:S(2)}) copy-start(s32[64]{0:T(128)} %param.11) | copy-start | bytes 772
  358.0 31.4 %copy-start.13 = (f32[2]{0:T(128)S(1)}, f32[2]{0:T(128)}, u32[]{:S(2)}) copy-start(f32[2]{0:T(128)} %param.16) | copy-start | bytes 28
  358.0 13.8 %collective-permute-start.21 = (f32[768,768]{1,0:T(8,128)S(1)}, f32[768,768]{1,0:T(8,128)S(1)}, u32[]{:S(2)}, u32[]{:S(2)}) collective-permute-start(f32[768,768]{1,0:T(8,128)S(1)} %convert_multiply_fusion.2.early_ref), channel_id=1, source_target_pairs={{0,1},{1,0},{2,3},{3,2},{4,5},{5,4},{6,7},{7,6},{8,9},{9,8},{10,11... | collective-permute-start | bytes 7077896 | tf_op jit(solution)/shard_map/ppermute | solution.py:704
  358.1 8.1 %collective-permute-start.18 = (f16[80,768]{1,0:T(8,128)(2,1)S(1)}, f16[80,768]{1,0:T(8,128)(2,1)S(1)}, u32[]{:S(2)}, u32[]{:S(2)}) collective-permute-start(f16[80,768]{1,0:T(8,128)(2,1)S(1)} %multiply_convert_fusion.1), channel_id=1, source_target_pairs={{0,24},{4,28},{8,16},{12,20},{16,8},{20,12},{24,0},{28,4},{1,25},{... | collective-permute-start | bytes 368648 | tf_op jit(solution)/shard_map/ppermute | solution.py:704
  359.8 11.7 %collective-permute-start.19 = (f16[80,768]{1,0:T(8,128)(2,1)S(1)}, f16[80,768]{1,0:T(8,128)(2,1)S(1)}, u32[]{:S(2)}, u32[]{:S(2)}) collective-permute-start(f16[80,768]{1,0:T(8,128)(2,1)S(1)} %multiply_convert_fusion.1), channel_id=1, source_target_pairs={{0,16},{4,20},{8,24},{12,28},{16,0},{20,4},{24,8},{28,12},{1,17},{... | collective-permute-start | bytes 368648 | tf_op jit(solution)/shard_map/ppermute | solution.py:704
  359.9 11.6 %collective-permute-start.20 = (f16[80,768]{1,0:T(8,128)(2,1)S(1)}, f16[80,768]{1,0:T(8,128)(2,1)S(1)}, u32[]{:S(2)}, u32[]{:S(2)}) collective-permute-start(f16[80,768]{1,0:T(8,128)(2,1)S(1)} %multiply_convert_fusion.1), channel_id=1, source_target_pairs={{0,8},{4,12},{8,0},{12,4},{16,24},{20,28},{24,16},{28,20},{1,9},{5... | collective-permute-start | bytes 368648 | tf_op jit(solution)/shard_map/ppermute | solution.py:704
  373.2 12.8 %collective-permute-start.22 = (f16[320,768]{1,0:T(8,128)(2,1)S(1)}, f16[320,768]{1,0:T(8,128)(2,1)S(1)}, u32[]{:S(2)}, u32[]{:S(2)}) collective-permute-start(f16[320,768]{1,0:T(8,128)(2,1)S(1)} %pad_maximum_fusion.6), channel_id=1, source_target_pairs={{0,4},{4,0},{8,12},{12,8},{16,20},{20,16},{24,28},{28,24},{1,5},{5... | collective-permute-start | bytes 1474568 | tf_op jit(solution)/shard_map/ppermute | solution.py:704
  387.5 7.2 %collective-permute-start.23 = (f32[512,768]{1,0:T(8,128)}, f32[512,768]{1,0:T(8,128)}, u32[]{:S(2)}, u32[]{:S(2)}) collective-permute-start(f32[512,768]{1,0:T(8,128)} %convert_multiply_fusion.3.late_ref), channel_id=1, source_target_pairs={{0,1},{1,0},{2,3},{3,2},{4,5},{5,4},{6,7},{7,6},{8,9},{9,8},{10,11... | collective-permute-start | bytes 4718600 | tf_op jit(solution)/shard_map/ppermute | solution.py:704
  390.0 76.4 %all-to-all-start.2 = ((bf16[16,128,768]{2,1,0:T(8,128)(2,1)}), bf16[16,128,768]{2,1,0:T(8,128)(2,1)}, u32[]{:S(2)}, u32[]{:S(2)}) async-start(bf16[16,128,768]{2,1,0:T(8,128)(2,1)} %bitcast.160), calls=%async_computation.2 | async-start | bytes 6291456 | tf_op jit(solution)/shard_map/all_to_all | solution.py:830
  394.8 18.5 %copy-start.6 = (f32[942080]{0:T(1024)S(1)}, f32[942080]{0:T(1024)}, u32[]{:S(2)}) copy-start(f32[942080]{0:T(1024)} %param.15) | copy-start | bytes 11304964
  407.5 5.8 %copy-start.5 = (f32[942080]{0:T(1024)S(1)}, f32[942080]{0:T(1024)}, u32[]{:S(2)}) copy-start(f32[942080]{0:T(1024)} %param.14) | copy-start | bytes 11304964
  411.2 29.9 %collective-permute-start.25 = (f16[7360,128]{1,0:T(8,128)(2,1)}, f16[7360,128]{1,0:T(8,128)(2,1)}, u32[]{:S(2)}, u32[]{:S(2)}) collective-permute-start(f16[7360,128]{1,0:T(8,128)(2,1)} %convert_element_type.216), channel_id=1, source_target_pairs={{0,1},{1,0},{2,3},{3,2},{4,5},{5,4},{6,7},{7,6},{8,9},{9,8},{10,11... | collective-permute-start | bytes 5652488 | tf_op jit(solution)/shard_map/ppermute | solution.py:704
  411.7 43.3 %collective-permute-start.24 = (f16[7360,128]{1,0:T(8,128)(2,1)}, f16[7360,128]{1,0:T(8,128)(2,1)}, u32[]{:S(2)}, u32[]{:S(2)}) collective-permute-start(f16[7360,128]{1,0:T(8,128)(2,1)} %convert_element_type.216), channel_id=1, source_target_pairs={{0,2},{1,3},{2,0},{3,1},{4,6},{5,7},{6,4},{7,5},{8,10},{9,11},{10,... | collective-permute-start | bytes 5652488 | tf_op jit(solution)/shard_map/ppermute | solution.py:704
  419.5 16.4 %slice-start = ((s8[15073280]{0:T(1024)(128)(4,1)}), s8[2490368]{0:T(1024)(128)(4,1)S(1)}, s32[]{:S(2)}) async-start(s8[15073280]{0:T(1024)(128)(4,1)} %bitcast.144), calls=%async_computation.5 | async-start | bytes 4980736
  424.0 11.9 %slice-start.1 = ((s8[15073280]{0:T(1024)(128)(4,1)}), s8[4194304]{0:T(1024)(128)(4,1)S(1)}, s32[]{:S(2)}) async-start(s8[15073280]{0:T(1024)(128)(4,1)} %bitcast.144), calls=%async_computation.6 | async-start | bytes 8388608
  424.0 11.9 %slice-start.2 = ((s8[15073280]{0:T(1024)(128)(4,1)}), s8[4194304]{0:T(1024)(128)(4,1)S(1)}, s32[]{:S(2)}) async-start(s8[15073280]{0:T(1024)(128)(4,1)} %bitcast.144), calls=%async_computation.7 | async-start | bytes 8388608
  428.3 7.6 %slice-start.3 = ((s8[15073280]{0:T(1024)(128)(4,1)}), s8[4194304]{0:T(1024)(128)(4,1)S(1)}, s32[]{:S(2)}) async-start(s8[15073280]{0:T(1024)(128)(4,1)} %bitcast.144), calls=%async_computation.8 | async-start | bytes 8388608
  455.0 5.2 %collective-permute-start.26 = (f16[7360,128]{1,0:T(8,128)(2,1)}, f16[7360,128]{1,0:T(8,128)(2,1)S(1)}, u32[]{:S(2)}, u32[]{:S(2)}) collective-permute-start(f16[7360,128]{1,0:T(8,128)(2,1)} %collective-permute-done.24), channel_id=1, source_target_pairs={{0,1},{1,0},{2,3},{3,2},{4,5},{5,4},{6,7},{7,6},{8,9},{9,8},{10,11... | collective-permute-start | bytes 5652488 | tf_op jit(solution)/shard_map/ppermute | solution.py:704
  (5 other events, 8.2 us)
Sparse Core Ops, SparseCore 0:
  16.1 56.1 all-gather.2
  73.8 96.2 all-gather.4

commit v5 on v4

--- a/solution.py
+++ b/solution.py
@@ -517,7 +517,7 @@
 LATE_START = NORM_ROWS + INNER * NORM_ROWS
 LEAD = 896
 STAGE_ROWS = 16264
-ADAM_BLOCKS = 10
+STAGE_BLOCKS = 5
 MARK = 16
 
 
@@ -616,17 +616,16 @@
     )(flat)
 
 
-def adam_kernel(
-    who_ref, rate_ref, early_ref, early_other_ref, late_ref, late_other_ref, small_ref,
-    first_ref, second_ref,
-    grad_ref, ratio_ref,
+def stage_kernel(
+    who_ref, early_ref, early_other_ref, late_ref, late_other_ref, small_ref,
+    grad_ref,
     stage_ref,
 ):
     step = pl.program_id(0)
     upper = who_ref[0]
     mine = who_ref[1]
-    block = first_ref.shape[0]
-    half = 2 * block * ADAM_BLOCKS
+    block = grad_ref.shape[0]
+    half = 2 * block * STAGE_BLOCKS
 
     @pl.when(step == 0)
     def _():
@@ -664,39 +663,27 @@
     @pl.when(step > 0)
     def _():
         at = LEAD + mine * (half // 2) + (step - 1) * block
-        grad = stage_ref[pl.ds(pl.multiple_of(at, 8), block), :]
-        grad_ref[...] = grad
-        first = BETA_ONE * first_ref[...] + (1.0 - BETA_ONE) * grad
-        second = BETA_TWO * second_ref[...] + (1.0 - BETA_TWO) * grad * grad
-        ratio_ref[...] = (first * rate_ref[0]) / (jnp.sqrt(second * rate_ref[1]) + EPS_ADAM)
-
-
-def run_adam(who, rates, early, early_other, late, late_other, small, first, second):
-    rows = first.shape[0]
-    block = rows // ADAM_BLOCKS
-
-    def at(i):
-        return (jnp.maximum(i - 1, 0), 0)
-
-    spec = pl.BlockSpec((block, LANES), at)
-    out = jax.ShapeDtypeStruct((rows, LANES), F32)
+        grad_ref[...] = stage_ref[pl.ds(pl.multiple_of(at, 8), block), :]
+
+
+def run_stage(who, rows, early, early_other, late, late_other, small):
+    block = rows // STAGE_BLOCKS
     return pl.pallas_call(
-        adam_kernel,
-        grid=(ADAM_BLOCKS + 1,),
+        stage_kernel,
+        grid=(STAGE_BLOCKS + 1,),
         in_specs=[
-            pl.BlockSpec(memory_space=pltpu.SMEM), pl.BlockSpec(memory_space=pltpu.SMEM),
+            pl.BlockSpec(memory_space=pltpu.SMEM),
             const_spec(early.shape), const_spec(early.shape),
             const_spec(late.shape), const_spec(late.shape), const_spec(small.shape),
-            spec, spec,
-        ],
-        out_specs=[spec, spec],
-        out_shape=[out, out],
+        ],
+        out_specs=pl.BlockSpec((block, LANES), lambda i: (jnp.maximum(i - 1, 0), 0)),
+        out_shape=jax.ShapeDtypeStruct((rows, LANES), F32),
         scratch_shapes=[pltpu.VMEM((STAGE_ROWS, LANES), F32)],
         compiler_params=pltpu.CompilerParams(
             dimension_semantics=("arbitrary",), vmem_limit_bytes=48 * 2**20),
         cost_estimate=pl.CostEstimate(
-            flops=10**8, bytes_accessed=24 * 2**20, transcendentals=10**6),
-    )(who, rates, early, early_other, late, late_other, small, first, second)
+            flops=10**6, bytes_accessed=12 * 2**20, transcendentals=0),
+    )(who, early, early_other, late, late_other, small)
 
 
 def swap(values, axis, bit):
@@ -797,7 +784,6 @@
     group_order = lax.dynamic_index_in_dim(arranged, zero_index, 1, keepdims=False).reshape(-1)
     local_ids = group_order - zero_index * group_seqs
     dealt = tokens.at[local_ids].get(mode="promise_in_bounds")
-    own, dealt = tie((own, dealt))
     flat = lax.all_gather(own.astype(BF16), "zero", axis=0, tiled=True)
 
     local_tok = lax.all_to_all(dealt, "dp", split_axis=0, concat_axis=0, tiled=True)
@@ -865,32 +851,31 @@
         preferred_element_type=F32)
     late_power = late_power[0:1, 0:1]
     late, late_power = scatter(late, late_power, "zero", 1)
+    late = late.reshape(WINDOW, D)
     early, early_power = scatter(early, early_power, "dp", *groups[0])
     small = add_pair(small, "zero", 1)
-    late, late_power, early, early_power, small = tie(
-        (late.reshape(WINDOW, D), late_power, early, early_power, small))
+    early, early_power, grad_tok, _ = tie((early, early_power, grad_tok, late))
     late, late_power = scatter(late, late_power, "zero", 2)
+    small = add_pair(small, "zero", 2)
     for group in groups[1:]:
         early, early_power = scatter(early, early_power, "dp", *group)
     early = to_wire(early, early_power)
-    small = add_pair(small, "zero", 2)
     picked_grad = spread(grad_tok)
     lines = small.shape[0]
     late = jnp.concatenate([late, small, jnp.zeros((WINDOW // 8 - lines, D), F32)])
-    late, late_power, early, picked_grad = tie((late, late_power, early, picked_grad))
+    early, _ = tie((early, late))
     late, late_power = scatter(late, late_power, "dp", *groups[0])
     for group in reversed(groups[1:]):
         early = gather(early, "dp", *group)
-    late, late_power, early = tie((late, late_power, early))
+    early, _ = tie((early, late))
     for group in groups[1:]:
         late, late_power = scatter(late, late_power, "dp", *group)
     late = to_wire(late, late_power)
     early = from_wire(gather(early, "dp", *groups[0]), early_power)
-    late, early = tie((late, early))
+    early, picked_grad, _ = tie((early, picked_grad, late))
     for group in reversed(groups[1:]):
         late = gather(late, "dp", *group)
     early_other = swap(early, "zero", 1)
-    late, early_other, picked_grad = tie((late, early_other, picked_grad))
     back_grad = send_back(picked_grad)
     wire = gather(late, "dp", *groups[0])
     late = from_wire(wire[: WINDOW // 2], late_power)
@@ -898,37 +883,56 @@
     late_other = swap(late, "zero", 1)
 
     steps_f = iteration_tally[0].astype(F32)
-    rates = jnp.stack([
-        1.0 / (1.0 - jnp.power(BETA_ONE, steps_f)), 1.0 / (1.0 - jnp.power(BETA_TWO, steps_f))])
     who = jnp.stack([zero_index // 2, zero_index % 2]).astype(jnp.int32)
     first = moment_one.reshape(shard_rows, LANES)
     second = moment_two.reshape(shard_rows, LANES)
-    grad_shard, ratio = run_adam(
-        who, rates, early, early_other, late, late_other, small, first, second)
-    mine = ratio.astype(jnp.float16)
-    mine, grad_shard, back_out = tie((mine, grad_shard, back_out))
-    core = swap(mine, "zero", 1)
-    across = swap(mine, "zero", 2)
-    first_next = BETA_ONE * first + (1.0 - BETA_ONE) * grad_shard
-    second_next = BETA_TWO * second + (1.0 - BETA_TWO) * grad_shard * grad_shard
+    grad_shard = run_stage(who, shard_rows, early, early_other, late, late_other, small)
+    first_scale = 1.0 / (1.0 - jnp.power(BETA_ONE, steps_f))
+    second_scale = 1.0 / (1.0 - jnp.power(BETA_TWO, steps_f))
+
+    def moments(grad, first, second):
+        return (
+            BETA_ONE * first + (1.0 - BETA_ONE) * grad,
+            BETA_TWO * second + (1.0 - BETA_TWO) * grad * grad)
+
+    def quotient(rows):
+        first_next, second_next = moments(grad_shard[rows], first[rows], second[rows])
+        return ((first_next * first_scale) / (
+            jnp.sqrt(second_next * second_scale) + EPS_ADAM)).astype(jnp.float16)
+
+    part = shard_rows // 2
+    whole_master = whole_master.reshape(2 * group_devices, part, LANES)
+    new_master = jnp.zeros((2 * group_devices, part, LANES), F32)
+
+    def put(new_master, piece, offset, half):
+        place = 2 * (zero_index ^ offset) + half
+        old = lax.dynamic_index_in_dim(whole_master, place, 0, keepdims=False)
+        new = old - adam_rates[0] * (piece.astype(F32) + adam_rates[1] * old)
+        return lax.dynamic_update_index_in_dim(new_master, new, place, 0)
+
+    front = quotient(slice(0, part))
+    front, grad_late, back_out = tie((front, grad_shard, back_out))
+    front_across = swap(front, "zero", 2)
+    grad_shard = grad_late
+    back = quotient(slice(part, shard_rows))
+    back, grad_shard, new_master = tie((back, grad_shard, new_master))
+    back_across = swap(back, "zero", 2)
+    front_core = swap(front, "zero", 1)
+    back_core = swap(back, "zero", 1)
+    first_next, second_next = moments(grad_shard, first, second)
     back_rows = back_out.at[restore].get(mode="promise_in_bounds")
     tokens_out = jnp.where(live, back_rows, tokens)
-    new_master = jnp.zeros((group_devices, shard_rows, LANES), F32)
-    whole_master = whole_master.reshape(group_devices, shard_rows, LANES)
-
-    def put(new_master, piece, offset):
-        shard = zero_index ^ offset
-        old = lax.dynamic_index_in_dim(whole_master, shard, 0, keepdims=False)
-        new = old - adam_rates[0] * (piece.astype(F32) + adam_rates[1] * old)
-        return lax.dynamic_update_index_in_dim(new_master, new, shard, 0)
-
-    new_master = put(put(new_master, mine, 0), core, 1)
-    across, new_master, tokens_out, first_next, second_next = tie(
-        (across, new_master, tokens_out, first_next, second_next))
-    across_core = swap(across, "zero", 1)
-    new_master = put(new_master, across, 2)
-    across_core, new_master = tie((across_core, new_master))
-    new_master = put(new_master, across_core, 3)
+    new_master = put(put(new_master, front, 0, 0), front_core, 1, 0)
+    front_across, new_master, tokens_out, first_next, second_next = tie(
+        (front_across, new_master, tokens_out, first_next, second_next))
+    front_last = swap(front_across, "zero", 1)
+    new_master = put(put(new_master, back, 0, 1), back_core, 1, 1)
+    new_master = put(put(new_master, front_across, 2, 0), front_last, 3, 0)
+    back_across, new_master = tie((back_across, new_master))
+    back_last = swap(back_across, "zero", 1)
+    new_master = put(new_master, back_across, 2, 1)
+    back_last, new_master = tie((back_last, new_master))
+    new_master = put(new_master, back_last, 3, 1)
     back_grad, new_master = tie((back_grad, new_master))
     grad_tokens = jnp.where(
         live, back_grad.at[restore].get(mode="promise_in_bounds"), jnp.zeros((), BF16))

time: 486 us -> 476 us (0.979)
  waiting for transfers between devices: 129 us -> 116 us
  other arithmetic: 67.7 us -> 78.2 us
  Pallas kernels: 111 us -> 105 us
    ppermute x27 -> x30, waiting for transfers between devices: 71.2 us -> 52.6 us  [swap(): return lax.ppermute(values, axis, [(i, i ^ bit) for i in range(size)])]
    dynamic_update_slice x4 -> x8, other arithmetic: 19.2 us -> 28.7 us  [put(): return lax.dynamic_update_index_in_dim(new_master, new, place, 0)]
    pallas_call x1, Pallas kernels: 12.7 us -> 6.15 us  [run_stage(): pl.pallas_call(stage_kernel, grid=(STAGE_BLOCKS + 1,), in_specs=[pl.Block...]
    all_to_all x2, waiting for transfers between devices: 4.58 us -> 9.94 us  [send_back(): return lax.all_to_all(picked, 'dp', split_axis=0, concat_axis=0, tiled=True)]
    ppermute x27 -> x30, starting transfers between devices: 29.2 us -> 31.4 us  [swap(): return lax.ppermute(values, axis, [(i, i ^ bit) for i in range(size)])]
    unnamed x44 -> x54, local copies, waits for them, and re-layouts: 11.8 us -> 11.2 us
  transfers between devices with their start and end apart: 32 -> 35, of which waited for: 17 -> 14; matrix products, arithmetic and copies ran while one was open for 24% -> 27% of each run, Pallas kernels for 23% -> 22%
where the time goes in v5:
time: 476 us; the launch traced here: 468 us
  waiting for transfers between devices  116 us (24%)
  Pallas kernels  105 us (22%)
  other arithmetic  78.2 us (16%)
  matrix products  52 us (11%)
  starting transfers between devices  48.3 us (10%)
  between operations  34.7 us (7%)
  local copies, waits for them, and re-layouts  34.3 us (7%)
    pallas_call x1, Pallas kernels, run_backward(): pl.pallas_call(backward_kernel, grid=(steps,), in_specs=[pl.BlockSpec(mem...  57.7 us
    ppermute x30, waiting for transfers between devices, swap(): return lax.ppermute(values, axis, [(i, i ^ bit) for i in range(size)])  52.6 us
    all_gather x1, waiting for transfers between devices, on_device(): flat = lax.all_gather(own.astype(BF16), 'zero', axis=0, tiled=True)  40.7 us
    pallas_call x1, Pallas kernels, run_forward(): pl.pallas_call(forward_kernel, grid=(steps,), in_specs=[pl.BlockSpec(memo...  35.1 us
    ppermute x30, starting transfers between devices, swap(): return lax.ppermute(values, axis, [(i, i ^ bit) for i in range(size)])  31.4 us
    dynamic_update_slice x8, other arithmetic, put(): return lax.dynamic_update_index_in_dim(new_master, new, place, 0)  28.7 us
    dot_general x3, matrix products, dot(): lax.dot_general(a, b, (((1,), (0,)), ((), ())), preferred_element_type=F32)  21.4 us
    dot_general x3, matrix products, dot_nt(): lax.dot_general(a, b, (((1,), (1,)), ((), ())), preferred_element_type=F32)  15 us
  transfers between devices with their start and end apart: 35, of which 14 were waited for; matrix products, arithmetic and copies ran while one was open for 27% of the time, Pallas kernels for 22%

profile of v5, /device:TPU:0, one launch (start us, length us, event | category | flops | bytes accessed | tf_op | source)
XLA Modules:
  0.0 468.1 jit_solution(992326064770322202)
XLA Ops:
  7.2 3.5 bitcast_convert_fusion
  12.6 2.4 gather_fusion
  15.1 7.4 %all-to-all-start = ((bf16[16,128,768]{2,1,0:T(8,128)(2,1)}), bf16[16,128,768]{2,1,0:T(8,128)(2,1)}, u32[]{:S(2)}, u32[]{:S(2)}) async-start(bf16[16,128,768]{2,1,0:T(8,128)(2,1)} %gather_fusion), calls=%async_computation | async-start | bytes 6291456 | tf_op jit(solution)/shard_map/all_to_all | solution.py:789
  26.3 40.7 %all-gather.3.cloned.1.call-done.flat_ref = bf16[29440,128]{1,0:T(8,128)(2,1)} async-done(((bf16[7360,128]{1,0:T(8,128)(2,1)}), bf16[29440,128]{1,0:T(8,128)(2,1)}) %all-gather.3.cloned.1.call-update) | async-done | bytes 7536656 | tf_op jit(solution)/shard_map/all_gather | solution.py:787
  67.0 6.0 %shard_map.136 = (bf16[3584,768]{1,0:T(8,128)(2,1)S(1)}, bf16[1536,768]{1,0:T(8,128)(2,1)S(1)}, f32[1,768]{1,0:T(1,128)S(1)}, f32[8,1792]{1,0:T(8,128)S(1)}, f32...) custom-call(bf16[29440,128]{1,0:T(8,128)(2,1)} %all-gather.3.cloned., ...), custom_call_target="tpu_custom_call" | custom-call | flops 1000000000 | bytes 16777216 | tf_op jit(solution)/shard_map/pallas_call | solution.py:593
  73.0 2.6 copy-done
  77.0 4.6 fusion.84.gm_ref
  81.6 11.6 %all-to-all-done = bf16[16,128,768]{2,1,0:T(8,128)(2,1)} async-done(((bf16[16,128,768]{2,1,0:T(8,128)(2,1)}), bf16[16,128,768]{2,1,0:T(8,128)(2,1)}, u32[]{:S(2)}, u32[]{:S(2)}) %all-to-all-start) | async-done | bytes 3145760 | tf_op jit(solution)/shard_map/all_to_all | solution.py:789
  93.3 5.8 %fusion.11 = (f32[1024]{0:T(1024)S(1)}, bf16[1024,768]{1,0:T(8,128)(2,1)S(1)}) fusion(bf16[2048,768]{1,0:T(8,128)(2,1)} %bitcast.9, s32[1024]{0:T(1024)S(1)} %fusion.64), kind=kOutput, calls=%fused_computation.27 | convolution fusion | flops 3226467328 | bytes 4726784 | tf_op jit(solution)/shard_map/dot_general | solution.py:29
  99.1 4.6 fusion.22.z_ref
  103.7 5.8 %fusion.20.proj_ref.before_ref = f32[1024,1816]{1,0:T(8,128)} fusion(bf16[3584,768]{1,0:T(8,128)(2,1)S(1)} %copy-done.1, bf16[1024,768]{1,0:T(8,128)(2,1)S(1)} %get-tuple-element.153.tok_ref, f32[768]{0:T(1024)S(1)} %reduce.2, f32[1024]{0:T(1024)S(1)} %add_rsqrt_fusion), kind=kOutput, calls=%fused_computation.41 | convolution fusion | flops 2859466752 | bytes 11808768 | tf_op jit(solution)/shard_map/dot_general | solution.py:33
  109.5 35.1 %shard_map.137 = (bf16[2,1024,1536]{2,1,0:T(8,128)(2,1)}, f32[1024,1536]{1,0:T(8,128)}, f32[1024,128]{1,0:T(8,128)S(1)}, f32[8,128,1536]{2,1,0:T(8,128)}, f32[1,1536]{1,0:T(1,128)S(1)}, /*index=5*/f32[8,128]{1,0:T(8,128)S(1)}) custom-call(s32[1]{0:T(128)} %dynamic_slice.172.bound_ref, f32[1]{0:T(128)S(6)} %convert.1.cot_ref, f32[1024,1536]{1,0:T(8,128)} %fusion.22.z_ref, ...), custom_call_target="tpu_custom_call" | custom-call | flops 30000001024 | bytes 41943040 | tf_op jit(solution)/shard_map/pallas_call | solution.py:221
  144.6 10.5 %fusion.7 = bf16[2048,768]{1,0:T(8,128)(2,1)} fusion(s32[2048]{0:T(1024)S(1)} %bitcast.240, bf16[1024,768]{1,0:T(8,128)(2,1)S(1)} %get-tuple-element.153.tok_ref, bf16[1536,768]{1,0:T(8,128)(2,1)} %copy-done.2, bf16[2,1024,1536]{2,1,0:T(8,128)(2,1)} %get-tuple-element.83.gz_ref), kind=kOutput, calls=%fused_computation.22 | convolution fusion | flops 5643173888 | bytes 10231808 | tf_op jit(solution)/shard_map/dot_general | solution.py:29
  156.8 8.5 %fusion.9 = f32[2,1536,768]{2,1,0:T(8,128)S(1)} fusion(bf16[2,1024,1536]{2,1,0:T(8,128)(2,1)} %get-tuple-element.83.gz_ref, bf16[1,1024,768]{2,1,0:T(8,128)(2,1)S(1)} %fusion.88, bf16[1,1024,768]{2,1,0:T(8,128)(2,1)S(1)} %copy-done.15), kind=kOutput, calls=%fused_computation.25 | convolution fusion | flops 4833411072 | bytes 18874368 | tf_op jit(solution)/shard_map/dot_general | solution.py:837
  165.3 3.7 copy-done.12
  169.0 2.7 select_convert_fusion
  171.7 4.6 all-to-all-start.1
  179.3 3.6 multiply_add_fusion
  184.8 57.7 %shard_map.138 = (bf16[2,1024,1024]{2,1,0:T(8,128)(2,1)}, bf16[1024,768]{1,0:T(8,128)(2,1)S(1)}, f32[48,768]{1,0:T(8,128)S(1)}, f32[8,128]{1,0:T(8,128)S(1)}) custom-call(s32[1]{0:T(128)} %dynamic_slice.172.bound_ref, f32[1024,1816]{1,0:T(8,128)} %fusion.20.proj_ref.before_ref, f32[1024,1816]{1,0:T(8,128)} %fusion.20.proj_ref.before_ref, ...), custom_call_target="tpu_custom_call" | custom-call | flops 49999998976 | bytes 52428800 | tf_op jit(solution)/shard_map/pallas_call | solution.py:453
  248.0 7.1 %fusion.10 = f32[2,1024,768]{2,1,0:T(8,128)S(1)} fusion(bf16[2,1024,1024]{2,1,0:T(8,128)(2,1)} %get-tuple-element.99, bf16[1,1024,768]{2,1,0:T(8,128)(2,1)} %copy-done.16), kind=kOutput, calls=%fused_computation.26 | convolution fusion | flops 3222798336 | bytes 12058624 | tf_op jit(solution)/shard_map/dot_general | solution.py:849
  257.8 2.2 select_convert_fusion.1
  260.1 3.8 collective-permute-done.3
  266.5 2.7 multiply_add_fusion.1
  276.6 17.4 %collective-permute-done.9 = f32[48,768]{1,0:T(8,128)S(1)} collective-permute-done((f32[48,768]{1,0:T(8,128)S(1)}, f32[48,768]{1,0:T(8,128)S(1)}, u32[]{:S(2)}, u32[]{:S(2)}) %collective-permute-start.9) | collective-permute-done | bytes 147488 | tf_op jit(solution)/shard_map/ppermute | solution.py:691
  306.4 2.2 collective-permute-start.6
  308.6 6.6 %collective-permute-done.4 = f16[112,768]{1,0:T(8,128)(2,1)S(1)} collective-permute-done((f16[112,768]{1,0:T(8,128)(2,1)S(1)}, f16[112,768]{1,0:T(8,128)(2,1)S(1)}, u32[]{:S(2)}, u32[]{:S(2)}) %collective-permute-start.4) | collective-permute-done | bytes 172064 | tf_op jit(solution)/shard_map/ppermute | solution.py:691
  332.7 8.6 %collective-permute-done.11 = f16[96,768]{1,0:T(8,128)(2,1)S(1)} collective-permute-done((f16[96,768]{1,0:T(8,128)(2,1)S(1)}, f16[96,768]{1,0:T(8,128)(2,1)S(1)}, u32[]{:S(2)}, u32[]{:S(2)}) %collective-permute-start.11) | collective-permute-done | bytes 147488 | tf_op jit(solution)/shard_map/ppermute | solution.py:691
  351.1 2.3 collective-permute-start.19
  355.5 5.2 %fusion.8 = bf16[2048,768]{1,0:T(8,128)(2,1)} fusion(bf16[1024,768]{1,0:T(8,128)(2,1)S(1)} %copy-done.4, s32[2048]{0:T(1024)S(1)} %bitcast.241), kind=kOutput, calls=%fused_computation.23 | convolution fusion | flops 3224895488 | bytes 4726784 | tf_op jit(solution)/shard_map/dot_general | solution.py:29
  360.7 2.3 collective-permute-done.20
  365.6 10.2 %collective-permute-done.22 = f16[320,768]{1,0:T(8,128)(2,1)S(1)} collective-permute-done((f16[320,768]{1,0:T(8,128)(2,1)S(1)}, f16[320,768]{1,0:T(8,128)(2,1)S(1)}, u32[]{:S(2)}, u32[]{:S(2)}) %collective-permute-start.22) | collective-permute-done | bytes 491552 | tf_op jit(solution)/shard_map/ppermute | solution.py:691
  379.9 4.8 %all-to-all-start.2 = ((bf16[16,128,768]{2,1,0:T(8,128)(2,1)}), bf16[16,128,768]{2,1,0:T(8,128)(2,1)}, u32[]{:S(2)}, u32[]{:S(2)}) async-start(bf16[16,128,768]{2,1,0:T(8,128)(2,1)} %bitcast.237), calls=%async_computation.2 | async-start | bytes 6291456 | tf_op jit(solution)/shard_map/all_to_all | solution.py:816
  384.8 6.1 %shard_map.139 = f32[7360,128]{1,0:T(8,128)} custom-call(s32[2]{0:T(128)S(1)} %pad_add_fusion.who_ref, f32[768,768]{1,0:T(8,128)S(1)} %convert_multiply_fusion.2.early_ref, f32[768,768]{1,0:T(8,128)} %collective-permute-done.18.early_other_ref, f32[512,768]{1,0:T(8,128)} %convert_multiply_fusion.3.late_ref, ...), custom_call_target="tpu_custom_call" | custom-call | flops 1000000 | bytes 12582912 | tf_op jit(solution)/shard_map/pallas_call | solution.py:671
  390.9 3.9 fusion.53
  398.7 4.2 fusion.6
  402.9 4.5 gather_fusion.1
  407.3 4.3 broadcast_select_fusion.1
  411.7 7.5 %broadcast_in_dim.173 = f32[8,3680,128]{2,1,0:T(8,128)} broadcast(f32[]{:T(128)} %constant.335.clone.1), dimensions={} | broadcast | bytes 15073284 | tf_op jit(solution)/shard_map/broadcast_in_dim | solution.py:905
  419.2 4.0 bitcast_dynamic-update-slice_fusion.7
  423.2 4.0 bitcast_dynamic-update-slice_fusion.6
  427.4 2.8 bitcast_dynamic-update-slice_fusion.5
  430.2 4.0 bitcast_dynamic-update-slice_fusion.4
  434.3 4.0 bitcast_dynamic-update-slice_fusion.3
  438.3 2.9 bitcast_dynamic-update-slice_fusion.2
  441.5 4.0 bitcast_dynamic-update-slice_fusion.1
  445.5 2.9 bitcast_dynamic-update-slice_fusion
  448.4 7.8 %all-to-all-done.2 = bf16[16,128,768]{2,1,0:T(8,128)(2,1)} async-done(((bf16[16,128,768]{2,1,0:T(8,128)(2,1)}), bf16[16,128,768]{2,1,0:T(8,128)(2,1)}, u32[]{:S(2)}, u32[]{:S(2)}) %all-to-all-start.2) | async-done | bytes 3145760 | tf_op jit(solution)/shard_map/all_to_all | solution.py:816
  456.2 2.6 gather_fusion.2
  (191 shorter events, 67.0 us)
Async XLA Ops:
  7.2 59.9 %all-gather.3.cloned.1.call-start = ((), (), s32[]{:S(2)}) async-start(), calls=%async_computation.3 | async-start | bytes 9420800 | tf_op jit(solution)/shard_map/all_gather | solution.py:787
  10.8 237.2 %all-gather.5.cloned.1.call-start = ((), (), s32[]{:S(2)}) async-start(), calls=%async_computation.4 | async-start | bytes 18841600 | tf_op jit(solution)/shard_map/all_gather | solution.py:800
  15.1 7.6 %copy-start.14 = (bf16[1,1024,768]{2,1,0:T(8,128)(2,1)S(1)}, bf16[1,1024,768]{2,1,0:T(8,128)(2,1)}, u32[]{:S(2)}) copy-start(bf16[1,1024,768]{2,1,0:T(8,128)(2,1)} %param.10) | copy-start | bytes 4718596
  15.1 9.2 %copy-start.20 = (s32[64]{0:T(128)S(1)}, s32[64]{0:T(128)}, u32[]{:S(2)}) copy-start(s32[64]{0:T(128)} %param.11) | copy-start | bytes 772
  15.1 78.2 %all-to-all-start = ((bf16[16,128,768]{2,1,0:T(8,128)(2,1)}), bf16[16,128,768]{2,1,0:T(8,128)(2,1)}, u32[]{:S(2)}, u32[]{:S(2)}) async-start(bf16[16,128,768]{2,1,0:T(8,128)(2,1)} %gather_fusion), calls=%async_computation | async-start | bytes 6291456 | tf_op jit(solution)/shard_map/all_to_all | solution.py:789
  156.7 8.5 %copy-start.16 = (bf16[1,1024,768]{2,1,0:T(8,128)(2,1)}, bf16[1,1024,768]{2,1,0:T(8,128)(2,1)S(1)}, u32[]{:S(2)}) copy-start(bf16[1,1024,768]{2,1,0:T(8,128)(2,1)S(1)} %fusion.88) | copy-start | bytes 4718596
  171.7 4.9 %collective-permute-start = (f16[2,784,768]{2,1,0:T(8,128)(2,1)}, f16[2,784,768]{2,1,0:T(8,128)(2,1)}, u32[]{:S(2)}, u32[]{:S(2)}) collective-permute-start(f16[2,784,768]{2,1,0:T(8,128)(2,1)} %select_convert_fusion), channel_id=1, source_target_pairs={{0,1},{1,0},{2,3},{3,2},{4,5},{5,4},{6,7},{7,6},{8,9},{9,8},{10,11... | collective-permute-start | bytes 7225352 | tf_op jit(solution)/shard_map/ppermute | solution.py:691
  171.7 76.3 %all-to-all-start.1 = ((bf16[16,128,768]{2,1,0:T(8,128)(2,1)}), bf16[16,128,768]{2,1,0:T(8,128)(2,1)}, u32[]{:S(2)}, u32[]{:S(2)}) async-start(bf16[16,128,768]{2,1,0:T(8,128)(2,1)} %bitcast.238), calls=%async_computation.1 | async-start | bytes 6291456 | tf_op jit(solution)/shard_map/all_to_all | solution.py:816
  183.2 60.4 %collective-permute-start.1 = (f16[784,768]{1,0:T(8,128)(2,1)S(1)}, f16[784,768]{1,0:T(8,128)(2,1)S(1)}, u32[]{:S(2)}, u32[]{:S(2)}) collective-permute-start(f16[784,768]{1,0:T(8,128)(2,1)S(1)} %select_convert_fusion.2), channel_id=1, source_target_pairs={{0,2},{1,3},{2,0},{3,1},{4,6},{5,7},{6,4},{7,5},{8,10},{9,11},{10,... | collective-permute-start | bytes 3612680 | tf_op jit(solution)/shard_map/ppermute | solution.py:691
  245.8 26.2 %copy-start.11 = (f32[768,768]{1,0:T(8,128)}, f32[768,768]{1,0:T(8,128)S(1)}, u32[]{:S(2)}) copy-start(f32[768,768]{1,0:T(8,128)S(1)} %multiply_add_fusion.2) | copy-start | bytes 7077892
  260.0 3.8 collective-permute-start.3
  270.5 27.6 %collective-permute-start.7 = (f16[528,768]{1,0:T(8,128)(2,1)}, f16[528,768]{1,0:T(8,128)(2,1)}, u32[]{:S(2)}, u32[]{:S(2)}) collective-permute-start(f16[528,768]{1,0:T(8,128)(2,1)} %select_convert_fusion.3), channel_id=1, source_target_pairs={{0,2},{1,3},{2,0},{3,1},{4,6},{5,7},{6,4},{7,5},{8,10},{9,11},{10,... | collective-permute-start | bytes 2433032 | tf_op jit(solution)/shard_map/ppermute | solution.py:691
  273.1 21.0 %collective-permute-start.2 = (f16[400,768]{1,0:T(8,128)(2,1)}, f16[400,768]{1,0:T(8,128)(2,1)}, u32[]{:S(2)}, u32[]{:S(2)}) collective-permute-start(f16[400,768]{1,0:T(8,128)(2,1)} %select_convert_fusion.4), channel_id=1, source_target_pairs={{0,4},{4,0},{8,12},{12,8},{16,20},{20,16},{24,28},{28,24},{1,5},{5... | collective-permute-start | bytes 1843208 | tf_op jit(solution)/shard_map/ppermute | solution.py:691
  274.5 1.4 collective-permute-start.8
  275.9 24.8 %copy-start.9 = (f32[2,512,768]{2,1,0:T(8,128)S(1)}, f32[2,512,768]{2,1,0:T(8,128)}, u32[]{:S(2)}) copy-start(f32[2,512,768]{2,1,0:T(8,128)} %copy-done.8) | copy-start | bytes 9437188
  275.9 18.1 %collective-permute-start.9 = (f32[48,768]{1,0:T(8,128)S(1)}, f32[48,768]{1,0:T(8,128)S(1)}, u32[]{:S(2)}, u32[]{:S(2)}) collective-permute-start(f32[48,768]{1,0:T(8,128)S(1)} %add.462), channel_id=1, source_target_pairs={{0,2},{1,3},{2,0},{3,1},{4,6},{5,7},{6,4},{7,5},{8,10},{9,11},{10,... | collective-permute-start | bytes 442376 | tf_op jit(solution)/shard_map/ppermute | solution.py:691
  302.4 23.6 %collective-permute-start.13 = (f16[336,768]{1,0:T(8,128)(2,1)S(1)}, f16[336,768]{1,0:T(8,128)(2,1)S(1)}, u32[]{:S(2)}, u32[]{:S(2)}) collective-permute-start(f16[336,768]{1,0:T(8,128)(2,1)S(1)} %select_convert_fusion.5), channel_id=1, source_target_pairs={{0,4},{4,0},{8,12},{12,8},{16,20},{20,16},{24,28},{28,24},{1,5},{5... | collective-permute-start | bytes 1548296 | tf_op jit(solution)/shard_map/ppermute | solution.py:691
  304.1 13.5 %collective-permute-start.5 = (f16[112,768]{1,0:T(8,128)(2,1)S(1)}, f16[112,768]{1,0:T(8,128)(2,1)S(1)}, u32[]{:S(2)}, u32[]{:S(2)}) collective-permute-start(f16[112,768]{1,0:T(8,128)(2,1)S(1)} %get-tuple-element.135), channel_id=1, source_target_pairs={{0,16},{4,20},{8,24},{12,28},{16,0},{20,4},{24,8},{28,12},{1,17},{... | collective-permute-start | bytes 516104 | tf_op jit(solution)/shard_map/ppermute | solution.py:691
  305.0 10.3 %collective-permute-start.4 = (f16[112,768]{1,0:T(8,128)(2,1)S(1)}, f16[112,768]{1,0:T(8,128)(2,1)S(1)}, u32[]{:S(2)}, u32[]{:S(2)}) collective-permute-start(f16[112,768]{1,0:T(8,128)(2,1)S(1)} %get-tuple-element.136), channel_id=1, source_target_pairs={{0,8},{4,12},{8,0},{12,4},{16,24},{20,28},{24,16},{28,20},{1,9},{5... | collective-permute-start | bytes 516104 | tf_op jit(solution)/shard_map/ppermute | solution.py:691
  306.4 13.0 %collective-permute-start.6 = (f16[112,768]{1,0:T(8,128)(2,1)S(1)}, f16[112,768]{1,0:T(8,128)(2,1)S(1)}, u32[]{:S(2)}, u32[]{:S(2)}) collective-permute-start(f16[112,768]{1,0:T(8,128)(2,1)S(1)} %get-tuple-element.134), channel_id=1, source_target_pairs={{0,24},{4,28},{8,16},{12,20},{16,8},{20,12},{24,0},{28,4},{1,25},{... | collective-permute-start | bytes 516104 | tf_op jit(solution)/shard_map/ppermute | solution.py:691
  321.6 9.2 %collective-permute-start.10 = (f16[96,768]{1,0:T(8,128)(2,1)S(1)}, f16[96,768]{1,0:T(8,128)(2,1)S(1)}, u32[]{:S(2)}, u32[]{:S(2)}) collective-permute-start(f16[96,768]{1,0:T(8,128)(2,1)S(1)} %multiply_convert_fusion), channel_id=1, source_target_pairs={{0,24},{4,28},{8,16},{12,20},{16,8},{20,12},{24,0},{28,4},{1,25},{... | collective-permute-start | bytes 442376 | tf_op jit(solution)/shard_map/ppermute | solution.py:691
  323.6 17.7 %collective-permute-start.11 = (f16[96,768]{1,0:T(8,128)(2,1)S(1)}, f16[96,768]{1,0:T(8,128)(2,1)S(1)}, u32[]{:S(2)}, u32[]{:S(2)}) collective-permute-start(f16[96,768]{1,0:T(8,128)(2,1)S(1)} %multiply_convert_fusion), channel_id=1, source_target_pairs={{0,16},{4,20},{8,24},{12,28},{16,0},{20,4},{24,8},{28,12},{1,17},{... | collective-permute-start | bytes 442376 | tf_op jit(solution)/shard_map/ppermute | solution.py:691
  325.0 16.3 %collective-permute-start.12 = (f16[96,768]{1,0:T(8,128)(2,1)S(1)}, f16[96,768]{1,0:T(8,128)(2,1)S(1)}, u32[]{:S(2)}, u32[]{:S(2)}) collective-permute-start(f16[96,768]{1,0:T(8,128)(2,1)S(1)} %multiply_convert_fusion), channel_id=1, source_target_pairs={{0,8},{4,12},{8,0},{12,4},{16,24},{20,28},{24,16},{28,20},{1,9},{5... | collective-permute-start | bytes 442376 | tf_op jit(solution)/shard_map/ppermute | solution.py:691
  328.1 27.5 %copy-start.4 = (bf16[1024,768]{1,0:T(8,128)(2,1)S(1)}, bf16[1024,768]{1,0:T(8,128)(2,1)}, u32[]{:S(2)}) copy-start(bf16[1024,768]{1,0:T(8,128)(2,1)} %copy-done.3) | copy-start | bytes 4718596
  328.2 18.9 %collective-permute-start.16 = (f16[96,768]{1,0:T(8,128)(2,1)S(1)}, f16[96,768]{1,0:T(8,128)(2,1)S(1)}, u32[]{:S(2)}, u32[]{:S(2)}) collective-permute-start(f16[96,768]{1,0:T(8,128)(2,1)S(1)} %get-tuple-element.140), channel_id=1, source_target_pairs={{0,16},{4,20},{8,24},{12,28},{16,0},{20,4},{24,8},{28,12},{1,17},{... | collective-permute-start | bytes 442376 | tf_op jit(solution)/shard_map/ppermute | solution.py:691
  330.2 13.6 %collective-permute-start.15 = (f16[96,768]{1,0:T(8,128)(2,1)S(1)}, f16[96,768]{1,0:T(8,128)(2,1)S(1)}, u32[]{:S(2)}, u32[]{:S(2)}) collective-permute-start(f16[96,768]{1,0:T(8,128)(2,1)S(1)} %get-tuple-element.141), channel_id=1, source_target_pairs={{0,8},{4,12},{8,0},{12,4},{16,24},{20,28},{24,16},{28,20},{1,9},{5... | collective-permute-start | bytes 442376 | tf_op jit(solution)/shard_map/ppermute | solution.py:691
  330.8 18.2 %collective-permute-start.17 = (f16[96,768]{1,0:T(8,128)(2,1)S(1)}, f16[96,768]{1,0:T(8,128)(2,1)S(1)}, u32[]{:S(2)}, u32[]{:S(2)}) collective-permute-start(f16[96,768]{1,0:T(8,128)(2,1)S(1)} %get-tuple-element.139), channel_id=1, source_target_pairs={{0,24},{4,28},{8,16},{12,20},{16,8},{20,12},{24,0},{28,4},{1,25},{... | collective-permute-start | bytes 442376 | tf_op jit(solution)/shard_map/ppermute | solution.py:691
  341.7 23.3 %collective-permute-start.14 = (f16[384,768]{1,0:T(8,128)(2,1)S(1)}, f16[384,768]{1,0:T(8,128)(2,1)S(1)}, u32[]{:S(2)}, u32[]{:S(2)}) collective-permute-start(f16[384,768]{1,0:T(8,128)(2,1)S(1)} %pad_maximum_fusion.5), channel_id=1, source_target_pairs={{0,4},{4,0},{8,12},{12,8},{16,20},{20,16},{24,28},{28,24},{1,5},{5... | collective-permute-start | bytes 1769480 | tf_op jit(solution)/shard_map/ppermute | solution.py:691
  351.1 9.7 %collective-permute-start.19 = (f16[80,768]{1,0:T(8,128)(2,1)S(1)}, f16[80,768]{1,0:T(8,128)(2,1)S(1)}, u32[]{:S(2)}, u32[]{:S(2)}) collective-permute-start(f16[80,768]{1,0:T(8,128)(2,1)S(1)} %multiply_convert_fusion.1), channel_id=1, source_target_pairs={{0,24},{4,28},{8,16},{12,20},{16,8},{20,12},{24,0},{28,4},{1,25},{... | collective-permute-start | bytes 368648 | tf_op jit(solution)/shard_map/ppermute | solution.py:691
  353.4 9.6 %collective-permute-start.20 = (f16[80,768]{1,0:T(8,128)(2,1)S(1)}, f16[80,768]{1,0:T(8,128)(2,1)S(1)}, u32[]{:S(2)}, u32[]{:S(2)}) collective-permute-start(f16[80,768]{1,0:T(8,128)(2,1)S(1)} %multiply_convert_fusion.1), channel_id=1, source_target_pairs={{0,16},{4,20},{8,24},{12,28},{16,0},{20,4},{24,8},{28,12},{1,17},{... | collective-permute-start | bytes 368648 | tf_op jit(solution)/shard_map/ppermute | solution.py:691
  353.4 9.6 %collective-permute-start.21 = (f16[80,768]{1,0:T(8,128)(2,1)S(1)}, f16[80,768]{1,0:T(8,128)(2,1)S(1)}, u32[]{:S(2)}, u32[]{:S(2)}) collective-permute-start(f16[80,768]{1,0:T(8,128)(2,1)S(1)} %multiply_convert_fusion.1), channel_id=1, source_target_pairs={{0,8},{4,12},{8,0},{12,4},{16,24},{20,28},{24,16},{28,20},{1,9},{5... | collective-permute-start | bytes 368648 | tf_op jit(solution)/shard_map/ppermute | solution.py:691
  363.3 12.5 %collective-permute-start.22 = (f16[320,768]{1,0:T(8,128)(2,1)S(1)}, f16[320,768]{1,0:T(8,128)(2,1)S(1)}, u32[]{:S(2)}, u32[]{:S(2)}) collective-permute-start(f16[320,768]{1,0:T(8,128)(2,1)S(1)} %pad_maximum_fusion.6), channel_id=1, source_target_pairs={{0,4},{4,0},{8,12},{12,8},{16,20},{20,16},{24,28},{28,24},{1,5},{5... | collective-permute-start | bytes 1474568 | tf_op jit(solution)/shard_map/ppermute | solution.py:691
  365.5 13.5 %copy-start.21 = (s32[64]{0:T(128)S(1)}, s32[64]{0:T(128)}, u32[]{:S(2)}) copy-start(s32[64]{0:T(128)} %param.11) | copy-start | bytes 772
  365.5 13.7 %copy-start.17 = (f32[2]{0:T(128)S(1)}, f32[2]{0:T(128)}, u32[]{:S(2)}) copy-start(f32[2]{0:T(128)} %param.16) | copy-start | bytes 28
  365.5 19.3 %collective-permute-start.18 = (f32[768,768]{1,0:T(8,128)S(1)}, f32[768,768]{1,0:T(8,128)}, u32[]{:S(2)}, u32[]{:S(2)}) collective-permute-start(f32[768,768]{1,0:T(8,128)S(1)} %convert_multiply_fusion.2.early_ref), channel_id=1, source_target_pairs={{0,1},{1,0},{2,3},{3,2},{4,5},{5,4},{6,7},{7,6},{8,9},{9,8},{10,11... | collective-permute-start | bytes 7077896 | tf_op jit(solution)/shard_map/ppermute | solution.py:691
  377.4 7.3 %collective-permute-start.23 = (f32[512,768]{1,0:T(8,128)}, f32[512,768]{1,0:T(8,128)}, u32[]{:S(2)}, u32[]{:S(2)}) collective-permute-start(f32[512,768]{1,0:T(8,128)} %convert_multiply_fusion.3.late_ref), channel_id=1, source_target_pairs={{0,1},{1,0},{2,3},{3,2},{4,5},{5,4},{6,7},{7,6},{8,9},{9,8},{10,11... | collective-permute-start | bytes 4718600 | tf_op jit(solution)/shard_map/ppermute | solution.py:691
  379.9 76.4 %all-to-all-start.2 = ((bf16[16,128,768]{2,1,0:T(8,128)(2,1)}), bf16[16,128,768]{2,1,0:T(8,128)(2,1)}, u32[]{:S(2)}, u32[]{:S(2)}) async-start(bf16[16,128,768]{2,1,0:T(8,128)(2,1)} %bitcast.237), calls=%async_computation.2 | async-start | bytes 6291456 | tf_op jit(solution)/shard_map/all_to_all | solution.py:816
  384.7 6.2 %copy-start.6 = (f32[942080]{0:T(1024)S(1)}, f32[942080]{0:T(1024)}, u32[]{:S(2)}) copy-start(f32[942080]{0:T(1024)} %param.15) | copy-start | bytes 11304964
  394.9 28.4 %collective-permute-start.25 = (f16[3680,128]{1,0:T(8,128)(2,1)}, f16[3680,128]{1,0:T(8,128)(2,1)}, u32[]{:S(2)}, u32[]{:S(2)}) collective-permute-start(f16[3680,128]{1,0:T(8,128)(2,1)} %fusion.53), channel_id=1, source_target_pairs={{0,1},{1,0},{2,3},{3,2},{4,5},{5,4},{6,7},{7,6},{8,9},{9,8},{10,11... | collective-permute-start | bytes 2826248 | tf_op jit(solution)/shard_map/ppermute | solution.py:691
  395.2 32.0 %collective-permute-start.24 = (f16[3680,128]{1,0:T(8,128)(2,1)}, f16[3680,128]{1,0:T(8,128)(2,1)}, u32[]{:S(2)}, u32[]{:S(2)}) collective-permute-start(f16[3680,128]{1,0:T(8,128)(2,1)} %fusion.53), channel_id=1, source_target_pairs={{0,2},{1,3},{2,0},{3,1},{4,6},{5,7},{6,4},{7,5},{8,10},{9,11},{10,... | collective-permute-start | bytes 2826248 | tf_op jit(solution)/shard_map/ppermute | solution.py:691
  398.0 32.2 %collective-permute-start.27 = (f16[3680,128]{1,0:T(8,128)(2,1)S(1)}, f16[3680,128]{1,0:T(8,128)(2,1)}, u32[]{:S(2)}, u32[]{:S(2)}) collective-permute-start(f16[3680,128]{1,0:T(8,128)(2,1)S(1)} %fusion.52), channel_id=1, source_target_pairs={{0,1},{1,0},{2,3},{3,2},{4,5},{5,4},{6,7},{7,6},{8,9},{9,8},{10,11... | collective-permute-start | bytes 2826248 | tf_op jit(solution)/shard_map/ppermute | solution.py:691
  398.1 43.1 %collective-permute-start.26 = (f16[3680,128]{1,0:T(8,128)(2,1)S(1)}, f16[3680,128]{1,0:T(8,128)(2,1)}, u32[]{:S(2)}, u32[]{:S(2)}) collective-permute-start(f16[3680,128]{1,0:T(8,128)(2,1)S(1)} %fusion.52), channel_id=1, source_target_pairs={{0,2},{1,3},{2,0},{3,1},{4,6},{5,7},{6,4},{7,5},{8,10},{9,11},{10,... | collective-permute-start | bytes 2826248 | tf_op jit(solution)/shard_map/ppermute | solution.py:691
  402.9 16.3 %slice-start = ((s8[15073280]{0:T(1024)(128)(4,1)}), s8[2490368]{0:T(1024)(128)(4,1)S(1)}, s32[]{:S(2)}) async-start(s8[15073280]{0:T(1024)(128)(4,1)} %bitcast.223), calls=%async_computation.5 | async-start | bytes 4980736
  407.3 11.9 %slice-start.1 = ((s8[15073280]{0:T(1024)(128)(4,1)}), s8[4194304]{0:T(1024)(128)(4,1)S(1)}, s32[]{:S(2)}) async-start(s8[15073280]{0:T(1024)(128)(4,1)} %bitcast.223), calls=%async_computation.6 | async-start | bytes 8388608
  407.3 11.9 %slice-start.2 = ((s8[15073280]{0:T(1024)(128)(4,1)}), s8[4194304]{0:T(1024)(128)(4,1)S(1)}, s32[]{:S(2)}) async-start(s8[15073280]{0:T(1024)(128)(4,1)} %bitcast.223), calls=%async_computation.7 | async-start | bytes 8388608
  411.7 7.5 %slice-start.3 = ((s8[15073280]{0:T(1024)(128)(4,1)}), s8[4194304]{0:T(1024)(128)(4,1)S(1)}, s32[]{:S(2)}) async-start(s8[15073280]{0:T(1024)(128)(4,1)} %bitcast.223), calls=%async_computation.8 | async-start | bytes 8388608
  427.2 11.0 %collective-permute-start.28 = (f16[3680,128]{1,0:T(8,128)(2,1)}, f16[3680,128]{1,0:T(8,128)(2,1)S(1)}, u32[]{:S(2)}, u32[]{:S(2)}) collective-permute-start(f16[3680,128]{1,0:T(8,128)(2,1)} %collective-permute-done.24), channel_id=1, source_target_pairs={{0,1},{1,0},{2,3},{3,2},{4,5},{5,4},{6,7},{7,6},{8,9},{9,8},{10,11... | collective-permute-start | bytes 2826248 | tf_op jit(solution)/shard_map/ppermute | solution.py:691
  441.2 4.4 collective-permute-start.29
  (13 other events, 40.9 us)
Sparse Core Ops, SparseCore 0:
  10.9 56.1 all-gather.2
  68.6 96.2 all-gather.4

commit v6 on v5

--- a/solution.py
+++ b/solution.py
@@ -699,13 +699,14 @@
     return values.astype(F32) * jnp.exp2(-power)
 
 
-def scatter(values, power, axis, bit=1, count=2):
+def scatter(values, power, axis, bit=1, count=2, after=None):
     place = (lax.axis_index(axis) // bit) % count
     rows = values.shape[-2] // count
     mark = min(MARK, rows)
     dim = values.ndim - 2
     total = lax.dynamic_slice_in_dim(values, place * rows, rows, dim)
     least = power
+    arrived = []
     for offset in range(1, count):
         to = place ^ offset
         last = to == count - 1
@@ -714,8 +715,11 @@
         line = lax.broadcasted_iota(jnp.int32, send.shape, dim)
         marked = jnp.where(last, line < mark, line >= rows)
         wire = jnp.where(marked, power, send * jnp.exp2(power)).astype(jnp.float16)
-        got = swap(wire, axis, bit * offset)
-        last = place == count - 1
+        arrived.append(swap(wire, axis, bit * offset))
+    if after is not None:
+        arrived, _ = lax.optimization_barrier((arrived, after))
+    last = place == count - 1
+    for got in arrived:
         got_power = lax.dynamic_slice_in_dim(got, jnp.where(last, 0, rows), 1, dim)
         got_power = got_power.reshape(-1, D)[0:1, 0:1].astype(F32)
         body = lax.dynamic_slice_in_dim(got, jnp.where(last, mark, 0), rows, dim)
@@ -740,8 +744,11 @@
     return jnp.concatenate(everyones(values, axis, bit, count))
 
 
-def add_pair(values, axis, bit):
-    return values + swap(values, axis, bit)
+def add_pair(values, axis, bit, after=None):
+    got = swap(values, axis, bit)
+    if after is not None:
+        got, _ = lax.optimization_barrier((got, after))
+    return values + got
 
 
 def data_groups():
@@ -842,8 +849,8 @@
     window, grad_tok, small, late_power = run_backward(
         proj, dy, through, states, pair, packed, cot, in_w, norm_gain, ggain,
         bound_arr, e2, et, params)
-    window, small, late_power, back_out, early, early_power, whole_master = tie(
-        (window, small, late_power, back_out, early, early_power, whole_master))
+    window, small, late_power, early, early_power, whole_master = tie(
+        (window, small, late_power, early, early_power, whole_master))
 
     groups = data_groups()
     late = lax.dot_general(
@@ -852,19 +859,25 @@
     late_power = late_power[0:1, 0:1]
     late, late_power = scatter(late, late_power, "zero", 1)
     late = late.reshape(WINDOW, D)
-    early, early_power = scatter(early, early_power, "dp", *groups[0])
     small = add_pair(small, "zero", 1)
     early, early_power, grad_tok, _ = tie((early, early_power, grad_tok, late))
     late, late_power = scatter(late, late_power, "zero", 2)
-    small = add_pair(small, "zero", 2)
-    for group in groups[1:]:
-        early, early_power = scatter(early, early_power, "dp", *group)
-    early = to_wire(early, early_power)
+    early, early_power = scatter(early, early_power, "dp", *groups[0])
+    small = add_pair(small, "zero", 2, late)
+    early_before, power_before = early, early_power
     picked_grad = spread(grad_tok)
+    tokens, back_out, _ = tie((tokens, back_out, grad_tok))
+    back_rows = back_out.at[restore].get(mode="promise_in_bounds")
+    tokens_out = jnp.where(live, back_rows, tokens)
+    new_master = jnp.zeros((group_devices, shard_rows, LANES), F32)
+    late, tokens_out, new_master, picked_grad = tie((late, tokens_out, new_master, picked_grad))
     lines = small.shape[0]
     late = jnp.concatenate([late, small, jnp.zeros((WINDOW // 8 - lines, D), F32)])
-    early, _ = tie((early, late))
     late, late_power = scatter(late, late_power, "dp", *groups[0])
+    early, early_power = early_before, power_before
+    for group in groups[1:]:
+        early, early_power = scatter(early, early_power, "dp", *group, after=late)
+    early = to_wire(early, early_power)
     for group in reversed(groups[1:]):
         early = gather(early, "dp", *group)
     early, _ = tie((early, late))
@@ -900,39 +913,25 @@
         return ((first_next * first_scale) / (
             jnp.sqrt(second_next * second_scale) + EPS_ADAM)).astype(jnp.float16)
 
-    part = shard_rows // 2
-    whole_master = whole_master.reshape(2 * group_devices, part, LANES)
-    new_master = jnp.zeros((2 * group_devices, part, LANES), F32)
-
-    def put(new_master, piece, offset, half):
-        place = 2 * (zero_index ^ offset) + half
-        old = lax.dynamic_index_in_dim(whole_master, place, 0, keepdims=False)
+    whole_master = whole_master.reshape(group_devices, shard_rows, LANES)
+
+    def put(new_master, piece, offset):
+        shard = zero_index ^ offset
+        old = lax.dynamic_index_in_dim(whole_master, shard, 0, keepdims=False)
         new = old - adam_rates[0] * (piece.astype(F32) + adam_rates[1] * old)
-        return lax.dynamic_update_index_in_dim(new_master, new, place, 0)
-
-    front = quotient(slice(0, part))
-    front, grad_late, back_out = tie((front, grad_shard, back_out))
-    front_across = swap(front, "zero", 2)
-    grad_shard = grad_late
-    back = quotient(slice(part, shard_rows))
-    back, grad_shard, new_master = tie((back, grad_shard, new_master))
-    back_across = swap(back, "zero", 2)
-    front_core = swap(front, "zero", 1)
-    back_core = swap(back, "zero", 1)
+        return lax.dynamic_update_index_in_dim(new_master, new, shard, 0)
+
+    own_part, first, second = tie((quotient(slice(0, shard_rows)), first, second))
+    across = swap(own_part, "zero", 2)
+    core = swap(own_part, "zero", 1)
     first_next, second_next = moments(grad_shard, first, second)
-    back_rows = back_out.at[restore].get(mode="promise_in_bounds")
-    tokens_out = jnp.where(live, back_rows, tokens)
-    new_master = put(put(new_master, front, 0, 0), front_core, 1, 0)
-    front_across, new_master, tokens_out, first_next, second_next = tie(
-        (front_across, new_master, tokens_out, first_next, second_next))
-    front_last = swap(front_across, "zero", 1)
-    new_master = put(put(new_master, back, 0, 1), back_core, 1, 1)
-    new_master = put(put(new_master, front_across, 2, 0), front_last, 3, 0)
-    back_across, new_master = tie((back_across, new_master))
-    back_last = swap(back_across, "zero", 1)
-    new_master = put(new_master, back_across, 2, 1)
-    back_last, new_master = tie((back_last, new_master))
-    new_master = put(new_master, back_last, 3, 1)
+    new_master = put(put(new_master, own_part, 0), core, 1)
+    across, new_master, first_next, second_next = tie(
+        (across, new_master, first_next, second_next))
+    last = swap(across, "zero", 1)
+    new_master = put(new_master, across, 2)
+    last, new_master = tie((last, new_master))
+    new_master = put(new_master, last, 3)
     back_grad, new_master = tie((back_grad, new_master))
     grad_tokens = jnp.where(
         live, back_grad.at[restore].get(mode="promise_in_bounds"), jnp.zeros((), BF16))

time: 476 us -> 476 us (level)
    dynamic_update_slice x8 -> x4, other arithmetic: 28.7 us -> 19.2 us  [put(): return lax.dynamic_update_index_in_dim(new_master, new, shard, 0)]
    ppermute x30 -> x27, waiting for transfers between devices: 52.6 us -> 58.5 us  [swap(): return lax.ppermute(values, axis, [(i, i ^ bit) for i in range(size)])]
    ppermute x30 -> x27, starting transfers between devices: 31.4 us -> 28.8 us  [swap(): return lax.ppermute(values, axis, [(i, i ^ bit) for i in range(size)])]
  transfers between devices with their start and end apart: 35 -> 32, of which waited for: 14 -> 14; matrix products, arithmetic and copies ran while one was open for 27% -> 30% of each run, Pallas kernels for 22% -> 22%
where the time goes in v6:
time: 476 us; the launch traced here: 468 us
  waiting for transfers between devices  119 us (25%)
  Pallas kernels  105 us (22%)
  other arithmetic  77.6 us (16%)
  matrix products  50.5 us (11%)
  starting transfers between devices  46.1 us (10%)
  local copies, waits for them, and re-layouts  35.8 us (8%)
  between operations  34.6 us (7%)
    ppermute x27, waiting for transfers between devices, swap(): return lax.ppermute(values, axis, [(i, i ^ bit) for i in range(size)])  58.5 us
    pallas_call x1, Pallas kernels, run_backward(): pl.pallas_call(backward_kernel, grid=(steps,), in_specs=[pl.BlockSpec(mem...  57.7 us
    all_gather x1, waiting for transfers between devices, on_device(): flat = lax.all_gather(own.astype(BF16), 'zero', axis=0, tiled=True)  40.8 us
    pallas_call x1, Pallas kernels, run_forward(): pl.pallas_call(forward_kernel, grid=(steps,), in_specs=[pl.BlockSpec(memo...  35.1 us
    ppermute x27, starting transfers between devices, swap(): return lax.ppermute(values, axis, [(i, i ^ bit) for i in range(size)])  28.8 us
    dot_general x3, matrix products, dot(): lax.dot_general(a, b, (((1,), (0,)), ((), ())), preferred_element_type=F32)  21.4 us
    dynamic_update_slice x4, other arithmetic, put(): return lax.dynamic_update_index_in_dim(new_master, new, shard, 0)  19.2 us
    dot_general x3, matrix products, dot_nt(): lax.dot_general(a, b, (((1,), (1,)), ((), ())), preferred_element_type=F32)  15 us
  transfers between devices with their start and end apart: 32, of which 14 were waited for; matrix products, arithmetic and copies ran while one was open for 30% of the time, Pallas kernels for 22%

profile of v6, /device:TPU:0, one launch (start us, length us, event | category | flops | bytes accessed | tf_op | source)
XLA Modules:
  0.0 468.3 jit_solution(12027762490118292907)
XLA Ops:
  7.2 3.5 bitcast_convert_fusion
  12.6 2.4 gather_fusion
  15.0 7.4 %all-to-all-start = ((bf16[16,128,768]{2,1,0:T(8,128)(2,1)}), bf16[16,128,768]{2,1,0:T(8,128)(2,1)}, u32[]{:S(2)}, u32[]{:S(2)}) async-start(bf16[16,128,768]{2,1,0:T(8,128)(2,1)} %gather_fusion), calls=%async_computation | async-start | bytes 6291456 | tf_op jit(solution)/shard_map/all_to_all | solution.py:796
  26.3 40.8 %all-gather.3.cloned.1.call-done.flat_ref = bf16[29440,128]{1,0:T(8,128)(2,1)} async-done(((bf16[7360,128]{1,0:T(8,128)(2,1)}), bf16[29440,128]{1,0:T(8,128)(2,1)}) %all-gather.3.cloned.1.call-update) | async-done | bytes 7536656 | tf_op jit(solution)/shard_map/all_gather | solution.py:794
  67.0 6.0 %shard_map.136 = (bf16[3584,768]{1,0:T(8,128)(2,1)S(1)}, bf16[1536,768]{1,0:T(8,128)(2,1)S(1)}, f32[1,768]{1,0:T(1,128)S(1)}, f32[8,1792]{1,0:T(8,128)S(1)}, f32...) custom-call(bf16[29440,128]{1,0:T(8,128)(2,1)} %all-gather.3.cloned., ...), custom_call_target="tpu_custom_call" | custom-call | flops 1000000000 | bytes 16777216 | tf_op jit(solution)/shard_map/pallas_call | solution.py:593
  73.0 2.6 copy-done
  77.0 4.6 fusion.61.gm_ref
  81.6 11.6 %all-to-all-done = bf16[16,128,768]{2,1,0:T(8,128)(2,1)} async-done(((bf16[16,128,768]{2,1,0:T(8,128)(2,1)}), bf16[16,128,768]{2,1,0:T(8,128)(2,1)}, u32[]{:S(2)}, u32[]{:S(2)}) %all-to-all-start) | async-done | bytes 3145760 | tf_op jit(solution)/shard_map/all_to_all | solution.py:796
  93.3 5.8 %fusion.18 = (f32[1024]{0:T(1024)S(1)}, bf16[1024,768]{1,0:T(8,128)(2,1)S(1)}) fusion(bf16[2048,768]{1,0:T(8,128)(2,1)} %bitcast.6, s32[1024]{0:T(1024)S(1)} %fusion.41), kind=kOutput, calls=%fused_computation.48 | convolution fusion | flops 3226467328 | bytes 4726784 | tf_op jit(solution)/shard_map/dot_general | solution.py:29
  99.1 4.6 fusion.29.z_ref
  103.7 5.8 %fusion.27.proj_ref.before_ref = f32[1024,1816]{1,0:T(8,128)} fusion(bf16[3584,768]{1,0:T(8,128)(2,1)S(1)} %copy-done.1, bf16[1024,768]{1,0:T(8,128)(2,1)S(1)} %get-tuple-element.157.tok_ref, f32[768]{0:T(1024)S(1)} %reduce.2, f32[1024]{0:T(1024)S(1)} %add_rsqrt_fusion), kind=kOutput, calls=%fused_computation.60 | convolution fusion | flops 2859466752 | bytes 11808768 | tf_op jit(solution)/shard_map/dot_general | solution.py:33
  109.5 35.1 %shard_map.137 = (bf16[2,1024,1536]{2,1,0:T(8,128)(2,1)}, f32[1024,1536]{1,0:T(8,128)}, f32[1024,128]{1,0:T(8,128)S(1)}, f32[8,128,1536]{2,1,0:T(8,128)}, f32[1,1536]{1,0:T(1,128)S(1)}, /*index=5*/f32[8,128]{1,0:T(8,128)S(1)}) custom-call(s32[1]{0:T(128)} %dynamic_slice.160.bound_ref, f32[1]{0:T(128)S(6)} %convert.1.cot_ref, f32[1024,1536]{1,0:T(8,128)} %fusion.29.z_ref, ...), custom_call_target="tpu_custom_call" | custom-call | flops 30000001024 | bytes 41943040 | tf_op jit(solution)/shard_map/pallas_call | solution.py:221
  144.6 10.4 %fusion.14 = bf16[2048,768]{1,0:T(8,128)(2,1)} fusion(s32[2048]{0:T(1024)S(1)} %bitcast.163, bf16[1024,768]{1,0:T(8,128)(2,1)S(1)} %get-tuple-element.157.tok_ref, bf16[1536,768]{1,0:T(8,128)(2,1)} %copy-done.2, bf16[2,1024,1536]{2,1,0:T(8,128)(2,1)} %get-tuple-element.85.gz_ref), kind=kOutput, calls=%fused_computation.43 | convolution fusion | flops 5643173888 | bytes 10231808 | tf_op jit(solution)/shard_map/dot_general | solution.py:29
  156.7 8.5 %fusion.16 = f32[2,1536,768]{2,1,0:T(8,128)S(1)} fusion(bf16[2,1024,1536]{2,1,0:T(8,128)(2,1)} %get-tuple-element.85.gz_ref, bf16[1,1024,768]{2,1,0:T(8,128)(2,1)S(1)} %fusion.65, bf16[1,1024,768]{2,1,0:T(8,128)(2,1)S(1)} %copy-done.14), kind=kOutput, calls=%fused_computation.46 | convolution fusion | flops 4833411072 | bytes 18874368 | tf_op jit(solution)/shard_map/dot_general | solution.py:844
  165.3 3.7 copy-done.10
  169.0 2.7 select_convert_fusion
  171.7 4.6 all-to-all-start.1
  179.2 3.6 multiply_add_fusion
  184.8 57.7 %shard_map.138 = (bf16[2,1024,1024]{2,1,0:T(8,128)(2,1)}, bf16[1024,768]{1,0:T(8,128)(2,1)S(1)}, f32[48,768]{1,0:T(8,128)S(1)}, f32[8,128]{1,0:T(8,128)S(1)}) custom-call(s32[1]{0:T(128)} %dynamic_slice.160.bound_ref, f32[1024,1816]{1,0:T(8,128)} %fusion.27.proj_ref.before_ref, f32[1024,1816]{1,0:T(8,128)} %fusion.27.proj_ref.before_ref, ...), custom_call_target="tpu_custom_call" | custom-call | flops 49999998976 | bytes 52428800 | tf_op jit(solution)/shard_map/pallas_call | solution.py:453
  248.4 5.6 %fusion.17 = f32[2,1024,768]{2,1,0:T(8,128)S(1)} fusion(bf16[2,1024,1024]{2,1,0:T(8,128)(2,1)} %get-tuple-element.97, bf16[1,1024,768]{2,1,0:T(8,128)(2,1)S(1)} %copy-done.16), kind=kOutput, calls=%fused_computation.47 | convolution fusion | flops 3222798336 | bytes 12058624 | tf_op jit(solution)/shard_map/dot_general | solution.py:856
  254.1 2.7 copy-done.12
  264.9 2.7 multiply_add_fusion.3
  270.3 2.3 select_convert_fusion.4
  274.3 4.3 gather_fusion.1
  278.6 4.3 broadcast_select_fusion.1
  282.9 5.1 %fusion.15 = bf16[2048,768]{1,0:T(8,128)(2,1)} fusion(bf16[1024,768]{1,0:T(8,128)(2,1)S(1)} %copy-done.4, s32[2048]{0:T(1024)S(1)} %bitcast.164), kind=kOutput, calls=%fused_computation.44 | convolution fusion | flops 3224895488 | bytes 4726784 | tf_op jit(solution)/shard_map/dot_general | solution.py:29
  303.6 2.4 collective-permute-start.6
  311.5 6.9 %collective-permute-done.6 = f16[112,768]{1,0:T(8,128)(2,1)S(1)} collective-permute-done((f16[112,768]{1,0:T(8,128)(2,1)S(1)}, f16[112,768]{1,0:T(8,128)(2,1)S(1)}, u32[]{:S(2)}, u32[]{:S(2)}) %collective-permute-start.6) | collective-permute-done | bytes 172064 | tf_op jit(solution)/shard_map/ppermute | solution.py:691
  324.2 2.3 collective-permute-start.11
  332.8 2.3 collective-permute-start.17
  335.1 11.7 %collective-permute-done.12 = f16[96,768]{1,0:T(8,128)(2,1)S(1)} collective-permute-done((f16[96,768]{1,0:T(8,128)(2,1)S(1)}, f16[96,768]{1,0:T(8,128)(2,1)S(1)}, u32[]{:S(2)}, u32[]{:S(2)}) %collective-permute-start.12) | collective-permute-done | bytes 147488 | tf_op jit(solution)/shard_map/ppermute | solution.py:691
  355.1 2.8 collective-permute-start.21
  358.0 2.8 collective-permute-done.19
  360.8 3.6 collective-permute-done.20
  365.8 11.0 %collective-permute-done.22 = f16[320,768]{1,0:T(8,128)(2,1)S(1)} collective-permute-done((f16[320,768]{1,0:T(8,128)(2,1)S(1)}, f16[320,768]{1,0:T(8,128)(2,1)S(1)}, u32[]{:S(2)}, u32[]{:S(2)}) %collective-permute-start.22) | collective-permute-done | bytes 491552 | tf_op jit(solution)/shard_map/ppermute | solution.py:691
  379.9 5.2 %all-to-all-start.2 = ((bf16[16,128,768]{2,1,0:T(8,128)(2,1)}), bf16[16,128,768]{2,1,0:T(8,128)(2,1)}, u32[]{:S(2)}, u32[]{:S(2)}) async-start(bf16[16,128,768]{2,1,0:T(8,128)(2,1)} %bitcast.160), calls=%async_computation.2 | async-start | bytes 6291456 | tf_op jit(solution)/shard_map/all_to_all | solution.py:823
  385.1 6.1 %shard_map.139 = f32[7360,128]{1,0:T(8,128)} custom-call(s32[2]{0:T(128)S(1)} %pad_add_fusion.who_ref, f32[768,768]{1,0:T(8,128)S(1)} %convert_multiply_fusion.2.early_ref, f32[768,768]{1,0:T(8,128)} %collective-permute-done.18.early_other_ref, f32[512,768]{1,0:T(8,128)} %convert_multiply_fusion.3.late_ref, ...), custom_call_target="tpu_custom_call" | custom-call | flops 1000000 | bytes 12582912 | tf_op jit(solution)/shard_map/pallas_call | solution.py:671
  391.3 5.8 %divide_convert_fusion = f16[7360,128]{1,0:T(8,128)(2,1)} fusion(f32[7360,128]{1,0:T(8,128)} %shard_map.139, f32[]{:T(128)} %bitcast.51, f32[]{:T(128)} %bitcast.49, f32[942080]{0:T(1024)S(1)} %copy-done.6, f32[942080]{0:T(1024)} %param.14), kind=kLoop, calls=%fused_computation.40 | loop fusion | flops 11304960 | bytes 13189128 | tf_op jit(solution)/shard_map/convert_element_type | solution.py:914
  398.6 6.9 %multiply_add_fusion.1 = (f32[7360,128]{1,0:T(8,128)}, f32[7360,128]{1,0:T(8,128)}) fusion(f32[7360,128]{1,0:T(8,128)S(1)} %bitcast.154, f32[7360,128]{1,0:T(8,128)S(1)} %copy-done.5, f32[7360,128]{1,0:T(8,128)} %bitcast.155), kind=kLoop, calls=%fused_computation.38 | loop fusion | flops 6594560 | bytes 18841600 | tf_op jit(solution)/shard_map/add | solution.py:909
  405.6 6.6 %broadcast_in_dim.154 = f32[4,7360,128]{2,1,0:T(8,128)} broadcast(f32[]{:T(128)} %constant.309.clone.1), dimensions={} | broadcast | bytes 15073284 | tf_op jit(solution)/shard_map/broadcast_in_dim | solution.py:872
  412.2 5.2 %bitcast_dynamic-update-slice_fusion.3 = f32[4,7360,128]{2,1,0:T(8,128)} fusion(f32[4,7360,128]{2,1,0:T(8,128)} %broadcast_in_dim.154, s32[]{:T(128)S(6)} %select_n.575, f16[7360,128]{1,0:T(8,128)(2,1)} %divide_convert_fusion, f32[4,7360,128]{2,1,0:T(8,128)S(1)} %bitcast.148, f32[]{:T(128)} %bitcast.55, f32[]{:T(128)} %bitcast.54), kind=kLoop, calls=%fused_computation.33 | loop fusion | flops 4710400 | bytes 9421828 | tf_op jit(solution)/shard_map/jit(dynamic_update_index_in_dim)/dynamic_update_slice | solution.py:922
  417.3 5.2 %bitcast_dynamic-update-slice_fusion.2 = f32[4,7360,128]{2,1,0:T(8,128)} fusion(f32[4,7360,128]{2,1,0:T(8,128)} %bitcast_dynamic-update-slice_fusion.3, s32[]{:T(128)S(6)} %select_n.697, f16[7360,128]{1,0:T(8,128)(2,1)} %collective-permute-done.25, f32[4,7360,128]{2,1,0:T(8,128)S(1)} %bitcast.149, f32[]{:T(128)} %bitcast.55, f32[]{:T(128)} %bitcast.54), kind=kLoop, calls=%fused_computation.28 | loop fusion | flops 4710400 | bytes 9421828 | tf_op jit(solution)/shard_map/jit(dynamic_update_index_in_dim)/dynamic_update_slice | solution.py:922
  422.5 18.1 %collective-permute-done.24 = f16[7360,128]{1,0:T(8,128)(2,1)} collective-permute-done((f16[7360,128]{1,0:T(8,128)(2,1)}, f16[7360,128]{1,0:T(8,128)(2,1)}, u32[]{:S(2)}, u32[]{:S(2)}) %collective-permute-start.24) | collective-permute-done | bytes 1884192 | tf_op jit(solution)/shard_map/ppermute | solution.py:691
  440.6 5.2 %bitcast_dynamic-update-slice_fusion.1 = f32[4,7360,128]{2,1,0:T(8,128)} fusion(f32[4,7360,128]{2,1,0:T(8,128)} %bitcast_dynamic-update-slice_fusion.2, s32[]{:T(128)S(6)} %select_n.698, f16[7360,128]{1,0:T(8,128)(2,1)} %collective-permute-done.24, f32[4,7360,128]{2,1,0:T(8,128)S(1)} %bitcast.150, f32[]{:T(128)} %bitcast.55, f32[]{:T(128)} %bitcast.54), kind=kLoop, calls=%fused_computation.23 | loop fusion | flops 4710400 | bytes 9421828 | tf_op jit(solution)/shard_map/jit(dynamic_update_index_in_dim)/dynamic_update_slice | solution.py:922
  445.8 3.7 bitcast_dynamic-update-slice_fusion
  449.5 7.0 %all-to-all-done.2 = bf16[16,128,768]{2,1,0:T(8,128)(2,1)} async-done(((bf16[16,128,768]{2,1,0:T(8,128)(2,1)}), bf16[16,128,768]{2,1,0:T(8,128)(2,1)}, u32[]{:S(2)}, u32[]{:S(2)}) %all-to-all-start.2) | async-done | bytes 3145760 | tf_op jit(solution)/shard_map/all_to_all | solution.py:823
  456.5 2.6 gather_fusion.2
  459.1 1.9 broadcast_select_fusion
  (180 shorter events, 60.1 us)
Async XLA Ops:
  7.2 59.9 %all-gather.3.cloned.1.call-start = ((), (), s32[]{:S(2)}) async-start(), calls=%async_computation.3 | async-start | bytes 9420800 | tf_op jit(solution)/shard_map/all_gather | solution.py:794
  10.7 236.5 %all-gather.5.cloned.1.call-start = ((), (), s32[]{:S(2)}) async-start(), calls=%async_computation.4 | async-start | bytes 18841600 | tf_op jit(solution)/shard_map/all_gather | solution.py:807
  15.0 7.6 %copy-start.13 = (bf16[1,1024,768]{2,1,0:T(8,128)(2,1)S(1)}, bf16[1,1024,768]{2,1,0:T(8,128)(2,1)}, u32[]{:S(2)}) copy-start(bf16[1,1024,768]{2,1,0:T(8,128)(2,1)} %param.10) | copy-start | bytes 4718596
  15.0 9.2 %copy-start.20 = (s32[64]{0:T(128)S(1)}, s32[64]{0:T(128)}, u32[]{:S(2)}) copy-start(s32[64]{0:T(128)} %param.11) | copy-start | bytes 772
  15.0 78.2 %all-to-all-start = ((bf16[16,128,768]{2,1,0:T(8,128)(2,1)}), bf16[16,128,768]{2,1,0:T(8,128)(2,1)}, u32[]{:S(2)}, u32[]{:S(2)}) async-start(bf16[16,128,768]{2,1,0:T(8,128)(2,1)} %gather_fusion), calls=%async_computation | async-start | bytes 6291456 | tf_op jit(solution)/shard_map/all_to_all | solution.py:796
  93.2 5.8 %copy-start.1 = (bf16[3584,768]{1,0:T(8,128)(2,1)S(1)}, bf16[3584,768]{1,0:T(8,128)(2,1)}, u32[]{:S(2)}) copy-start(bf16[3584,768]{1,0:T(8,128)(2,1)} %copy-done) | copy-start | bytes 16515076
  156.7 8.5 %copy-start.15 = (bf16[1,1024,768]{2,1,0:T(8,128)(2,1)}, bf16[1,1024,768]{2,1,0:T(8,128)(2,1)S(1)}, u32[]{:S(2)}) copy-start(bf16[1,1024,768]{2,1,0:T(8,128)(2,1)S(1)} %fusion.65) | copy-start | bytes 4718596
  171.7 4.9 %collective-permute-start = (f16[2,784,768]{2,1,0:T(8,128)(2,1)}, f16[2,784,768]{2,1,0:T(8,128)(2,1)}, u32[]{:S(2)}, u32[]{:S(2)}) collective-permute-start(f16[2,784,768]{2,1,0:T(8,128)(2,1)} %select_convert_fusion), channel_id=1, source_target_pairs={{0,1},{1,0},{2,3},{3,2},{4,5},{5,4},{6,7},{7,6},{8,9},{9,8},{10,11... | collective-permute-start | bytes 7225352 | tf_op jit(solution)/shard_map/ppermute | solution.py:691
  171.7 98.5 %all-to-all-start.1 = ((bf16[16,128,768]{2,1,0:T(8,128)(2,1)}), bf16[16,128,768]{2,1,0:T(8,128)(2,1)}, u32[]{:S(2)}, u32[]{:S(2)}) async-start(bf16[16,128,768]{2,1,0:T(8,128)(2,1)} %bitcast.161), calls=%async_computation.1 | async-start | bytes 6291456 | tf_op jit(solution)/shard_map/all_to_all | solution.py:823
  183.2 60.4 %collective-permute-start.1 = (f16[784,768]{1,0:T(8,128)(2,1)S(1)}, f16[784,768]{1,0:T(8,128)(2,1)S(1)}, u32[]{:S(2)}, u32[]{:S(2)}) collective-permute-start(f16[784,768]{1,0:T(8,128)(2,1)S(1)} %select_convert_fusion.2), channel_id=1, source_target_pairs={{0,2},{1,3},{2,0},{3,1},{4,6},{5,7},{6,4},{7,5},{8,10},{9,11},{10,... | collective-permute-start | bytes 3612680 | tf_op jit(solution)/shard_map/ppermute | solution.py:691
  243.6 4.8 %copy-start.16 = (bf16[1,1024,768]{2,1,0:T(8,128)(2,1)S(1)}, bf16[1,1024,768]{2,1,0:T(8,128)(2,1)}, u32[]{:S(2)}) copy-start(bf16[1,1024,768]{2,1,0:T(8,128)(2,1)} %copy-done.15) | copy-start | bytes 4718596
  254.1 4.9 %copy-start.21 = (s32[64]{0:T(128)S(1)}, s32[64]{0:T(128)}, u32[]{:S(2)}) copy-start(s32[64]{0:T(128)} %param.11) | copy-start | bytes 772
  257.9 4.4 collective-permute-start.2
  259.8 1.9 collective-permute-start.8
  261.7 31.0 %collective-permute-start.9 = (f32[48,768]{1,0:T(8,128)S(1)}, f32[48,768]{1,0:T(8,128)S(1)}, u32[]{:S(2)}, u32[]{:S(2)}) collective-permute-start(f32[48,768]{1,0:T(8,128)S(1)} %add.407), channel_id=1, source_target_pairs={{0,2},{1,3},{2,0},{3,1},{4,6},{5,7},{6,4},{7,5},{8,10},{9,11},{10,... | collective-permute-start | bytes 442376 | tf_op jit(solution)/shard_map/ppermute | solution.py:691
  268.7 20.1 %collective-permute-start.3 = (f16[528,768]{1,0:T(8,128)(2,1)}, f16[528,768]{1,0:T(8,128)(2,1)}, u32[]{:S(2)}, u32[]{:S(2)}) collective-permute-start(f16[528,768]{1,0:T(8,128)(2,1)} %select_convert_fusion.3), channel_id=1, source_target_pairs={{0,2},{1,3},{2,0},{3,1},{4,6},{5,7},{6,4},{7,5},{8,10},{9,11},{10,... | collective-permute-start | bytes 2433032 | tf_op jit(solution)/shard_map/ppermute | solution.py:691
  272.6 24.9 %collective-permute-start.4 = (f16[400,768]{1,0:T(8,128)(2,1)}, f16[400,768]{1,0:T(8,128)(2,1)}, u32[]{:S(2)}, u32[]{:S(2)}) collective-permute-start(f16[400,768]{1,0:T(8,128)(2,1)} %select_convert_fusion.4), channel_id=1, source_target_pairs={{0,4},{4,0},{8,12},{12,8},{16,20},{20,16},{24,28},{28,24},{1,5},{5... | collective-permute-start | bytes 1843208 | tf_op jit(solution)/shard_map/ppermute | solution.py:691
  278.6 4.3 copy-start.4
  292.7 7.3 %copy-start.9 = (f32[768,768]{1,0:T(8,128)S(1)}, f32[768,768]{1,0:T(8,128)}, u32[]{:S(2)}) copy-start(f32[768,768]{1,0:T(8,128)} %multiply_add_fusion.4) | copy-start | bytes 7077892
  295.2 13.0 %collective-permute-start.10 = (f16[336,768]{1,0:T(8,128)(2,1)}, f16[336,768]{1,0:T(8,128)(2,1)}, u32[]{:S(2)}, u32[]{:S(2)}) collective-permute-start(f16[336,768]{1,0:T(8,128)(2,1)} %select_convert_fusion.5), channel_id=1, source_target_pairs={{0,4},{4,0},{8,12},{12,8},{16,20},{20,16},{24,28},{28,24},{1,5},{5... | collective-permute-start | bytes 1548296 | tf_op jit(solution)/shard_map/ppermute | solution.py:691
  302.1 9.5 %collective-permute-start.5 = (f16[112,768]{1,0:T(8,128)(2,1)S(1)}, f16[112,768]{1,0:T(8,128)(2,1)S(1)}, u32[]{:S(2)}, u32[]{:S(2)}) collective-permute-start(f16[112,768]{1,0:T(8,128)(2,1)S(1)} %get-tuple-element.140), channel_id=1, source_target_pairs={{0,8},{4,12},{8,0},{12,4},{16,24},{20,28},{24,16},{28,20},{1,9},{5... | collective-permute-start | bytes 516104 | tf_op jit(solution)/shard_map/ppermute | solution.py:691
  303.6 14.8 %collective-permute-start.6 = (f16[112,768]{1,0:T(8,128)(2,1)S(1)}, f16[112,768]{1,0:T(8,128)(2,1)S(1)}, u32[]{:S(2)}, u32[]{:S(2)}) collective-permute-start(f16[112,768]{1,0:T(8,128)(2,1)S(1)} %get-tuple-element.139), channel_id=1, source_target_pairs={{0,16},{4,20},{8,24},{12,28},{16,0},{20,4},{24,8},{28,12},{1,17},{... | collective-permute-start | bytes 516104 | tf_op jit(solution)/shard_map/ppermute | solution.py:691
  306.0 12.4 %collective-permute-start.7 = (f16[112,768]{1,0:T(8,128)(2,1)S(1)}, f16[112,768]{1,0:T(8,128)(2,1)S(1)}, u32[]{:S(2)}, u32[]{:S(2)}) collective-permute-start(f16[112,768]{1,0:T(8,128)(2,1)S(1)} %get-tuple-element.138), channel_id=1, source_target_pairs={{0,24},{4,28},{8,16},{12,20},{16,8},{20,12},{24,0},{28,4},{1,25},{... | collective-permute-start | bytes 516104 | tf_op jit(solution)/shard_map/ppermute | solution.py:691
  324.2 8.6 %collective-permute-start.11 = (f16[96,768]{1,0:T(8,128)(2,1)S(1)}, f16[96,768]{1,0:T(8,128)(2,1)S(1)}, u32[]{:S(2)}, u32[]{:S(2)}) collective-permute-start(f16[96,768]{1,0:T(8,128)(2,1)S(1)} %multiply_convert_fusion), channel_id=1, source_target_pairs={{0,24},{4,28},{8,16},{12,20},{16,8},{20,12},{24,0},{28,4},{1,25},{... | collective-permute-start | bytes 442376 | tf_op jit(solution)/shard_map/ppermute | solution.py:691
  326.5 20.2 %collective-permute-start.12 = (f16[96,768]{1,0:T(8,128)(2,1)S(1)}, f16[96,768]{1,0:T(8,128)(2,1)S(1)}, u32[]{:S(2)}, u32[]{:S(2)}) collective-permute-start(f16[96,768]{1,0:T(8,128)(2,1)S(1)} %multiply_convert_fusion), channel_id=1, source_target_pairs={{0,16},{4,20},{8,24},{12,28},{16,0},{20,4},{24,8},{28,12},{1,17},{... | collective-permute-start | bytes 442376 | tf_op jit(solution)/shard_map/ppermute | solution.py:691
  328.1 18.6 %collective-permute-start.13 = (f16[96,768]{1,0:T(8,128)(2,1)S(1)}, f16[96,768]{1,0:T(8,128)(2,1)S(1)}, u32[]{:S(2)}, u32[]{:S(2)}) collective-permute-start(f16[96,768]{1,0:T(8,128)(2,1)S(1)} %multiply_convert_fusion), channel_id=1, source_target_pairs={{0,8},{4,12},{8,0},{12,4},{16,24},{20,28},{24,16},{28,20},{1,9},{5... | collective-permute-start | bytes 442376 | tf_op jit(solution)/shard_map/ppermute | solution.py:691
  329.5 17.4 %collective-permute-start.15 = (f16[96,768]{1,0:T(8,128)(2,1)S(1)}, f16[96,768]{1,0:T(8,128)(2,1)S(1)}, u32[]{:S(2)}, u32[]{:S(2)}) collective-permute-start(f16[96,768]{1,0:T(8,128)(2,1)S(1)} %get-tuple-element.145), channel_id=1, source_target_pairs={{0,8},{4,12},{8,0},{12,4},{16,24},{20,28},{24,16},{28,20},{1,9},{5... | collective-permute-start | bytes 442376 | tf_op jit(solution)/shard_map/ppermute | solution.py:691
  331.1 18.5 %collective-permute-start.16 = (f16[96,768]{1,0:T(8,128)(2,1)S(1)}, f16[96,768]{1,0:T(8,128)(2,1)S(1)}, u32[]{:S(2)}, u32[]{:S(2)}) collective-permute-start(f16[96,768]{1,0:T(8,128)(2,1)S(1)} %get-tuple-element.144), channel_id=1, source_target_pairs={{0,16},{4,20},{8,24},{12,28},{16,0},{20,4},{24,8},{28,12},{1,17},{... | collective-permute-start | bytes 442376 | tf_op jit(solution)/shard_map/ppermute | solution.py:691
  332.8 18.6 %collective-permute-start.17 = (f16[96,768]{1,0:T(8,128)(2,1)S(1)}, f16[96,768]{1,0:T(8,128)(2,1)S(1)}, u32[]{:S(2)}, u32[]{:S(2)}) collective-permute-start(f16[96,768]{1,0:T(8,128)(2,1)S(1)} %get-tuple-element.143), channel_id=1, source_target_pairs={{0,24},{4,28},{8,16},{12,20},{16,8},{20,12},{24,0},{28,4},{1,25},{... | collective-permute-start | bytes 442376 | tf_op jit(solution)/shard_map/ppermute | solution.py:691
  348.9 16.2 %collective-permute-start.14 = (f16[384,768]{1,0:T(8,128)(2,1)S(1)}, f16[384,768]{1,0:T(8,128)(2,1)S(1)}, u32[]{:S(2)}, u32[]{:S(2)}) collective-permute-start(f16[384,768]{1,0:T(8,128)(2,1)S(1)} %pad_maximum_fusion.5), channel_id=1, source_target_pairs={{0,4},{4,0},{8,12},{12,8},{16,20},{20,16},{24,28},{28,24},{1,5},{5... | collective-permute-start | bytes 1769480 | tf_op jit(solution)/shard_map/ppermute | solution.py:691
  353.5 7.3 %collective-permute-start.19 = (f16[80,768]{1,0:T(8,128)(2,1)S(1)}, f16[80,768]{1,0:T(8,128)(2,1)S(1)}, u32[]{:S(2)}, u32[]{:S(2)}) collective-permute-start(f16[80,768]{1,0:T(8,128)(2,1)S(1)} %multiply_convert_fusion.1), channel_id=1, source_target_pairs={{0,24},{4,28},{8,16},{12,20},{16,8},{20,12},{24,0},{28,4},{1,25},{... | collective-permute-start | bytes 368648 | tf_op jit(solution)/shard_map/ppermute | solution.py:691
  355.1 9.2 %collective-permute-start.20 = (f16[80,768]{1,0:T(8,128)(2,1)S(1)}, f16[80,768]{1,0:T(8,128)(2,1)S(1)}, u32[]{:S(2)}, u32[]{:S(2)}) collective-permute-start(f16[80,768]{1,0:T(8,128)(2,1)S(1)} %multiply_convert_fusion.1), channel_id=1, source_target_pairs={{0,16},{4,20},{8,24},{12,28},{16,0},{20,4},{24,8},{28,12},{1,17},{... | collective-permute-start | bytes 368648 | tf_op jit(solution)/shard_map/ppermute | solution.py:691
  355.1 9.2 %collective-permute-start.21 = (f16[80,768]{1,0:T(8,128)(2,1)S(1)}, f16[80,768]{1,0:T(8,128)(2,1)S(1)}, u32[]{:S(2)}, u32[]{:S(2)}) collective-permute-start(f16[80,768]{1,0:T(8,128)(2,1)S(1)} %multiply_convert_fusion.1), channel_id=1, source_target_pairs={{0,8},{4,12},{8,0},{12,4},{16,24},{20,28},{24,16},{28,20},{1,9},{5... | collective-permute-start | bytes 368648 | tf_op jit(solution)/shard_map/ppermute | solution.py:691
  364.7 12.1 %collective-permute-start.22 = (f16[320,768]{1,0:T(8,128)(2,1)S(1)}, f16[320,768]{1,0:T(8,128)(2,1)S(1)}, u32[]{:S(2)}, u32[]{:S(2)}) collective-permute-start(f16[320,768]{1,0:T(8,128)(2,1)S(1)} %pad_maximum_fusion.6), channel_id=1, source_target_pairs={{0,4},{4,0},{8,12},{12,8},{16,20},{20,16},{24,28},{28,24},{1,5},{5... | collective-permute-start | bytes 1474568 | tf_op jit(solution)/shard_map/ppermute | solution.py:691
  365.7 13.6 %copy-start.17 = (f32[2]{0:T(128)S(1)}, f32[2]{0:T(128)}, u32[]{:S(2)}) copy-start(f32[2]{0:T(128)} %param.16) | copy-start | bytes 28
  365.7 19.4 %collective-permute-start.18 = (f32[768,768]{1,0:T(8,128)S(1)}, f32[768,768]{1,0:T(8,128)}, u32[]{:S(2)}, u32[]{:S(2)}) collective-permute-start(f32[768,768]{1,0:T(8,128)S(1)} %convert_multiply_fusion.2.early_ref), channel_id=1, source_target_pairs={{0,1},{1,0},{2,3},{3,2},{4,5},{5,4},{6,7},{7,6},{8,9},{9,8},{10,11... | collective-permute-start | bytes 7077896 | tf_op jit(solution)/shard_map/ppermute | solution.py:691
  378.4 6.7 %collective-permute-start.23 = (f32[512,768]{1,0:T(8,128)}, f32[512,768]{1,0:T(8,128)}, u32[]{:S(2)}, u32[]{:S(2)}) collective-permute-start(f32[512,768]{1,0:T(8,128)} %convert_multiply_fusion.3.late_ref), channel_id=1, source_target_pairs={{0,1},{1,0},{2,3},{3,2},{4,5},{5,4},{6,7},{7,6},{8,9},{9,8},{10,11... | collective-permute-start | bytes 4718600 | tf_op jit(solution)/shard_map/ppermute | solution.py:691
  379.9 76.6 %all-to-all-start.2 = ((bf16[16,128,768]{2,1,0:T(8,128)(2,1)}), bf16[16,128,768]{2,1,0:T(8,128)(2,1)}, u32[]{:S(2)}, u32[]{:S(2)}) async-start(bf16[16,128,768]{2,1,0:T(8,128)(2,1)} %bitcast.160), calls=%async_computation.2 | async-start | bytes 6291456 | tf_op jit(solution)/shard_map/all_to_all | solution.py:823
  385.1 6.2 %copy-start.6 = (f32[942080]{0:T(1024)S(1)}, f32[942080]{0:T(1024)}, u32[]{:S(2)}) copy-start(f32[942080]{0:T(1024)} %param.15) | copy-start | bytes 11304964
  391.3 7.3 %copy-start.5 = (f32[7360,128]{1,0:T(8,128)S(1)}, f32[7360,128]{1,0:T(8,128)}, u32[]{:S(2)}) copy-start(f32[7360,128]{1,0:T(8,128)} %shard_map.139) | copy-start | bytes 11304964
  391.3 7.3 %copy-start.7 = (f32[942080]{0:T(1024)S(1)}, f32[942080]{0:T(1024)}, u32[]{:S(2)}) copy-start(f32[942080]{0:T(1024)} %param.15) | copy-start | bytes 11304964
  397.1 43.5 %collective-permute-start.24 = (f16[7360,128]{1,0:T(8,128)(2,1)}, f16[7360,128]{1,0:T(8,128)(2,1)}, u32[]{:S(2)}, u32[]{:S(2)}) collective-permute-start(f16[7360,128]{1,0:T(8,128)(2,1)} %divide_convert_fusion), channel_id=1, source_target_pairs={{0,2},{1,3},{2,0},{3,1},{4,6},{5,7},{6,4},{7,5},{8,10},{9,11},{10,... | collective-permute-start | bytes 5652488 | tf_op jit(solution)/shard_map/ppermute | solution.py:691
  398.6 18.7 %collective-permute-start.25 = (f16[7360,128]{1,0:T(8,128)(2,1)}, f16[7360,128]{1,0:T(8,128)(2,1)}, u32[]{:S(2)}, u32[]{:S(2)}) collective-permute-start(f16[7360,128]{1,0:T(8,128)(2,1)} %divide_convert_fusion), channel_id=1, source_target_pairs={{0,1},{1,0},{2,3},{3,2},{4,5},{5,4},{6,7},{7,6},{8,9},{9,8},{10,11... | collective-permute-start | bytes 5652488 | tf_op jit(solution)/shard_map/ppermute | solution.py:691
  398.6 13.5 %slice-start = ((s8[15073280]{0:T(1024)(128)(4,1)}), s8[4194304]{0:T(1024)(128)(4,1)S(1)}, s32[]{:S(2)}) async-start(s8[15073280]{0:T(1024)(128)(4,1)} %bitcast.146), calls=%async_computation.5 | async-start | bytes 8388608
  398.6 13.5 %slice-start.1 = ((s8[15073280]{0:T(1024)(128)(4,1)}), s8[4194304]{0:T(1024)(128)(4,1)S(1)}, s32[]{:S(2)}) async-start(s8[15073280]{0:T(1024)(128)(4,1)} %bitcast.146), calls=%async_computation.6 | async-start | bytes 8388608
  398.6 13.5 %slice-start.2 = ((s8[15073280]{0:T(1024)(128)(4,1)}), s8[2490368]{0:T(1024)(128)(4,1)S(1)}, s32[]{:S(2)}) async-start(s8[15073280]{0:T(1024)(128)(4,1)} %bitcast.146), calls=%async_computation.7 | async-start | bytes 4980736
  405.6 6.6 %slice-start.3 = ((s8[15073280]{0:T(1024)(128)(4,1)}), s8[4194304]{0:T(1024)(128)(4,1)S(1)}, s32[]{:S(2)}) async-start(s8[15073280]{0:T(1024)(128)(4,1)} %bitcast.146), calls=%async_computation.8 | async-start | bytes 8388608
  440.6 5.2 %collective-permute-start.26 = (f16[7360,128]{1,0:T(8,128)(2,1)}, f16[7360,128]{1,0:T(8,128)(2,1)S(1)}, u32[]{:S(2)}, u32[]{:S(2)}) collective-permute-start(f16[7360,128]{1,0:T(8,128)(2,1)} %collective-permute-done.24), channel_id=1, source_target_pairs={{0,1},{1,0},{2,3},{3,2},{4,5},{5,4},{6,7},{7,6},{8,9},{9,8},{10,11... | collective-permute-start | bytes 5652488 | tf_op jit(solution)/shard_map/ppermute | solution.py:691
  (10 other events, 20.5 us)
Sparse Core Ops, SparseCore 0:
  10.9 56.1 all-gather.2
  68.6 96.2 all-gather.4

commit v7 on v6

--- a/solution.py
+++ b/solution.py
@@ -699,7 +699,7 @@
     return values.astype(F32) * jnp.exp2(-power)
 
 
-def scatter(values, power, axis, bit=1, count=2, after=None):
+def scatter(values, power, axis, bit=1, count=2, after=None, sent=None):
     place = (lax.axis_index(axis) // bit) % count
     rows = values.shape[-2] // count
     mark = min(MARK, rows)
@@ -716,6 +716,8 @@
         marked = jnp.where(last, line < mark, line >= rows)
         wire = jnp.where(marked, power, send * jnp.exp2(power)).astype(jnp.float16)
         arrived.append(swap(wire, axis, bit * offset))
+        if sent is not None:
+            sent.append(wire)
     if after is not None:
         arrived, _ = lax.optimization_barrier((arrived, after))
     last = place == count - 1
@@ -726,6 +728,27 @@
         total = total + from_wire(body, got_power)
         least = jnp.minimum(least, got_power)
     return total, least - float(count.bit_length() - 1)
+
+
+def scatter_product(left, right, power, axis, bit):
+    def product(part):
+        return lax.dot_general(
+            part, right, (((1,), (1,)), ((0,), (0,))), preferred_element_type=F32)
+
+    side = (lax.axis_index(axis) // bit) % 2
+    rows = left.shape[2] // 2
+    send = product(jnp.where(side == 1, left[:, :, : rows + LANES], left[:, :, rows - LANES :]))
+    line = lax.broadcasted_iota(jnp.int32, send.shape, 1)
+    marked = jnp.where(side == 1, line >= rows, line < LANES)
+    wire = jnp.where(marked, power, send * jnp.exp2(power)).astype(jnp.float16)
+    got = swap(wire, axis, bit)
+    left, _ = lax.optimization_barrier((left, wire))
+    keep = product(jnp.where(side == 0, left[:, :, :rows], left[:, :, rows:]))
+    keep, got = lax.optimization_barrier((keep, got))
+    got_power = lax.dynamic_slice(
+        got, (0, (1 - side) * rows, 0), (1, 1, LANES))[0, :, 0:1].astype(F32)
+    body = lax.dynamic_slice_in_dim(got, side * LANES, rows, 1)
+    return keep + from_wire(body, got_power), jnp.minimum(power, got_power) - 1.0
 
 
 def everyones(values, axis, bit=1, count=2):
@@ -841,9 +864,8 @@
     picked, pair = tie((picked, pair))
     back_out = send_back(picked)
     early_power = early_power[0:1, 0:1]
-    early = lax.dot_general(
-        pair, jnp.stack([normed, cot]), (((1,), (1,)), ((0,), (0,))), preferred_element_type=F32)
-    early, early_power = scatter(early, early_power, "zero", 1)
+    early, early_power = scatter_product(
+        pair, jnp.stack([normed, cot]), early_power, "zero", 1)
     early, early_power, dy = tie((early.reshape(INNER, D), early_power, dy))
     early, early_power = scatter(early, early_power, "zero", 2)
     window, grad_tok, small, late_power = run_backward(
@@ -853,11 +875,9 @@
         (window, small, late_power, early, early_power, whole_master))
 
     groups = data_groups()
-    late = lax.dot_general(
-        window, jnp.stack([normed, normed]), (((1,), (1,)), ((0,), (0,))),
-        preferred_element_type=F32)
     late_power = late_power[0:1, 0:1]
-    late, late_power = scatter(late, late_power, "zero", 1)
+    late, late_power = scatter_product(
+        window, jnp.stack([normed, normed]), late_power, "zero", 1)
     late = late.reshape(WINDOW, D)
     small = add_pair(small, "zero", 1)
     early, early_power, grad_tok, _ = tie((early, early_power, grad_tok, late))
@@ -874,15 +894,16 @@
     lines = small.shape[0]
     late = jnp.concatenate([late, small, jnp.zeros((WINDOW // 8 - lines, D), F32)])
     late, late_power = scatter(late, late_power, "dp", *groups[0])
+    sent = []
+    for group in groups[1:]:
+        late, late_power = scatter(late, late_power, "dp", *group, sent=sent)
     early, early_power = early_before, power_before
     for group in groups[1:]:
-        early, early_power = scatter(early, early_power, "dp", *group, after=late)
+        early, early_power = scatter(early, early_power, "dp", *group, after=sent)
     early = to_wire(early, early_power)
     for group in reversed(groups[1:]):
         early = gather(early, "dp", *group)
     early, _ = tie((early, late))
-    for group in groups[1:]:
-        late, late_power = scatter(late, late_power, "dp", *group)
     late = to_wire(late, late_power)
     early = from_wire(gather(early, "dp", *groups[0]), early_power)
     early, picked_grad, _ = tie((early, picked_grad, late))

time: 476 us -> 470 us (0.987)
  matrix products: 50.5 us -> 63.3 us
  waiting for transfers between devices: 119 us -> 108 us
  local copies, waits for them, and re-layouts: 35.8 us -> 27.9 us
    dot_general x2 -> x4, matrix products: 14.1 us -> 26.8 us  [product(): lax.dot_general(part, right, (((1,), (1,)), ((0,), (0,))), preferred_elem...]
    ppermute x27, waiting for transfers between devices: 58.5 us -> 47.8 us  [swap(): return lax.ppermute(values, axis, [(i, i ^ bit) for i in range(size)])]
    add x6 -> x4, other arithmetic: 11.9 us -> 5.36 us  [scatter(): total = total + from_wire(body, got_power)]
    unnamed x54 -> x48, local copies, waits for them, and re-layouts: 13.8 us -> 7.33 us
  transfers between devices with their start and end apart: 32 -> 32, of which waited for: 14 -> 12; matrix products, arithmetic and copies ran while one was open for 30% -> 33% of each run, Pallas kernels for 22% -> 23%
where the time goes in v7:
time: 470 us; the launch traced here: 462 us
  waiting for transfers between devices  108 us (23%)
  Pallas kernels  105 us (22%)
  other arithmetic  76.2 us (16%)
  matrix products  63.3 us (13%)
  starting transfers between devices  48.4 us (10%)
  between operations  33.2 us (7%)
  local copies, waits for them, and re-layouts  27.9 us (6%)
    pallas_call x1, Pallas kernels, run_backward(): pl.pallas_call(backward_kernel, grid=(steps,), in_specs=[pl.BlockSpec(mem...  58.1 us
    ppermute x27, waiting for transfers between devices, swap(): return lax.ppermute(values, axis, [(i, i ^ bit) for i in range(size)])  47.8 us
    all_gather x1, waiting for transfers between devices, on_device(): flat = lax.all_gather(own.astype(BF16), 'zero', axis=0, tiled=True)  40.8 us
    pallas_call x1, Pallas kernels, run_forward(): pl.pallas_call(forward_kernel, grid=(steps,), in_specs=[pl.BlockSpec(memo...  34.8 us
    ppermute x27, starting transfers between devices, swap(): return lax.ppermute(values, axis, [(i, i ^ bit) for i in range(size)])  31.6 us
    dot_general x4, matrix products, product(): lax.dot_general(part, right, (((1,), (1,)), ((0,), (0,))), preferred_elem...  26.8 us
    dot_general x3, matrix products, dot(): lax.dot_general(a, b, (((1,), (0,)), ((), ())), preferred_element_type=F32)  21.4 us
    dynamic_update_slice x4, other arithmetic, put(): return lax.dynamic_update_index_in_dim(new_master, new, shard, 0)  19.5 us
  transfers between devices with their start and end apart: 32, of which 12 were waited for; matrix products, arithmetic and copies ran while one was open for 33% of the time, Pallas kernels for 23%

profile of v7, /device:TPU:0, one launch (start us, length us, event | category | flops | bytes accessed | tf_op | source)
XLA Modules:
  0.0 461.8 jit_solution(9288855457687759571)
XLA Ops:
  7.2 3.5 bitcast_convert_fusion
  12.6 2.4 gather_fusion
  15.0 7.4 %all-to-all-start = ((bf16[16,128,768]{2,1,0:T(8,128)(2,1)}), bf16[16,128,768]{2,1,0:T(8,128)(2,1)}, u32[]{:S(2)}, u32[]{:S(2)}) async-start(bf16[16,128,768]{2,1,0:T(8,128)(2,1)} %gather_fusion), calls=%async_computation | async-start | bytes 6291456 | tf_op jit(solution)/shard_map/all_to_all | solution.py:819
  26.3 40.8 %all-gather.3.cloned.1.call-done.flat_ref = bf16[29440,128]{1,0:T(8,128)(2,1)} async-done(((bf16[7360,128]{1,0:T(8,128)(2,1)}), bf16[29440,128]{1,0:T(8,128)(2,1)}) %all-gather.3.cloned.1.call-update) | async-done | bytes 7536656 | tf_op jit(solution)/shard_map/all_gather | solution.py:817
  67.0 6.0 %shard_map.136 = (bf16[3584,768]{1,0:T(8,128)(2,1)S(1)}, bf16[1536,768]{1,0:T(8,128)(2,1)S(1)}, f32[1,768]{1,0:T(1,128)S(1)}, f32[8,1792]{1,0:T(8,128)S(1)}, f32...) custom-call(bf16[29440,128]{1,0:T(8,128)(2,1)} %all-gather.3.cloned., ...), custom_call_target="tpu_custom_call" | custom-call | flops 1000000000 | bytes 16777216 | tf_op jit(solution)/shard_map/pallas_call | solution.py:593
  73.0 2.6 copy-done
  77.0 4.6 %fusion.81.gm_ref = f32[1024,1536]{1,0:T(8,128)} fusion(bf16[1536,768]{1,0:T(8,128)(2,1)S(1)} %get-tuple-element.76, bf16[1,1024,768]{2,1,0:T(8,128)(2,1)S(1)} %copy-done.12), kind=kOutput, calls=%fused_computation.214 | convolution fusion | flops 2415919104 | bytes 10223616 | tf_op jit(solution)/shard_map/dot_general | solution.py:33
  81.6 11.6 %all-to-all-done = bf16[16,128,768]{2,1,0:T(8,128)(2,1)} async-done(((bf16[16,128,768]{2,1,0:T(8,128)(2,1)}), bf16[16,128,768]{2,1,0:T(8,128)(2,1)}, u32[]{:S(2)}, u32[]{:S(2)}) %all-to-all-start) | async-done | bytes 3145760 | tf_op jit(solution)/shard_map/all_to_all | solution.py:819
  93.3 5.8 %fusion.21 = (f32[1024]{0:T(1024)S(1)}, bf16[1024,768]{1,0:T(8,128)(2,1)S(1)}) fusion(bf16[2048,768]{1,0:T(8,128)(2,1)} %bitcast.6, s32[1024]{0:T(1024)S(1)} %fusion.61), kind=kOutput, calls=%fused_computation.51 | convolution fusion | flops 3226467328 | bytes 4726784 | tf_op jit(solution)/shard_map/dot_general | solution.py:29
  99.1 4.7 %fusion.41.z_ref = f32[1024,1536]{1,0:T(8,128)} fusion(bf16[3584,768]{1,0:T(8,128)(2,1)S(1)} %copy-done.1, bf16[1024,768]{1,0:T(8,128)(2,1)S(1)} %get-tuple-element.171.tok_ref, f32[768]{0:T(1024)S(1)} %reduce.2, f32[1024]{0:T(1024)S(1)} %add_rsqrt_fusion), kind=kOutput, calls=%fused_computation.77 | convolution fusion | flops 2419064832 | bytes 10231808 | tf_op jit(solution)/shard_map/dot_general | solution.py:33
  103.8 5.8 %fusion.35.proj_ref.before_ref = f32[1024,1816]{1,0:T(8,128)} fusion(bf16[3584,768]{1,0:T(8,128)(2,1)S(1)} %copy-done.1, bf16[1024,768]{1,0:T(8,128)(2,1)S(1)} %get-tuple-element.171.tok_ref, f32[768]{0:T(1024)S(1)} %reduce.2, f32[1024]{0:T(1024)S(1)} %add_rsqrt_fusion), kind=kOutput, calls=%fused_computation.68 | convolution fusion | flops 2859466752 | bytes 11808768 | tf_op jit(solution)/shard_map/dot_general | solution.py:33
  109.6 34.8 %shard_map.137 = (bf16[2,1024,1536]{2,1,0:T(8,128)(2,1)}, f32[1024,1536]{1,0:T(8,128)}, f32[1024,128]{1,0:T(8,128)S(1)}, f32[8,128,1536]{2,1,0:T(8,128)}, f32[1,1536]{1,0:T(1,128)S(1)}, /*index=5*/f32[8,128]{1,0:T(8,128)S(1)}) custom-call(s32[1]{0:T(128)} %dynamic_slice.148.bound_ref, f32[1]{0:T(128)S(6)} %convert.5.cot_ref, f32[1024,1536]{1,0:T(8,128)} %fusion.41.z_ref, ...), custom_call_target="tpu_custom_call" | custom-call | flops 30000001024 | bytes 41943040 | tf_op jit(solution)/shard_map/pallas_call | solution.py:221
  144.4 10.5 %fusion.19 = bf16[2048,768]{1,0:T(8,128)(2,1)} fusion(s32[2048]{0:T(1024)S(1)} %bitcast.161, bf16[1024,768]{1,0:T(8,128)(2,1)S(1)} %get-tuple-element.171.tok_ref, bf16[1536,768]{1,0:T(8,128)(2,1)} %copy-done.2, bf16[2,1024,1536]{2,1,0:T(8,128)(2,1)} %get-tuple-element.93.gz_ref), kind=kOutput, calls=%fused_computation.49 | convolution fusion | flops 5643173888 | bytes 10231808 | tf_op jit(solution)/shard_map/dot_general | solution.py:29
  156.5 9.0 %select_convert_fusion = f16[2,896,768]{2,1,0:T(8,128)(2,1)} fusion(f32[]{:T(128)} %bitcast.12, f32[]{:T(128)} %bitcast.10, pred[896]{0:T(1024)(128)(4,1)S(1)} %fusion.71, bf16[1,1024,768]{2,1,0:T(8,128)(2,1)S(1)} %fusion.87, bf16[1,1024,768]{2,1,0:T(8,128)(2,1)S(1)} %copy-done.13, bf16[2,1024,1536]{2,1,0:T(8,128)(2,1)} %get-tuple-element.93.gz_ref, ...), kind=kOutput, calls=%fused_computation.10 | convolution fusion | flops 2826108928 | bytes 13240193 | tf_op jit(solution)/shard_map/dot_general | solution.py:735
  165.6 4.7 %all-to-all-start.1 = ((bf16[16,128,768]{2,1,0:T(8,128)(2,1)}), bf16[16,128,768]{2,1,0:T(8,128)(2,1)}, u32[]{:S(2)}, u32[]{:S(2)}) async-start(bf16[16,128,768]{2,1,0:T(8,128)(2,1)} %bitcast.159), calls=%async_computation.1 | async-start | bytes 6291456 | tf_op jit(solution)/shard_map/all_to_all | solution.py:846
  170.3 6.5 %fusion.27 = f32[2,768,768]{2,1,0:T(8,128)S(1)} fusion(bf16[2,1024,1536]{2,1,0:T(8,128)(2,1)} %get-tuple-element.93.gz_ref, pred[]{:T(512)S(6)} %eq.110, bf16[1,1024,768]{2,1,0:T(8,128)(2,1)} %copy-done.14, bf16[1,1024,768]{2,1,0:T(8,128)(2,1)} %param.10), kind=kOutput, calls=%fused_computation.58 | convolution fusion | flops 2419064832 | bytes 14155777 | tf_op jit(solution)/shard_map/dot_general | solution.py:735
  178.3 2.1 multiply_add_fusion
  182.4 58.1 %shard_map.138 = (bf16[2,1024,1024]{2,1,0:T(8,128)(2,1)}, bf16[1024,768]{1,0:T(8,128)(2,1)S(1)}, f32[48,768]{1,0:T(8,128)S(1)}, f32[8,128]{1,0:T(8,128)S(1)}) custom-call(s32[1]{0:T(128)} %dynamic_slice.148.bound_ref, f32[1024,1816]{1,0:T(8,128)} %fusion.35.proj_ref.before_ref, f32[1024,1816]{1,0:T(8,128)} %fusion.35.proj_ref.before_ref, ...), custom_call_target="tpu_custom_call" | custom-call | flops 49999998976 | bytes 52428800 | tf_op jit(solution)/shard_map/pallas_call | solution.py:453
  246.4 7.0 %select_convert_fusion.1 = f16[2,640,768]{2,1,0:T(8,128)(2,1)} fusion(f32[]{:T(128)} %bitcast.21, f32[]{:T(128)} %bitcast.20, pred[640]{0:T(1024)(128)(4,1)S(1)} %fusion.73, bf16[1,1024,768]{2,1,0:T(8,128)(2,1)S(1)} %copy-done.15, bf16[2,1024,1024]{2,1,0:T(8,128)(2,1)} %get-tuple-element.108, pred[]{:T(512)S(6)} %eq.117), kind=kOutput, calls=%fused_computation.18 | convolution fusion | flops 2019098624 | bytes 8783489 | tf_op jit(solution)/shard_map/dot_general | solution.py:735
  255.4 4.3 fusion.33
  266.3 2.3 select_convert_fusion.4
  268.6 2.0 collective-permute-start.4
  270.5 4.3 gather_fusion.1
  274.8 4.4 broadcast_select_fusion.1
  279.3 5.1 %fusion.20 = bf16[2048,768]{1,0:T(8,128)(2,1)} fusion(bf16[1024,768]{1,0:T(8,128)(2,1)S(1)} %copy-done.4, s32[2048]{0:T(1024)S(1)} %bitcast.162), kind=kOutput, calls=%fused_computation.50 | convolution fusion | flops 3224895488 | bytes 4726784 | tf_op jit(solution)/shard_map/dot_general | solution.py:29
  299.9 2.4 collective-permute-start.6
  309.9 4.8 %collective-permute-done.6 = f16[112,768]{1,0:T(8,128)(2,1)S(1)} collective-permute-done((f16[112,768]{1,0:T(8,128)(2,1)S(1)}, f16[112,768]{1,0:T(8,128)(2,1)S(1)}, u32[]{:S(2)}, u32[]{:S(2)}) %collective-permute-start.6) | collective-permute-done | bytes 172064 | tf_op jit(solution)/shard_map/ppermute | solution.py:691
  316.5 3.5 collective-permute-start.15
  326.9 2.5 collective-permute-start.11
  329.4 2.0 collective-permute-start.13
  338.9 5.5 %collective-permute-done.12 = f16[96,768]{1,0:T(8,128)(2,1)S(1)} collective-permute-done((f16[96,768]{1,0:T(8,128)(2,1)S(1)}, f16[96,768]{1,0:T(8,128)(2,1)S(1)}, u32[]{:S(2)}, u32[]{:S(2)}) %collective-permute-start.12) | collective-permute-done | bytes 147488 | tf_op jit(solution)/shard_map/ppermute | solution.py:691
  348.0 3.0 collective-permute-start.21
  351.0 3.6 collective-permute-done.19
  354.7 2.8 collective-permute-done.20
  361.5 9.3 %collective-permute-done.22 = f16[320,768]{1,0:T(8,128)(2,1)S(1)} collective-permute-done((f16[320,768]{1,0:T(8,128)(2,1)S(1)}, f16[320,768]{1,0:T(8,128)(2,1)S(1)}, u32[]{:S(2)}, u32[]{:S(2)}) %collective-permute-start.22) | collective-permute-done | bytes 491552 | tf_op jit(solution)/shard_map/ppermute | solution.py:691
  373.9 4.7 %all-to-all-start.2 = ((bf16[16,128,768]{2,1,0:T(8,128)(2,1)}), bf16[16,128,768]{2,1,0:T(8,128)(2,1)}, u32[]{:S(2)}, u32[]{:S(2)}) async-start(bf16[16,128,768]{2,1,0:T(8,128)(2,1)} %bitcast.158), calls=%async_computation.2 | async-start | bytes 6291456 | tf_op jit(solution)/shard_map/all_to_all | solution.py:846
  378.6 6.1 %shard_map.139 = f32[7360,128]{1,0:T(8,128)} custom-call(s32[2]{0:T(128)S(1)} %pad_add_fusion.who_ref, f32[768,768]{1,0:T(8,128)S(1)} %convert_multiply_fusion.2.early_ref, f32[768,768]{1,0:T(8,128)} %collective-permute-done.18.early_other_ref, f32[512,768]{1,0:T(8,128)} %convert_multiply_fusion.3.late_ref, ...), custom_call_target="tpu_custom_call" | custom-call | flops 1000000 | bytes 12582912 | tf_op jit(solution)/shard_map/pallas_call | solution.py:671
  384.8 5.8 %divide_convert_fusion = f16[7360,128]{1,0:T(8,128)(2,1)} fusion(f32[7360,128]{1,0:T(8,128)} %shard_map.139, f32[]{:T(128)} %bitcast.55, f32[]{:T(128)} %bitcast.53, f32[942080]{0:T(1024)S(1)} %copy-done.6, f32[942080]{0:T(1024)} %param.14), kind=kLoop, calls=%fused_computation.41 | loop fusion | flops 11304960 | bytes 13189128 | tf_op jit(solution)/shard_map/convert_element_type | solution.py:935
  392.3 6.9 %multiply_add_fusion.1 = (f32[7360,128]{1,0:T(8,128)}, f32[7360,128]{1,0:T(8,128)}) fusion(f32[7360,128]{1,0:T(8,128)S(1)} %bitcast.152, f32[7360,128]{1,0:T(8,128)S(1)} %copy-done.5, f32[7360,128]{1,0:T(8,128)} %bitcast.153), kind=kLoop, calls=%fused_computation.39 | loop fusion | flops 6594560 | bytes 18841600 | tf_op jit(solution)/shard_map/add | solution.py:930
  399.3 6.6 %broadcast_in_dim.154 = f32[4,7360,128]{2,1,0:T(8,128)} broadcast(f32[]{:T(128)} %constant.307.clone.1), dimensions={} | broadcast | bytes 15073284 | tf_op jit(solution)/shard_map/broadcast_in_dim | solution.py:892
  405.9 5.2 %bitcast_dynamic-update-slice_fusion.3 = f32[4,7360,128]{2,1,0:T(8,128)} fusion(f32[4,7360,128]{2,1,0:T(8,128)} %broadcast_in_dim.154, s32[]{:T(128)S(6)} %select_n.591, f16[7360,128]{1,0:T(8,128)(2,1)} %divide_convert_fusion, f32[4,7360,128]{2,1,0:T(8,128)S(1)} %bitcast.146, f32[]{:T(128)} %bitcast.59, f32[]{:T(128)} %bitcast.58), kind=kLoop, calls=%fused_computation.34 | loop fusion | flops 4710400 | bytes 9421828 | tf_op jit(solution)/shard_map/jit(dynamic_update_index_in_dim)/dynamic_update_slice | solution.py:943
  411.1 5.2 %bitcast_dynamic-update-slice_fusion.2 = f32[4,7360,128]{2,1,0:T(8,128)} fusion(f32[4,7360,128]{2,1,0:T(8,128)} %bitcast_dynamic-update-slice_fusion.3, s32[]{:T(128)S(6)} %select_n.715, f16[7360,128]{1,0:T(8,128)(2,1)} %collective-permute-done.25, f32[4,7360,128]{2,1,0:T(8,128)S(1)} %bitcast.147, f32[]{:T(128)} %bitcast.59, f32[]{:T(128)} %bitcast.58), kind=kLoop, calls=%fused_computation.29 | loop fusion | flops 4710400 | bytes 9421828 | tf_op jit(solution)/shard_map/jit(dynamic_update_index_in_dim)/dynamic_update_slice | solution.py:943
  416.3 18.0 %collective-permute-done.24 = f16[7360,128]{1,0:T(8,128)(2,1)} collective-permute-done((f16[7360,128]{1,0:T(8,128)(2,1)}, f16[7360,128]{1,0:T(8,128)(2,1)}, u32[]{:S(2)}, u32[]{:S(2)}) %collective-permute-start.24) | collective-permute-done | bytes 1884192 | tf_op jit(solution)/shard_map/ppermute | solution.py:691
  434.4 5.2 %bitcast_dynamic-update-slice_fusion.1 = f32[4,7360,128]{2,1,0:T(8,128)} fusion(f32[4,7360,128]{2,1,0:T(8,128)} %bitcast_dynamic-update-slice_fusion.2, s32[]{:T(128)S(6)} %select_n.716, f16[7360,128]{1,0:T(8,128)(2,1)} %collective-permute-done.24, f32[4,7360,128]{2,1,0:T(8,128)S(1)} %bitcast.148, f32[]{:T(128)} %bitcast.59, f32[]{:T(128)} %bitcast.58), kind=kLoop, calls=%fused_computation.24 | loop fusion | flops 4710400 | bytes 9421828 | tf_op jit(solution)/shard_map/jit(dynamic_update_index_in_dim)/dynamic_update_slice | solution.py:943
  439.6 3.8 bitcast_dynamic-update-slice_fusion
  443.4 6.8 %all-to-all-done.2 = bf16[16,128,768]{2,1,0:T(8,128)(2,1)} async-done(((bf16[16,128,768]{2,1,0:T(8,128)(2,1)}), bf16[16,128,768]{2,1,0:T(8,128)(2,1)}, u32[]{:S(2)}, u32[]{:S(2)}) %all-to-all-start.2) | async-done | bytes 3145760 | tf_op jit(solution)/shard_map/all_to_all | solution.py:846
  450.2 2.6 gather_fusion.2
  452.9 1.9 broadcast_select_fusion
  (172 shorter events, 60.0 us)
Async XLA Ops:
  7.2 59.9 %all-gather.3.cloned.1.call-start = ((), (), s32[]{:S(2)}) async-start(), calls=%async_computation.3 | async-start | bytes 9420800 | tf_op jit(solution)/shard_map/all_gather | solution.py:817
  10.7 234.5 %all-gather.5.cloned.1.call-start = ((), (), s32[]{:S(2)}) async-start(), calls=%async_computation.4 | async-start | bytes 18841600 | tf_op jit(solution)/shard_map/all_gather | solution.py:830
  15.0 7.4 %copy-start.12 = (bf16[1,1024,768]{2,1,0:T(8,128)(2,1)S(1)}, bf16[1,1024,768]{2,1,0:T(8,128)(2,1)}, u32[]{:S(2)}) copy-start(bf16[1,1024,768]{2,1,0:T(8,128)(2,1)} %param.10) | copy-start | bytes 4718596
  15.0 9.2 %copy-start.19 = (s32[64]{0:T(128)S(1)}, s32[64]{0:T(128)}, u32[]{:S(2)}) copy-start(s32[64]{0:T(128)} %param.11) | copy-start | bytes 772
  15.0 78.2 %all-to-all-start = ((bf16[16,128,768]{2,1,0:T(8,128)(2,1)}), bf16[16,128,768]{2,1,0:T(8,128)(2,1)}, u32[]{:S(2)}, u32[]{:S(2)}) async-start(bf16[16,128,768]{2,1,0:T(8,128)(2,1)} %gather_fusion), calls=%async_computation | async-start | bytes 6291456 | tf_op jit(solution)/shard_map/all_to_all | solution.py:819
  93.2 5.8 %copy-start.1 = (bf16[3584,768]{1,0:T(8,128)(2,1)S(1)}, bf16[3584,768]{1,0:T(8,128)(2,1)}, u32[]{:S(2)}) copy-start(bf16[3584,768]{1,0:T(8,128)(2,1)} %copy-done) | copy-start | bytes 16515076
  156.5 9.1 %copy-start.14 = (bf16[1,1024,768]{2,1,0:T(8,128)(2,1)}, bf16[1,1024,768]{2,1,0:T(8,128)(2,1)S(1)}, u32[]{:S(2)}) copy-start(bf16[1,1024,768]{2,1,0:T(8,128)(2,1)S(1)} %fusion.87) | copy-start | bytes 4718596
  165.6 11.3 %collective-permute-start = (f16[2,896,768]{2,1,0:T(8,128)(2,1)}, f16[2,896,768]{2,1,0:T(8,128)(2,1)}, u32[]{:S(2)}, u32[]{:S(2)}) collective-permute-start(f16[2,896,768]{2,1,0:T(8,128)(2,1)} %select_convert_fusion), channel_id=1, source_target_pairs={{0,1},{1,0},{2,3},{3,2},{4,5},{5,4},{6,7},{7,6},{8,9},{9,8},{10,11... | collective-permute-start | bytes 8257544 | tf_op jit(solution)/shard_map/ppermute | solution.py:691
  165.6 100.6 %all-to-all-start.1 = ((bf16[16,128,768]{2,1,0:T(8,128)(2,1)}), bf16[16,128,768]{2,1,0:T(8,128)(2,1)}, u32[]{:S(2)}, u32[]{:S(2)}) async-start(bf16[16,128,768]{2,1,0:T(8,128)(2,1)} %bitcast.159), calls=%async_computation.1 | async-start | bytes 6291456 | tf_op jit(solution)/shard_map/all_to_all | solution.py:846
  180.8 60.8 %collective-permute-start.1 = (f16[784,768]{1,0:T(8,128)(2,1)S(1)}, f16[784,768]{1,0:T(8,128)(2,1)S(1)}, u32[]{:S(2)}, u32[]{:S(2)}) collective-permute-start(f16[784,768]{1,0:T(8,128)(2,1)S(1)} %select_convert_fusion.2), channel_id=1, source_target_pairs={{0,2},{1,3},{2,0},{3,1},{4,6},{5,7},{6,4},{7,5},{8,10},{9,11},{10,... | collective-permute-start | bytes 3612680 | tf_op jit(solution)/shard_map/ppermute | solution.py:691
  241.6 4.8 %copy-start.15 = (bf16[1,1024,768]{2,1,0:T(8,128)(2,1)S(1)}, bf16[1,1024,768]{2,1,0:T(8,128)(2,1)}, u32[]{:S(2)}) copy-start(bf16[1,1024,768]{2,1,0:T(8,128)(2,1)} %copy-done.14) | copy-start | bytes 4718596
  253.4 6.9 %collective-permute-start.2 = (f16[2,640,768]{2,1,0:T(8,128)(2,1)}, f16[2,640,768]{2,1,0:T(8,128)(2,1)}, u32[]{:S(2)}, u32[]{:S(2)}) collective-permute-start(f16[2,640,768]{2,1,0:T(8,128)(2,1)} %select_convert_fusion.1), channel_id=1, source_target_pairs={{0,1},{1,0},{2,3},{3,2},{4,5},{5,4},{6,7},{7,6},{8,9},{9,8},{10,11... | collective-permute-start | bytes 5898248 | tf_op jit(solution)/shard_map/ppermute | solution.py:691
  255.1 4.6 collective-permute-start.8
  259.7 29.1 %collective-permute-start.9 = (f32[48,768]{1,0:T(8,128)S(1)}, f32[48,768]{1,0:T(8,128)S(1)}, u32[]{:S(2)}, u32[]{:S(2)}) collective-permute-start(f32[48,768]{1,0:T(8,128)S(1)} %add.403), channel_id=1, source_target_pairs={{0,2},{1,3},{2,0},{3,1},{4,6},{5,7},{6,4},{7,5},{8,10},{9,11},{10,... | collective-permute-start | bytes 442376 | tf_op jit(solution)/shard_map/ppermute | solution.py:691
  264.7 20.2 %collective-permute-start.3 = (f16[528,768]{1,0:T(8,128)(2,1)}, f16[528,768]{1,0:T(8,128)(2,1)}, u32[]{:S(2)}, u32[]{:S(2)}) collective-permute-start(f16[528,768]{1,0:T(8,128)(2,1)} %select_convert_fusion.3), channel_id=1, source_target_pairs={{0,2},{1,3},{2,0},{3,1},{4,6},{5,7},{6,4},{7,5},{8,10},{9,11},{10,... | collective-permute-start | bytes 2433032 | tf_op jit(solution)/shard_map/ppermute | solution.py:691
  268.6 25.1 %collective-permute-start.4 = (f16[400,768]{1,0:T(8,128)(2,1)}, f16[400,768]{1,0:T(8,128)(2,1)}, u32[]{:S(2)}, u32[]{:S(2)}) collective-permute-start(f16[400,768]{1,0:T(8,128)(2,1)} %select_convert_fusion.4), channel_id=1, source_target_pairs={{0,4},{4,0},{8,12},{12,8},{16,20},{20,16},{24,28},{28,24},{1,5},{5... | collective-permute-start | bytes 1843208 | tf_op jit(solution)/shard_map/ppermute | solution.py:691
  288.8 7.6 %copy-start.9 = (f32[768,768]{1,0:T(8,128)S(1)}, f32[768,768]{1,0:T(8,128)}, u32[]{:S(2)}) copy-start(f32[768,768]{1,0:T(8,128)} %multiply_add_fusion.4) | copy-start | bytes 7077892
  291.3 13.1 %collective-permute-start.10 = (f16[336,768]{1,0:T(8,128)(2,1)}, f16[336,768]{1,0:T(8,128)(2,1)}, u32[]{:S(2)}, u32[]{:S(2)}) collective-permute-start(f16[336,768]{1,0:T(8,128)(2,1)} %select_convert_fusion.5), channel_id=1, source_target_pairs={{0,4},{4,0},{8,12},{12,8},{16,20},{20,16},{24,28},{28,24},{1,5},{5... | collective-permute-start | bytes 1548296 | tf_op jit(solution)/shard_map/ppermute | solution.py:691
  293.7 13.3 %copy-start.11 = (f32[640,768]{1,0:T(8,128)S(1)}, f32[640,768]{1,0:T(8,128)}, u32[]{:S(2)}) copy-start(f32[640,768]{1,0:T(8,128)} %copy-done.10) | copy-start | bytes 5898244
  296.4 11.7 %copy-start.17 = (pred[96]{0:T(512)(128)(4,1)S(1)}, pred[96]{0:T(512)(128)(4,1)}, u32[]{:S(2)}) copy-start(pred[96]{0:T(512)(128)(4,1)} %broadcast_select_fusion.24) | copy-start | bytes 292
  298.4 11.5 %collective-permute-start.5 = (f16[112,768]{1,0:T(8,128)(2,1)S(1)}, f16[112,768]{1,0:T(8,128)(2,1)S(1)}, u32[]{:S(2)}, u32[]{:S(2)}) collective-permute-start(f16[112,768]{1,0:T(8,128)(2,1)S(1)} %get-tuple-element.154), channel_id=1, source_target_pairs={{0,8},{4,12},{8,0},{12,4},{16,24},{20,28},{24,16},{28,20},{1,9},{5... | collective-permute-start | bytes 516104 | tf_op jit(solution)/shard_map/ppermute | solution.py:691
  299.9 14.7 %collective-permute-start.6 = (f16[112,768]{1,0:T(8,128)(2,1)S(1)}, f16[112,768]{1,0:T(8,128)(2,1)S(1)}, u32[]{:S(2)}, u32[]{:S(2)}) collective-permute-start(f16[112,768]{1,0:T(8,128)(2,1)S(1)} %get-tuple-element.153), channel_id=1, source_target_pairs={{0,16},{4,20},{8,24},{12,28},{16,0},{20,4},{24,8},{28,12},{1,17},{... | collective-permute-start | bytes 516104 | tf_op jit(solution)/shard_map/ppermute | solution.py:691
  302.3 12.3 %collective-permute-start.7 = (f16[112,768]{1,0:T(8,128)(2,1)S(1)}, f16[112,768]{1,0:T(8,128)(2,1)}, u32[]{:S(2)}, u32[]{:S(2)}) collective-permute-start(f16[112,768]{1,0:T(8,128)(2,1)S(1)} %get-tuple-element.152), channel_id=1, source_target_pairs={{0,24},{4,28},{8,16},{12,20},{16,8},{20,12},{24,0},{28,4},{1,25},{... | collective-permute-start | bytes 516104 | tf_op jit(solution)/shard_map/ppermute | solution.py:691
  308.2 21.1 %collective-permute-start.14 = (f16[96,768]{1,0:T(8,128)(2,1)S(1)}, f16[96,768]{1,0:T(8,128)(2,1)}, u32[]{:S(2)}, u32[]{:S(2)}) collective-permute-start(f16[96,768]{1,0:T(8,128)(2,1)S(1)} %get-tuple-element.159), channel_id=1, source_target_pairs={{0,8},{4,12},{8,0},{12,4},{16,24},{20,28},{24,16},{28,20},{1,9},{5... | collective-permute-start | bytes 442376 | tf_op jit(solution)/shard_map/ppermute | solution.py:691
  316.5 17.4 %collective-permute-start.15 = (f16[96,768]{1,0:T(8,128)(2,1)S(1)}, f16[96,768]{1,0:T(8,128)(2,1)}, u32[]{:S(2)}, u32[]{:S(2)}) collective-permute-start(f16[96,768]{1,0:T(8,128)(2,1)S(1)} %get-tuple-element.158), channel_id=1, source_target_pairs={{0,16},{4,20},{8,24},{12,28},{16,0},{20,4},{24,8},{28,12},{1,17},{... | collective-permute-start | bytes 442376 | tf_op jit(solution)/shard_map/ppermute | solution.py:691
  319.9 16.4 %collective-permute-start.16 = (f16[96,768]{1,0:T(8,128)(2,1)S(1)}, f16[96,768]{1,0:T(8,128)(2,1)}, u32[]{:S(2)}, u32[]{:S(2)}) collective-permute-start(f16[96,768]{1,0:T(8,128)(2,1)S(1)} %get-tuple-element.157), channel_id=1, source_target_pairs={{0,24},{4,28},{8,16},{12,20},{16,8},{20,12},{24,0},{28,4},{1,25},{... | collective-permute-start | bytes 442376 | tf_op jit(solution)/shard_map/ppermute | solution.py:691
  326.9 12.0 %collective-permute-start.11 = (f16[96,768]{1,0:T(8,128)(2,1)S(1)}, f16[96,768]{1,0:T(8,128)(2,1)S(1)}, u32[]{:S(2)}, u32[]{:S(2)}) collective-permute-start(f16[96,768]{1,0:T(8,128)(2,1)S(1)} %multiply_convert_fusion), channel_id=1, source_target_pairs={{0,24},{4,28},{8,16},{12,20},{16,8},{20,12},{24,0},{28,4},{1,25},{... | collective-permute-start | bytes 442376 | tf_op jit(solution)/shard_map/ppermute | solution.py:691
  329.3 15.1 %collective-permute-start.12 = (f16[96,768]{1,0:T(8,128)(2,1)S(1)}, f16[96,768]{1,0:T(8,128)(2,1)S(1)}, u32[]{:S(2)}, u32[]{:S(2)}) collective-permute-start(f16[96,768]{1,0:T(8,128)(2,1)S(1)} %multiply_convert_fusion), channel_id=1, source_target_pairs={{0,16},{4,20},{8,24},{12,28},{16,0},{20,4},{24,8},{28,12},{1,17},{... | collective-permute-start | bytes 442376 | tf_op jit(solution)/shard_map/ppermute | solution.py:691
  329.4 15.1 %collective-permute-start.13 = (f16[96,768]{1,0:T(8,128)(2,1)S(1)}, f16[96,768]{1,0:T(8,128)(2,1)S(1)}, u32[]{:S(2)}, u32[]{:S(2)}) collective-permute-start(f16[96,768]{1,0:T(8,128)(2,1)S(1)} %multiply_convert_fusion), channel_id=1, source_target_pairs={{0,8},{4,12},{8,0},{12,4},{16,24},{20,28},{24,16},{28,20},{1,9},{5... | collective-permute-start | bytes 442376 | tf_op jit(solution)/shard_map/ppermute | solution.py:691
  346.0 14.9 %collective-permute-start.17 = (f16[384,768]{1,0:T(8,128)(2,1)S(1)}, f16[384,768]{1,0:T(8,128)(2,1)S(1)}, u32[]{:S(2)}, u32[]{:S(2)}) collective-permute-start(f16[384,768]{1,0:T(8,128)(2,1)S(1)} %pad_maximum_fusion.11), channel_id=1, source_target_pairs={{0,4},{4,0},{8,12},{12,8},{16,20},{20,16},{24,28},{28,24},{1,5},{5... | collective-permute-start | bytes 1769480 | tf_op jit(solution)/shard_map/ppermute | solution.py:691
  346.6 8.1 %collective-permute-start.19 = (f16[80,768]{1,0:T(8,128)(2,1)S(1)}, f16[80,768]{1,0:T(8,128)(2,1)S(1)}, u32[]{:S(2)}, u32[]{:S(2)}) collective-permute-start(f16[80,768]{1,0:T(8,128)(2,1)S(1)} %multiply_convert_fusion.1), channel_id=1, source_target_pairs={{0,24},{4,28},{8,16},{12,20},{16,8},{20,12},{24,0},{28,4},{1,25},{... | collective-permute-start | bytes 368648 | tf_op jit(solution)/shard_map/ppermute | solution.py:691
  348.0 9.5 %collective-permute-start.20 = (f16[80,768]{1,0:T(8,128)(2,1)S(1)}, f16[80,768]{1,0:T(8,128)(2,1)S(1)}, u32[]{:S(2)}, u32[]{:S(2)}) collective-permute-start(f16[80,768]{1,0:T(8,128)(2,1)S(1)} %multiply_convert_fusion.1), channel_id=1, source_target_pairs={{0,16},{4,20},{8,24},{12,28},{16,0},{20,4},{24,8},{28,12},{1,17},{... | collective-permute-start | bytes 368648 | tf_op jit(solution)/shard_map/ppermute | solution.py:691
  348.0 9.5 %collective-permute-start.21 = (f16[80,768]{1,0:T(8,128)(2,1)S(1)}, f16[80,768]{1,0:T(8,128)(2,1)S(1)}, u32[]{:S(2)}, u32[]{:S(2)}) collective-permute-start(f16[80,768]{1,0:T(8,128)(2,1)S(1)} %multiply_convert_fusion.1), channel_id=1, source_target_pairs={{0,8},{4,12},{8,0},{12,4},{16,24},{20,28},{24,16},{28,20},{1,9},{5... | collective-permute-start | bytes 368648 | tf_op jit(solution)/shard_map/ppermute | solution.py:691
  357.8 12.9 %collective-permute-start.22 = (f16[320,768]{1,0:T(8,128)(2,1)S(1)}, f16[320,768]{1,0:T(8,128)(2,1)S(1)}, u32[]{:S(2)}, u32[]{:S(2)}) collective-permute-start(f16[320,768]{1,0:T(8,128)(2,1)S(1)} %pad_maximum_fusion.12), channel_id=1, source_target_pairs={{0,4},{4,0},{8,12},{12,8},{16,20},{20,16},{24,28},{28,24},{1,5},{5... | collective-permute-start | bytes 1474568 | tf_op jit(solution)/shard_map/ppermute | solution.py:691
  361.4 11.9 %copy-start.16 = (f32[2]{0:T(128)S(1)}, f32[2]{0:T(128)}, u32[]{:S(2)}) copy-start(f32[2]{0:T(128)} %param.16) | copy-start | bytes 28
  361.4 17.2 %collective-permute-start.18 = (f32[768,768]{1,0:T(8,128)S(1)}, f32[768,768]{1,0:T(8,128)}, u32[]{:S(2)}, u32[]{:S(2)}) collective-permute-start(f32[768,768]{1,0:T(8,128)S(1)} %convert_multiply_fusion.2.early_ref), channel_id=1, source_target_pairs={{0,1},{1,0},{2,3},{3,2},{4,5},{5,4},{6,7},{7,6},{8,9},{9,8},{10,11... | collective-permute-start | bytes 7077896 | tf_op jit(solution)/shard_map/ppermute | solution.py:691
  372.4 6.2 %collective-permute-start.23 = (f32[512,768]{1,0:T(8,128)}, f32[512,768]{1,0:T(8,128)}, u32[]{:S(2)}, u32[]{:S(2)}) collective-permute-start(f32[512,768]{1,0:T(8,128)} %convert_multiply_fusion.3.late_ref), channel_id=1, source_target_pairs={{0,1},{1,0},{2,3},{3,2},{4,5},{5,4},{6,7},{7,6},{8,9},{9,8},{10,11... | collective-permute-start | bytes 4718600 | tf_op jit(solution)/shard_map/ppermute | solution.py:691
  373.9 76.3 %all-to-all-start.2 = ((bf16[16,128,768]{2,1,0:T(8,128)(2,1)}), bf16[16,128,768]{2,1,0:T(8,128)(2,1)}, u32[]{:S(2)}, u32[]{:S(2)}) async-start(bf16[16,128,768]{2,1,0:T(8,128)(2,1)} %bitcast.158), calls=%async_computation.2 | async-start | bytes 6291456 | tf_op jit(solution)/shard_map/all_to_all | solution.py:846
  378.6 6.2 %copy-start.6 = (f32[942080]{0:T(1024)S(1)}, f32[942080]{0:T(1024)}, u32[]{:S(2)}) copy-start(f32[942080]{0:T(1024)} %param.15) | copy-start | bytes 11304964
  384.8 7.5 %copy-start.5 = (f32[7360,128]{1,0:T(8,128)S(1)}, f32[7360,128]{1,0:T(8,128)}, u32[]{:S(2)}) copy-start(f32[7360,128]{1,0:T(8,128)} %shard_map.139) | copy-start | bytes 11304964
  384.8 7.5 %copy-start.7 = (f32[942080]{0:T(1024)S(1)}, f32[942080]{0:T(1024)}, u32[]{:S(2)}) copy-start(f32[942080]{0:T(1024)} %param.15) | copy-start | bytes 11304964
  390.6 43.8 %collective-permute-start.24 = (f16[7360,128]{1,0:T(8,128)(2,1)}, f16[7360,128]{1,0:T(8,128)(2,1)}, u32[]{:S(2)}, u32[]{:S(2)}) collective-permute-start(f16[7360,128]{1,0:T(8,128)(2,1)} %divide_convert_fusion), channel_id=1, source_target_pairs={{0,2},{1,3},{2,0},{3,1},{4,6},{5,7},{6,4},{7,5},{8,10},{9,11},{10,... | collective-permute-start | bytes 5652488 | tf_op jit(solution)/shard_map/ppermute | solution.py:691
  392.1 19.0 %collective-permute-start.25 = (f16[7360,128]{1,0:T(8,128)(2,1)}, f16[7360,128]{1,0:T(8,128)(2,1)}, u32[]{:S(2)}, u32[]{:S(2)}) collective-permute-start(f16[7360,128]{1,0:T(8,128)(2,1)} %divide_convert_fusion), channel_id=1, source_target_pairs={{0,1},{1,0},{2,3},{3,2},{4,5},{5,4},{6,7},{7,6},{8,9},{9,8},{10,11... | collective-permute-start | bytes 5652488 | tf_op jit(solution)/shard_map/ppermute | solution.py:691
  392.3 13.5 %slice-start = ((s8[15073280]{0:T(1024)(128)(4,1)}), s8[4194304]{0:T(1024)(128)(4,1)S(1)}, s32[]{:S(2)}) async-start(s8[15073280]{0:T(1024)(128)(4,1)} %bitcast.144), calls=%async_computation.5 | async-start | bytes 8388608
  392.3 13.5 %slice-start.1 = ((s8[15073280]{0:T(1024)(128)(4,1)}), s8[4194304]{0:T(1024)(128)(4,1)S(1)}, s32[]{:S(2)}) async-start(s8[15073280]{0:T(1024)(128)(4,1)} %bitcast.144), calls=%async_computation.6 | async-start | bytes 8388608
  392.3 13.5 %slice-start.2 = ((s8[15073280]{0:T(1024)(128)(4,1)}), s8[2490368]{0:T(1024)(128)(4,1)S(1)}, s32[]{:S(2)}) async-start(s8[15073280]{0:T(1024)(128)(4,1)} %bitcast.144), calls=%async_computation.7 | async-start | bytes 4980736
  399.3 6.6 %slice-start.3 = ((s8[15073280]{0:T(1024)(128)(4,1)}), s8[4194304]{0:T(1024)(128)(4,1)S(1)}, s32[]{:S(2)}) async-start(s8[15073280]{0:T(1024)(128)(4,1)} %bitcast.144), calls=%async_computation.8 | async-start | bytes 8388608
  434.4 5.2 %collective-permute-start.26 = (f16[7360,128]{1,0:T(8,128)(2,1)}, f16[7360,128]{1,0:T(8,128)(2,1)S(1)}, u32[]{:S(2)}, u32[]{:S(2)}) collective-permute-start(f16[7360,128]{1,0:T(8,128)(2,1)} %collective-permute-done.24), channel_id=1, source_target_pairs={{0,1},{1,0},{2,3},{3,2},{4,5},{5,4},{6,7},{7,6},{8,9},{9,8},{10,11... | collective-permute-start | bytes 5652488 | tf_op jit(solution)/shard_map/ppermute | solution.py:691
  (8 other events, 15.2 us)
Sparse Core Ops, SparseCore 0:
  10.9 56.1 all-gather.2
  68.6 96.2 all-gather.4

commit v8 on v7

--- a/solution.py
+++ b/solution.py
@@ -722,8 +722,8 @@
         arrived, _ = lax.optimization_barrier((arrived, after))
     last = place == count - 1
     for got in arrived:
-        got_power = lax.dynamic_slice_in_dim(got, jnp.where(last, 0, rows), 1, dim)
-        got_power = got_power.reshape(-1, D)[0:1, 0:1].astype(F32)
+        got_power = lax.dynamic_slice_in_dim(
+            got, jnp.where(last, 0, rows), 1, dim).reshape(1, D).astype(F32)
         body = lax.dynamic_slice_in_dim(got, jnp.where(last, mark, 0), rows, dim)
         total = total + from_wire(body, got_power)
         least = jnp.minimum(least, got_power)
@@ -746,7 +746,7 @@
     keep = product(jnp.where(side == 0, left[:, :, :rows], left[:, :, rows:]))
     keep, got = lax.optimization_barrier((keep, got))
     got_power = lax.dynamic_slice(
-        got, (0, (1 - side) * rows, 0), (1, 1, LANES))[0, :, 0:1].astype(F32)
+        got, (0, (1 - side) * rows, 0), (1, 1, D))[0].astype(F32)
     body = lax.dynamic_slice_in_dim(got, side * LANES, rows, 1)
     return keep + from_wire(body, got_power), jnp.minimum(power, got_power) - 1.0
 

time: 470 us -> 457 us (0.972)
  between operations: 33.2 us -> 18 us
  other arithmetic: 76.2 us -> 67.1 us
  starting transfers between devices: 48.4 us -> 56.8 us
  waiting for transfers between devices: 108 us -> 115 us
    convert_element_type x10 -> x0, other arithmetic: 9.9 us -> none  [scatter(): got_power = got_power.reshape(-1, D)[0:1, 0:1].astype(F32)]
    ppermute x27, starting transfers between devices: 31.6 us -> 39.6 us  [swap(): return lax.ppermute(values, axis, [(i, i ^ bit) for i in range(size)])]
    ppermute x27, waiting for transfers between devices: 47.8 us -> 55.3 us  [swap(): return lax.ppermute(values, axis, [(i, i ^ bit) for i in range(size)])]
  transfers between devices with their start and end apart: 32 -> 32, of which waited for: 12 -> 12; matrix products, arithmetic and copies ran while one was open for 33% -> 31% of each run, Pallas kernels for 23% -> 23%
where the time goes in v8:
time: 457 us; the launch traced here: 449 us
  waiting for transfers between devices  115 us (25%)
  Pallas kernels  105 us (23%)
  other arithmetic  67.1 us (15%)
  matrix products  60.2 us (13%)
  starting transfers between devices  56.8 us (12%)
  local copies, waits for them, and re-layouts  26.8 us (6%)
  between operations  18 us (4%)
    pallas_call x1, Pallas kernels, run_backward(): pl.pallas_call(backward_kernel, grid=(steps,), in_specs=[pl.BlockSpec(mem...  57.9 us
    ppermute x27, waiting for transfers between devices, swap(): return lax.ppermute(values, axis, [(i, i ^ bit) for i in range(size)])  55.3 us
    all_gather x1, waiting for transfers between devices, on_device(): flat = lax.all_gather(own.astype(BF16), 'zero', axis=0, tiled=True)  40.8 us
    ppermute x27, starting transfers between devices, swap(): return lax.ppermute(values, axis, [(i, i ^ bit) for i in range(size)])  39.6 us
    pallas_call x1, Pallas kernels, run_forward(): pl.pallas_call(forward_kernel, grid=(steps,), in_specs=[pl.BlockSpec(memo...  34.8 us
    dot_general x4, matrix products, product(): lax.dot_general(part, right, (((1,), (1,)), ((0,), (0,))), preferred_elem...  23.8 us
    dot_general x3, matrix products, dot(): lax.dot_general(a, b, (((1,), (0,)), ((), ())), preferred_element_type=F32)  21.4 us
    dynamic_update_slice x4, other arithmetic, put(): return lax.dynamic_update_index_in_dim(new_master, new, shard, 0)  20 us
  transfers between devices with their start and end apart: 32, of which 12 were waited for; matrix products, arithmetic and copies ran while one was open for 31% of the time, Pallas kernels for 23%

profile of v8, /device:TPU:0, one launch (start us, length us, event | category | flops | bytes accessed | tf_op | source)
XLA Modules:
  0.0 448.7 jit_solution(14686871222688347311)
XLA Ops:
  7.2 3.5 bitcast_convert_fusion
  12.6 2.4 gather_fusion
  15.0 7.4 %all-to-all-start = ((bf16[16,128,768]{2,1,0:T(8,128)(2,1)}), bf16[16,128,768]{2,1,0:T(8,128)(2,1)}, u32[]{:S(2)}, u32[]{:S(2)}) async-start(bf16[16,128,768]{2,1,0:T(8,128)(2,1)} %gather_fusion), calls=%async_computation | async-start | bytes 6291456 | tf_op jit(solution)/shard_map/all_to_all | solution.py:819
  26.3 40.8 %all-gather.3.cloned.1.call-done.flat_ref = bf16[29440,128]{1,0:T(8,128)(2,1)} async-done(((bf16[7360,128]{1,0:T(8,128)(2,1)}), bf16[29440,128]{1,0:T(8,128)(2,1)}) %all-gather.3.cloned.1.call-update) | async-done | bytes 7536656 | tf_op jit(solution)/shard_map/all_gather | solution.py:817
  67.0 6.0 %shard_map.136 = (bf16[3584,768]{1,0:T(8,128)(2,1)S(1)}, bf16[1536,768]{1,0:T(8,128)(2,1)S(1)}, f32[1,768]{1,0:T(1,128)S(1)}, f32[8,1792]{1,0:T(8,128)S(1)}, f32...) custom-call(bf16[29440,128]{1,0:T(8,128)(2,1)} %all-gather.3.cloned., ...), custom_call_target="tpu_custom_call" | custom-call | flops 1000000000 | bytes 16777216 | tf_op jit(solution)/shard_map/pallas_call | solution.py:593
  73.0 2.6 copy-done
  77.0 4.6 %fusion.94.gm_ref = f32[1024,1536]{1,0:T(8,128)} fusion(bf16[1536,768]{1,0:T(8,128)(2,1)S(1)} %get-tuple-element.76, bf16[1,1024,768]{2,1,0:T(8,128)(2,1)S(1)} %copy-done.10), kind=kOutput, calls=%fused_computation.257 | convolution fusion | flops 2415919104 | bytes 10223616 | tf_op jit(solution)/shard_map/dot_general | solution.py:33
  81.6 11.6 %all-to-all-done = bf16[16,128,768]{2,1,0:T(8,128)(2,1)} async-done(((bf16[16,128,768]{2,1,0:T(8,128)(2,1)}), bf16[16,128,768]{2,1,0:T(8,128)(2,1)}, u32[]{:S(2)}, u32[]{:S(2)}) %all-to-all-start) | async-done | bytes 3145760 | tf_op jit(solution)/shard_map/all_to_all | solution.py:819
  93.3 5.8 %fusion.21 = (f32[1024]{0:T(1024)S(1)}, bf16[1024,768]{1,0:T(8,128)(2,1)S(1)}) fusion(bf16[2048,768]{1,0:T(8,128)(2,1)} %bitcast.6, s32[1024]{0:T(1024)S(1)} %fusion.61), kind=kOutput, calls=%fused_computation.51 | convolution fusion | flops 3226467328 | bytes 4726784 | tf_op jit(solution)/shard_map/dot_general | solution.py:29
  99.1 4.7 %fusion.41.z_ref = f32[1024,1536]{1,0:T(8,128)} fusion(bf16[3584,768]{1,0:T(8,128)(2,1)S(1)} %copy-done.1, bf16[1024,768]{1,0:T(8,128)(2,1)S(1)} %get-tuple-element.205.tok_ref, f32[768]{0:T(1024)S(1)} %reduce.2, f32[1024]{0:T(1024)S(1)} %add_rsqrt_fusion), kind=kOutput, calls=%fused_computation.77 | convolution fusion | flops 2419064832 | bytes 10231808 | tf_op jit(solution)/shard_map/dot_general | solution.py:33
  103.8 5.8 %fusion.35.proj_ref.before_ref = f32[1024,1816]{1,0:T(8,128)} fusion(bf16[3584,768]{1,0:T(8,128)(2,1)S(1)} %copy-done.1, bf16[1024,768]{1,0:T(8,128)(2,1)S(1)} %get-tuple-element.205.tok_ref, f32[768]{0:T(1024)S(1)} %reduce.2, f32[1024]{0:T(1024)S(1)} %add_rsqrt_fusion), kind=kOutput, calls=%fused_computation.68 | convolution fusion | flops 2859466752 | bytes 11808768 | tf_op jit(solution)/shard_map/dot_general | solution.py:33
  109.6 34.8 %shard_map.137 = (bf16[2,1024,1536]{2,1,0:T(8,128)(2,1)}, f32[1024,1536]{1,0:T(8,128)}, f32[1024,128]{1,0:T(8,128)S(1)}, f32[8,128,1536]{2,1,0:T(8,128)}, f32[1,1536]{1,0:T(1,128)S(1)}, /*index=5*/f32[8,128]{1,0:T(8,128)S(1)}) custom-call(s32[1]{0:T(128)} %dynamic_slice.148.bound_ref, f32[1]{0:T(128)S(6)} %convert.1.cot_ref, f32[1024,1536]{1,0:T(8,128)} %fusion.41.z_ref, ...), custom_call_target="tpu_custom_call" | custom-call | flops 30000001024 | bytes 41943040 | tf_op jit(solution)/shard_map/pallas_call | solution.py:221
  144.4 10.5 %fusion.19 = bf16[2048,768]{1,0:T(8,128)(2,1)} fusion(s32[2048]{0:T(1024)S(1)} %bitcast.134, bf16[1024,768]{1,0:T(8,128)(2,1)S(1)} %get-tuple-element.205.tok_ref, bf16[1536,768]{1,0:T(8,128)(2,1)} %copy-done.2, bf16[2,1024,1536]{2,1,0:T(8,128)(2,1)} %get-tuple-element.93.gz_ref), kind=kOutput, calls=%fused_computation.49 | convolution fusion | flops 5643173888 | bytes 10231808 | tf_op jit(solution)/shard_map/dot_general | solution.py:29
  156.5 9.0 %select_convert_fusion = f16[2,896,768]{2,1,0:T(8,128)(2,1)} fusion(f32[]{:T(128)} %bitcast.12, f32[]{:T(128)} %bitcast.10, pred[896]{0:T(1024)(128)(4,1)S(1)} %fusion.71, bf16[1,1024,768]{2,1,0:T(8,128)(2,1)S(1)} %fusion.101, bf16[1,1024,768]{2,1,0:T(8,128)(2,1)S(1)} %copy-done.11, bf16[2,1024,1536]{2,1,0:T(8,128)(2,1)} %get-tuple-element.93.gz_ref, ...), kind=kOutput, calls=%fused_computation.10 | convolution fusion | flops 2826108928 | bytes 13240193 | tf_op jit(solution)/shard_map/dot_general | solution.py:735
  167.5 4.9 %all-to-all-start.1 = ((bf16[16,128,768]{2,1,0:T(8,128)(2,1)}), bf16[16,128,768]{2,1,0:T(8,128)(2,1)}, u32[]{:S(2)}, u32[]{:S(2)}) async-start(bf16[16,128,768]{2,1,0:T(8,128)(2,1)} %bitcast.131), calls=%async_computation.1 | async-start | bytes 6291456 | tf_op jit(solution)/shard_map/all_to_all | solution.py:846
  172.3 6.6 %fusion.27 = f32[2,768,768]{2,1,0:T(8,128)S(1)} fusion(bf16[2,1024,1536]{2,1,0:T(8,128)(2,1)} %get-tuple-element.93.gz_ref, pred[]{:T(512)S(6)} %eq.110, bf16[1,1024,768]{2,1,0:T(8,128)(2,1)} %copy-done.12, bf16[1,1024,768]{2,1,0:T(8,128)(2,1)} %param.10), kind=kOutput, calls=%fused_computation.58 | convolution fusion | flops 2419064832 | bytes 14155777 | tf_op jit(solution)/shard_map/dot_general | solution.py:735
  180.3 2.1 multiply_add_fusion
  184.4 57.9 %shard_map.138 = (bf16[2,1024,1024]{2,1,0:T(8,128)(2,1)}, bf16[1024,768]{1,0:T(8,128)(2,1)S(1)}, f32[48,768]{1,0:T(8,128)S(1)}, f32[8,128]{1,0:T(8,128)S(1)}) custom-call(s32[1]{0:T(128)} %dynamic_slice.148.bound_ref, f32[1024,1816]{1,0:T(8,128)} %fusion.35.proj_ref.before_ref, f32[1024,1816]{1,0:T(8,128)} %fusion.35.proj_ref.before_ref, ...), custom_call_target="tpu_custom_call" | custom-call | flops 49999998976 | bytes 52428800 | tf_op jit(solution)/shard_map/pallas_call | solution.py:453
  246.5 6.0 %select_convert_fusion.1 = f16[2,640,768]{2,1,0:T(8,128)(2,1)S(1)} fusion(f32[]{:T(128)} %bitcast.16, f32[]{:T(128)} %bitcast.15, pred[640]{0:T(1024)(128)(4,1)S(1)} %fusion.73, bf16[1,1024,768]{2,1,0:T(8,128)(2,1)S(1)} %copy-done.13, bf16[2,1024,1024]{2,1,0:T(8,128)(2,1)} %get-tuple-element.108, pred[]{:T(512)S(6)} %eq.117), kind=kOutput, calls=%fused_computation.18 | convolution fusion | flops 2019098624 | bytes 8783489 | tf_op jit(solution)/shard_map/dot_general | solution.py:735
  256.0 2.1 fusion.33
  262.7 2.3 select_convert_fusion.4
  267.0 4.3 gather_fusion.1
  271.3 4.3 broadcast_select_fusion.1
  275.6 5.1 %fusion.20 = bf16[2048,768]{1,0:T(8,128)(2,1)} fusion(bf16[1024,768]{1,0:T(8,128)(2,1)S(1)} %copy-done.4, s32[2048]{0:T(1024)S(1)} %bitcast.135), kind=kOutput, calls=%fused_computation.50 | convolution fusion | flops 3224895488 | bytes 4726784 | tf_op jit(solution)/shard_map/dot_general | solution.py:29
  290.5 2.4 collective-permute-start.6
  293.4 4.6 %collective-permute-done.10 = f16[336,768]{1,0:T(8,128)(2,1)S(1)} collective-permute-done((f16[336,768]{1,0:T(8,128)(2,1)S(1)}, f16[336,768]{1,0:T(8,128)(2,1)S(1)}, u32[]{:S(2)}, u32[]{:S(2)}) %collective-permute-start.10) | collective-permute-done | bytes 516128 | tf_op jit(solution)/shard_map/ppermute | solution.py:691
  300.0 2.4 collective-permute-start.16
  302.4 4.3 collective-permute-done.6
  306.9 2.4 collective-permute-start.11
  309.3 13.3 %collective-permute-start.12 = (f16[96,768]{1,0:T(8,128)(2,1)S(1)}, f16[96,768]{1,0:T(8,128)(2,1)S(1)}, u32[]{:S(2)}, u32[]{:S(2)}) collective-permute-start(f16[96,768]{1,0:T(8,128)(2,1)S(1)} %multiply_convert_fusion), channel_id=1, source_target_pairs={{0,16},{4,20},{8,24},{12,28},{16,0},{20,4},{24,8},{28,12},{1,17},{... | collective-permute-start | bytes 442376 | tf_op jit(solution)/shard_map/ppermute | solution.py:691
  322.6 5.6 %collective-permute-done.15 = f16[96,768]{1,0:T(8,128)(2,1)S(1)} collective-permute-done((f16[96,768]{1,0:T(8,128)(2,1)S(1)}, f16[96,768]{1,0:T(8,128)(2,1)S(1)}, u32[]{:S(2)}, u32[]{:S(2)}) %collective-permute-start.15) | collective-permute-done | bytes 147488 | tf_op jit(solution)/shard_map/ppermute | solution.py:691
  328.3 4.4 collective-permute-done.12
  333.9 2.3 collective-permute-start.19
  338.3 3.2 collective-permute-done.19
  341.5 3.7 collective-permute-done.20
  347.6 10.0 %collective-permute-done.22 = f16[320,768]{1,0:T(8,128)(2,1)S(1)} collective-permute-done((f16[320,768]{1,0:T(8,128)(2,1)S(1)}, f16[320,768]{1,0:T(8,128)(2,1)S(1)}, u32[]{:S(2)}, u32[]{:S(2)}) %collective-permute-start.22) | collective-permute-done | bytes 491552 | tf_op jit(solution)/shard_map/ppermute | solution.py:691
  360.8 4.8 %all-to-all-start.2 = ((bf16[16,128,768]{2,1,0:T(8,128)(2,1)}), bf16[16,128,768]{2,1,0:T(8,128)(2,1)}, u32[]{:S(2)}, u32[]{:S(2)}) async-start(bf16[16,128,768]{2,1,0:T(8,128)(2,1)} %bitcast.132), calls=%async_computation.2 | async-start | bytes 6291456 | tf_op jit(solution)/shard_map/all_to_all | solution.py:846
  365.7 6.1 %shard_map.139 = f32[7360,128]{1,0:T(8,128)} custom-call(s32[2]{0:T(128)S(1)} %pad_add_fusion.who_ref, f32[768,768]{1,0:T(8,128)S(1)} %convert_multiply_fusion.2.early_ref, f32[768,768]{1,0:T(8,128)} %collective-permute-done.18.early_other_ref, f32[512,768]{1,0:T(8,128)} %convert_multiply_fusion.3.late_ref, ...), custom_call_target="tpu_custom_call" | custom-call | flops 1000000 | bytes 12582912 | tf_op jit(solution)/shard_map/pallas_call | solution.py:671
  371.8 5.8 %divide_convert_fusion = f16[7360,128]{1,0:T(8,128)(2,1)} fusion(f32[7360,128]{1,0:T(8,128)} %shard_map.139, f32[]{:T(128)} %bitcast.25, f32[]{:T(128)} %bitcast.23, f32[942080]{0:T(1024)S(1)} %copy-done.6, f32[942080]{0:T(1024)} %param.14), kind=kLoop, calls=%fused_computation.41 | loop fusion | flops 11304960 | bytes 13189128 | tf_op jit(solution)/shard_map/convert_element_type | solution.py:935
  378.5 6.9 %multiply_add_fusion.1 = (f32[7360,128]{1,0:T(8,128)}, f32[7360,128]{1,0:T(8,128)}) fusion(f32[7360,128]{1,0:T(8,128)S(1)} %bitcast.125, f32[7360,128]{1,0:T(8,128)S(1)} %copy-done.5, f32[7360,128]{1,0:T(8,128)} %bitcast.126), kind=kLoop, calls=%fused_computation.39 | loop fusion | flops 6594560 | bytes 18841600 | tf_op jit(solution)/shard_map/add | solution.py:930
  385.5 6.6 %broadcast_in_dim.151 = f32[4,7360,128]{2,1,0:T(8,128)} broadcast(f32[]{:T(128)} %constant.308.clone.1), dimensions={} | broadcast | bytes 15073284 | tf_op jit(solution)/shard_map/broadcast_in_dim | solution.py:892
  392.0 5.4 %bitcast_dynamic-update-slice_fusion.3 = f32[4,7360,128]{2,1,0:T(8,128)} fusion(f32[4,7360,128]{2,1,0:T(8,128)} %broadcast_in_dim.151, s32[]{:T(128)S(6)} %select_n.591, f16[7360,128]{1,0:T(8,128)(2,1)} %divide_convert_fusion, f32[4,7360,128]{2,1,0:T(8,128)S(1)} %bitcast.119, f32[]{:T(128)} %bitcast.29, f32[]{:T(128)} %bitcast.28), kind=kLoop, calls=%fused_computation.34 | loop fusion | flops 4710400 | bytes 9421828 | tf_op jit(solution)/shard_map/jit(dynamic_update_index_in_dim)/dynamic_update_slice | solution.py:943
  397.4 5.4 %bitcast_dynamic-update-slice_fusion.2 = f32[4,7360,128]{2,1,0:T(8,128)} fusion(f32[4,7360,128]{2,1,0:T(8,128)} %bitcast_dynamic-update-slice_fusion.3, s32[]{:T(128)S(6)} %select_n.715, f16[7360,128]{1,0:T(8,128)(2,1)} %collective-permute-done.25, f32[4,7360,128]{2,1,0:T(8,128)S(1)} %bitcast.120, f32[]{:T(128)} %bitcast.29, f32[]{:T(128)} %bitcast.28), kind=kLoop, calls=%fused_computation.29 | loop fusion | flops 4710400 | bytes 9421828 | tf_op jit(solution)/shard_map/jit(dynamic_update_index_in_dim)/dynamic_update_slice | solution.py:943
  402.8 18.5 %collective-permute-done.24 = f16[7360,128]{1,0:T(8,128)(2,1)} collective-permute-done((f16[7360,128]{1,0:T(8,128)(2,1)}, f16[7360,128]{1,0:T(8,128)(2,1)}, u32[]{:S(2)}, u32[]{:S(2)}) %collective-permute-start.24) | collective-permute-done | bytes 1884192 | tf_op jit(solution)/shard_map/ppermute | solution.py:691
  421.2 5.4 %bitcast_dynamic-update-slice_fusion.1 = f32[4,7360,128]{2,1,0:T(8,128)} fusion(f32[4,7360,128]{2,1,0:T(8,128)} %bitcast_dynamic-update-slice_fusion.2, s32[]{:T(128)S(6)} %select_n.716, f16[7360,128]{1,0:T(8,128)(2,1)} %collective-permute-done.24, f32[4,7360,128]{2,1,0:T(8,128)S(1)} %bitcast.121, f32[]{:T(128)} %bitcast.29, f32[]{:T(128)} %bitcast.28), kind=kLoop, calls=%fused_computation.24 | loop fusion | flops 4710400 | bytes 9421828 | tf_op jit(solution)/shard_map/jit(dynamic_update_index_in_dim)/dynamic_update_slice | solution.py:943
  426.6 3.9 bitcast_dynamic-update-slice_fusion
  430.5 6.6 %all-to-all-done.2 = bf16[16,128,768]{2,1,0:T(8,128)(2,1)} async-done(((bf16[16,128,768]{2,1,0:T(8,128)(2,1)}), bf16[16,128,768]{2,1,0:T(8,128)(2,1)}, u32[]{:S(2)}, u32[]{:S(2)}) %all-to-all-start.2) | async-done | bytes 3145760 | tf_op jit(solution)/shard_map/all_to_all | solution.py:846
  437.1 2.6 gather_fusion.2
  (185 shorter events, 49.1 us)
Async XLA Ops:
  7.2 59.9 %all-gather.3.cloned.1.call-start = ((), (), s32[]{:S(2)}) async-start(), calls=%async_computation.3 | async-start | bytes 9420800 | tf_op jit(solution)/shard_map/all_gather | solution.py:817
  10.7 234.4 %all-gather.5.cloned.1.call-start = ((), (), s32[]{:S(2)}) async-start(), calls=%async_computation.4 | async-start | bytes 18841600 | tf_op jit(solution)/shard_map/all_gather | solution.py:830
  15.0 7.4 %copy-start.10 = (bf16[1,1024,768]{2,1,0:T(8,128)(2,1)S(1)}, bf16[1,1024,768]{2,1,0:T(8,128)(2,1)}, u32[]{:S(2)}) copy-start(bf16[1,1024,768]{2,1,0:T(8,128)(2,1)} %param.10) | copy-start | bytes 4718596
  15.0 9.2 %copy-start.23 = (s32[64]{0:T(128)S(1)}, s32[64]{0:T(128)}, u32[]{:S(2)}) copy-start(s32[64]{0:T(128)} %param.11) | copy-start | bytes 772
  15.0 78.2 %all-to-all-start = ((bf16[16,128,768]{2,1,0:T(8,128)(2,1)}), bf16[16,128,768]{2,1,0:T(8,128)(2,1)}, u32[]{:S(2)}, u32[]{:S(2)}) async-start(bf16[16,128,768]{2,1,0:T(8,128)(2,1)} %gather_fusion), calls=%async_computation | async-start | bytes 6291456 | tf_op jit(solution)/shard_map/all_to_all | solution.py:819
  93.2 5.8 %copy-start.1 = (bf16[3584,768]{1,0:T(8,128)(2,1)S(1)}, bf16[3584,768]{1,0:T(8,128)(2,1)}, u32[]{:S(2)}) copy-start(bf16[3584,768]{1,0:T(8,128)(2,1)} %copy-done) | copy-start | bytes 16515076
  156.4 9.1 %copy-start.12 = (bf16[1,1024,768]{2,1,0:T(8,128)(2,1)}, bf16[1,1024,768]{2,1,0:T(8,128)(2,1)S(1)}, u32[]{:S(2)}) copy-start(bf16[1,1024,768]{2,1,0:T(8,128)(2,1)S(1)} %fusion.101) | copy-start | bytes 4718596
  165.5 13.4 %collective-permute-start = (f16[2,896,768]{2,1,0:T(8,128)(2,1)}, f16[2,896,768]{2,1,0:T(8,128)(2,1)}, u32[]{:S(2)}, u32[]{:S(2)}) collective-permute-start(f16[2,896,768]{2,1,0:T(8,128)(2,1)} %select_convert_fusion), channel_id=1, source_target_pairs={{0,1},{1,0},{2,3},{3,2},{4,5},{5,4},{6,7},{7,6},{8,9},{9,8},{10,11... | collective-permute-start | bytes 8257544 | tf_op jit(solution)/shard_map/ppermute | solution.py:691
  167.5 95.2 %all-to-all-start.1 = ((bf16[16,128,768]{2,1,0:T(8,128)(2,1)}), bf16[16,128,768]{2,1,0:T(8,128)(2,1)}, u32[]{:S(2)}, u32[]{:S(2)}) async-start(bf16[16,128,768]{2,1,0:T(8,128)(2,1)} %bitcast.131), calls=%async_computation.1 | async-start | bytes 6291456 | tf_op jit(solution)/shard_map/all_to_all | solution.py:846
  182.8 60.6 %collective-permute-start.1 = (f16[784,768]{1,0:T(8,128)(2,1)S(1)}, f16[784,768]{1,0:T(8,128)(2,1)S(1)}, u32[]{:S(2)}, u32[]{:S(2)}) collective-permute-start(f16[784,768]{1,0:T(8,128)(2,1)S(1)} %select_convert_fusion.2), channel_id=1, source_target_pairs={{0,2},{1,3},{2,0},{3,1},{4,6},{5,7},{6,4},{7,5},{8,10},{9,11},{10,... | collective-permute-start | bytes 3612680 | tf_op jit(solution)/shard_map/ppermute | solution.py:691
  246.5 9.1 %copy-start.24 = (s32[16]{0:T(128)S(1)}, s32[16]{0:T(128)}, u32[]{:S(2)}) copy-start(s32[16]{0:T(128)} %scatter_custom_fusion) | copy-start | bytes 196
  246.5 9.1 %copy-start.22 = (s32[16]{0:T(128)S(1)}, s32[16]{0:T(128)}, u32[]{:S(2)}) copy-start(s32[16]{0:T(128)} %dynamic_slice.161) | copy-start | bytes 196
  246.5 9.5 %copy-start.25 = (bf16[2,1024,1024]{2,1,0:T(8,128)(2,1)S(1)}, bf16[2,1024,1024]{2,1,0:T(8,128)(2,1)}, u32[]{:S(2)}) copy-start(bf16[2,1024,1024]{2,1,0:T(8,128)(2,1)} %get-tuple-element.108) | copy-start | bytes 12582916
  252.6 6.2 %collective-permute-start.2 = (f16[2,640,768]{2,1,0:T(8,128)(2,1)S(1)}, f16[2,640,768]{2,1,0:T(8,128)(2,1)S(1)}, u32[]{:S(2)}, u32[]{:S(2)}) collective-permute-start(f16[2,640,768]{2,1,0:T(8,128)(2,1)S(1)} %select_convert_fusion.1), channel_id=1, source_target_pairs={{0,1},{1,0},{2,3},{3,2},{4,5},{5,4},{6,7},{7,6},{8,9},{9,8},{10,11... | collective-permute-start | bytes 5898248 | tf_op jit(solution)/shard_map/ppermute | solution.py:691
  255.7 2.4 collective-permute-start.8
  258.2 26.3 %collective-permute-start.9 = (f32[48,768]{1,0:T(8,128)S(1)}, f32[48,768]{1,0:T(8,128)S(1)}, u32[]{:S(2)}, u32[]{:S(2)}) collective-permute-start(f32[48,768]{1,0:T(8,128)S(1)} %add.426), channel_id=1, source_target_pairs={{0,2},{1,3},{2,0},{3,1},{4,6},{5,7},{6,4},{7,5},{8,10},{9,11},{10,... | collective-permute-start | bytes 442376 | tf_op jit(solution)/shard_map/ppermute | solution.py:691
  261.2 20.5 %collective-permute-start.3 = (f16[528,768]{1,0:T(8,128)(2,1)}, f16[528,768]{1,0:T(8,128)(2,1)}, u32[]{:S(2)}, u32[]{:S(2)}) collective-permute-start(f16[528,768]{1,0:T(8,128)(2,1)} %select_convert_fusion.3), channel_id=1, source_target_pairs={{0,2},{1,3},{2,0},{3,1},{4,6},{5,7},{6,4},{7,5},{8,10},{9,11},{10,... | collective-permute-start | bytes 2433032 | tf_op jit(solution)/shard_map/ppermute | solution.py:691
  265.1 21.7 %collective-permute-start.4 = (f16[400,768]{1,0:T(8,128)(2,1)}, f16[400,768]{1,0:T(8,128)(2,1)}, u32[]{:S(2)}, u32[]{:S(2)}) collective-permute-start(f16[400,768]{1,0:T(8,128)(2,1)} %select_convert_fusion.4), channel_id=1, source_target_pairs={{0,4},{4,0},{8,12},{12,8},{16,20},{20,16},{24,28},{28,24},{1,5},{5... | collective-permute-start | bytes 1843208 | tf_op jit(solution)/shard_map/ppermute | solution.py:691
  284.9 13.1 %collective-permute-start.10 = (f16[336,768]{1,0:T(8,128)(2,1)S(1)}, f16[336,768]{1,0:T(8,128)(2,1)S(1)}, u32[]{:S(2)}, u32[]{:S(2)}) collective-permute-start(f16[336,768]{1,0:T(8,128)(2,1)S(1)} %select_convert_fusion.5), channel_id=1, source_target_pairs={{0,4},{4,0},{8,12},{12,8},{16,20},{20,16},{24,28},{28,24},{1,5},{5... | collective-permute-start | bytes 1548296 | tf_op jit(solution)/shard_map/ppermute | solution.py:691
  287.5 10.7 %copy-start.17 = (pred[96]{0:T(512)(128)(4,1)S(1)}, pred[96]{0:T(512)(128)(4,1)}, u32[]{:S(2)}) copy-start(pred[96]{0:T(512)(128)(4,1)} %broadcast_select_fusion.24) | copy-start | bytes 292
  289.0 13.4 %collective-permute-start.5 = (f16[112,768]{1,0:T(8,128)(2,1)S(1)}, f16[112,768]{1,0:T(8,128)(2,1)S(1)}, u32[]{:S(2)}, u32[]{:S(2)}) collective-permute-start(f16[112,768]{1,0:T(8,128)(2,1)S(1)} %get-tuple-element.175), channel_id=1, source_target_pairs={{0,8},{4,12},{8,0},{12,4},{16,24},{20,28},{24,16},{28,20},{1,9},{5... | collective-permute-start | bytes 516104 | tf_op jit(solution)/shard_map/ppermute | solution.py:691
  290.5 16.2 %collective-permute-start.6 = (f16[112,768]{1,0:T(8,128)(2,1)S(1)}, f16[112,768]{1,0:T(8,128)(2,1)S(1)}, u32[]{:S(2)}, u32[]{:S(2)}) collective-permute-start(f16[112,768]{1,0:T(8,128)(2,1)S(1)} %get-tuple-element.174), channel_id=1, source_target_pairs={{0,16},{4,20},{8,24},{12,28},{16,0},{20,4},{24,8},{28,12},{1,17},{... | collective-permute-start | bytes 516104 | tf_op jit(solution)/shard_map/ppermute | solution.py:691
  292.9 13.8 %collective-permute-start.7 = (f16[112,768]{1,0:T(8,128)(2,1)S(1)}, f16[112,768]{1,0:T(8,128)(2,1)S(1)}, u32[]{:S(2)}, u32[]{:S(2)}) collective-permute-start(f16[112,768]{1,0:T(8,128)(2,1)S(1)} %get-tuple-element.173), channel_id=1, source_target_pairs={{0,24},{4,28},{8,16},{12,20},{16,8},{20,12},{24,0},{28,4},{1,25},{... | collective-permute-start | bytes 516104 | tf_op jit(solution)/shard_map/ppermute | solution.py:691
  298.4 24.2 %collective-permute-start.14 = (f16[96,768]{1,0:T(8,128)(2,1)S(1)}, f16[96,768]{1,0:T(8,128)(2,1)S(1)}, u32[]{:S(2)}, u32[]{:S(2)}) collective-permute-start(f16[96,768]{1,0:T(8,128)(2,1)S(1)} %get-tuple-element.180), channel_id=1, source_target_pairs={{0,8},{4,12},{8,0},{12,4},{16,24},{20,28},{24,16},{28,20},{1,9},{5... | collective-permute-start | bytes 442376 | tf_op jit(solution)/shard_map/ppermute | solution.py:691
  300.0 22.6 %collective-permute-start.16 = (f16[96,768]{1,0:T(8,128)(2,1)S(1)}, f16[96,768]{1,0:T(8,128)(2,1)S(1)}, u32[]{:S(2)}, u32[]{:S(2)}) collective-permute-start(f16[96,768]{1,0:T(8,128)(2,1)S(1)} %get-tuple-element.178), channel_id=1, source_target_pairs={{0,24},{4,28},{8,16},{12,20},{16,8},{20,12},{24,0},{28,4},{1,25},{... | collective-permute-start | bytes 442376 | tf_op jit(solution)/shard_map/ppermute | solution.py:691
  302.4 25.8 %collective-permute-start.15 = (f16[96,768]{1,0:T(8,128)(2,1)S(1)}, f16[96,768]{1,0:T(8,128)(2,1)S(1)}, u32[]{:S(2)}, u32[]{:S(2)}) collective-permute-start(f16[96,768]{1,0:T(8,128)(2,1)S(1)} %get-tuple-element.179), channel_id=1, source_target_pairs={{0,16},{4,20},{8,24},{12,28},{16,0},{20,4},{24,8},{28,12},{1,17},{... | collective-permute-start | bytes 442376 | tf_op jit(solution)/shard_map/ppermute | solution.py:691
  306.9 21.4 %collective-permute-start.11 = (f16[96,768]{1,0:T(8,128)(2,1)S(1)}, f16[96,768]{1,0:T(8,128)(2,1)S(1)}, u32[]{:S(2)}, u32[]{:S(2)}) collective-permute-start(f16[96,768]{1,0:T(8,128)(2,1)S(1)} %multiply_convert_fusion), channel_id=1, source_target_pairs={{0,24},{4,28},{8,16},{12,20},{16,8},{20,12},{24,0},{28,4},{1,25},{... | collective-permute-start | bytes 442376 | tf_op jit(solution)/shard_map/ppermute | solution.py:691
  309.3 23.4 %collective-permute-start.12 = (f16[96,768]{1,0:T(8,128)(2,1)S(1)}, f16[96,768]{1,0:T(8,128)(2,1)S(1)}, u32[]{:S(2)}, u32[]{:S(2)}) collective-permute-start(f16[96,768]{1,0:T(8,128)(2,1)S(1)} %multiply_convert_fusion), channel_id=1, source_target_pairs={{0,16},{4,20},{8,24},{12,28},{16,0},{20,4},{24,8},{28,12},{1,17},{... | collective-permute-start | bytes 442376 | tf_op jit(solution)/shard_map/ppermute | solution.py:691
  322.6 10.1 %collective-permute-start.13 = (f16[96,768]{1,0:T(8,128)(2,1)S(1)}, f16[96,768]{1,0:T(8,128)(2,1)S(1)}, u32[]{:S(2)}, u32[]{:S(2)}) collective-permute-start(f16[96,768]{1,0:T(8,128)(2,1)S(1)} %multiply_convert_fusion), channel_id=1, source_target_pairs={{0,8},{4,12},{8,0},{12,4},{16,24},{20,28},{24,16},{28,20},{1,9},{5... | collective-permute-start | bytes 442376 | tf_op jit(solution)/shard_map/ppermute | solution.py:691
  333.2 13.8 %collective-permute-start.17 = (f16[384,768]{1,0:T(8,128)(2,1)S(1)}, f16[384,768]{1,0:T(8,128)(2,1)S(1)}, u32[]{:S(2)}, u32[]{:S(2)}) collective-permute-start(f16[384,768]{1,0:T(8,128)(2,1)S(1)} %pad_maximum_fusion.11), channel_id=1, source_target_pairs={{0,4},{4,0},{8,12},{12,8},{16,20},{20,16},{24,28},{28,24},{1,5},{5... | collective-permute-start | bytes 1769480 | tf_op jit(solution)/shard_map/ppermute | solution.py:691
  333.9 7.6 %collective-permute-start.19 = (f16[80,768]{1,0:T(8,128)(2,1)S(1)}, f16[80,768]{1,0:T(8,128)(2,1)S(1)}, u32[]{:S(2)}, u32[]{:S(2)}) collective-permute-start(f16[80,768]{1,0:T(8,128)(2,1)S(1)} %multiply_convert_fusion.1), channel_id=1, source_target_pairs={{0,24},{4,28},{8,16},{12,20},{16,8},{20,12},{24,0},{28,4},{1,25},{... | collective-permute-start | bytes 368648 | tf_op jit(solution)/shard_map/ppermute | solution.py:691
  336.2 9.0 %collective-permute-start.20 = (f16[80,768]{1,0:T(8,128)(2,1)S(1)}, f16[80,768]{1,0:T(8,128)(2,1)S(1)}, u32[]{:S(2)}, u32[]{:S(2)}) collective-permute-start(f16[80,768]{1,0:T(8,128)(2,1)S(1)} %multiply_convert_fusion.1), channel_id=1, source_target_pairs={{0,16},{4,20},{8,24},{12,28},{16,0},{20,4},{24,8},{28,12},{1,17},{... | collective-permute-start | bytes 368648 | tf_op jit(solution)/shard_map/ppermute | solution.py:691
  336.2 9.0 %collective-permute-start.21 = (f16[80,768]{1,0:T(8,128)(2,1)S(1)}, f16[80,768]{1,0:T(8,128)(2,1)S(1)}, u32[]{:S(2)}, u32[]{:S(2)}) collective-permute-start(f16[80,768]{1,0:T(8,128)(2,1)S(1)} %multiply_convert_fusion.1), channel_id=1, source_target_pairs={{0,8},{4,12},{8,0},{12,4},{16,24},{20,28},{24,16},{28,20},{1,9},{5... | collective-permute-start | bytes 368648 | tf_op jit(solution)/shard_map/ppermute | solution.py:691
  345.5 12.1 %collective-permute-start.22 = (f16[320,768]{1,0:T(8,128)(2,1)S(1)}, f16[320,768]{1,0:T(8,128)(2,1)S(1)}, u32[]{:S(2)}, u32[]{:S(2)}) collective-permute-start(f16[320,768]{1,0:T(8,128)(2,1)S(1)} %pad_maximum_fusion.12), channel_id=1, source_target_pairs={{0,4},{4,0},{8,12},{12,8},{16,20},{20,16},{24,28},{28,24},{1,5},{5... | collective-permute-start | bytes 1474568 | tf_op jit(solution)/shard_map/ppermute | solution.py:691
  347.5 12.7 %copy-start.16 = (f32[2]{0:T(128)S(1)}, f32[2]{0:T(128)}, u32[]{:S(2)}) copy-start(f32[2]{0:T(128)} %param.16) | copy-start | bytes 28
  347.5 18.2 %collective-permute-start.18 = (f32[768,768]{1,0:T(8,128)S(1)}, f32[768,768]{1,0:T(8,128)}, u32[]{:S(2)}, u32[]{:S(2)}) collective-permute-start(f32[768,768]{1,0:T(8,128)S(1)} %convert_multiply_fusion.2.early_ref), channel_id=1, source_target_pairs={{0,1},{1,0},{2,3},{3,2},{4,5},{5,4},{6,7},{7,6},{8,9},{9,8},{10,11... | collective-permute-start | bytes 7077896 | tf_op jit(solution)/shard_map/ppermute | solution.py:691
  359.2 6.4 %collective-permute-start.23 = (f32[512,768]{1,0:T(8,128)}, f32[512,768]{1,0:T(8,128)}, u32[]{:S(2)}, u32[]{:S(2)}) collective-permute-start(f32[512,768]{1,0:T(8,128)} %convert_multiply_fusion.3.late_ref), channel_id=1, source_target_pairs={{0,1},{1,0},{2,3},{3,2},{4,5},{5,4},{6,7},{7,6},{8,9},{9,8},{10,11... | collective-permute-start | bytes 4718600 | tf_op jit(solution)/shard_map/ppermute | solution.py:691
  360.8 76.3 %all-to-all-start.2 = ((bf16[16,128,768]{2,1,0:T(8,128)(2,1)}), bf16[16,128,768]{2,1,0:T(8,128)(2,1)}, u32[]{:S(2)}, u32[]{:S(2)}) async-start(bf16[16,128,768]{2,1,0:T(8,128)(2,1)} %bitcast.132), calls=%async_computation.2 | async-start | bytes 6291456 | tf_op jit(solution)/shard_map/all_to_all | solution.py:846
  365.6 6.2 %copy-start.6 = (f32[942080]{0:T(1024)S(1)}, f32[942080]{0:T(1024)}, u32[]{:S(2)}) copy-start(f32[942080]{0:T(1024)} %param.15) | copy-start | bytes 11304964
  371.8 6.7 %copy-start.5 = (f32[7360,128]{1,0:T(8,128)S(1)}, f32[7360,128]{1,0:T(8,128)}, u32[]{:S(2)}) copy-start(f32[7360,128]{1,0:T(8,128)} %shard_map.139) | copy-start | bytes 11304964
  371.8 6.7 %copy-start.7 = (f32[942080]{0:T(1024)S(1)}, f32[942080]{0:T(1024)}, u32[]{:S(2)}) copy-start(f32[942080]{0:T(1024)} %param.15) | copy-start | bytes 11304964
  377.6 43.6 %collective-permute-start.24 = (f16[7360,128]{1,0:T(8,128)(2,1)}, f16[7360,128]{1,0:T(8,128)(2,1)}, u32[]{:S(2)}, u32[]{:S(2)}) collective-permute-start(f16[7360,128]{1,0:T(8,128)(2,1)} %divide_convert_fusion), channel_id=1, source_target_pairs={{0,2},{1,3},{2,0},{3,1},{4,6},{5,7},{6,4},{7,5},{8,10},{9,11},{10,... | collective-permute-start | bytes 5652488 | tf_op jit(solution)/shard_map/ppermute | solution.py:691
  378.5 18.9 %collective-permute-start.25 = (f16[7360,128]{1,0:T(8,128)(2,1)}, f16[7360,128]{1,0:T(8,128)(2,1)}, u32[]{:S(2)}, u32[]{:S(2)}) collective-permute-start(f16[7360,128]{1,0:T(8,128)(2,1)} %divide_convert_fusion), channel_id=1, source_target_pairs={{0,1},{1,0},{2,3},{3,2},{4,5},{5,4},{6,7},{7,6},{8,9},{9,8},{10,11... | collective-permute-start | bytes 5652488 | tf_op jit(solution)/shard_map/ppermute | solution.py:691
  378.5 13.5 %slice-start = ((s8[15073280]{0:T(1024)(128)(4,1)}), s8[4194304]{0:T(1024)(128)(4,1)S(1)}, s32[]{:S(2)}) async-start(s8[15073280]{0:T(1024)(128)(4,1)} %bitcast.117), calls=%async_computation.5 | async-start | bytes 8388608
  378.5 13.5 %slice-start.1 = ((s8[15073280]{0:T(1024)(128)(4,1)}), s8[4194304]{0:T(1024)(128)(4,1)S(1)}, s32[]{:S(2)}) async-start(s8[15073280]{0:T(1024)(128)(4,1)} %bitcast.117), calls=%async_computation.6 | async-start | bytes 8388608
  378.5 13.5 %slice-start.2 = ((s8[15073280]{0:T(1024)(128)(4,1)}), s8[2490368]{0:T(1024)(128)(4,1)S(1)}, s32[]{:S(2)}) async-start(s8[15073280]{0:T(1024)(128)(4,1)} %bitcast.117), calls=%async_computation.7 | async-start | bytes 4980736
  385.5 6.6 %slice-start.3 = ((s8[15073280]{0:T(1024)(128)(4,1)}), s8[4194304]{0:T(1024)(128)(4,1)S(1)}, s32[]{:S(2)}) async-start(s8[15073280]{0:T(1024)(128)(4,1)} %bitcast.117), calls=%async_computation.8 | async-start | bytes 8388608
  421.2 5.4 %collective-permute-start.26 = (f16[7360,128]{1,0:T(8,128)(2,1)}, f16[7360,128]{1,0:T(8,128)(2,1)S(1)}, u32[]{:S(2)}, u32[]{:S(2)}) collective-permute-start(f16[7360,128]{1,0:T(8,128)(2,1)} %collective-permute-done.24), channel_id=1, source_target_pairs={{0,1},{1,0},{2,3},{3,2},{4,5},{5,4},{6,7},{7,6},{8,9},{9,8},{10,11... | collective-permute-start | bytes 5652488 | tf_op jit(solution)/shard_map/ppermute | solution.py:691
  (14 other events, 34.1 us)
Sparse Core Ops, SparseCore 0:
  10.9 56.1 all-gather.2
  68.6 96.2 all-gather.4

commit v9 on v8

--- a/solution.py
+++ b/solution.py
@@ -882,7 +882,8 @@
     small = add_pair(small, "zero", 1)
     early, early_power, grad_tok, _ = tie((early, early_power, grad_tok, late))
     late, late_power = scatter(late, late_power, "zero", 2)
-    early, early_power = scatter(early, early_power, "dp", *groups[0])
+    pairs = [(1 << k, 2) for k in range(data_devices.bit_length() - 1)]
+    early, early_power = scatter(early, early_power, "dp", *pairs[0])
     small = add_pair(small, "zero", 2, late)
     early_before, power_before = early, early_power
     picked_grad = spread(grad_tok)
@@ -898,17 +899,18 @@
     for group in groups[1:]:
         late, late_power = scatter(late, late_power, "dp", *group, sent=sent)
     early, early_power = early_before, power_before
-    for group in groups[1:]:
-        early, early_power = scatter(early, early_power, "dp", *group, after=sent)
+    for pair_of in pairs[1:]:
+        early, early_power = scatter(early, early_power, "dp", *pair_of, after=sent)
     early = to_wire(early, early_power)
-    for group in reversed(groups[1:]):
-        early = gather(early, "dp", *group)
-    early, _ = tie((early, late))
     late = to_wire(late, late_power)
-    early = from_wire(gather(early, "dp", *groups[0]), early_power)
+    for pair_of in reversed(pairs[2:]):
+        early = gather(early, "dp", *pair_of)
     early, picked_grad, _ = tie((early, picked_grad, late))
+    early = gather(early, "dp", *pairs[1])
     for group in reversed(groups[1:]):
         late = gather(late, "dp", *group)
+    early, _ = tie((early, late))
+    early = from_wire(gather(early, "dp", *pairs[0]), early_power)
     early_other = swap(early, "zero", 1)
     back_grad = send_back(picked_grad)
     wire = gather(late, "dp", *groups[0])

time: 457 us -> 471 us (1.031)
  waiting for transfers between devices: 115 us -> 145 us
  starting transfers between devices: 56.8 us -> 41.3 us
    ppermute x27 -> x25, waiting for transfers between devices: 55.3 us -> 85.7 us  [swap(): return lax.ppermute(values, axis, [(i, i ^ bit) for i in range(size)])]
    ppermute x27 -> x25, starting transfers between devices: 39.6 us -> 24.3 us  [swap(): return lax.ppermute(values, axis, [(i, i ^ bit) for i in range(size)])]
  transfers between devices with their start and end apart: 32 -> 30, of which waited for: 12 -> 14; matrix products, arithmetic and copies ran while one was open for 31% -> 30% of each run, Pallas kernels for 23% -> 23%
where the time goes in v9:
time: 471 us; the launch traced here: 463 us
  waiting for transfers between devices  145 us (31%)
  Pallas kernels  105 us (22%)
  other arithmetic  66.4 us (14%)
  matrix products  60.1 us (13%)
  starting transfers between devices  41.3 us (9%)
  local copies, waits for them, and re-layouts  26.8 us (6%)
  between operations  17.9 us (4%)
    ppermute x25, waiting for transfers between devices, swap(): return lax.ppermute(values, axis, [(i, i ^ bit) for i in range(size)])  85.7 us
    pallas_call x1, Pallas kernels, run_backward(): pl.pallas_call(backward_kernel, grid=(steps,), in_specs=[pl.BlockSpec(mem...  57.9 us
    all_gather x1, waiting for transfers between devices, on_device(): flat = lax.all_gather(own.astype(BF16), 'zero', axis=0, tiled=True)  40.8 us
    pallas_call x1, Pallas kernels, run_forward(): pl.pallas_call(forward_kernel, grid=(steps,), in_specs=[pl.BlockSpec(memo...  34.8 us
    ppermute x25, starting transfers between devices, swap(): return lax.ppermute(values, axis, [(i, i ^ bit) for i in range(size)])  24.3 us
    dot_general x4, matrix products, product(): lax.dot_general(part, right, (((1,), (1,)), ((0,), (0,))), preferred_elem...  23.6 us
    dot_general x3, matrix products, dot(): lax.dot_general(a, b, (((1,), (0,)), ((), ())), preferred_element_type=F32)  21.4 us
    dynamic_update_slice x4, other arithmetic, put(): return lax.dynamic_update_index_in_dim(new_master, new, shard, 0)  19.8 us
  transfers between devices with their start and end apart: 30, of which 14 were waited for; matrix products, arithmetic and copies ran while one was open for 30% of the time, Pallas kernels for 23%

profile of v9, /device:TPU:0, one launch (start us, length us, event | category | flops | bytes accessed | tf_op | source)
XLA Modules:
  0.0 462.7 jit_solution(384847449664429984)
XLA Ops:
  7.2 3.5 bitcast_convert_fusion
  12.6 2.4 gather_fusion
  15.0 7.4 %all-to-all-start = ((bf16[16,128,768]{2,1,0:T(8,128)(2,1)}), bf16[16,128,768]{2,1,0:T(8,128)(2,1)}, u32[]{:S(2)}, u32[]{:S(2)}) async-start(bf16[16,128,768]{2,1,0:T(8,128)(2,1)} %gather_fusion), calls=%async_computation | async-start | bytes 6291456 | tf_op jit(solution)/shard_map/all_to_all | solution.py:819
  26.3 40.8 %all-gather.3.cloned.1.call-done.flat_ref = bf16[29440,128]{1,0:T(8,128)(2,1)} async-done(((bf16[7360,128]{1,0:T(8,128)(2,1)}), bf16[29440,128]{1,0:T(8,128)(2,1)}) %all-gather.3.cloned.1.call-update) | async-done | bytes 7536656 | tf_op jit(solution)/shard_map/all_gather | solution.py:817
  67.0 6.0 %shard_map.136 = (bf16[3584,768]{1,0:T(8,128)(2,1)S(1)}, bf16[1536,768]{1,0:T(8,128)(2,1)S(1)}, f32[1,768]{1,0:T(1,128)S(1)}, f32[8,1792]{1,0:T(8,128)S(1)}, f32...) custom-call(bf16[29440,128]{1,0:T(8,128)(2,1)} %all-gather.3.cloned., ...), custom_call_target="tpu_custom_call" | custom-call | flops 1000000000 | bytes 16777216 | tf_op jit(solution)/shard_map/pallas_call | solution.py:593
  73.0 2.6 copy-done
  77.0 4.6 %fusion.93.gm_ref = f32[1024,1536]{1,0:T(8,128)} fusion(bf16[1536,768]{1,0:T(8,128)(2,1)S(1)} %get-tuple-element.75, bf16[1,1024,768]{2,1,0:T(8,128)(2,1)S(1)} %copy-done.10), kind=kOutput, calls=%fused_computation.249 | convolution fusion | flops 2415919104 | bytes 10223616 | tf_op jit(solution)/shard_map/dot_general | solution.py:33
  81.7 11.6 %all-to-all-done = bf16[16,128,768]{2,1,0:T(8,128)(2,1)} async-done(((bf16[16,128,768]{2,1,0:T(8,128)(2,1)}), bf16[16,128,768]{2,1,0:T(8,128)(2,1)}, u32[]{:S(2)}, u32[]{:S(2)}) %all-to-all-start) | async-done | bytes 3145760 | tf_op jit(solution)/shard_map/all_to_all | solution.py:819
  93.3 5.8 %fusion.21 = (f32[1024]{0:T(1024)S(1)}, bf16[1024,768]{1,0:T(8,128)(2,1)S(1)}) fusion(bf16[2048,768]{1,0:T(8,128)(2,1)} %bitcast.6, s32[1024]{0:T(1024)S(1)} %fusion.61), kind=kOutput, calls=%fused_computation.51 | convolution fusion | flops 3226467328 | bytes 4726784 | tf_op jit(solution)/shard_map/dot_general | solution.py:29
  99.1 4.7 %fusion.41.z_ref = f32[1024,1536]{1,0:T(8,128)} fusion(bf16[3584,768]{1,0:T(8,128)(2,1)S(1)} %copy-done.1, bf16[1024,768]{1,0:T(8,128)(2,1)S(1)} %get-tuple-element.200.tok_ref, f32[768]{0:T(1024)S(1)} %reduce.2, f32[1024]{0:T(1024)S(1)} %add_rsqrt_fusion), kind=kOutput, calls=%fused_computation.77 | convolution fusion | flops 2419064832 | bytes 10231808 | tf_op jit(solution)/shard_map/dot_general | solution.py:33
  103.8 5.8 %fusion.35.proj_ref.before_ref = f32[1024,1816]{1,0:T(8,128)} fusion(bf16[3584,768]{1,0:T(8,128)(2,1)S(1)} %copy-done.1, bf16[1024,768]{1,0:T(8,128)(2,1)S(1)} %get-tuple-element.200.tok_ref, f32[768]{0:T(1024)S(1)} %reduce.2, f32[1024]{0:T(1024)S(1)} %add_rsqrt_fusion), kind=kOutput, calls=%fused_computation.68 | convolution fusion | flops 2859466752 | bytes 11808768 | tf_op jit(solution)/shard_map/dot_general | solution.py:33
  109.6 34.8 %shard_map.137 = (bf16[2,1024,1536]{2,1,0:T(8,128)(2,1)}, f32[1024,1536]{1,0:T(8,128)}, f32[1024,128]{1,0:T(8,128)S(1)}, f32[8,128,1536]{2,1,0:T(8,128)}, f32[1,1536]{1,0:T(1,128)S(1)}, /*index=5*/f32[8,128]{1,0:T(8,128)S(1)}) custom-call(s32[1]{0:T(128)} %dynamic_slice.142.bound_ref, f32[1]{0:T(128)S(6)} %convert.1.cot_ref, f32[1024,1536]{1,0:T(8,128)} %fusion.41.z_ref, ...), custom_call_target="tpu_custom_call" | custom-call | flops 30000001024 | bytes 41943040 | tf_op jit(solution)/shard_map/pallas_call | solution.py:221
  144.3 10.5 %fusion.19 = bf16[2048,768]{1,0:T(8,128)(2,1)} fusion(s32[2048]{0:T(1024)S(1)} %bitcast.134, bf16[1024,768]{1,0:T(8,128)(2,1)S(1)} %get-tuple-element.200.tok_ref, bf16[1536,768]{1,0:T(8,128)(2,1)} %copy-done.2, bf16[2,1024,1536]{2,1,0:T(8,128)(2,1)} %get-tuple-element.92.gz_ref), kind=kOutput, calls=%fused_computation.49 | convolution fusion | flops 5643173888 | bytes 10231808 | tf_op jit(solution)/shard_map/dot_general | solution.py:29
  156.4 9.0 %select_convert_fusion = f16[2,896,768]{2,1,0:T(8,128)(2,1)} fusion(f32[]{:T(128)} %bitcast.12, f32[]{:T(128)} %bitcast.10, pred[896]{0:T(1024)(128)(4,1)S(1)} %fusion.71, bf16[1,1024,768]{2,1,0:T(8,128)(2,1)S(1)} %fusion.100, bf16[1,1024,768]{2,1,0:T(8,128)(2,1)S(1)} %copy-done.11, bf16[2,1024,1536]{2,1,0:T(8,128)(2,1)} %get-tuple-element.92.gz_ref, ...), kind=kOutput, calls=%fused_computation.10 | convolution fusion | flops 2826108928 | bytes 13240193 | tf_op jit(solution)/shard_map/dot_general | solution.py:735
  167.4 4.9 %all-to-all-start.1 = ((bf16[16,128,768]{2,1,0:T(8,128)(2,1)}), bf16[16,128,768]{2,1,0:T(8,128)(2,1)}, u32[]{:S(2)}, u32[]{:S(2)}) async-start(bf16[16,128,768]{2,1,0:T(8,128)(2,1)} %bitcast.131), calls=%async_computation.1 | async-start | bytes 6291456 | tf_op jit(solution)/shard_map/all_to_all | solution.py:846
  172.2 6.6 %fusion.27 = f32[2,768,768]{2,1,0:T(8,128)S(1)} fusion(bf16[2,1024,1536]{2,1,0:T(8,128)(2,1)} %get-tuple-element.92.gz_ref, pred[]{:T(512)S(6)} %eq.124, bf16[1,1024,768]{2,1,0:T(8,128)(2,1)} %copy-done.12, bf16[1,1024,768]{2,1,0:T(8,128)(2,1)} %param.10), kind=kOutput, calls=%fused_computation.58 | convolution fusion | flops 2419064832 | bytes 14155777 | tf_op jit(solution)/shard_map/dot_general | solution.py:735
  180.2 2.1 multiply_add_fusion
  184.3 57.9 %shard_map.138 = (bf16[2,1024,1024]{2,1,0:T(8,128)(2,1)}, bf16[1024,768]{1,0:T(8,128)(2,1)S(1)}, f32[48,768]{1,0:T(8,128)S(1)}, f32[8,128]{1,0:T(8,128)S(1)}) custom-call(s32[1]{0:T(128)} %dynamic_slice.142.bound_ref, f32[1024,1816]{1,0:T(8,128)} %fusion.35.proj_ref.before_ref, f32[1024,1816]{1,0:T(8,128)} %fusion.35.proj_ref.before_ref, ...), custom_call_target="tpu_custom_call" | custom-call | flops 49999998976 | bytes 52428800 | tf_op jit(solution)/shard_map/pallas_call | solution.py:453
  246.3 5.9 %select_convert_fusion.1 = f16[2,640,768]{2,1,0:T(8,128)(2,1)S(1)} fusion(f32[]{:T(128)} %bitcast.16, f32[]{:T(128)} %bitcast.15, pred[640]{0:T(1024)(128)(4,1)S(1)} %fusion.73, bf16[1,1024,768]{2,1,0:T(8,128)(2,1)S(1)} %copy-done.13, bf16[2,1024,1024]{2,1,0:T(8,128)(2,1)} %get-tuple-element.107, pred[]{:T(512)S(6)} %eq.131), kind=kOutput, calls=%fused_computation.18 | convolution fusion | flops 2019098624 | bytes 8783489 | tf_op jit(solution)/shard_map/dot_general | solution.py:735
  255.1 2.1 fusion.33
  261.8 2.3 select_convert_fusion.4
  266.1 4.3 gather_fusion.1
  270.4 4.3 broadcast_select_fusion.1
  274.7 5.1 %fusion.20 = bf16[2048,768]{1,0:T(8,128)(2,1)} fusion(bf16[1024,768]{1,0:T(8,128)(2,1)S(1)} %copy-done.4, s32[2048]{0:T(1024)S(1)} %bitcast.135), kind=kOutput, calls=%fused_computation.50 | convolution fusion | flops 3224895488 | bytes 4726784 | tf_op jit(solution)/shard_map/dot_general | solution.py:29
  289.4 7.6 %collective-permute-done.8 = f16[336,768]{1,0:T(8,128)(2,1)S(1)} collective-permute-done((f16[336,768]{1,0:T(8,128)(2,1)S(1)}, f16[336,768]{1,0:T(8,128)(2,1)S(1)}, u32[]{:S(2)}, u32[]{:S(2)}) %collective-permute-start.8) | collective-permute-done | bytes 516128 | tf_op jit(solution)/shard_map/ppermute | solution.py:691
  298.9 2.4 collective-permute-start.13
  301.6 3.0 collective-permute-start.9
  304.5 4.7 %collective-permute-done.13 = f16[96,768]{1,0:T(8,128)(2,1)S(1)} collective-permute-done((f16[96,768]{1,0:T(8,128)(2,1)S(1)}, f16[96,768]{1,0:T(8,128)(2,1)S(1)}, u32[]{:S(2)}, u32[]{:S(2)}) %collective-permute-start.13) | collective-permute-done | bytes 147488 | tf_op jit(solution)/shard_map/ppermute | solution.py:691
  309.2 8.9 %collective-permute-done.12 = f16[96,768]{1,0:T(8,128)(2,1)S(1)} collective-permute-done((f16[96,768]{1,0:T(8,128)(2,1)S(1)}, f16[96,768]{1,0:T(8,128)(2,1)S(1)}, u32[]{:S(2)}, u32[]{:S(2)}) %collective-permute-start.12) | collective-permute-done | bytes 147488 | tf_op jit(solution)/shard_map/ppermute | solution.py:691
  318.2 2.0 collective-permute-done.9
  320.5 2.7 collective-permute-start.15
  325.2 8.7 %collective-permute-done.10 = f16[96,768]{1,0:T(8,128)(2,1)S(1)} collective-permute-done((f16[96,768]{1,0:T(8,128)(2,1)S(1)}, f16[96,768]{1,0:T(8,128)(2,1)S(1)}, u32[]{:S(2)}, u32[]{:S(2)}) %collective-permute-start.10) | collective-permute-done | bytes 147488 | tf_op jit(solution)/shard_map/ppermute | solution.py:691
  334.2 5.0 %collective-permute-done.16 = f16[80,768]{1,0:T(8,128)(2,1)S(1)} collective-permute-done((f16[80,768]{1,0:T(8,128)(2,1)S(1)}, f16[80,768]{1,0:T(8,128)(2,1)S(1)}, u32[]{:S(2)}, u32[]{:S(2)}) %collective-permute-start.16) | collective-permute-done | bytes 122912 | tf_op jit(solution)/shard_map/ppermute | solution.py:691
  339.5 5.9 %collective-permute-done.14 = f16[192,768]{1,0:T(8,128)(2,1)S(1)} collective-permute-done((f16[192,768]{1,0:T(8,128)(2,1)S(1)}, f16[192,768]{1,0:T(8,128)(2,1)S(1)}, u32[]{:S(2)}, u32[]{:S(2)}) %collective-permute-start.14) | collective-permute-done | bytes 294944 | tf_op jit(solution)/shard_map/ppermute | solution.py:691
  347.8 14.2 %collective-permute-done.18 = f16[384,768]{1,0:T(8,128)(2,1)S(1)} collective-permute-done((f16[384,768]{1,0:T(8,128)(2,1)S(1)}, f16[384,768]{1,0:T(8,128)(2,1)S(1)}, u32[]{:S(2)}, u32[]{:S(2)}) %collective-permute-start.18) | collective-permute-done | bytes 589856 | tf_op jit(solution)/shard_map/ppermute | solution.py:691
  362.6 9.0 %collective-permute-done.20 = f16[320,768]{1,0:T(8,128)(2,1)S(1)} collective-permute-done((f16[320,768]{1,0:T(8,128)(2,1)S(1)}, f16[320,768]{1,0:T(8,128)(2,1)S(1)}, u32[]{:S(2)}, u32[]{:S(2)}) %collective-permute-start.20) | collective-permute-done | bytes 491552 | tf_op jit(solution)/shard_map/ppermute | solution.py:691
  374.7 4.7 %all-to-all-start.2 = ((bf16[16,128,768]{2,1,0:T(8,128)(2,1)}), bf16[16,128,768]{2,1,0:T(8,128)(2,1)}, u32[]{:S(2)}, u32[]{:S(2)}) async-start(bf16[16,128,768]{2,1,0:T(8,128)(2,1)} %bitcast.132), calls=%async_computation.2 | async-start | bytes 6291456 | tf_op jit(solution)/shard_map/all_to_all | solution.py:846
  379.5 6.1 %shard_map.139 = f32[7360,128]{1,0:T(8,128)} custom-call(s32[2]{0:T(128)S(1)} %pad_add_fusion.who_ref, f32[768,768]{1,0:T(8,128)S(1)} %convert_multiply_fusion.2.early_ref, f32[768,768]{1,0:T(8,128)} %collective-permute-done.19.early_other_ref, f32[512,768]{1,0:T(8,128)} %convert_multiply_fusion.3.late_ref, ...), custom_call_target="tpu_custom_call" | custom-call | flops 1000000 | bytes 12582912 | tf_op jit(solution)/shard_map/pallas_call | solution.py:671
  385.6 5.8 %divide_convert_fusion = f16[7360,128]{1,0:T(8,128)(2,1)} fusion(f32[7360,128]{1,0:T(8,128)} %shard_map.139, f32[]{:T(128)} %bitcast.25, f32[]{:T(128)} %bitcast.23, f32[942080]{0:T(1024)S(1)} %copy-done.6, f32[942080]{0:T(1024)} %param.14), kind=kLoop, calls=%fused_computation.41 | loop fusion | flops 11304960 | bytes 13189128 | tf_op jit(solution)/shard_map/convert_element_type | solution.py:937
  392.3 6.9 %multiply_add_fusion.1 = (f32[7360,128]{1,0:T(8,128)}, f32[7360,128]{1,0:T(8,128)}) fusion(f32[7360,128]{1,0:T(8,128)S(1)} %bitcast.125, f32[7360,128]{1,0:T(8,128)S(1)} %copy-done.5, f32[7360,128]{1,0:T(8,128)} %bitcast.126), kind=kLoop, calls=%fused_computation.39 | loop fusion | flops 6594560 | bytes 18841600 | tf_op jit(solution)/shard_map/add | solution.py:932
  399.2 6.6 %broadcast_in_dim.155 = f32[4,7360,128]{2,1,0:T(8,128)} broadcast(f32[]{:T(128)} %constant.348.clone.1), dimensions={} | broadcast | bytes 15073284 | tf_op jit(solution)/shard_map/broadcast_in_dim | solution.py:893
  405.8 5.3 %bitcast_dynamic-update-slice_fusion.3 = f32[4,7360,128]{2,1,0:T(8,128)} fusion(f32[4,7360,128]{2,1,0:T(8,128)} %broadcast_in_dim.155, s32[]{:T(128)S(6)} %select_n.591, f16[7360,128]{1,0:T(8,128)(2,1)} %divide_convert_fusion, f32[4,7360,128]{2,1,0:T(8,128)S(1)} %bitcast.119, f32[]{:T(128)} %bitcast.29, f32[]{:T(128)} %bitcast.28), kind=kLoop, calls=%fused_computation.34 | loop fusion | flops 4710400 | bytes 9421828 | tf_op jit(solution)/shard_map/jit(dynamic_update_index_in_dim)/dynamic_update_slice | solution.py:945
  411.1 5.3 %bitcast_dynamic-update-slice_fusion.2 = f32[4,7360,128]{2,1,0:T(8,128)} fusion(f32[4,7360,128]{2,1,0:T(8,128)} %bitcast_dynamic-update-slice_fusion.3, s32[]{:T(128)S(6)} %select_n.718, f16[7360,128]{1,0:T(8,128)(2,1)} %collective-permute-done.23, f32[4,7360,128]{2,1,0:T(8,128)S(1)} %bitcast.120, f32[]{:T(128)} %bitcast.29, f32[]{:T(128)} %bitcast.28), kind=kLoop, calls=%fused_computation.29 | loop fusion | flops 4710400 | bytes 9421828 | tf_op jit(solution)/shard_map/jit(dynamic_update_index_in_dim)/dynamic_update_slice | solution.py:945
  416.5 18.7 %collective-permute-done.22 = f16[7360,128]{1,0:T(8,128)(2,1)} collective-permute-done((f16[7360,128]{1,0:T(8,128)(2,1)}, f16[7360,128]{1,0:T(8,128)(2,1)}, u32[]{:S(2)}, u32[]{:S(2)}) %collective-permute-start.22) | collective-permute-done | bytes 1884192 | tf_op jit(solution)/shard_map/ppermute | solution.py:691
  435.2 5.3 %bitcast_dynamic-update-slice_fusion.1 = f32[4,7360,128]{2,1,0:T(8,128)} fusion(f32[4,7360,128]{2,1,0:T(8,128)} %bitcast_dynamic-update-slice_fusion.2, s32[]{:T(128)S(6)} %select_n.719, f16[7360,128]{1,0:T(8,128)(2,1)} %collective-permute-done.22, f32[4,7360,128]{2,1,0:T(8,128)S(1)} %bitcast.121, f32[]{:T(128)} %bitcast.29, f32[]{:T(128)} %bitcast.28), kind=kLoop, calls=%fused_computation.24 | loop fusion | flops 4710400 | bytes 9421828 | tf_op jit(solution)/shard_map/jit(dynamic_update_index_in_dim)/dynamic_update_slice | solution.py:945
  440.5 3.9 bitcast_dynamic-update-slice_fusion
  444.4 6.7 %all-to-all-done.2 = bf16[16,128,768]{2,1,0:T(8,128)(2,1)} async-done(((bf16[16,128,768]{2,1,0:T(8,128)(2,1)}), bf16[16,128,768]{2,1,0:T(8,128)(2,1)}, u32[]{:S(2)}, u32[]{:S(2)}) %all-to-all-start.2) | async-done | bytes 3145760 | tf_op jit(solution)/shard_map/all_to_all | solution.py:846
  451.1 2.6 gather_fusion.2
  (184 shorter events, 48.0 us)
Async XLA Ops:
  7.2 59.9 %all-gather.3.cloned.1.call-start = ((), (), s32[]{:S(2)}) async-start(), calls=%async_computation.3 | async-start | bytes 9420800 | tf_op jit(solution)/shard_map/all_gather | solution.py:817
  10.7 234.4 %all-gather.5.cloned.1.call-start = ((), (), s32[]{:S(2)}) async-start(), calls=%async_computation.4 | async-start | bytes 18841600 | tf_op jit(solution)/shard_map/all_gather | solution.py:830
  15.0 7.4 %copy-start.10 = (bf16[1,1024,768]{2,1,0:T(8,128)(2,1)S(1)}, bf16[1,1024,768]{2,1,0:T(8,128)(2,1)}, u32[]{:S(2)}) copy-start(bf16[1,1024,768]{2,1,0:T(8,128)(2,1)} %param.10) | copy-start | bytes 4718596
  15.0 9.2 %copy-start.22 = (s32[64]{0:T(128)S(1)}, s32[64]{0:T(128)}, u32[]{:S(2)}) copy-start(s32[64]{0:T(128)} %param.11) | copy-start | bytes 772
  15.0 78.2 %all-to-all-start = ((bf16[16,128,768]{2,1,0:T(8,128)(2,1)}), bf16[16,128,768]{2,1,0:T(8,128)(2,1)}, u32[]{:S(2)}, u32[]{:S(2)}) async-start(bf16[16,128,768]{2,1,0:T(8,128)(2,1)} %gather_fusion), calls=%async_computation | async-start | bytes 6291456 | tf_op jit(solution)/shard_map/all_to_all | solution.py:819
  93.2 5.8 %copy-start.1 = (bf16[3584,768]{1,0:T(8,128)(2,1)S(1)}, bf16[3584,768]{1,0:T(8,128)(2,1)}, u32[]{:S(2)}) copy-start(bf16[3584,768]{1,0:T(8,128)(2,1)} %copy-done) | copy-start | bytes 16515076
  156.4 9.1 %copy-start.12 = (bf16[1,1024,768]{2,1,0:T(8,128)(2,1)}, bf16[1,1024,768]{2,1,0:T(8,128)(2,1)S(1)}, u32[]{:S(2)}) copy-start(bf16[1,1024,768]{2,1,0:T(8,128)(2,1)S(1)} %fusion.100) | copy-start | bytes 4718596
  165.5 13.3 %collective-permute-start = (f16[2,896,768]{2,1,0:T(8,128)(2,1)}, f16[2,896,768]{2,1,0:T(8,128)(2,1)}, u32[]{:S(2)}, u32[]{:S(2)}) collective-permute-start(f16[2,896,768]{2,1,0:T(8,128)(2,1)} %select_convert_fusion), channel_id=1, source_target_pairs={{0,1},{1,0},{2,3},{3,2},{4,5},{5,4},{6,7},{7,6},{8,9},{9,8},{10,11... | collective-permute-start | bytes 8257544 | tf_op jit(solution)/shard_map/ppermute | solution.py:691
  167.4 94.4 %all-to-all-start.1 = ((bf16[16,128,768]{2,1,0:T(8,128)(2,1)}), bf16[16,128,768]{2,1,0:T(8,128)(2,1)}, u32[]{:S(2)}, u32[]{:S(2)}) async-start(bf16[16,128,768]{2,1,0:T(8,128)(2,1)} %bitcast.131), calls=%async_computation.1 | async-start | bytes 6291456 | tf_op jit(solution)/shard_map/all_to_all | solution.py:846
  182.7 60.6 %collective-permute-start.1 = (f16[784,768]{1,0:T(8,128)(2,1)S(1)}, f16[784,768]{1,0:T(8,128)(2,1)S(1)}, u32[]{:S(2)}, u32[]{:S(2)}) collective-permute-start(f16[784,768]{1,0:T(8,128)(2,1)S(1)} %select_convert_fusion.2), channel_id=1, source_target_pairs={{0,2},{1,3},{2,0},{3,1},{4,6},{5,7},{6,4},{7,5},{8,10},{9,11},{10,... | collective-permute-start | bytes 3612680 | tf_op jit(solution)/shard_map/ppermute | solution.py:691
  246.3 8.4 %copy-start.23 = (s32[16]{0:T(128)S(1)}, s32[16]{0:T(128)}, u32[]{:S(2)}) copy-start(s32[16]{0:T(128)} %scatter_custom_fusion) | copy-start | bytes 196
  246.3 8.4 %copy-start.20 = (s32[16]{0:T(128)S(1)}, s32[16]{0:T(128)}, u32[]{:S(2)}) copy-start(s32[16]{0:T(128)} %dynamic_slice.155) | copy-start | bytes 196
  246.3 8.8 %copy-start.24 = (bf16[2,1024,1024]{2,1,0:T(8,128)(2,1)S(1)}, bf16[2,1024,1024]{2,1,0:T(8,128)(2,1)}, u32[]{:S(2)}) copy-start(bf16[2,1024,1024]{2,1,0:T(8,128)(2,1)} %get-tuple-element.107) | copy-start | bytes 12582916
  252.1 5.7 %collective-permute-start.2 = (f16[2,640,768]{2,1,0:T(8,128)(2,1)S(1)}, f16[2,640,768]{2,1,0:T(8,128)(2,1)S(1)}, u32[]{:S(2)}, u32[]{:S(2)}) collective-permute-start(f16[2,640,768]{2,1,0:T(8,128)(2,1)S(1)} %select_convert_fusion.1), channel_id=1, source_target_pairs={{0,1},{1,0},{2,3},{3,2},{4,5},{5,4},{6,7},{7,6},{8,9},{9,8},{10,11... | collective-permute-start | bytes 5898248 | tf_op jit(solution)/shard_map/ppermute | solution.py:691
  254.8 2.4 collective-permute-start.6
  257.3 26.2 %collective-permute-start.7 = (f32[48,768]{1,0:T(8,128)S(1)}, f32[48,768]{1,0:T(8,128)S(1)}, u32[]{:S(2)}, u32[]{:S(2)}) collective-permute-start(f32[48,768]{1,0:T(8,128)S(1)} %add.433), channel_id=1, source_target_pairs={{0,2},{1,3},{2,0},{3,1},{4,6},{5,7},{6,4},{7,5},{8,10},{9,11},{10,... | collective-permute-start | bytes 442376 | tf_op jit(solution)/shard_map/ppermute | solution.py:691
  260.2 20.5 %collective-permute-start.3 = (f16[528,768]{1,0:T(8,128)(2,1)}, f16[528,768]{1,0:T(8,128)(2,1)}, u32[]{:S(2)}, u32[]{:S(2)}) collective-permute-start(f16[528,768]{1,0:T(8,128)(2,1)} %select_convert_fusion.3), channel_id=1, source_target_pairs={{0,2},{1,3},{2,0},{3,1},{4,6},{5,7},{6,4},{7,5},{8,10},{9,11},{10,... | collective-permute-start | bytes 2433032 | tf_op jit(solution)/shard_map/ppermute | solution.py:691
  264.1 21.5 %collective-permute-start.4 = (f16[400,768]{1,0:T(8,128)(2,1)}, f16[400,768]{1,0:T(8,128)(2,1)}, u32[]{:S(2)}, u32[]{:S(2)}) collective-permute-start(f16[400,768]{1,0:T(8,128)(2,1)} %select_convert_fusion.4), channel_id=1, source_target_pairs={{0,4},{4,0},{8,12},{12,8},{16,20},{20,16},{24,28},{28,24},{1,5},{5... | collective-permute-start | bytes 1843208 | tf_op jit(solution)/shard_map/ppermute | solution.py:691
  270.4 4.3 copy-start.4
  283.7 4.0 copy-start.16
  283.8 13.1 %collective-permute-start.8 = (f16[336,768]{1,0:T(8,128)(2,1)S(1)}, f16[336,768]{1,0:T(8,128)(2,1)S(1)}, u32[]{:S(2)}, u32[]{:S(2)}) collective-permute-start(f16[336,768]{1,0:T(8,128)(2,1)S(1)} %select_convert_fusion.5), channel_id=1, source_target_pairs={{0,4},{4,0},{8,12},{12,8},{16,20},{20,16},{24,28},{28,24},{1,5},{5... | collective-permute-start | bytes 1548296 | tf_op jit(solution)/shard_map/ppermute | solution.py:691
  287.7 13.8 %copy-start.21 = (pred[112]{0:T(512)(128)(4,1)S(1)}, pred[112]{0:T(512)(128)(4,1)}, u32[]{:S(2)}) copy-start(pred[112]{0:T(512)(128)(4,1)} %compare_select_fusion.2) | copy-start | bytes 340
  287.8 13.5 %collective-permute-start.5 = (f16[208,768]{1,0:T(8,128)(2,1)S(1)}, f16[208,768]{1,0:T(8,128)(2,1)S(1)}, u32[]{:S(2)}, u32[]{:S(2)}) collective-permute-start(f16[208,768]{1,0:T(8,128)(2,1)S(1)} %select_convert_fusion.6), channel_id=1, source_target_pairs={{0,8},{4,12},{8,0},{12,4},{16,24},{20,28},{24,16},{28,20},{1,9},{5... | collective-permute-start | bytes 958472 | tf_op jit(solution)/shard_map/ppermute | solution.py:691
  297.3 7.2 %collective-permute-start.11 = (f16[96,768]{1,0:T(8,128)(2,1)S(1)}, f16[96,768]{1,0:T(8,128)(2,1)S(1)}, u32[]{:S(2)}, u32[]{:S(2)}) collective-permute-start(f16[96,768]{1,0:T(8,128)(2,1)S(1)} %get-tuple-element.176), channel_id=1, source_target_pairs={{0,8},{4,12},{8,0},{12,4},{16,24},{20,28},{24,16},{28,20},{1,9},{5... | collective-permute-start | bytes 442376 | tf_op jit(solution)/shard_map/ppermute | solution.py:691
  298.9 10.3 %collective-permute-start.13 = (f16[96,768]{1,0:T(8,128)(2,1)S(1)}, f16[96,768]{1,0:T(8,128)(2,1)S(1)}, u32[]{:S(2)}, u32[]{:S(2)}) collective-permute-start(f16[96,768]{1,0:T(8,128)(2,1)S(1)} %get-tuple-element.174), channel_id=1, source_target_pairs={{0,24},{4,28},{8,16},{12,20},{16,8},{20,12},{24,0},{28,4},{1,25},{... | collective-permute-start | bytes 442376 | tf_op jit(solution)/shard_map/ppermute | solution.py:691
  301.3 16.8 %collective-permute-start.12 = (f16[96,768]{1,0:T(8,128)(2,1)S(1)}, f16[96,768]{1,0:T(8,128)(2,1)S(1)}, u32[]{:S(2)}, u32[]{:S(2)}) collective-permute-start(f16[96,768]{1,0:T(8,128)(2,1)S(1)} %get-tuple-element.175), channel_id=1, source_target_pairs={{0,16},{4,20},{8,24},{12,28},{16,0},{20,4},{24,8},{28,12},{1,17},{... | collective-permute-start | bytes 442376 | tf_op jit(solution)/shard_map/ppermute | solution.py:691
  301.6 18.6 %collective-permute-start.9 = (f16[112,768]{1,0:T(8,128)(2,1)S(1)}, f16[112,768]{1,0:T(8,128)(2,1)S(1)}, u32[]{:S(2)}, u32[]{:S(2)}) collective-permute-start(f16[112,768]{1,0:T(8,128)(2,1)S(1)} %select_convert_fusion.7), channel_id=1, source_target_pairs={{0,16},{4,20},{8,24},{12,28},{16,0},{20,4},{24,8},{28,12},{1,17},{... | collective-permute-start | bytes 516104 | tf_op jit(solution)/shard_map/ppermute | solution.py:691
  320.3 13.6 %collective-permute-start.10 = (f16[96,768]{1,0:T(8,128)(2,1)S(1)}, f16[96,768]{1,0:T(8,128)(2,1)S(1)}, u32[]{:S(2)}, u32[]{:S(2)}) collective-permute-start(f16[96,768]{1,0:T(8,128)(2,1)S(1)} %multiply_convert_fusion), channel_id=1, source_target_pairs={{0,16},{4,20},{8,24},{12,28},{16,0},{20,4},{24,8},{28,12},{1,17},{... | collective-permute-start | bytes 442376 | tf_op jit(solution)/shard_map/ppermute | solution.py:691
  320.5 13.6 %collective-permute-start.15 = (f16[80,768]{1,0:T(8,128)(2,1)S(1)}, f16[80,768]{1,0:T(8,128)(2,1)S(1)}, u32[]{:S(2)}, u32[]{:S(2)}) collective-permute-start(f16[80,768]{1,0:T(8,128)(2,1)S(1)} %multiply_convert_fusion.1), channel_id=1, source_target_pairs={{0,24},{4,28},{8,16},{12,20},{16,8},{20,12},{24,0},{28,4},{1,25},{... | collective-permute-start | bytes 368648 | tf_op jit(solution)/shard_map/ppermute | solution.py:691
  323.2 16.0 %collective-permute-start.16 = (f16[80,768]{1,0:T(8,128)(2,1)S(1)}, f16[80,768]{1,0:T(8,128)(2,1)S(1)}, u32[]{:S(2)}, u32[]{:S(2)}) collective-permute-start(f16[80,768]{1,0:T(8,128)(2,1)S(1)} %multiply_convert_fusion.1), channel_id=1, source_target_pairs={{0,16},{4,20},{8,24},{12,28},{16,0},{20,4},{24,8},{28,12},{1,17},{... | collective-permute-start | bytes 368648 | tf_op jit(solution)/shard_map/ppermute | solution.py:691
  325.2 14.0 %collective-permute-start.17 = (f16[80,768]{1,0:T(8,128)(2,1)S(1)}, f16[80,768]{1,0:T(8,128)(2,1)S(1)}, u32[]{:S(2)}, u32[]{:S(2)}) collective-permute-start(f16[80,768]{1,0:T(8,128)(2,1)S(1)} %multiply_convert_fusion.1), channel_id=1, source_target_pairs={{0,8},{4,12},{8,0},{12,4},{16,24},{20,28},{24,16},{28,20},{1,9},{5... | collective-permute-start | bytes 368648 | tf_op jit(solution)/shard_map/ppermute | solution.py:691
  334.1 11.3 %collective-permute-start.14 = (f16[192,768]{1,0:T(8,128)(2,1)S(1)}, f16[192,768]{1,0:T(8,128)(2,1)S(1)}, u32[]{:S(2)}, u32[]{:S(2)}) collective-permute-start(f16[192,768]{1,0:T(8,128)(2,1)S(1)} %pad_maximum_fusion.13), channel_id=1, source_target_pairs={{0,8},{4,12},{8,0},{12,4},{16,24},{20,28},{24,16},{28,20},{1,9},{5... | collective-permute-start | bytes 884744 | tf_op jit(solution)/shard_map/ppermute | solution.py:691
  345.7 16.3 %collective-permute-start.18 = (f16[384,768]{1,0:T(8,128)(2,1)S(1)}, f16[384,768]{1,0:T(8,128)(2,1)S(1)}, u32[]{:S(2)}, u32[]{:S(2)}) collective-permute-start(f16[384,768]{1,0:T(8,128)(2,1)S(1)} %pad_maximum_fusion.11), channel_id=1, source_target_pairs={{0,4},{4,0},{8,12},{12,8},{16,20},{20,16},{24,28},{28,24},{1,5},{5... | collective-permute-start | bytes 1769480 | tf_op jit(solution)/shard_map/ppermute | solution.py:691
  347.2 24.3 %collective-permute-start.20 = (f16[320,768]{1,0:T(8,128)(2,1)S(1)}, f16[320,768]{1,0:T(8,128)(2,1)S(1)}, u32[]{:S(2)}, u32[]{:S(2)}) collective-permute-start(f16[320,768]{1,0:T(8,128)(2,1)S(1)} %pad_maximum_fusion.12), channel_id=1, source_target_pairs={{0,4},{4,0},{8,12},{12,8},{16,20},{20,16},{24,28},{28,24},{1,5},{5... | collective-permute-start | bytes 1474568 | tf_op jit(solution)/shard_map/ppermute | solution.py:691
  362.5 11.6 %copy-start.15 = (f32[2]{0:T(128)S(1)}, f32[2]{0:T(128)}, u32[]{:S(2)}) copy-start(f32[2]{0:T(128)} %param.16) | copy-start | bytes 28
  362.5 17.0 %collective-permute-start.19 = (f32[768,768]{1,0:T(8,128)S(1)}, f32[768,768]{1,0:T(8,128)}, u32[]{:S(2)}, u32[]{:S(2)}) collective-permute-start(f32[768,768]{1,0:T(8,128)S(1)} %convert_multiply_fusion.2.early_ref), channel_id=1, source_target_pairs={{0,1},{1,0},{2,3},{3,2},{4,5},{5,4},{6,7},{7,6},{8,9},{9,8},{10,11... | collective-permute-start | bytes 7077896 | tf_op jit(solution)/shard_map/ppermute | solution.py:691
  373.2 6.3 %collective-permute-start.21 = (f32[512,768]{1,0:T(8,128)}, f32[512,768]{1,0:T(8,128)}, u32[]{:S(2)}, u32[]{:S(2)}) collective-permute-start(f32[512,768]{1,0:T(8,128)} %convert_multiply_fusion.3.late_ref), channel_id=1, source_target_pairs={{0,1},{1,0},{2,3},{3,2},{4,5},{5,4},{6,7},{7,6},{8,9},{9,8},{10,11... | collective-permute-start | bytes 4718600 | tf_op jit(solution)/shard_map/ppermute | solution.py:691
  374.7 76.3 %all-to-all-start.2 = ((bf16[16,128,768]{2,1,0:T(8,128)(2,1)}), bf16[16,128,768]{2,1,0:T(8,128)(2,1)}, u32[]{:S(2)}, u32[]{:S(2)}) async-start(bf16[16,128,768]{2,1,0:T(8,128)(2,1)} %bitcast.132), calls=%async_computation.2 | async-start | bytes 6291456 | tf_op jit(solution)/shard_map/all_to_all | solution.py:846
  379.4 6.2 %copy-start.6 = (f32[942080]{0:T(1024)S(1)}, f32[942080]{0:T(1024)}, u32[]{:S(2)}) copy-start(f32[942080]{0:T(1024)} %param.15) | copy-start | bytes 11304964
  385.6 6.6 %copy-start.5 = (f32[7360,128]{1,0:T(8,128)S(1)}, f32[7360,128]{1,0:T(8,128)}, u32[]{:S(2)}) copy-start(f32[7360,128]{1,0:T(8,128)} %shard_map.139) | copy-start | bytes 11304964
  385.6 6.6 %copy-start.7 = (f32[942080]{0:T(1024)S(1)}, f32[942080]{0:T(1024)}, u32[]{:S(2)}) copy-start(f32[942080]{0:T(1024)} %param.15) | copy-start | bytes 11304964
  391.4 43.8 %collective-permute-start.22 = (f16[7360,128]{1,0:T(8,128)(2,1)}, f16[7360,128]{1,0:T(8,128)(2,1)}, u32[]{:S(2)}, u32[]{:S(2)}) collective-permute-start(f16[7360,128]{1,0:T(8,128)(2,1)} %divide_convert_fusion), channel_id=1, source_target_pairs={{0,2},{1,3},{2,0},{3,1},{4,6},{5,7},{6,4},{7,5},{8,10},{9,11},{10,... | collective-permute-start | bytes 5652488 | tf_op jit(solution)/shard_map/ppermute | solution.py:691
  392.0 19.1 %collective-permute-start.23 = (f16[7360,128]{1,0:T(8,128)(2,1)}, f16[7360,128]{1,0:T(8,128)(2,1)}, u32[]{:S(2)}, u32[]{:S(2)}) collective-permute-start(f16[7360,128]{1,0:T(8,128)(2,1)} %divide_convert_fusion), channel_id=1, source_target_pairs={{0,1},{1,0},{2,3},{3,2},{4,5},{5,4},{6,7},{7,6},{8,9},{9,8},{10,11... | collective-permute-start | bytes 5652488 | tf_op jit(solution)/shard_map/ppermute | solution.py:691
  392.3 13.5 %slice-start = ((s8[15073280]{0:T(1024)(128)(4,1)}), s8[4194304]{0:T(1024)(128)(4,1)S(1)}, s32[]{:S(2)}) async-start(s8[15073280]{0:T(1024)(128)(4,1)} %bitcast.117), calls=%async_computation.5 | async-start | bytes 8388608
  392.3 13.5 %slice-start.1 = ((s8[15073280]{0:T(1024)(128)(4,1)}), s8[4194304]{0:T(1024)(128)(4,1)S(1)}, s32[]{:S(2)}) async-start(s8[15073280]{0:T(1024)(128)(4,1)} %bitcast.117), calls=%async_computation.6 | async-start | bytes 8388608
  392.3 13.5 %slice-start.2 = ((s8[15073280]{0:T(1024)(128)(4,1)}), s8[2490368]{0:T(1024)(128)(4,1)S(1)}, s32[]{:S(2)}) async-start(s8[15073280]{0:T(1024)(128)(4,1)} %bitcast.117), calls=%async_computation.7 | async-start | bytes 4980736
  399.2 6.6 %slice-start.3 = ((s8[15073280]{0:T(1024)(128)(4,1)}), s8[4194304]{0:T(1024)(128)(4,1)S(1)}, s32[]{:S(2)}) async-start(s8[15073280]{0:T(1024)(128)(4,1)} %bitcast.117), calls=%async_computation.8 | async-start | bytes 8388608
  435.2 5.3 %collective-permute-start.24 = (f16[7360,128]{1,0:T(8,128)(2,1)}, f16[7360,128]{1,0:T(8,128)(2,1)S(1)}, u32[]{:S(2)}, u32[]{:S(2)}) collective-permute-start(f16[7360,128]{1,0:T(8,128)(2,1)} %collective-permute-done.22), channel_id=1, source_target_pairs={{0,1},{1,0},{2,3},{3,2},{4,5},{5,4},{6,7},{7,6},{8,9},{9,8},{10,11... | collective-permute-start | bytes 5652488 | tf_op jit(solution)/shard_map/ppermute | solution.py:691
  (11 other events, 21.6 us)
Sparse Core Ops, SparseCore 0:
  10.9 56.1 all-gather.2
  68.6 96.2 all-gather.4

commit v10 on v8

--- a/solution.py
+++ b/solution.py
@@ -838,9 +838,11 @@
     within = blocks + jnp.arange(span, dtype=jnp.int32)[None, None, :]
     within = within + jnp.arange(slots, dtype=jnp.int32)[None, :, None] * bound
     unpack_rows = jnp.minimum(within, seq_len - 1).reshape(-1)
-
-    def spread(rows):
-        return pick_rows(unpack_rows, rows).reshape(data_devices * slots, span, D)
+    ends = jnp.stack([bound, jnp.int32(seq_len)])[None, :, None]
+    live_rows = jnp.where(within < ends, within, -1).reshape(-1)
+
+    def spread(rows, index):
+        return pick_rows(index, rows).reshape(data_devices * slots, span, D)
 
     def send_back(picked):
         return lax.all_to_all(picked, "dp", split_axis=0, concat_axis=0, tiled=True)
@@ -860,7 +862,7 @@
     pair, dy, through, states, ggain, early_power = run_forward(
         proj_z, proj, gm, bound_arr, cot_top, norm_gain, e2, et, params)
     result = (tok + dot(pair[1], out_w)).astype(BF16)
-    picked = spread(result)
+    picked = spread(result, unpack_rows)
     picked, pair = tie((picked, pair))
     back_out = send_back(picked)
     early_power = early_power[0:1, 0:1]
@@ -885,7 +887,7 @@
     early, early_power = scatter(early, early_power, "dp", *groups[0])
     small = add_pair(small, "zero", 2, late)
     early_before, power_before = early, early_power
-    picked_grad = spread(grad_tok)
+    picked_grad = spread(grad_tok, live_rows)
     tokens, back_out, _ = tie((tokens, back_out, grad_tok))
     back_rows = back_out.at[restore].get(mode="promise_in_bounds")
     tokens_out = jnp.where(live, back_rows, tokens)
@@ -954,8 +956,7 @@
     last, new_master = tie((last, new_master))
     new_master = put(new_master, last, 3)
     back_grad, new_master = tie((back_grad, new_master))
-    grad_tokens = jnp.where(
-        live, back_grad.at[restore].get(mode="promise_in_bounds"), jnp.zeros((), BF16))
+    grad_tokens = back_grad.at[restore].get(mode="promise_in_bounds")
     return (
         tokens_out, grad_tokens, new_master.reshape(-1), grad_shard.reshape(-1),
         first_next.reshape(-1), second_next.reshape(-1))

time: 457 us -> 455 us (level)
  no operation moved by 1% of the time
where the time goes in v10:
time: 455 us; the launch traced here: 447 us
  waiting for transfers between devices  114 us (25%)
  Pallas kernels  105 us (23%)
  other arithmetic  65.5 us (14%)
  matrix products  60.2 us (13%)
  starting transfers between devices  56.8 us (12%)
  local copies, waits for them, and re-layouts  28.4 us (6%)
  between operations  18 us (4%)
    pallas_call x1, Pallas kernels, run_backward(): pl.pallas_call(backward_kernel, grid=(steps,), in_specs=[pl.BlockSpec(mem...  57.9 us
    ppermute x27, waiting for transfers between devices, swap(): return lax.ppermute(values, axis, [(i, i ^ bit) for i in range(size)])  55.3 us
    ppermute x27, starting transfers between devices, swap(): return lax.ppermute(values, axis, [(i, i ^ bit) for i in range(size)])  39.7 us
    all_gather x1, waiting for transfers between devices, on_device(): flat = lax.all_gather(own.astype(BF16), 'zero', axis=0, tiled=True)  39.4 us
    pallas_call x1, Pallas kernels, run_forward(): pl.pallas_call(forward_kernel, grid=(steps,), in_specs=[pl.BlockSpec(memo...  34.8 us
    dot_general x4, matrix products, product(): lax.dot_general(part, right, (((1,), (1,)), ((0,), (0,))), preferred_elem...  23.8 us
    dot_general x3, matrix products, dot(): lax.dot_general(a, b, (((1,), (0,)), ((), ())), preferred_element_type=F32)  21.4 us
    dynamic_update_slice x4, other arithmetic, put(): return lax.dynamic_update_index_in_dim(new_master, new, shard, 0)  20 us
  transfers between devices with their start and end apart: 32, of which 12 were waited for; matrix products, arithmetic and copies ran while one was open for 31% of the time, Pallas kernels for 23%

profile of v10, /device:TPU:0, one launch (start us, length us, event | category | flops | bytes accessed | tf_op | source)
XLA Modules:
  0.0 447.4 jit_solution(2726908245190734928)
XLA Ops:
  7.2 3.5 bitcast_convert_fusion
  12.6 2.4 gather_fusion
  15.0 7.4 %all-to-all-start = ((bf16[16,128,768]{2,1,0:T(8,128)(2,1)}), bf16[16,128,768]{2,1,0:T(8,128)(2,1)}, u32[]{:S(2)}, u32[]{:S(2)}) async-start(bf16[16,128,768]{2,1,0:T(8,128)(2,1)} %gather_fusion), calls=%async_computation | async-start | bytes 6291456 | tf_op jit(solution)/shard_map/all_to_all | solution.py:819
  27.7 39.4 %all-gather.3.cloned.1.call-done.flat_ref = bf16[29440,128]{1,0:T(8,128)(2,1)} async-done(((bf16[7360,128]{1,0:T(8,128)(2,1)}), bf16[29440,128]{1,0:T(8,128)(2,1)}) %all-gather.3.cloned.1.call-update) | async-done | bytes 7536656 | tf_op jit(solution)/shard_map/all_gather | solution.py:817
  67.0 6.0 %shard_map.136 = (bf16[3584,768]{1,0:T(8,128)(2,1)S(1)}, bf16[1536,768]{1,0:T(8,128)(2,1)S(1)}, f32[1,768]{1,0:T(1,128)S(1)}, f32[8,1792]{1,0:T(8,128)S(1)}, f32...) custom-call(bf16[29440,128]{1,0:T(8,128)(2,1)} %all-gather.3.cloned., ...), custom_call_target="tpu_custom_call" | custom-call | flops 1000000000 | bytes 16777216 | tf_op jit(solution)/shard_map/pallas_call | solution.py:593
  73.0 2.6 copy-done
  77.0 4.6 %fusion.94.gm_ref = f32[1024,1536]{1,0:T(8,128)} fusion(bf16[1536,768]{1,0:T(8,128)(2,1)S(1)} %get-tuple-element.76, bf16[1,1024,768]{2,1,0:T(8,128)(2,1)S(1)} %copy-done.10), kind=kOutput, calls=%fused_computation.260 | convolution fusion | flops 2415919104 | bytes 10223616 | tf_op jit(solution)/shard_map/dot_general | solution.py:33
  81.6 11.6 %all-to-all-done = bf16[16,128,768]{2,1,0:T(8,128)(2,1)} async-done(((bf16[16,128,768]{2,1,0:T(8,128)(2,1)}), bf16[16,128,768]{2,1,0:T(8,128)(2,1)}, u32[]{:S(2)}, u32[]{:S(2)}) %all-to-all-start) | async-done | bytes 3145760 | tf_op jit(solution)/shard_map/all_to_all | solution.py:819
  93.3 5.8 %fusion.21 = (f32[1024]{0:T(1024)S(1)}, bf16[1024,768]{1,0:T(8,128)(2,1)S(1)}) fusion(bf16[2048,768]{1,0:T(8,128)(2,1)} %bitcast.6, s32[1024]{0:T(1024)S(1)} %fusion.61), kind=kOutput, calls=%fused_computation.52 | convolution fusion | flops 3226467328 | bytes 4726784 | tf_op jit(solution)/shard_map/dot_general | solution.py:29
  99.1 4.7 %fusion.41.z_ref = f32[1024,1536]{1,0:T(8,128)} fusion(bf16[3584,768]{1,0:T(8,128)(2,1)S(1)} %copy-done.1, bf16[1024,768]{1,0:T(8,128)(2,1)S(1)} %get-tuple-element.207.tok_ref, f32[768]{0:T(1024)S(1)} %reduce.2, f32[1024]{0:T(1024)S(1)} %add_rsqrt_fusion), kind=kOutput, calls=%fused_computation.77 | convolution fusion | flops 2419064832 | bytes 10231808 | tf_op jit(solution)/shard_map/dot_general | solution.py:33
  103.8 5.8 %fusion.35.proj_ref.before_ref = f32[1024,1816]{1,0:T(8,128)} fusion(bf16[3584,768]{1,0:T(8,128)(2,1)S(1)} %copy-done.1, bf16[1024,768]{1,0:T(8,128)(2,1)S(1)} %get-tuple-element.207.tok_ref, f32[768]{0:T(1024)S(1)} %reduce.2, f32[1024]{0:T(1024)S(1)} %add_rsqrt_fusion), kind=kOutput, calls=%fused_computation.68 | convolution fusion | flops 2859466752 | bytes 11808768 | tf_op jit(solution)/shard_map/dot_general | solution.py:33
  109.6 34.8 %shard_map.137 = (bf16[2,1024,1536]{2,1,0:T(8,128)(2,1)}, f32[1024,1536]{1,0:T(8,128)}, f32[1024,128]{1,0:T(8,128)S(1)}, f32[8,128,1536]{2,1,0:T(8,128)}, f32[1,1536]{1,0:T(1,128)S(1)}, /*index=5*/f32[8,128]{1,0:T(8,128)S(1)}) custom-call(s32[1]{0:T(128)} %dynamic_slice.148.bound_ref, f32[1]{0:T(128)S(6)} %convert.1.cot_ref, f32[1024,1536]{1,0:T(8,128)} %fusion.41.z_ref, ...), custom_call_target="tpu_custom_call" | custom-call | flops 30000001024 | bytes 41943040 | tf_op jit(solution)/shard_map/pallas_call | solution.py:221
  144.4 10.5 %fusion.20 = bf16[2048,768]{1,0:T(8,128)(2,1)} fusion(s32[2048]{0:T(1024)S(1)} %get-tuple-element.203, bf16[1024,768]{1,0:T(8,128)(2,1)S(1)} %get-tuple-element.207.tok_ref, bf16[1536,768]{1,0:T(8,128)(2,1)} %copy-done.2, bf16[2,1024,1536]{2,1,0:T(8,128)(2,1)} %get-tuple-element.93.gz_ref), kind=kOutput, calls=%fused_computation.51 | convolution fusion | flops 5643173888 | bytes 10231808 | tf_op jit(solution)/shard_map/dot_general | solution.py:29
  156.5 9.0 %select_convert_fusion = f16[2,896,768]{2,1,0:T(8,128)(2,1)} fusion(f32[]{:T(128)} %bitcast.12, f32[]{:T(128)} %bitcast.10, pred[896]{0:T(1024)(128)(4,1)S(1)} %fusion.71, bf16[1,1024,768]{2,1,0:T(8,128)(2,1)S(1)} %fusion.101, bf16[1,1024,768]{2,1,0:T(8,128)(2,1)S(1)} %copy-done.11, bf16[2,1024,1536]{2,1,0:T(8,128)(2,1)} %get-tuple-element.93.gz_ref, ...), kind=kOutput, calls=%fused_computation.11 | convolution fusion | flops 2826108928 | bytes 13240193 | tf_op jit(solution)/shard_map/dot_general | solution.py:735
  167.4 4.9 %all-to-all-start.1 = ((bf16[16,128,768]{2,1,0:T(8,128)(2,1)}), bf16[16,128,768]{2,1,0:T(8,128)(2,1)}, u32[]{:S(2)}, u32[]{:S(2)}) async-start(bf16[16,128,768]{2,1,0:T(8,128)(2,1)} %bitcast.132), calls=%async_computation.1 | async-start | bytes 6291456 | tf_op jit(solution)/shard_map/all_to_all | solution.py:848
  172.2 6.6 %fusion.27 = f32[2,768,768]{2,1,0:T(8,128)S(1)} fusion(bf16[2,1024,1536]{2,1,0:T(8,128)(2,1)} %get-tuple-element.93.gz_ref, pred[]{:T(512)S(6)} %eq.116, bf16[1,1024,768]{2,1,0:T(8,128)(2,1)} %copy-done.12, bf16[1,1024,768]{2,1,0:T(8,128)(2,1)} %param.10), kind=kOutput, calls=%fused_computation.59 | convolution fusion | flops 2419064832 | bytes 14155777 | tf_op jit(solution)/shard_map/dot_general | solution.py:735
  180.2 2.1 multiply_add_fusion
  184.3 57.9 %shard_map.138 = (bf16[2,1024,1024]{2,1,0:T(8,128)(2,1)}, bf16[1024,768]{1,0:T(8,128)(2,1)S(1)}, f32[48,768]{1,0:T(8,128)S(1)}, f32[8,128]{1,0:T(8,128)S(1)}) custom-call(s32[1]{0:T(128)} %dynamic_slice.148.bound_ref, f32[1024,1816]{1,0:T(8,128)} %fusion.35.proj_ref.before_ref, f32[1024,1816]{1,0:T(8,128)} %fusion.35.proj_ref.before_ref, ...), custom_call_target="tpu_custom_call" | custom-call | flops 49999998976 | bytes 52428800 | tf_op jit(solution)/shard_map/pallas_call | solution.py:453
  246.5 6.0 %select_convert_fusion.1 = f16[2,640,768]{2,1,0:T(8,128)(2,1)S(1)} fusion(f32[]{:T(128)} %bitcast.16, f32[]{:T(128)} %bitcast.15, pred[640]{0:T(1024)(128)(4,1)S(1)} %fusion.73, bf16[1,1024,768]{2,1,0:T(8,128)(2,1)S(1)} %copy-done.13, bf16[2,1024,1024]{2,1,0:T(8,128)(2,1)} %get-tuple-element.108, pred[]{:T(512)S(6)} %eq.123), kind=kOutput, calls=%fused_computation.19 | convolution fusion | flops 2019098624 | bytes 8783489 | tf_op jit(solution)/shard_map/dot_general | solution.py:735
  254.9 2.1 fusion.33
  261.6 2.3 select_convert_fusion.4
  265.9 4.3 gather_fusion.1
  270.2 4.3 broadcast_select_fusion
  274.5 5.1 %fusion.19 = bf16[2048,768]{1,0:T(8,128)(2,1)} fusion(bf16[1024,768]{1,0:T(8,128)(2,1)S(1)} %copy-done.4, s32[2048]{0:T(1024)S(1)} %copy-done.15), kind=kOutput, calls=%fused_computation.50 | convolution fusion | flops 3224895488 | bytes 4726784 | tf_op jit(solution)/shard_map/dot_general | solution.py:29
  289.4 2.4 collective-permute-start.6
  292.3 4.6 %collective-permute-done.10 = f16[336,768]{1,0:T(8,128)(2,1)S(1)} collective-permute-done((f16[336,768]{1,0:T(8,128)(2,1)S(1)}, f16[336,768]{1,0:T(8,128)(2,1)S(1)}, u32[]{:S(2)}, u32[]{:S(2)}) %collective-permute-start.10) | collective-permute-done | bytes 516128 | tf_op jit(solution)/shard_map/ppermute | solution.py:691
  298.9 2.4 collective-permute-start.16
  301.3 4.3 collective-permute-done.6
  305.8 2.4 collective-permute-start.11
  308.2 13.3 %collective-permute-start.12 = (f16[96,768]{1,0:T(8,128)(2,1)S(1)}, f16[96,768]{1,0:T(8,128)(2,1)S(1)}, u32[]{:S(2)}, u32[]{:S(2)}) collective-permute-start(f16[96,768]{1,0:T(8,128)(2,1)S(1)} %multiply_convert_fusion), channel_id=1, source_target_pairs={{0,16},{4,20},{8,24},{12,28},{16,0},{20,4},{24,8},{28,12},{1,17},{... | collective-permute-start | bytes 442376 | tf_op jit(solution)/shard_map/ppermute | solution.py:691
  321.5 5.6 %collective-permute-done.15 = f16[96,768]{1,0:T(8,128)(2,1)S(1)} collective-permute-done((f16[96,768]{1,0:T(8,128)(2,1)S(1)}, f16[96,768]{1,0:T(8,128)(2,1)S(1)}, u32[]{:S(2)}, u32[]{:S(2)}) %collective-permute-start.15) | collective-permute-done | bytes 147488 | tf_op jit(solution)/shard_map/ppermute | solution.py:691
  327.2 4.4 collective-permute-done.12
  332.8 2.3 collective-permute-start.19
  337.2 3.2 collective-permute-done.19
  340.4 3.7 collective-permute-done.20
  346.4 10.1 %collective-permute-done.22 = f16[320,768]{1,0:T(8,128)(2,1)S(1)} collective-permute-done((f16[320,768]{1,0:T(8,128)(2,1)S(1)}, f16[320,768]{1,0:T(8,128)(2,1)S(1)}, u32[]{:S(2)}, u32[]{:S(2)}) %collective-permute-start.22) | collective-permute-done | bytes 491552 | tf_op jit(solution)/shard_map/ppermute | solution.py:691
  359.7 4.8 %all-to-all-start.2 = ((bf16[16,128,768]{2,1,0:T(8,128)(2,1)}), bf16[16,128,768]{2,1,0:T(8,128)(2,1)}, u32[]{:S(2)}, u32[]{:S(2)}) async-start(bf16[16,128,768]{2,1,0:T(8,128)(2,1)} %bitcast.133), calls=%async_computation.2 | async-start | bytes 6291456 | tf_op jit(solution)/shard_map/all_to_all | solution.py:848
  364.6 6.1 %shard_map.139 = f32[7360,128]{1,0:T(8,128)} custom-call(s32[2]{0:T(128)S(1)} %pad_add_fusion.1.who_ref, f32[768,768]{1,0:T(8,128)S(1)} %convert_multiply_fusion.2.early_ref, f32[768,768]{1,0:T(8,128)} %collective-permute-done.18.early_other_ref, f32[512,768]{1,0:T(8,128)} %convert_multiply_fusion.3.late_ref, ...), custom_call_target="tpu_custom_call" | custom-call | flops 1000000 | bytes 12582912 | tf_op jit(solution)/shard_map/pallas_call | solution.py:671
  370.7 5.8 %divide_convert_fusion = f16[7360,128]{1,0:T(8,128)(2,1)} fusion(f32[7360,128]{1,0:T(8,128)} %shard_map.139, f32[]{:T(128)} %bitcast.26, f32[]{:T(128)} %bitcast.24, f32[942080]{0:T(1024)S(1)} %copy-done.6, f32[942080]{0:T(1024)} %param.14), kind=kLoop, calls=%fused_computation.42 | loop fusion | flops 11304960 | bytes 13189128 | tf_op jit(solution)/shard_map/convert_element_type | solution.py:937
  377.4 6.9 %multiply_add_fusion.1 = (f32[7360,128]{1,0:T(8,128)}, f32[7360,128]{1,0:T(8,128)}) fusion(f32[7360,128]{1,0:T(8,128)S(1)} %bitcast.126, f32[7360,128]{1,0:T(8,128)S(1)} %copy-done.5, f32[7360,128]{1,0:T(8,128)} %bitcast.127), kind=kLoop, calls=%fused_computation.40 | loop fusion | flops 6594560 | bytes 18841600 | tf_op jit(solution)/shard_map/add | solution.py:932
  384.3 6.6 %broadcast_in_dim.146 = f32[4,7360,128]{2,1,0:T(8,128)} broadcast(f32[]{:T(128)} %constant.309.clone.1), dimensions={} | broadcast | bytes 15073284 | tf_op jit(solution)/shard_map/broadcast_in_dim | solution.py:894
  390.9 5.4 %bitcast_dynamic-update-slice_fusion.3 = f32[4,7360,128]{2,1,0:T(8,128)} fusion(f32[4,7360,128]{2,1,0:T(8,128)} %broadcast_in_dim.146, s32[]{:T(128)S(6)} %select_n.595, f16[7360,128]{1,0:T(8,128)(2,1)} %divide_convert_fusion, f32[4,7360,128]{2,1,0:T(8,128)S(1)} %bitcast.120, f32[]{:T(128)} %bitcast.30, f32[]{:T(128)} %bitcast.29), kind=kLoop, calls=%fused_computation.35 | loop fusion | flops 4710400 | bytes 9421828 | tf_op jit(solution)/shard_map/jit(dynamic_update_index_in_dim)/dynamic_update_slice | solution.py:945
  396.3 5.4 %bitcast_dynamic-update-slice_fusion.2 = f32[4,7360,128]{2,1,0:T(8,128)} fusion(f32[4,7360,128]{2,1,0:T(8,128)} %bitcast_dynamic-update-slice_fusion.3, s32[]{:T(128)S(6)} %select_n.720, f16[7360,128]{1,0:T(8,128)(2,1)} %collective-permute-done.25, f32[4,7360,128]{2,1,0:T(8,128)S(1)} %bitcast.121, f32[]{:T(128)} %bitcast.30, f32[]{:T(128)} %bitcast.29), kind=kLoop, calls=%fused_computation.30 | loop fusion | flops 4710400 | bytes 9421828 | tf_op jit(solution)/shard_map/jit(dynamic_update_index_in_dim)/dynamic_update_slice | solution.py:945
  401.7 18.5 %collective-permute-done.24 = f16[7360,128]{1,0:T(8,128)(2,1)} collective-permute-done((f16[7360,128]{1,0:T(8,128)(2,1)}, f16[7360,128]{1,0:T(8,128)(2,1)}, u32[]{:S(2)}, u32[]{:S(2)}) %collective-permute-start.24) | collective-permute-done | bytes 1884192 | tf_op jit(solution)/shard_map/ppermute | solution.py:691
  420.1 5.4 %bitcast_dynamic-update-slice_fusion.1 = f32[4,7360,128]{2,1,0:T(8,128)} fusion(f32[4,7360,128]{2,1,0:T(8,128)} %bitcast_dynamic-update-slice_fusion.2, s32[]{:T(128)S(6)} %select_n.721, f16[7360,128]{1,0:T(8,128)(2,1)} %collective-permute-done.24, f32[4,7360,128]{2,1,0:T(8,128)S(1)} %bitcast.122, f32[]{:T(128)} %bitcast.30, f32[]{:T(128)} %bitcast.29), kind=kLoop, calls=%fused_computation.25 | loop fusion | flops 4710400 | bytes 9421828 | tf_op jit(solution)/shard_map/jit(dynamic_update_index_in_dim)/dynamic_update_slice | solution.py:945
  425.5 3.9 bitcast_dynamic-update-slice_fusion
  429.4 6.6 %all-to-all-done.2 = bf16[16,128,768]{2,1,0:T(8,128)(2,1)} async-done(((bf16[16,128,768]{2,1,0:T(8,128)(2,1)}), bf16[16,128,768]{2,1,0:T(8,128)(2,1)}, u32[]{:S(2)}, u32[]{:S(2)}) %all-to-all-start.2) | async-done | bytes 3145760 | tf_op jit(solution)/shard_map/all_to_all | solution.py:848
  436.0 4.3 gather_fusion.2
  (185 shorter events, 47.5 us)
Async XLA Ops:
  7.2 59.9 %all-gather.3.cloned.1.call-start = ((), (), s32[]{:S(2)}) async-start(), calls=%async_computation.3 | async-start | bytes 9420800 | tf_op jit(solution)/shard_map/all_gather | solution.py:817
  10.7 234.4 %all-gather.5.cloned.1.call-start = ((), (), s32[]{:S(2)}) async-start(), calls=%async_computation.4 | async-start | bytes 18841600 | tf_op jit(solution)/shard_map/all_gather | solution.py:830
  15.0 7.4 %copy-start.10 = (bf16[1,1024,768]{2,1,0:T(8,128)(2,1)S(1)}, bf16[1,1024,768]{2,1,0:T(8,128)(2,1)}, u32[]{:S(2)}) copy-start(bf16[1,1024,768]{2,1,0:T(8,128)(2,1)} %param.10) | copy-start | bytes 4718596
  15.0 9.2 %copy-start.22 = (s32[64]{0:T(128)S(1)}, s32[64]{0:T(128)}, u32[]{:S(2)}) copy-start(s32[64]{0:T(128)} %param.11) | copy-start | bytes 772
  15.0 78.2 %all-to-all-start = ((bf16[16,128,768]{2,1,0:T(8,128)(2,1)}), bf16[16,128,768]{2,1,0:T(8,128)(2,1)}, u32[]{:S(2)}, u32[]{:S(2)}) async-start(bf16[16,128,768]{2,1,0:T(8,128)(2,1)} %gather_fusion), calls=%async_computation | async-start | bytes 6291456 | tf_op jit(solution)/shard_map/all_to_all | solution.py:819
  93.2 5.8 %copy-start.1 = (bf16[3584,768]{1,0:T(8,128)(2,1)S(1)}, bf16[3584,768]{1,0:T(8,128)(2,1)}, u32[]{:S(2)}) copy-start(bf16[3584,768]{1,0:T(8,128)(2,1)} %copy-done) | copy-start | bytes 16515076
  156.4 9.1 %copy-start.12 = (bf16[1,1024,768]{2,1,0:T(8,128)(2,1)}, bf16[1,1024,768]{2,1,0:T(8,128)(2,1)S(1)}, u32[]{:S(2)}) copy-start(bf16[1,1024,768]{2,1,0:T(8,128)(2,1)S(1)} %fusion.101) | copy-start | bytes 4718596
  165.5 13.3 %collective-permute-start = (f16[2,896,768]{2,1,0:T(8,128)(2,1)}, f16[2,896,768]{2,1,0:T(8,128)(2,1)}, u32[]{:S(2)}, u32[]{:S(2)}) collective-permute-start(f16[2,896,768]{2,1,0:T(8,128)(2,1)} %select_convert_fusion), channel_id=1, source_target_pairs={{0,1},{1,0},{2,3},{3,2},{4,5},{5,4},{6,7},{7,6},{8,9},{9,8},{10,11... | collective-permute-start | bytes 8257544 | tf_op jit(solution)/shard_map/ppermute | solution.py:691
  167.4 94.2 %all-to-all-start.1 = ((bf16[16,128,768]{2,1,0:T(8,128)(2,1)}), bf16[16,128,768]{2,1,0:T(8,128)(2,1)}, u32[]{:S(2)}, u32[]{:S(2)}) async-start(bf16[16,128,768]{2,1,0:T(8,128)(2,1)} %bitcast.132), calls=%async_computation.1 | async-start | bytes 6291456 | tf_op jit(solution)/shard_map/all_to_all | solution.py:848
  182.7 60.6 %collective-permute-start.1 = (f16[784,768]{1,0:T(8,128)(2,1)S(1)}, f16[784,768]{1,0:T(8,128)(2,1)S(1)}, u32[]{:S(2)}, u32[]{:S(2)}) collective-permute-start(f16[784,768]{1,0:T(8,128)(2,1)S(1)} %select_convert_fusion.2), channel_id=1, source_target_pairs={{0,2},{1,3},{2,0},{3,1},{4,6},{5,7},{6,4},{7,5},{8,10},{9,11},{10,... | collective-permute-start | bytes 3612680 | tf_op jit(solution)/shard_map/ppermute | solution.py:691
  246.4 8.1 %copy-start.23 = (s32[16]{0:T(128)S(1)}, s32[16]{0:T(128)}, u32[]{:S(2)}) copy-start(s32[16]{0:T(128)} %scatter_custom_fusion) | copy-start | bytes 196
  246.5 8.1 %copy-start.21 = (s32[16]{0:T(128)S(1)}, s32[16]{0:T(128)}, u32[]{:S(2)}) copy-start(s32[16]{0:T(128)} %dynamic_slice.161) | copy-start | bytes 196
  246.5 8.5 %copy-start.24 = (bf16[2,1024,1024]{2,1,0:T(8,128)(2,1)S(1)}, bf16[2,1024,1024]{2,1,0:T(8,128)(2,1)}, u32[]{:S(2)}) copy-start(bf16[2,1024,1024]{2,1,0:T(8,128)(2,1)} %get-tuple-element.108) | copy-start | bytes 12582916
  252.5 5.2 %collective-permute-start.2 = (f16[2,640,768]{2,1,0:T(8,128)(2,1)S(1)}, f16[2,640,768]{2,1,0:T(8,128)(2,1)S(1)}, u32[]{:S(2)}, u32[]{:S(2)}) collective-permute-start(f16[2,640,768]{2,1,0:T(8,128)(2,1)S(1)} %select_convert_fusion.1), channel_id=1, source_target_pairs={{0,1},{1,0},{2,3},{3,2},{4,5},{5,4},{6,7},{7,6},{8,9},{9,8},{10,11... | collective-permute-start | bytes 5898248 | tf_op jit(solution)/shard_map/ppermute | solution.py:691
  254.6 2.4 collective-permute-start.8
  257.1 26.3 %collective-permute-start.9 = (f32[48,768]{1,0:T(8,128)S(1)}, f32[48,768]{1,0:T(8,128)S(1)}, u32[]{:S(2)}, u32[]{:S(2)}) collective-permute-start(f32[48,768]{1,0:T(8,128)S(1)} %add.432), channel_id=1, source_target_pairs={{0,2},{1,3},{2,0},{3,1},{4,6},{5,7},{6,4},{7,5},{8,10},{9,11},{10,... | collective-permute-start | bytes 442376 | tf_op jit(solution)/shard_map/ppermute | solution.py:691
  260.1 20.5 %collective-permute-start.3 = (f16[528,768]{1,0:T(8,128)(2,1)}, f16[528,768]{1,0:T(8,128)(2,1)}, u32[]{:S(2)}, u32[]{:S(2)}) collective-permute-start(f16[528,768]{1,0:T(8,128)(2,1)} %select_convert_fusion.3), channel_id=1, source_target_pairs={{0,2},{1,3},{2,0},{3,1},{4,6},{5,7},{6,4},{7,5},{8,10},{9,11},{10,... | collective-permute-start | bytes 2433032 | tf_op jit(solution)/shard_map/ppermute | solution.py:691
  264.0 21.7 %collective-permute-start.4 = (f16[400,768]{1,0:T(8,128)(2,1)}, f16[400,768]{1,0:T(8,128)(2,1)}, u32[]{:S(2)}, u32[]{:S(2)}) collective-permute-start(f16[400,768]{1,0:T(8,128)(2,1)} %select_convert_fusion.4), channel_id=1, source_target_pairs={{0,4},{4,0},{8,12},{12,8},{16,20},{20,16},{24,28},{28,24},{1,5},{5... | collective-permute-start | bytes 1843208 | tf_op jit(solution)/shard_map/ppermute | solution.py:691
  270.2 4.3 copy-start.15
  283.8 13.1 %collective-permute-start.10 = (f16[336,768]{1,0:T(8,128)(2,1)S(1)}, f16[336,768]{1,0:T(8,128)(2,1)S(1)}, u32[]{:S(2)}, u32[]{:S(2)}) collective-permute-start(f16[336,768]{1,0:T(8,128)(2,1)S(1)} %select_convert_fusion.5), channel_id=1, source_target_pairs={{0,4},{4,0},{8,12},{12,8},{16,20},{20,16},{24,28},{28,24},{1,5},{5... | collective-permute-start | bytes 1548296 | tf_op jit(solution)/shard_map/ppermute | solution.py:691
  287.8 13.4 %collective-permute-start.5 = (f16[112,768]{1,0:T(8,128)(2,1)S(1)}, f16[112,768]{1,0:T(8,128)(2,1)S(1)}, u32[]{:S(2)}, u32[]{:S(2)}) collective-permute-start(f16[112,768]{1,0:T(8,128)(2,1)S(1)} %get-tuple-element.175), channel_id=1, source_target_pairs={{0,8},{4,12},{8,0},{12,4},{16,24},{20,28},{24,16},{28,20},{1,9},{5... | collective-permute-start | bytes 516104 | tf_op jit(solution)/shard_map/ppermute | solution.py:691
  289.4 16.2 %collective-permute-start.6 = (f16[112,768]{1,0:T(8,128)(2,1)S(1)}, f16[112,768]{1,0:T(8,128)(2,1)S(1)}, u32[]{:S(2)}, u32[]{:S(2)}) collective-permute-start(f16[112,768]{1,0:T(8,128)(2,1)S(1)} %get-tuple-element.174), channel_id=1, source_target_pairs={{0,16},{4,20},{8,24},{12,28},{16,0},{20,4},{24,8},{28,12},{1,17},{... | collective-permute-start | bytes 516104 | tf_op jit(solution)/shard_map/ppermute | solution.py:691
  291.8 13.8 %collective-permute-start.7 = (f16[112,768]{1,0:T(8,128)(2,1)S(1)}, f16[112,768]{1,0:T(8,128)(2,1)S(1)}, u32[]{:S(2)}, u32[]{:S(2)}) collective-permute-start(f16[112,768]{1,0:T(8,128)(2,1)S(1)} %get-tuple-element.173), channel_id=1, source_target_pairs={{0,24},{4,28},{8,16},{12,20},{16,8},{20,12},{24,0},{28,4},{1,25},{... | collective-permute-start | bytes 516104 | tf_op jit(solution)/shard_map/ppermute | solution.py:691
  297.3 24.2 %collective-permute-start.14 = (f16[96,768]{1,0:T(8,128)(2,1)S(1)}, f16[96,768]{1,0:T(8,128)(2,1)S(1)}, u32[]{:S(2)}, u32[]{:S(2)}) collective-permute-start(f16[96,768]{1,0:T(8,128)(2,1)S(1)} %get-tuple-element.180), channel_id=1, source_target_pairs={{0,8},{4,12},{8,0},{12,4},{16,24},{20,28},{24,16},{28,20},{1,9},{5... | collective-permute-start | bytes 442376 | tf_op jit(solution)/shard_map/ppermute | solution.py:691
  298.9 22.6 %collective-permute-start.16 = (f16[96,768]{1,0:T(8,128)(2,1)S(1)}, f16[96,768]{1,0:T(8,128)(2,1)S(1)}, u32[]{:S(2)}, u32[]{:S(2)}) collective-permute-start(f16[96,768]{1,0:T(8,128)(2,1)S(1)} %get-tuple-element.178), channel_id=1, source_target_pairs={{0,24},{4,28},{8,16},{12,20},{16,8},{20,12},{24,0},{28,4},{1,25},{... | collective-permute-start | bytes 442376 | tf_op jit(solution)/shard_map/ppermute | solution.py:691
  301.3 25.8 %collective-permute-start.15 = (f16[96,768]{1,0:T(8,128)(2,1)S(1)}, f16[96,768]{1,0:T(8,128)(2,1)S(1)}, u32[]{:S(2)}, u32[]{:S(2)}) collective-permute-start(f16[96,768]{1,0:T(8,128)(2,1)S(1)} %get-tuple-element.179), channel_id=1, source_target_pairs={{0,16},{4,20},{8,24},{12,28},{16,0},{20,4},{24,8},{28,12},{1,17},{... | collective-permute-start | bytes 442376 | tf_op jit(solution)/shard_map/ppermute | solution.py:691
  305.8 21.4 %collective-permute-start.11 = (f16[96,768]{1,0:T(8,128)(2,1)S(1)}, f16[96,768]{1,0:T(8,128)(2,1)S(1)}, u32[]{:S(2)}, u32[]{:S(2)}) collective-permute-start(f16[96,768]{1,0:T(8,128)(2,1)S(1)} %multiply_convert_fusion), channel_id=1, source_target_pairs={{0,24},{4,28},{8,16},{12,20},{16,8},{20,12},{24,0},{28,4},{1,25},{... | collective-permute-start | bytes 442376 | tf_op jit(solution)/shard_map/ppermute | solution.py:691
  308.2 23.4 %collective-permute-start.12 = (f16[96,768]{1,0:T(8,128)(2,1)S(1)}, f16[96,768]{1,0:T(8,128)(2,1)S(1)}, u32[]{:S(2)}, u32[]{:S(2)}) collective-permute-start(f16[96,768]{1,0:T(8,128)(2,1)S(1)} %multiply_convert_fusion), channel_id=1, source_target_pairs={{0,16},{4,20},{8,24},{12,28},{16,0},{20,4},{24,8},{28,12},{1,17},{... | collective-permute-start | bytes 442376 | tf_op jit(solution)/shard_map/ppermute | solution.py:691
  321.5 10.1 %collective-permute-start.13 = (f16[96,768]{1,0:T(8,128)(2,1)S(1)}, f16[96,768]{1,0:T(8,128)(2,1)S(1)}, u32[]{:S(2)}, u32[]{:S(2)}) collective-permute-start(f16[96,768]{1,0:T(8,128)(2,1)S(1)} %multiply_convert_fusion), channel_id=1, source_target_pairs={{0,8},{4,12},{8,0},{12,4},{16,24},{20,28},{24,16},{28,20},{1,9},{5... | collective-permute-start | bytes 442376 | tf_op jit(solution)/shard_map/ppermute | solution.py:691
  332.1 13.8 %collective-permute-start.17 = (f16[384,768]{1,0:T(8,128)(2,1)S(1)}, f16[384,768]{1,0:T(8,128)(2,1)S(1)}, u32[]{:S(2)}, u32[]{:S(2)}) collective-permute-start(f16[384,768]{1,0:T(8,128)(2,1)S(1)} %pad_maximum_fusion.11), channel_id=1, source_target_pairs={{0,4},{4,0},{8,12},{12,8},{16,20},{20,16},{24,28},{28,24},{1,5},{5... | collective-permute-start | bytes 1769480 | tf_op jit(solution)/shard_map/ppermute | solution.py:691
  332.8 7.6 %collective-permute-start.19 = (f16[80,768]{1,0:T(8,128)(2,1)S(1)}, f16[80,768]{1,0:T(8,128)(2,1)S(1)}, u32[]{:S(2)}, u32[]{:S(2)}) collective-permute-start(f16[80,768]{1,0:T(8,128)(2,1)S(1)} %multiply_convert_fusion.1), channel_id=1, source_target_pairs={{0,24},{4,28},{8,16},{12,20},{16,8},{20,12},{24,0},{28,4},{1,25},{... | collective-permute-start | bytes 368648 | tf_op jit(solution)/shard_map/ppermute | solution.py:691
  335.1 9.0 %collective-permute-start.20 = (f16[80,768]{1,0:T(8,128)(2,1)S(1)}, f16[80,768]{1,0:T(8,128)(2,1)S(1)}, u32[]{:S(2)}, u32[]{:S(2)}) collective-permute-start(f16[80,768]{1,0:T(8,128)(2,1)S(1)} %multiply_convert_fusion.1), channel_id=1, source_target_pairs={{0,16},{4,20},{8,24},{12,28},{16,0},{20,4},{24,8},{28,12},{1,17},{... | collective-permute-start | bytes 368648 | tf_op jit(solution)/shard_map/ppermute | solution.py:691
  335.1 9.0 %collective-permute-start.21 = (f16[80,768]{1,0:T(8,128)(2,1)S(1)}, f16[80,768]{1,0:T(8,128)(2,1)S(1)}, u32[]{:S(2)}, u32[]{:S(2)}) collective-permute-start(f16[80,768]{1,0:T(8,128)(2,1)S(1)} %multiply_convert_fusion.1), channel_id=1, source_target_pairs={{0,8},{4,12},{8,0},{12,4},{16,24},{20,28},{24,16},{28,20},{1,9},{5... | collective-permute-start | bytes 368648 | tf_op jit(solution)/shard_map/ppermute | solution.py:691
  344.4 12.1 %collective-permute-start.22 = (f16[320,768]{1,0:T(8,128)(2,1)S(1)}, f16[320,768]{1,0:T(8,128)(2,1)S(1)}, u32[]{:S(2)}, u32[]{:S(2)}) collective-permute-start(f16[320,768]{1,0:T(8,128)(2,1)S(1)} %pad_maximum_fusion.12), channel_id=1, source_target_pairs={{0,4},{4,0},{8,12},{12,8},{16,20},{20,16},{24,28},{28,24},{1,5},{5... | collective-permute-start | bytes 1474568 | tf_op jit(solution)/shard_map/ppermute | solution.py:691
  346.4 12.7 %copy-start.16 = (f32[2]{0:T(128)S(1)}, f32[2]{0:T(128)}, u32[]{:S(2)}) copy-start(f32[2]{0:T(128)} %param.16) | copy-start | bytes 28
  346.4 18.2 %collective-permute-start.18 = (f32[768,768]{1,0:T(8,128)S(1)}, f32[768,768]{1,0:T(8,128)}, u32[]{:S(2)}, u32[]{:S(2)}) collective-permute-start(f32[768,768]{1,0:T(8,128)S(1)} %convert_multiply_fusion.2.early_ref), channel_id=1, source_target_pairs={{0,1},{1,0},{2,3},{3,2},{4,5},{5,4},{6,7},{7,6},{8,9},{9,8},{10,11... | collective-permute-start | bytes 7077896 | tf_op jit(solution)/shard_map/ppermute | solution.py:691
  358.1 6.4 %collective-permute-start.23 = (f32[512,768]{1,0:T(8,128)}, f32[512,768]{1,0:T(8,128)}, u32[]{:S(2)}, u32[]{:S(2)}) collective-permute-start(f32[512,768]{1,0:T(8,128)} %convert_multiply_fusion.3.late_ref), channel_id=1, source_target_pairs={{0,1},{1,0},{2,3},{3,2},{4,5},{5,4},{6,7},{7,6},{8,9},{9,8},{10,11... | collective-permute-start | bytes 4718600 | tf_op jit(solution)/shard_map/ppermute | solution.py:691
  359.7 76.3 %all-to-all-start.2 = ((bf16[16,128,768]{2,1,0:T(8,128)(2,1)}), bf16[16,128,768]{2,1,0:T(8,128)(2,1)}, u32[]{:S(2)}, u32[]{:S(2)}) async-start(bf16[16,128,768]{2,1,0:T(8,128)(2,1)} %bitcast.133), calls=%async_computation.2 | async-start | bytes 6291456 | tf_op jit(solution)/shard_map/all_to_all | solution.py:848
  364.5 6.2 %copy-start.6 = (f32[942080]{0:T(1024)S(1)}, f32[942080]{0:T(1024)}, u32[]{:S(2)}) copy-start(f32[942080]{0:T(1024)} %param.15) | copy-start | bytes 11304964
  370.7 6.7 %copy-start.5 = (f32[7360,128]{1,0:T(8,128)S(1)}, f32[7360,128]{1,0:T(8,128)}, u32[]{:S(2)}) copy-start(f32[7360,128]{1,0:T(8,128)} %shard_map.139) | copy-start | bytes 11304964
  370.7 6.7 %copy-start.7 = (f32[942080]{0:T(1024)S(1)}, f32[942080]{0:T(1024)}, u32[]{:S(2)}) copy-start(f32[942080]{0:T(1024)} %param.15) | copy-start | bytes 11304964
  376.5 43.7 %collective-permute-start.24 = (f16[7360,128]{1,0:T(8,128)(2,1)}, f16[7360,128]{1,0:T(8,128)(2,1)}, u32[]{:S(2)}, u32[]{:S(2)}) collective-permute-start(f16[7360,128]{1,0:T(8,128)(2,1)} %divide_convert_fusion), channel_id=1, source_target_pairs={{0,2},{1,3},{2,0},{3,1},{4,6},{5,7},{6,4},{7,5},{8,10},{9,11},{10,... | collective-permute-start | bytes 5652488 | tf_op jit(solution)/shard_map/ppermute | solution.py:691
  377.3 19.0 %collective-permute-start.25 = (f16[7360,128]{1,0:T(8,128)(2,1)}, f16[7360,128]{1,0:T(8,128)(2,1)}, u32[]{:S(2)}, u32[]{:S(2)}) collective-permute-start(f16[7360,128]{1,0:T(8,128)(2,1)} %divide_convert_fusion), channel_id=1, source_target_pairs={{0,1},{1,0},{2,3},{3,2},{4,5},{5,4},{6,7},{7,6},{8,9},{9,8},{10,11... | collective-permute-start | bytes 5652488 | tf_op jit(solution)/shard_map/ppermute | solution.py:691
  377.4 13.5 %slice-start = ((s8[15073280]{0:T(1024)(128)(4,1)}), s8[4194304]{0:T(1024)(128)(4,1)S(1)}, s32[]{:S(2)}) async-start(s8[15073280]{0:T(1024)(128)(4,1)} %bitcast.118), calls=%async_computation.5 | async-start | bytes 8388608
  377.4 13.5 %slice-start.1 = ((s8[15073280]{0:T(1024)(128)(4,1)}), s8[4194304]{0:T(1024)(128)(4,1)S(1)}, s32[]{:S(2)}) async-start(s8[15073280]{0:T(1024)(128)(4,1)} %bitcast.118), calls=%async_computation.6 | async-start | bytes 8388608
  377.4 13.5 %slice-start.2 = ((s8[15073280]{0:T(1024)(128)(4,1)}), s8[2490368]{0:T(1024)(128)(4,1)S(1)}, s32[]{:S(2)}) async-start(s8[15073280]{0:T(1024)(128)(4,1)} %bitcast.118), calls=%async_computation.7 | async-start | bytes 4980736
  384.3 6.6 %slice-start.3 = ((s8[15073280]{0:T(1024)(128)(4,1)}), s8[4194304]{0:T(1024)(128)(4,1)S(1)}, s32[]{:S(2)}) async-start(s8[15073280]{0:T(1024)(128)(4,1)} %bitcast.118), calls=%async_computation.8 | async-start | bytes 8388608
  420.1 5.4 %collective-permute-start.26 = (f16[7360,128]{1,0:T(8,128)(2,1)}, f16[7360,128]{1,0:T(8,128)(2,1)S(1)}, u32[]{:S(2)}, u32[]{:S(2)}) collective-permute-start(f16[7360,128]{1,0:T(8,128)(2,1)} %collective-permute-done.24), channel_id=1, source_target_pairs={{0,1},{1,0},{2,3},{3,2},{4,5},{5,4},{6,7},{7,6},{8,9},{9,8},{10,11... | collective-permute-start | bytes 5652488 | tf_op jit(solution)/shard_map/ppermute | solution.py:691
  (13 other events, 30.0 us)
Sparse Core Ops, SparseCore 0:
  10.9 56.1 all-gather.2
  68.6 96.2 all-gather.4

commit v11 on v10

--- a/solution.py
+++ b/solution.py
@@ -256,7 +256,7 @@
             pltpu.VMEM((128, Q), F32),
         ],
         compiler_params=pltpu.CompilerParams(
-            dimension_semantics=("arbitrary",), vmem_limit_bytes=48 * 2**20),
+            dimension_semantics=("arbitrary",), vmem_limit_bytes=26 * 2**20),
         cost_estimate=pl.CostEstimate(
             flops=30 * 10**9, bytes_accessed=40 * 2**20, transcendentals=10**7),
     )(bound, cot_top, z, proj, gm, norm_gain, e2, et, *params)
@@ -494,7 +494,7 @@
             pltpu.VMEM((128, Q), F32),
         ],
         compiler_params=pltpu.CompilerParams(
-            dimension_semantics=("arbitrary",), vmem_limit_bytes=48 * 2**20),
+            dimension_semantics=("arbitrary",), vmem_limit_bytes=36 * 2**20),
         cost_estimate=pl.CostEstimate(
             flops=50 * 10**9, bytes_accessed=50 * 2**20, transcendentals=2 * 10**7),
     )(bound, proj, proj, dy, through, states, pair, tok, cot, in_w, norm_gain, ggain,

time: 455 us -> 467 us (1.026)
  local copies, waits for them, and re-layouts: 28.4 us -> 37.8 us
  starting transfers between devices: 56.8 us -> 63.7 us
    unnamed x58 -> x72, local copies, waits for them, and re-layouts: 6.26 us -> 16.8 us
    all_to_all x2, starting transfers between devices: 9.67 us -> 17.5 us  [send_back(): return lax.all_to_all(picked, 'dp', split_axis=0, concat_axis=0, tiled=True)]
  transfers between devices with their start and end apart: 32 -> 32, of which waited for: 12 -> 13; matrix products, arithmetic and copies ran while one was open for 31% -> 30% of each run, Pallas kernels for 23% -> 23%
where the time goes in v11:
time: 467 us; the launch traced here: 459 us
  waiting for transfers between devices  113 us (24%)
  Pallas kernels  103 us (22%)
  starting transfers between devices  63.7 us (14%)
  other arithmetic  63.1 us (14%)
  matrix products  60 us (13%)
  local copies, waits for them, and re-layouts  37.8 us (8%)
  between operations  18.2 us (4%)
    ppermute x27, waiting for transfers between devices, swap(): return lax.ppermute(values, axis, [(i, i ^ bit) for i in range(size)])  57.9 us
    pallas_call x1, Pallas kernels, run_backward(): pl.pallas_call(backward_kernel, grid=(steps,), in_specs=[pl.BlockSpec(mem...  55.3 us
    all_gather x1, waiting for transfers between devices, on_device(): flat = lax.all_gather(own.astype(BF16), 'zero', axis=0, tiled=True)  39.4 us
    ppermute x27, starting transfers between devices, swap(): return lax.ppermute(values, axis, [(i, i ^ bit) for i in range(size)])  38.8 us
    pallas_call x1, Pallas kernels, run_forward(): pl.pallas_call(forward_kernel, grid=(steps,), in_specs=[pl.BlockSpec(memo...  34 us
    dot_general x4, matrix products, product(): lax.dot_general(part, right, (((1,), (1,)), ((0,), (0,))), preferred_elem...  23.2 us
    dot_general x3, matrix products, dot(): lax.dot_general(a, b, (((1,), (0,)), ((), ())), preferred_element_type=F32)  21.3 us
    dynamic_update_slice x4, other arithmetic, put(): return lax.dynamic_update_index_in_dim(new_master, new, shard, 0)  19.2 us
  transfers between devices with their start and end apart: 32, of which 13 were waited for; matrix products, arithmetic and copies ran while one was open for 30% of the time, Pallas kernels for 23%

profile of v11, /device:TPU:0, one launch (start us, length us, event | category | flops | bytes accessed | tf_op | source)
XLA Modules:
  0.0 458.7 jit_solution(349179990956532235)
XLA Ops:
  7.2 3.5 bitcast_convert_fusion
  12.6 2.4 gather_fusion
  15.0 7.4 %all-to-all-start = ((bf16[16,128,768]{2,1,0:T(8,128)(2,1)}), bf16[16,128,768]{2,1,0:T(8,128)(2,1)}, u32[]{:S(2)}, u32[]{:S(2)}) async-start(bf16[16,128,768]{2,1,0:T(8,128)(2,1)} %gather_fusion), calls=%async_computation | async-start | bytes 6291456 | tf_op jit(solution)/shard_map/all_to_all | solution.py:819
  27.6 39.4 %all-gather.3.cloned.1.call-done.flat_ref = bf16[29440,128]{1,0:T(8,128)(2,1)} async-done(((bf16[7360,128]{1,0:T(8,128)(2,1)}), bf16[29440,128]{1,0:T(8,128)(2,1)}) %all-gather.3.cloned.1.call-update) | async-done | bytes 7536656 | tf_op jit(solution)/shard_map/all_gather | solution.py:817
  67.0 7.8 %shard_map.136 = (bf16[3584,768]{1,0:T(8,128)(2,1)S(1)}, bf16[1536,768]{1,0:T(8,128)(2,1)}, f32[1,768]{1,0:T(1,128)S(1)}, f32[8,1792]{1,0:T(8,128)S(1)}, f32[1,1...) custom-call(bf16[29440,128]{1,0:T(8,128)(2,1)} %all-gather.3.cloned., ...), custom_call_target="tpu_custom_call" | custom-call | flops 1000000000 | bytes 16777216 | tf_op jit(solution)/shard_map/pallas_call | solution.py:593
  74.8 2.8 copy-done.1
  78.5 7.0 %fusion.94.gm_ref = f32[1024,1536]{1,0:T(8,128)} fusion(bf16[1536,768]{1,0:T(8,128)(2,1)} %get-tuple-element.76, bf16[1,1024,768]{2,1,0:T(8,128)(2,1)S(1)} %copy-done), kind=kOutput, calls=%fused_computation.260 | convolution fusion | flops 2415919104 | bytes 10223616 | tf_op jit(solution)/shard_map/dot_general | solution.py:33
  85.5 7.7 %all-to-all-done = bf16[16,128,768]{2,1,0:T(8,128)(2,1)} async-done(((bf16[16,128,768]{2,1,0:T(8,128)(2,1)}), bf16[16,128,768]{2,1,0:T(8,128)(2,1)}, u32[]{:S(2)}, u32[]{:S(2)}) %all-to-all-start) | async-done | bytes 3145760 | tf_op jit(solution)/shard_map/all_to_all | solution.py:819
  93.3 5.8 %fusion.21 = (f32[1024]{0:T(1024)S(1)}, bf16[1024,768]{1,0:T(8,128)(2,1)S(1)}) fusion(bf16[2048,768]{1,0:T(8,128)(2,1)} %bitcast.6, s32[1024]{0:T(1024)S(1)} %fusion.61), kind=kOutput, calls=%fused_computation.52 | convolution fusion | flops 3226467328 | bytes 4726784 | tf_op jit(solution)/shard_map/dot_general | solution.py:29
  99.1 2.7 fusion.41.z_ref
  101.8 5.8 %fusion.35.proj_ref.before_ref = f32[1024,1816]{1,0:T(8,128)} fusion(bf16[3584,768]{1,0:T(8,128)(2,1)S(1)} %copy-done.2, bf16[1024,768]{1,0:T(8,128)(2,1)S(1)} %get-tuple-element.207.tok_ref, f32[768]{0:T(1024)S(1)} %reduce.2, f32[1024]{0:T(1024)S(1)} %add_rsqrt_fusion), kind=kOutput, calls=%fused_computation.68 | convolution fusion | flops 2859466752 | bytes 11808768 | tf_op jit(solution)/shard_map/dot_general | solution.py:33
  107.6 34.0 %shard_map.137 = (bf16[2,1024,1536]{2,1,0:T(8,128)(2,1)S(1)}, f32[1024,1536]{1,0:T(8,128)S(1)}, f32[1024,128]{1,0:T(8,128)S(1)}, f32[8,128,1536]{2,1,0:T(8,128)S...) custom-call(s32[1]{0:T(128)} %dynamic_slice.148.bound_ref, f32[1]{0:T(128)S(6)} %convert.1.cot_ref, ...), custom_call_target="tpu_custom_call" | custom-call | flops 30000001024 | bytes 41943040 | tf_op jit(solution)/shard_map/pallas_call | solution.py:221
  141.6 2.6 copy-done.9
  144.1 2.7 copy-done.14
  146.8 2.6 copy-done.15
  150.2 10.4 %fusion.20 = bf16[2048,768]{1,0:T(8,128)(2,1)} fusion(s32[2048]{0:T(1024)S(1)} %get-tuple-element.203, bf16[1024,768]{1,0:T(8,128)(2,1)S(1)} %get-tuple-element.207.tok_ref, bf16[1536,768]{1,0:T(8,128)(2,1)} %get-tuple-element.76, bf16[2,1024,1536]{2,1,0:T(8,128)(2,1)} %copy-done.9), kind=kOutput, calls=%fused_computation.51 | convolution fusion | flops 5643173888 | bytes 10231808 | tf_op jit(solution)/shard_map/dot_general | solution.py:29
  162.3 9.1 %select_convert_fusion = f16[2,896,768]{2,1,0:T(8,128)(2,1)} fusion(f32[]{:T(128)} %bitcast.12, f32[]{:T(128)} %bitcast.10, pred[896]{0:T(1024)(128)(4,1)S(1)} %fusion.71, bf16[1,1024,768]{2,1,0:T(8,128)(2,1)S(1)} %fusion.101, bf16[1,1024,768]{2,1,0:T(8,128)(2,1)S(1)} %copy-done, bf16[2,1024,1536]{2,1,0:T(8,128)(2,1)} %copy-done.9, pred[]{:T(512)S(6)} %eq.123), kind=kOutput, calls=%fused_computation.11 | convolution fusion | flops 2826108928 | bytes 13240193 | tf_op jit(solution)/shard_map/dot_general | solution.py:735
  172.2 12.7 %all-to-all-start.1 = ((bf16[16,128,768]{2,1,0:T(8,128)(2,1)}), bf16[16,128,768]{2,1,0:T(8,128)(2,1)}, u32[]{:S(2)}, u32[]{:S(2)}) async-start(bf16[16,128,768]{2,1,0:T(8,128)(2,1)} %bitcast.135), calls=%async_computation.1 | async-start | bytes 6291456 | tf_op jit(solution)/shard_map/all_to_all | solution.py:848
  184.9 6.1 %fusion.27 = f32[2,768,768]{2,1,0:T(8,128)S(1)} fusion(bf16[2,1024,1536]{2,1,0:T(8,128)(2,1)} %copy-done.9, pred[]{:T(512)S(6)} %eq.116, bf16[1,1024,768]{2,1,0:T(8,128)(2,1)} %copy-done.23, bf16[1,1024,768]{2,1,0:T(8,128)(2,1)S(1)} %copy-done), kind=kOutput, calls=%fused_computation.59 | convolution fusion | flops 2419064832 | bytes 14155777 | tf_op jit(solution)/shard_map/dot_general | solution.py:735
  196.6 55.3 %shard_map.138 = (bf16[2,1024,1024]{2,1,0:T(8,128)(2,1)S(1)}, bf16[1024,768]{1,0:T(8,128)(2,1)S(1)}, f32[48,768]{1,0:T(8,128)S(1)}, f32[8,128]{1,0:T(8,128)S(1)}) custom-call(s32[1]{0:T(128)} %dynamic_slice.148.bound_ref, f32[1024,1816]{1,0:T(8,128)} %fusion.35.proj_ref.before_ref, f32[1024,1816]{1,0:T(8,128)} %fusion.35.proj_ref.before_ref, ...), custom_call_target="tpu_custom_call" | custom-call | flops 49999998976 | bytes 52428800 | tf_op jit(solution)/shard_map/pallas_call | solution.py:453
  258.1 5.9 %select_convert_fusion.1 = f16[2,640,768]{2,1,0:T(8,128)(2,1)S(1)} fusion(f32[]{:T(128)} %bitcast.16, f32[]{:T(128)} %bitcast.15, pred[640]{0:T(1024)(128)(4,1)S(1)} %fusion.73, bf16[1,1024,768]{2,1,0:T(8,128)(2,1)S(1)} %copy-done.24, bf16[2,1024,1024]{2,1,0:T(8,128)(2,1)} %copy-done.10, pred[]{:T(512)S(6)} %eq.123), kind=kOutput, calls=%fused_computation.19 | convolution fusion | flops 2019098624 | bytes 8783489 | tf_op jit(solution)/shard_map/dot_general | solution.py:735
  272.8 2.3 select_convert_fusion.4
  276.9 4.3 gather_fusion.1
  281.2 4.3 broadcast_select_fusion
  285.5 5.1 %fusion.19 = bf16[2048,768]{1,0:T(8,128)(2,1)} fusion(bf16[1024,768]{1,0:T(8,128)(2,1)S(1)} %copy-done.13, s32[2048]{0:T(1024)S(1)} %copy-done.26), kind=kOutput, calls=%fused_computation.50 | convolution fusion | flops 3224895488 | bytes 4726784 | tf_op jit(solution)/shard_map/dot_general | solution.py:29
  300.6 2.4 collective-permute-start.6
  303.6 4.7 %collective-permute-done.10 = f16[336,768]{1,0:T(8,128)(2,1)S(1)} collective-permute-done((f16[336,768]{1,0:T(8,128)(2,1)S(1)}, f16[336,768]{1,0:T(8,128)(2,1)S(1)}, u32[]{:S(2)}, u32[]{:S(2)}) %collective-permute-start.10) | collective-permute-done | bytes 516128 | tf_op jit(solution)/shard_map/ppermute | solution.py:691
  310.1 2.4 collective-permute-start.16
  312.5 4.3 collective-permute-done.6
  317.0 2.4 collective-permute-start.11
  319.5 13.2 %collective-permute-start.12 = (f16[96,768]{1,0:T(8,128)(2,1)S(1)}, f16[96,768]{1,0:T(8,128)(2,1)S(1)}, u32[]{:S(2)}, u32[]{:S(2)}) collective-permute-start(f16[96,768]{1,0:T(8,128)(2,1)S(1)} %multiply_convert_fusion), channel_id=1, source_target_pairs={{0,16},{4,20},{8,24},{12,28},{16,0},{20,4},{24,8},{28,12},{1,17},{... | collective-permute-start | bytes 442376 | tf_op jit(solution)/shard_map/ppermute | solution.py:691
  332.6 5.6 %collective-permute-done.15 = f16[96,768]{1,0:T(8,128)(2,1)S(1)} collective-permute-done((f16[96,768]{1,0:T(8,128)(2,1)S(1)}, f16[96,768]{1,0:T(8,128)(2,1)S(1)}, u32[]{:S(2)}, u32[]{:S(2)}) %collective-permute-start.15) | collective-permute-done | bytes 147488 | tf_op jit(solution)/shard_map/ppermute | solution.py:691
  338.3 4.4 collective-permute-done.12
  348.4 3.2 collective-permute-done.19
  351.5 3.8 collective-permute-done.20
  357.5 10.2 %collective-permute-done.22 = f16[320,768]{1,0:T(8,128)(2,1)S(1)} collective-permute-done((f16[320,768]{1,0:T(8,128)(2,1)S(1)}, f16[320,768]{1,0:T(8,128)(2,1)S(1)}, u32[]{:S(2)}, u32[]{:S(2)}) %collective-permute-start.22) | collective-permute-done | bytes 491552 | tf_op jit(solution)/shard_map/ppermute | solution.py:691
  370.8 4.8 %all-to-all-start.2 = ((bf16[16,128,768]{2,1,0:T(8,128)(2,1)}), bf16[16,128,768]{2,1,0:T(8,128)(2,1)}, u32[]{:S(2)}, u32[]{:S(2)}) async-start(bf16[16,128,768]{2,1,0:T(8,128)(2,1)} %bitcast.136), calls=%async_computation.2 | async-start | bytes 6291456 | tf_op jit(solution)/shard_map/all_to_all | solution.py:848
  375.6 6.1 %shard_map.139 = f32[7360,128]{1,0:T(8,128)} custom-call(s32[2]{0:T(128)S(1)} %pad_add_fusion.1.who_ref, f32[768,768]{1,0:T(8,128)S(1)} %convert_multiply_fusion.2.early_ref, f32[768,768]{1,0:T(8,128)} %collective-permute-done.18.early_other_ref, f32[512,768]{1,0:T(8,128)} %convert_multiply_fusion.3.late_ref, ...), custom_call_target="tpu_custom_call" | custom-call | flops 1000000 | bytes 12582912 | tf_op jit(solution)/shard_map/pallas_call | solution.py:671
  381.8 5.8 %divide_convert_fusion = f16[7360,128]{1,0:T(8,128)(2,1)} fusion(f32[7360,128]{1,0:T(8,128)} %shard_map.139, f32[]{:T(128)} %bitcast.26, f32[]{:T(128)} %bitcast.24, f32[942080]{0:T(1024)S(1)} %copy-done.19, f32[942080]{0:T(1024)} %param.14), kind=kLoop, calls=%fused_computation.42 | loop fusion | flops 11304960 | bytes 13189128 | tf_op jit(solution)/shard_map/convert_element_type | solution.py:937
  388.6 6.9 %multiply_add_fusion.1 = (f32[7360,128]{1,0:T(8,128)}, f32[7360,128]{1,0:T(8,128)}) fusion(f32[7360,128]{1,0:T(8,128)S(1)} %bitcast.129, f32[7360,128]{1,0:T(8,128)S(1)} %copy-done.18, f32[7360,128]{1,0:T(8,128)} %bitcast.130), kind=kLoop, calls=%fused_computation.40 | loop fusion | flops 6594560 | bytes 18841600 | tf_op jit(solution)/shard_map/add | solution.py:932
  395.5 6.6 %broadcast_in_dim.146 = f32[4,7360,128]{2,1,0:T(8,128)} broadcast(f32[]{:T(128)} %constant.309.clone.1), dimensions={} | broadcast | bytes 15073284 | tf_op jit(solution)/shard_map/broadcast_in_dim | solution.py:894
  402.1 5.2 %bitcast_dynamic-update-slice_fusion.3 = f32[4,7360,128]{2,1,0:T(8,128)} fusion(f32[4,7360,128]{2,1,0:T(8,128)} %broadcast_in_dim.146, s32[]{:T(128)S(6)} %select_n.595, f16[7360,128]{1,0:T(8,128)(2,1)} %divide_convert_fusion, f32[4,7360,128]{2,1,0:T(8,128)S(1)} %bitcast.123, f32[]{:T(128)} %bitcast.30, f32[]{:T(128)} %bitcast.29), kind=kLoop, calls=%fused_computation.35 | loop fusion | flops 4710400 | bytes 9421828 | tf_op jit(solution)/shard_map/jit(dynamic_update_index_in_dim)/dynamic_update_slice | solution.py:945
  407.3 5.2 %bitcast_dynamic-update-slice_fusion.2 = f32[4,7360,128]{2,1,0:T(8,128)} fusion(f32[4,7360,128]{2,1,0:T(8,128)} %bitcast_dynamic-update-slice_fusion.3, s32[]{:T(128)S(6)} %select_n.720, f16[7360,128]{1,0:T(8,128)(2,1)} %collective-permute-done.25, f32[4,7360,128]{2,1,0:T(8,128)S(1)} %bitcast.124, f32[]{:T(128)} %bitcast.30, f32[]{:T(128)} %bitcast.29), kind=kLoop, calls=%fused_computation.30 | loop fusion | flops 4710400 | bytes 9421828 | tf_op jit(solution)/shard_map/jit(dynamic_update_index_in_dim)/dynamic_update_slice | solution.py:945
  412.5 18.8 %collective-permute-done.24 = f16[7360,128]{1,0:T(8,128)(2,1)} collective-permute-done((f16[7360,128]{1,0:T(8,128)(2,1)}, f16[7360,128]{1,0:T(8,128)(2,1)}, u32[]{:S(2)}, u32[]{:S(2)}) %collective-permute-start.24) | collective-permute-done | bytes 1884192 | tf_op jit(solution)/shard_map/ppermute | solution.py:691
  431.3 5.2 %bitcast_dynamic-update-slice_fusion.1 = f32[4,7360,128]{2,1,0:T(8,128)} fusion(f32[4,7360,128]{2,1,0:T(8,128)} %bitcast_dynamic-update-slice_fusion.2, s32[]{:T(128)S(6)} %select_n.721, f16[7360,128]{1,0:T(8,128)(2,1)} %collective-permute-done.24, f32[4,7360,128]{2,1,0:T(8,128)S(1)} %bitcast.125, f32[]{:T(128)} %bitcast.30, f32[]{:T(128)} %bitcast.29), kind=kLoop, calls=%fused_computation.25 | loop fusion | flops 4710400 | bytes 9421828 | tf_op jit(solution)/shard_map/jit(dynamic_update_index_in_dim)/dynamic_update_slice | solution.py:945
  436.5 3.7 bitcast_dynamic-update-slice_fusion
  440.2 6.9 %all-to-all-done.2 = bf16[16,128,768]{2,1,0:T(8,128)(2,1)} async-done(((bf16[16,128,768]{2,1,0:T(8,128)(2,1)}), bf16[16,128,768]{2,1,0:T(8,128)(2,1)}, u32[]{:S(2)}, u32[]{:S(2)}) %all-to-all-start.2) | async-done | bytes 3145760 | tf_op jit(solution)/shard_map/all_to_all | solution.py:848
  447.1 4.3 gather_fusion.2
  (200 shorter events, 54.9 us)
Async XLA Ops:
  7.2 59.9 %all-gather.3.cloned.1.call-start = ((), (), s32[]{:S(2)}) async-start(), calls=%async_computation.3 | async-start | bytes 9420800 | tf_op jit(solution)/shard_map/all_gather | solution.py:817
  10.7 246.1 %all-gather.5.cloned.1.call-start = ((), (), s32[]{:S(2)}) async-start(), calls=%async_computation.4 | async-start | bytes 18841600 | tf_op jit(solution)/shard_map/all_gather | solution.py:830
  15.0 7.4 %copy-start = (bf16[1,1024,768]{2,1,0:T(8,128)(2,1)S(1)}, bf16[1,1024,768]{2,1,0:T(8,128)(2,1)}, u32[]{:S(2)}) copy-start(bf16[1,1024,768]{2,1,0:T(8,128)(2,1)} %param.10) | copy-start | bytes 4718596
  15.0 9.2 %copy-start.29 = (s32[64]{0:T(128)S(1)}, s32[64]{0:T(128)}, u32[]{:S(2)}) copy-start(s32[64]{0:T(128)} %param.11) | copy-start | bytes 772
  15.0 78.2 %all-to-all-start = ((bf16[16,128,768]{2,1,0:T(8,128)(2,1)}), bf16[16,128,768]{2,1,0:T(8,128)(2,1)}, u32[]{:S(2)}, u32[]{:S(2)}) async-start(bf16[16,128,768]{2,1,0:T(8,128)(2,1)} %gather_fusion), calls=%async_computation | async-start | bytes 6291456 | tf_op jit(solution)/shard_map/all_to_all | solution.py:819
  78.5 7.0 %copy-start.6 = (bf16[1536,128]{1,0:T(8,128)(2,1)}, bf16[1536,128]{1,0:T(8,128)(2,1)S(1)}, u32[]{:S(2)}) copy-start(bf16[1536,128]{1,0:T(8,128)(2,1)S(1)} %get-tuple-element.83.et_ref) | copy-start | bytes 1179652
  93.2 5.8 %copy-start.2 = (bf16[3584,768]{1,0:T(8,128)(2,1)S(1)}, bf16[3584,768]{1,0:T(8,128)(2,1)}, u32[]{:S(2)}) copy-start(bf16[3584,768]{1,0:T(8,128)(2,1)} %copy-done.1) | copy-start | bytes 16515076
  101.8 5.8 %copy-start.4 = (bf16[256,1536]{1,0:T(8,128)(2,1)S(1)}, bf16[256,1536]{1,0:T(8,128)(2,1)}, u32[]{:S(2)}) copy-start(bf16[256,1536]{1,0:T(8,128)(2,1)} %copy-done.3) | copy-start | bytes 2359300
  101.8 5.8 %copy-start.7 = (bf16[1536,128]{1,0:T(8,128)(2,1)S(1)}, bf16[1536,128]{1,0:T(8,128)(2,1)}, u32[]{:S(2)}) copy-start(bf16[1536,128]{1,0:T(8,128)(2,1)} %copy-done.6) | copy-start | bytes 1179652
  162.3 9.1 %copy-start.23 = (bf16[1,1024,768]{2,1,0:T(8,128)(2,1)}, bf16[1,1024,768]{2,1,0:T(8,128)(2,1)S(1)}, u32[]{:S(2)}) copy-start(bf16[1,1024,768]{2,1,0:T(8,128)(2,1)S(1)} %fusion.101) | copy-start | bytes 4718596
  171.4 19.6 %collective-permute-start = (f16[2,896,768]{2,1,0:T(8,128)(2,1)}, f16[2,896,768]{2,1,0:T(8,128)(2,1)}, u32[]{:S(2)}, u32[]{:S(2)}) collective-permute-start(f16[2,896,768]{2,1,0:T(8,128)(2,1)} %select_convert_fusion), channel_id=1, source_target_pairs={{0,1},{1,0},{2,3},{3,2},{4,5},{5,4},{6,7},{7,6},{8,9},{9,8},{10,11... | collective-permute-start | bytes 8257544 | tf_op jit(solution)/shard_map/ppermute | solution.py:691
  172.2 100.6 %all-to-all-start.1 = ((bf16[16,128,768]{2,1,0:T(8,128)(2,1)}), bf16[16,128,768]{2,1,0:T(8,128)(2,1)}, u32[]{:S(2)}, u32[]{:S(2)}) async-start(bf16[16,128,768]{2,1,0:T(8,128)(2,1)} %bitcast.135), calls=%async_computation.1 | async-start | bytes 6291456 | tf_op jit(solution)/shard_map/all_to_all | solution.py:848
  195.1 60.0 %collective-permute-start.1 = (f16[784,768]{1,0:T(8,128)(2,1)S(1)}, f16[784,768]{1,0:T(8,128)(2,1)S(1)}, u32[]{:S(2)}, u32[]{:S(2)}) collective-permute-start(f16[784,768]{1,0:T(8,128)(2,1)S(1)} %select_convert_fusion.2), channel_id=1, source_target_pairs={{0,2},{1,3},{2,0},{3,1},{4,6},{5,7},{6,4},{7,5},{8,10},{9,11},{10,... | collective-permute-start | bytes 3612680 | tf_op jit(solution)/shard_map/ppermute | solution.py:691
  258.1 6.7 %copy-start.11 = (bf16[2,1024,1024]{2,1,0:T(8,128)(2,1)S(1)}, bf16[2,1024,1024]{2,1,0:T(8,128)(2,1)}, u32[]{:S(2)}) copy-start(bf16[2,1024,1024]{2,1,0:T(8,128)(2,1)} %copy-done.10) | copy-start | bytes 12582916
  264.0 5.5 %collective-permute-start.2 = (f16[2,640,768]{2,1,0:T(8,128)(2,1)S(1)}, f16[2,640,768]{2,1,0:T(8,128)(2,1)S(1)}, u32[]{:S(2)}, u32[]{:S(2)}) collective-permute-start(f16[2,640,768]{2,1,0:T(8,128)(2,1)S(1)} %select_convert_fusion.1), channel_id=1, source_target_pairs={{0,1},{1,0},{2,3},{3,2},{4,5},{5,4},{6,7},{7,6},{8,9},{9,8},{10,11... | collective-permute-start | bytes 5898248 | tf_op jit(solution)/shard_map/ppermute | solution.py:691
  264.6 3.7 collective-permute-start.8
  268.3 26.7 %collective-permute-start.9 = (f32[48,768]{1,0:T(8,128)S(1)}, f32[48,768]{1,0:T(8,128)S(1)}, u32[]{:S(2)}, u32[]{:S(2)}) collective-permute-start(f32[48,768]{1,0:T(8,128)S(1)} %add.432), channel_id=1, source_target_pairs={{0,2},{1,3},{2,0},{3,1},{4,6},{5,7},{6,4},{7,5},{8,10},{9,11},{10,... | collective-permute-start | bytes 442376 | tf_op jit(solution)/shard_map/ppermute | solution.py:691
  271.9 20.4 %collective-permute-start.3 = (f16[528,768]{1,0:T(8,128)(2,1)}, f16[528,768]{1,0:T(8,128)(2,1)}, u32[]{:S(2)}, u32[]{:S(2)}) collective-permute-start(f16[528,768]{1,0:T(8,128)(2,1)} %select_convert_fusion.3), channel_id=1, source_target_pairs={{0,2},{1,3},{2,0},{3,1},{4,6},{5,7},{6,4},{7,5},{8,10},{9,11},{10,... | collective-permute-start | bytes 2433032 | tf_op jit(solution)/shard_map/ppermute | solution.py:691
  275.1 21.8 %collective-permute-start.4 = (f16[400,768]{1,0:T(8,128)(2,1)}, f16[400,768]{1,0:T(8,128)(2,1)}, u32[]{:S(2)}, u32[]{:S(2)}) collective-permute-start(f16[400,768]{1,0:T(8,128)(2,1)} %select_convert_fusion.4), channel_id=1, source_target_pairs={{0,4},{4,0},{8,12},{12,8},{16,20},{20,16},{24,28},{28,24},{1,5},{5... | collective-permute-start | bytes 1843208 | tf_op jit(solution)/shard_map/ppermute | solution.py:691
  295.4 13.0 %collective-permute-start.10 = (f16[336,768]{1,0:T(8,128)(2,1)S(1)}, f16[336,768]{1,0:T(8,128)(2,1)S(1)}, u32[]{:S(2)}, u32[]{:S(2)}) collective-permute-start(f16[336,768]{1,0:T(8,128)(2,1)S(1)} %select_convert_fusion.5), channel_id=1, source_target_pairs={{0,4},{4,0},{8,12},{12,8},{16,20},{20,16},{24,28},{28,24},{1,5},{5... | collective-permute-start | bytes 1548296 | tf_op jit(solution)/shard_map/ppermute | solution.py:691
  299.1 13.3 %collective-permute-start.5 = (f16[112,768]{1,0:T(8,128)(2,1)S(1)}, f16[112,768]{1,0:T(8,128)(2,1)S(1)}, u32[]{:S(2)}, u32[]{:S(2)}) collective-permute-start(f16[112,768]{1,0:T(8,128)(2,1)S(1)} %get-tuple-element.175), channel_id=1, source_target_pairs={{0,8},{4,12},{8,0},{12,4},{16,24},{20,28},{24,16},{28,20},{1,9},{5... | collective-permute-start | bytes 516104 | tf_op jit(solution)/shard_map/ppermute | solution.py:691
  300.6 16.2 %collective-permute-start.6 = (f16[112,768]{1,0:T(8,128)(2,1)S(1)}, f16[112,768]{1,0:T(8,128)(2,1)S(1)}, u32[]{:S(2)}, u32[]{:S(2)}) collective-permute-start(f16[112,768]{1,0:T(8,128)(2,1)S(1)} %get-tuple-element.174), channel_id=1, source_target_pairs={{0,16},{4,20},{8,24},{12,28},{16,0},{20,4},{24,8},{28,12},{1,17},{... | collective-permute-start | bytes 516104 | tf_op jit(solution)/shard_map/ppermute | solution.py:691
  303.0 13.8 %collective-permute-start.7 = (f16[112,768]{1,0:T(8,128)(2,1)S(1)}, f16[112,768]{1,0:T(8,128)(2,1)S(1)}, u32[]{:S(2)}, u32[]{:S(2)}) collective-permute-start(f16[112,768]{1,0:T(8,128)(2,1)S(1)} %get-tuple-element.173), channel_id=1, source_target_pairs={{0,24},{4,28},{8,16},{12,20},{16,8},{20,12},{24,0},{28,4},{1,25},{... | collective-permute-start | bytes 516104 | tf_op jit(solution)/shard_map/ppermute | solution.py:691
  308.7 23.9 %collective-permute-start.14 = (f16[96,768]{1,0:T(8,128)(2,1)S(1)}, f16[96,768]{1,0:T(8,128)(2,1)S(1)}, u32[]{:S(2)}, u32[]{:S(2)}) collective-permute-start(f16[96,768]{1,0:T(8,128)(2,1)S(1)} %get-tuple-element.180), channel_id=1, source_target_pairs={{0,8},{4,12},{8,0},{12,4},{16,24},{20,28},{24,16},{28,20},{1,9},{5... | collective-permute-start | bytes 442376 | tf_op jit(solution)/shard_map/ppermute | solution.py:691
  310.1 22.6 %collective-permute-start.16 = (f16[96,768]{1,0:T(8,128)(2,1)S(1)}, f16[96,768]{1,0:T(8,128)(2,1)S(1)}, u32[]{:S(2)}, u32[]{:S(2)}) collective-permute-start(f16[96,768]{1,0:T(8,128)(2,1)S(1)} %get-tuple-element.178), channel_id=1, source_target_pairs={{0,24},{4,28},{8,16},{12,20},{16,8},{20,12},{24,0},{28,4},{1,25},{... | collective-permute-start | bytes 442376 | tf_op jit(solution)/shard_map/ppermute | solution.py:691
  312.4 25.8 %collective-permute-start.15 = (f16[96,768]{1,0:T(8,128)(2,1)S(1)}, f16[96,768]{1,0:T(8,128)(2,1)S(1)}, u32[]{:S(2)}, u32[]{:S(2)}) collective-permute-start(f16[96,768]{1,0:T(8,128)(2,1)S(1)} %get-tuple-element.179), channel_id=1, source_target_pairs={{0,16},{4,20},{8,24},{12,28},{16,0},{20,4},{24,8},{28,12},{1,17},{... | collective-permute-start | bytes 442376 | tf_op jit(solution)/shard_map/ppermute | solution.py:691
  317.0 21.3 %collective-permute-start.11 = (f16[96,768]{1,0:T(8,128)(2,1)S(1)}, f16[96,768]{1,0:T(8,128)(2,1)S(1)}, u32[]{:S(2)}, u32[]{:S(2)}) collective-permute-start(f16[96,768]{1,0:T(8,128)(2,1)S(1)} %multiply_convert_fusion), channel_id=1, source_target_pairs={{0,24},{4,28},{8,16},{12,20},{16,8},{20,12},{24,0},{28,4},{1,25},{... | collective-permute-start | bytes 442376 | tf_op jit(solution)/shard_map/ppermute | solution.py:691
  319.5 23.2 %collective-permute-start.12 = (f16[96,768]{1,0:T(8,128)(2,1)S(1)}, f16[96,768]{1,0:T(8,128)(2,1)S(1)}, u32[]{:S(2)}, u32[]{:S(2)}) collective-permute-start(f16[96,768]{1,0:T(8,128)(2,1)S(1)} %multiply_convert_fusion), channel_id=1, source_target_pairs={{0,16},{4,20},{8,24},{12,28},{16,0},{20,4},{24,8},{28,12},{1,17},{... | collective-permute-start | bytes 442376 | tf_op jit(solution)/shard_map/ppermute | solution.py:691
  332.6 10.0 %collective-permute-start.13 = (f16[96,768]{1,0:T(8,128)(2,1)S(1)}, f16[96,768]{1,0:T(8,128)(2,1)S(1)}, u32[]{:S(2)}, u32[]{:S(2)}) collective-permute-start(f16[96,768]{1,0:T(8,128)(2,1)S(1)} %multiply_convert_fusion), channel_id=1, source_target_pairs={{0,8},{4,12},{8,0},{12,4},{16,24},{20,28},{24,16},{28,20},{1,9},{5... | collective-permute-start | bytes 442376 | tf_op jit(solution)/shard_map/ppermute | solution.py:691
  343.2 13.7 %collective-permute-start.17 = (f16[384,768]{1,0:T(8,128)(2,1)S(1)}, f16[384,768]{1,0:T(8,128)(2,1)S(1)}, u32[]{:S(2)}, u32[]{:S(2)}) collective-permute-start(f16[384,768]{1,0:T(8,128)(2,1)S(1)} %pad_maximum_fusion.11), channel_id=1, source_target_pairs={{0,4},{4,0},{8,12},{12,8},{16,20},{20,16},{24,28},{28,24},{1,5},{5... | collective-permute-start | bytes 1769480 | tf_op jit(solution)/shard_map/ppermute | solution.py:691
  344.0 7.6 %collective-permute-start.19 = (f16[80,768]{1,0:T(8,128)(2,1)S(1)}, f16[80,768]{1,0:T(8,128)(2,1)S(1)}, u32[]{:S(2)}, u32[]{:S(2)}) collective-permute-start(f16[80,768]{1,0:T(8,128)(2,1)S(1)} %multiply_convert_fusion.1), channel_id=1, source_target_pairs={{0,24},{4,28},{8,16},{12,20},{16,8},{20,12},{24,0},{28,4},{1,25},{... | collective-permute-start | bytes 368648 | tf_op jit(solution)/shard_map/ppermute | solution.py:691
  346.3 9.0 %collective-permute-start.20 = (f16[80,768]{1,0:T(8,128)(2,1)S(1)}, f16[80,768]{1,0:T(8,128)(2,1)S(1)}, u32[]{:S(2)}, u32[]{:S(2)}) collective-permute-start(f16[80,768]{1,0:T(8,128)(2,1)S(1)} %multiply_convert_fusion.1), channel_id=1, source_target_pairs={{0,16},{4,20},{8,24},{12,28},{16,0},{20,4},{24,8},{28,12},{1,17},{... | collective-permute-start | bytes 368648 | tf_op jit(solution)/shard_map/ppermute | solution.py:691
  346.3 9.0 %collective-permute-start.21 = (f16[80,768]{1,0:T(8,128)(2,1)S(1)}, f16[80,768]{1,0:T(8,128)(2,1)S(1)}, u32[]{:S(2)}, u32[]{:S(2)}) collective-permute-start(f16[80,768]{1,0:T(8,128)(2,1)S(1)} %multiply_convert_fusion.1), channel_id=1, source_target_pairs={{0,8},{4,12},{8,0},{12,4},{16,24},{20,28},{24,16},{28,20},{1,9},{5... | collective-permute-start | bytes 368648 | tf_op jit(solution)/shard_map/ppermute | solution.py:691
  355.6 12.1 %collective-permute-start.22 = (f16[320,768]{1,0:T(8,128)(2,1)S(1)}, f16[320,768]{1,0:T(8,128)(2,1)S(1)}, u32[]{:S(2)}, u32[]{:S(2)}) collective-permute-start(f16[320,768]{1,0:T(8,128)(2,1)S(1)} %pad_maximum_fusion.12), channel_id=1, source_target_pairs={{0,4},{4,0},{8,12},{12,8},{16,20},{20,16},{24,28},{28,24},{1,5},{5... | collective-permute-start | bytes 1474568 | tf_op jit(solution)/shard_map/ppermute | solution.py:691
  357.4 12.8 %copy-start.27 = (f32[2]{0:T(128)S(1)}, f32[2]{0:T(128)}, u32[]{:S(2)}) copy-start(f32[2]{0:T(128)} %param.16) | copy-start | bytes 28
  357.4 18.2 %collective-permute-start.18 = (f32[768,768]{1,0:T(8,128)S(1)}, f32[768,768]{1,0:T(8,128)}, u32[]{:S(2)}, u32[]{:S(2)}) collective-permute-start(f32[768,768]{1,0:T(8,128)S(1)} %convert_multiply_fusion.2.early_ref), channel_id=1, source_target_pairs={{0,1},{1,0},{2,3},{3,2},{4,5},{5,4},{6,7},{7,6},{8,9},{9,8},{10,11... | collective-permute-start | bytes 7077896 | tf_op jit(solution)/shard_map/ppermute | solution.py:691
  369.3 6.3 %collective-permute-start.23 = (f32[512,768]{1,0:T(8,128)}, f32[512,768]{1,0:T(8,128)}, u32[]{:S(2)}, u32[]{:S(2)}) collective-permute-start(f32[512,768]{1,0:T(8,128)} %convert_multiply_fusion.3.late_ref), channel_id=1, source_target_pairs={{0,1},{1,0},{2,3},{3,2},{4,5},{5,4},{6,7},{7,6},{8,9},{9,8},{10,11... | collective-permute-start | bytes 4718600 | tf_op jit(solution)/shard_map/ppermute | solution.py:691
  370.8 76.4 %all-to-all-start.2 = ((bf16[16,128,768]{2,1,0:T(8,128)(2,1)}), bf16[16,128,768]{2,1,0:T(8,128)(2,1)}, u32[]{:S(2)}, u32[]{:S(2)}) async-start(bf16[16,128,768]{2,1,0:T(8,128)(2,1)} %bitcast.136), calls=%async_computation.2 | async-start | bytes 6291456 | tf_op jit(solution)/shard_map/all_to_all | solution.py:848
  375.6 6.2 %copy-start.19 = (f32[942080]{0:T(1024)S(1)}, f32[942080]{0:T(1024)}, u32[]{:S(2)}) copy-start(f32[942080]{0:T(1024)} %param.15) | copy-start | bytes 11304964
  381.8 6.8 %copy-start.18 = (f32[7360,128]{1,0:T(8,128)S(1)}, f32[7360,128]{1,0:T(8,128)}, u32[]{:S(2)}) copy-start(f32[7360,128]{1,0:T(8,128)} %shard_map.139) | copy-start | bytes 11304964
  381.8 6.8 %copy-start.20 = (f32[942080]{0:T(1024)S(1)}, f32[942080]{0:T(1024)}, u32[]{:S(2)}) copy-start(f32[942080]{0:T(1024)} %param.15) | copy-start | bytes 11304964
  387.6 43.7 %collective-permute-start.24 = (f16[7360,128]{1,0:T(8,128)(2,1)}, f16[7360,128]{1,0:T(8,128)(2,1)}, u32[]{:S(2)}, u32[]{:S(2)}) collective-permute-start(f16[7360,128]{1,0:T(8,128)(2,1)} %divide_convert_fusion), channel_id=1, source_target_pairs={{0,2},{1,3},{2,0},{3,1},{4,6},{5,7},{6,4},{7,5},{8,10},{9,11},{10,... | collective-permute-start | bytes 5652488 | tf_op jit(solution)/shard_map/ppermute | solution.py:691
  388.4 18.9 %collective-permute-start.25 = (f16[7360,128]{1,0:T(8,128)(2,1)}, f16[7360,128]{1,0:T(8,128)(2,1)}, u32[]{:S(2)}, u32[]{:S(2)}) collective-permute-start(f16[7360,128]{1,0:T(8,128)(2,1)} %divide_convert_fusion), channel_id=1, source_target_pairs={{0,1},{1,0},{2,3},{3,2},{4,5},{5,4},{6,7},{7,6},{8,9},{9,8},{10,11... | collective-permute-start | bytes 5652488 | tf_op jit(solution)/shard_map/ppermute | solution.py:691
  388.6 13.5 %slice-start.2 = ((s8[15073280]{0:T(1024)(128)(4,1)}), s8[2490368]{0:T(1024)(128)(4,1)S(1)}, s32[]{:S(2)}) async-start(s8[15073280]{0:T(1024)(128)(4,1)} %bitcast.121), calls=%async_computation.7 | async-start | bytes 4980736
  388.6 13.5 %slice-start.3 = ((s8[15073280]{0:T(1024)(128)(4,1)}), s8[4194304]{0:T(1024)(128)(4,1)S(1)}, s32[]{:S(2)}) async-start(s8[15073280]{0:T(1024)(128)(4,1)} %bitcast.121), calls=%async_computation.8 | async-start | bytes 8388608
  388.6 13.5 %slice-start.4 = ((s8[15073280]{0:T(1024)(128)(4,1)}), s8[4194304]{0:T(1024)(128)(4,1)S(1)}, s32[]{:S(2)}) async-start(s8[15073280]{0:T(1024)(128)(4,1)} %bitcast.121), calls=%async_computation.9 | async-start | bytes 8388608
  395.5 6.6 %slice-start.5 = ((s8[15073280]{0:T(1024)(128)(4,1)}), s8[4194304]{0:T(1024)(128)(4,1)S(1)}, s32[]{:S(2)}) async-start(s8[15073280]{0:T(1024)(128)(4,1)} %bitcast.121), calls=%async_computation.10 | async-start | bytes 8388608
  431.3 5.2 %collective-permute-start.26 = (f16[7360,128]{1,0:T(8,128)(2,1)}, f16[7360,128]{1,0:T(8,128)(2,1)S(1)}, u32[]{:S(2)}, u32[]{:S(2)}) collective-permute-start(f16[7360,128]{1,0:T(8,128)(2,1)} %collective-permute-done.24), channel_id=1, source_target_pairs={{0,1},{1,0},{2,3},{3,2},{4,5},{5,4},{6,7},{7,6},{8,9},{9,8},{10,11... | collective-permute-start | bytes 5652488 | tf_op jit(solution)/shard_map/ppermute | solution.py:691
  (20 other events, 47.7 us)
Sparse Core Ops, SparseCore 0:
  10.9 56.1 all-gather.2
  68.6 96.2 all-gather.4

commit v12 on v10

--- a/solution.py
+++ b/solution.py
@@ -494,7 +494,7 @@
             pltpu.VMEM((128, Q), F32),
         ],
         compiler_params=pltpu.CompilerParams(
-            dimension_semantics=("arbitrary",), vmem_limit_bytes=48 * 2**20),
+            dimension_semantics=("arbitrary",), vmem_limit_bytes=40 * 2**20),
         cost_estimate=pl.CostEstimate(
             flops=50 * 10**9, bytes_accessed=50 * 2**20, transcendentals=2 * 10**7),
     )(bound, proj, proj, dy, through, states, pair, tok, cot, in_w, norm_gain, ggain,

time: 455 us -> 455 us (level)
  transfers between devices with their start and end apart: 32 -> 32, of which waited for: 12 -> 13; matrix products, arithmetic and copies ran while one was open for 31% -> 31% of each run, Pallas kernels for 23% -> 24%
where the time goes in v12:
time: 455 us; the launch traced here: 448 us
  waiting for transfers between devices  111 us (24%)
  Pallas kernels  106 us (23%)
  other arithmetic  63.3 us (14%)
  matrix products  61.8 us (14%)
  starting transfers between devices  56.8 us (12%)
  local copies, waits for them, and re-layouts  30 us (7%)
  between operations  17.8 us (4%)
    pallas_call x1, Pallas kernels, run_backward(): pl.pallas_call(backward_kernel, grid=(steps,), in_specs=[pl.BlockSpec(mem...  57.2 us
    ppermute x27, waiting for transfers between devices, swap(): return lax.ppermute(values, axis, [(i, i ^ bit) for i in range(size)])  56.9 us
    ppermute x27, starting transfers between devices, swap(): return lax.ppermute(values, axis, [(i, i ^ bit) for i in range(size)])  39.7 us
    all_gather x1, waiting for transfers between devices, on_device(): flat = lax.all_gather(own.astype(BF16), 'zero', axis=0, tiled=True)  39.4 us
    pallas_call x1, Pallas kernels, run_forward(): pl.pallas_call(forward_kernel, grid=(steps,), in_specs=[pl.BlockSpec(memo...  35.2 us
    dot_general x4, matrix products, product(): lax.dot_general(part, right, (((1,), (1,)), ((0,), (0,))), preferred_elem...  23 us
    dot_general x3, matrix products, dot(): lax.dot_general(a, b, (((1,), (0,)), ((), ())), preferred_element_type=F32)  21.3 us
    dynamic_update_slice x4, other arithmetic, put(): return lax.dynamic_update_index_in_dim(new_master, new, shard, 0)  19.7 us
  transfers between devices with their start and end apart: 32, of which 13 were waited for; matrix products, arithmetic and copies ran while one was open for 31% of the time, Pallas kernels for 24%

profile of v12, /device:TPU:0, one launch (start us, length us, event | category | flops | bytes accessed | tf_op | source)
XLA Modules:
  0.0 447.5 jit_solution(7866188370746228)
XLA Ops:
  7.2 3.5 bitcast_convert_fusion
  12.6 2.4 gather_fusion
  15.0 7.4 %all-to-all-start = ((bf16[16,128,768]{2,1,0:T(8,128)(2,1)}), bf16[16,128,768]{2,1,0:T(8,128)(2,1)}, u32[]{:S(2)}, u32[]{:S(2)}) async-start(bf16[16,128,768]{2,1,0:T(8,128)(2,1)} %gather_fusion), calls=%async_computation | async-start | bytes 6291456 | tf_op jit(solution)/shard_map/all_to_all | solution.py:819
  27.6 39.4 %all-gather.3.cloned.1.call-done.flat_ref = bf16[29440,128]{1,0:T(8,128)(2,1)} async-done(((bf16[7360,128]{1,0:T(8,128)(2,1)}), bf16[29440,128]{1,0:T(8,128)(2,1)}) %all-gather.3.cloned.1.call-update) | async-done | bytes 7536656 | tf_op jit(solution)/shard_map/all_gather | solution.py:817
  67.0 7.8 %shard_map.136 = (bf16[3584,768]{1,0:T(8,128)(2,1)S(1)}, bf16[1536,768]{1,0:T(8,128)(2,1)}, f32[1,768]{1,0:T(1,128)S(1)}, f32[8,1792]{1,0:T(8,128)S(1)}, f32[1,1...) custom-call(bf16[29440,128]{1,0:T(8,128)(2,1)} %all-gather.3.cloned., ...), custom_call_target="tpu_custom_call" | custom-call | flops 1000000000 | bytes 16777216 | tf_op jit(solution)/shard_map/pallas_call | solution.py:593
  74.8 2.8 copy-done.1
  78.5 7.0 %fusion.94.gm_ref = f32[1024,1536]{1,0:T(8,128)} fusion(bf16[1536,768]{1,0:T(8,128)(2,1)} %get-tuple-element.76, bf16[1,1024,768]{2,1,0:T(8,128)(2,1)S(1)} %copy-done), kind=kOutput, calls=%fused_computation.260 | convolution fusion | flops 2415919104 | bytes 10223616 | tf_op jit(solution)/shard_map/dot_general | solution.py:33
  85.5 7.7 %all-to-all-done = bf16[16,128,768]{2,1,0:T(8,128)(2,1)} async-done(((bf16[16,128,768]{2,1,0:T(8,128)(2,1)}), bf16[16,128,768]{2,1,0:T(8,128)(2,1)}, u32[]{:S(2)}, u32[]{:S(2)}) %all-to-all-start) | async-done | bytes 3145760 | tf_op jit(solution)/shard_map/all_to_all | solution.py:819
  93.3 5.8 %fusion.21 = (f32[1024]{0:T(1024)S(1)}, bf16[1024,768]{1,0:T(8,128)(2,1)S(1)}) fusion(bf16[2048,768]{1,0:T(8,128)(2,1)} %bitcast.6, s32[1024]{0:T(1024)S(1)} %fusion.61), kind=kOutput, calls=%fused_computation.52 | convolution fusion | flops 3226467328 | bytes 4726784 | tf_op jit(solution)/shard_map/dot_general | solution.py:29
  99.1 4.7 %fusion.41.z_ref = f32[1024,1536]{1,0:T(8,128)} fusion(bf16[3584,768]{1,0:T(8,128)(2,1)S(1)} %copy-done.2, bf16[1024,768]{1,0:T(8,128)(2,1)S(1)} %get-tuple-element.207.tok_ref, f32[768]{0:T(1024)S(1)} %reduce.2, f32[1024]{0:T(1024)S(1)} %add_rsqrt_fusion), kind=kOutput, calls=%fused_computation.77 | convolution fusion | flops 2419064832 | bytes 10231808 | tf_op jit(solution)/shard_map/dot_general | solution.py:33
  103.7 5.8 %fusion.35.proj_ref.before_ref = f32[1024,1816]{1,0:T(8,128)} fusion(bf16[3584,768]{1,0:T(8,128)(2,1)S(1)} %copy-done.2, bf16[1024,768]{1,0:T(8,128)(2,1)S(1)} %get-tuple-element.207.tok_ref, f32[768]{0:T(1024)S(1)} %reduce.2, f32[1024]{0:T(1024)S(1)} %add_rsqrt_fusion), kind=kOutput, calls=%fused_computation.68 | convolution fusion | flops 2859466752 | bytes 11808768 | tf_op jit(solution)/shard_map/dot_general | solution.py:33
  109.5 35.2 %shard_map.137 = (bf16[2,1024,1536]{2,1,0:T(8,128)(2,1)}, f32[1024,1536]{1,0:T(8,128)}, f32[1024,128]{1,0:T(8,128)S(1)}, f32[8,128,1536]{2,1,0:T(8,128)}, f32[1,1536]{1,0:T(1,128)S(1)}, /*index=5*/f32[8,128]{1,0:T(8,128)S(1)}) custom-call(s32[1]{0:T(128)} %dynamic_slice.148.bound_ref, f32[1]{0:T(128)S(6)} %convert.1.cot_ref, f32[1024,1536]{1,0:T(8,128)} %fusion.41.z_ref, ...), custom_call_target="tpu_custom_call" | custom-call | flops 30000001024 | bytes 41943040 | tf_op jit(solution)/shard_map/pallas_call | solution.py:221
  145.5 10.4 %fusion.20 = bf16[2048,768]{1,0:T(8,128)(2,1)} fusion(s32[2048]{0:T(1024)S(1)} %get-tuple-element.203, bf16[1024,768]{1,0:T(8,128)(2,1)S(1)} %get-tuple-element.207.tok_ref, bf16[1536,768]{1,0:T(8,128)(2,1)} %get-tuple-element.76, bf16[2,1024,1536]{2,1,0:T(8,128)(2,1)} %get-tuple-element.93.gz_ref), kind=kOutput, calls=%fused_computation.51 | convolution fusion | flops 5643173888 | bytes 10231808 | tf_op jit(solution)/shard_map/dot_general | solution.py:29
  157.4 8.9 %select_convert_fusion = f16[2,896,768]{2,1,0:T(8,128)(2,1)} fusion(f32[]{:T(128)} %bitcast.12, f32[]{:T(128)} %bitcast.10, pred[896]{0:T(1024)(128)(4,1)S(1)} %fusion.71, bf16[1,1024,768]{2,1,0:T(8,128)(2,1)S(1)} %fusion.101, bf16[1,1024,768]{2,1,0:T(8,128)(2,1)S(1)} %copy-done, bf16[2,1024,1536]{2,1,0:T(8,128)(2,1)} %get-tuple-element.93.gz_ref, pred[]{:T(512)S(6)} %eq.123), kind=kOutput, calls=%fused_computation.11 | convolution fusion | flops 2826108928 | bytes 13240193 | tf_op jit(solution)/shard_map/dot_general | solution.py:735
  167.2 4.9 %all-to-all-start.1 = ((bf16[16,128,768]{2,1,0:T(8,128)(2,1)}), bf16[16,128,768]{2,1,0:T(8,128)(2,1)}, u32[]{:S(2)}, u32[]{:S(2)}) async-start(bf16[16,128,768]{2,1,0:T(8,128)(2,1)} %bitcast.133), calls=%async_computation.1 | async-start | bytes 6291456 | tf_op jit(solution)/shard_map/all_to_all | solution.py:848
  172.0 6.1 %fusion.27 = f32[2,768,768]{2,1,0:T(8,128)S(1)} fusion(bf16[2,1024,1536]{2,1,0:T(8,128)(2,1)} %get-tuple-element.93.gz_ref, pred[]{:T(512)S(6)} %eq.116, bf16[1,1024,768]{2,1,0:T(8,128)(2,1)} %copy-done.20, bf16[1,1024,768]{2,1,0:T(8,128)(2,1)S(1)} %copy-done), kind=kOutput, calls=%fused_computation.59 | convolution fusion | flops 2419064832 | bytes 14155777 | tf_op jit(solution)/shard_map/dot_general | solution.py:735
  179.4 2.1 multiply_add_fusion
  183.6 57.2 %shard_map.138 = (bf16[2,1024,1024]{2,1,0:T(8,128)(2,1)S(1)}, bf16[1024,768]{1,0:T(8,128)(2,1)S(1)}, f32[48,768]{1,0:T(8,128)S(1)}, f32[8,128]{1,0:T(8,128)S(1)}) custom-call(s32[1]{0:T(128)} %dynamic_slice.148.bound_ref, f32[1024,1816]{1,0:T(8,128)} %fusion.35.proj_ref.before_ref, f32[1024,1816]{1,0:T(8,128)} %fusion.35.proj_ref.before_ref, ...), custom_call_target="tpu_custom_call" | custom-call | flops 49999998976 | bytes 52428800 | tf_op jit(solution)/shard_map/pallas_call | solution.py:453
  247.0 5.9 %select_convert_fusion.1 = f16[2,640,768]{2,1,0:T(8,128)(2,1)S(1)} fusion(f32[]{:T(128)} %bitcast.16, f32[]{:T(128)} %bitcast.15, pred[640]{0:T(1024)(128)(4,1)S(1)} %fusion.73, bf16[1,1024,768]{2,1,0:T(8,128)(2,1)S(1)} %copy-done.21, bf16[2,1024,1024]{2,1,0:T(8,128)(2,1)} %copy-done.9, pred[]{:T(512)S(6)} %eq.123), kind=kOutput, calls=%fused_computation.19 | convolution fusion | flops 2019098624 | bytes 8783489 | tf_op jit(solution)/shard_map/dot_general | solution.py:735
  253.8 2.1 fusion.33
  261.8 2.3 select_convert_fusion.4
  266.1 4.3 gather_fusion.1
  270.4 4.3 broadcast_select_fusion
  274.7 5.1 %fusion.19 = bf16[2048,768]{1,0:T(8,128)(2,1)} fusion(bf16[1024,768]{1,0:T(8,128)(2,1)S(1)} %copy-done.12, s32[2048]{0:T(1024)S(1)} %copy-done.23), kind=kOutput, calls=%fused_computation.50 | convolution fusion | flops 3224895488 | bytes 4726784 | tf_op jit(solution)/shard_map/dot_general | solution.py:29
  289.6 2.4 collective-permute-start.6
  292.5 4.6 %collective-permute-done.10 = f16[336,768]{1,0:T(8,128)(2,1)S(1)} collective-permute-done((f16[336,768]{1,0:T(8,128)(2,1)S(1)}, f16[336,768]{1,0:T(8,128)(2,1)S(1)}, u32[]{:S(2)}, u32[]{:S(2)}) %collective-permute-start.10) | collective-permute-done | bytes 516128 | tf_op jit(solution)/shard_map/ppermute | solution.py:691
  299.1 2.4 collective-permute-start.16
  301.5 4.3 collective-permute-done.6
  306.0 2.4 collective-permute-start.11
  308.5 13.2 %collective-permute-start.12 = (f16[96,768]{1,0:T(8,128)(2,1)S(1)}, f16[96,768]{1,0:T(8,128)(2,1)S(1)}, u32[]{:S(2)}, u32[]{:S(2)}) collective-permute-start(f16[96,768]{1,0:T(8,128)(2,1)S(1)} %multiply_convert_fusion), channel_id=1, source_target_pairs={{0,16},{4,20},{8,24},{12,28},{16,0},{20,4},{24,8},{28,12},{1,17},{... | collective-permute-start | bytes 442376 | tf_op jit(solution)/shard_map/ppermute | solution.py:691
  321.7 5.6 %collective-permute-done.15 = f16[96,768]{1,0:T(8,128)(2,1)S(1)} collective-permute-done((f16[96,768]{1,0:T(8,128)(2,1)S(1)}, f16[96,768]{1,0:T(8,128)(2,1)S(1)}, u32[]{:S(2)}, u32[]{:S(2)}) %collective-permute-start.15) | collective-permute-done | bytes 147488 | tf_op jit(solution)/shard_map/ppermute | solution.py:691
  327.3 4.4 collective-permute-done.12
  333.0 2.3 collective-permute-start.19
  337.4 3.2 collective-permute-done.19
  340.5 3.7 collective-permute-done.20
  346.5 10.2 %collective-permute-done.22 = f16[320,768]{1,0:T(8,128)(2,1)S(1)} collective-permute-done((f16[320,768]{1,0:T(8,128)(2,1)S(1)}, f16[320,768]{1,0:T(8,128)(2,1)S(1)}, u32[]{:S(2)}, u32[]{:S(2)}) %collective-permute-start.22) | collective-permute-done | bytes 491552 | tf_op jit(solution)/shard_map/ppermute | solution.py:691
  359.8 4.8 %all-to-all-start.2 = ((bf16[16,128,768]{2,1,0:T(8,128)(2,1)}), bf16[16,128,768]{2,1,0:T(8,128)(2,1)}, u32[]{:S(2)}, u32[]{:S(2)}) async-start(bf16[16,128,768]{2,1,0:T(8,128)(2,1)} %bitcast.134), calls=%async_computation.2 | async-start | bytes 6291456 | tf_op jit(solution)/shard_map/all_to_all | solution.py:848
  364.6 6.1 %shard_map.139 = f32[7360,128]{1,0:T(8,128)} custom-call(s32[2]{0:T(128)S(1)} %pad_add_fusion.1.who_ref, f32[768,768]{1,0:T(8,128)S(1)} %convert_multiply_fusion.2.early_ref, f32[768,768]{1,0:T(8,128)} %collective-permute-done.18.early_other_ref, f32[512,768]{1,0:T(8,128)} %convert_multiply_fusion.3.late_ref, ...), custom_call_target="tpu_custom_call" | custom-call | flops 1000000 | bytes 12582912 | tf_op jit(solution)/shard_map/pallas_call | solution.py:671
  370.8 5.8 %divide_convert_fusion = f16[7360,128]{1,0:T(8,128)(2,1)} fusion(f32[7360,128]{1,0:T(8,128)} %shard_map.139, f32[]{:T(128)} %bitcast.26, f32[]{:T(128)} %bitcast.24, f32[942080]{0:T(1024)S(1)} %copy-done.16, f32[942080]{0:T(1024)} %param.14), kind=kLoop, calls=%fused_computation.42 | loop fusion | flops 11304960 | bytes 13189128 | tf_op jit(solution)/shard_map/convert_element_type | solution.py:937
  377.8 6.9 %multiply_add_fusion.1 = (f32[7360,128]{1,0:T(8,128)}, f32[7360,128]{1,0:T(8,128)}) fusion(f32[7360,128]{1,0:T(8,128)S(1)} %bitcast.127, f32[7360,128]{1,0:T(8,128)S(1)} %copy-done.15, f32[7360,128]{1,0:T(8,128)} %bitcast.128), kind=kLoop, calls=%fused_computation.40 | loop fusion | flops 6594560 | bytes 18841600 | tf_op jit(solution)/shard_map/add | solution.py:932
  384.7 6.6 %broadcast_in_dim.146 = f32[4,7360,128]{2,1,0:T(8,128)} broadcast(f32[]{:T(128)} %constant.309.clone.1), dimensions={} | broadcast | bytes 15073284 | tf_op jit(solution)/shard_map/broadcast_in_dim | solution.py:894
  391.3 5.3 %bitcast_dynamic-update-slice_fusion.3 = f32[4,7360,128]{2,1,0:T(8,128)} fusion(f32[4,7360,128]{2,1,0:T(8,128)} %broadcast_in_dim.146, s32[]{:T(128)S(6)} %select_n.595, f16[7360,128]{1,0:T(8,128)(2,1)} %divide_convert_fusion, f32[4,7360,128]{2,1,0:T(8,128)S(1)} %bitcast.121, f32[]{:T(128)} %bitcast.30, f32[]{:T(128)} %bitcast.29), kind=kLoop, calls=%fused_computation.35 | loop fusion | flops 4710400 | bytes 9421828 | tf_op jit(solution)/shard_map/jit(dynamic_update_index_in_dim)/dynamic_update_slice | solution.py:945
  396.6 5.3 %bitcast_dynamic-update-slice_fusion.2 = f32[4,7360,128]{2,1,0:T(8,128)} fusion(f32[4,7360,128]{2,1,0:T(8,128)} %bitcast_dynamic-update-slice_fusion.3, s32[]{:T(128)S(6)} %select_n.720, f16[7360,128]{1,0:T(8,128)(2,1)} %collective-permute-done.25, f32[4,7360,128]{2,1,0:T(8,128)S(1)} %bitcast.122, f32[]{:T(128)} %bitcast.30, f32[]{:T(128)} %bitcast.29), kind=kLoop, calls=%fused_computation.30 | loop fusion | flops 4710400 | bytes 9421828 | tf_op jit(solution)/shard_map/jit(dynamic_update_index_in_dim)/dynamic_update_slice | solution.py:945
  401.9 18.4 %collective-permute-done.24 = f16[7360,128]{1,0:T(8,128)(2,1)} collective-permute-done((f16[7360,128]{1,0:T(8,128)(2,1)}, f16[7360,128]{1,0:T(8,128)(2,1)}, u32[]{:S(2)}, u32[]{:S(2)}) %collective-permute-start.24) | collective-permute-done | bytes 1884192 | tf_op jit(solution)/shard_map/ppermute | solution.py:691
  420.3 5.3 %bitcast_dynamic-update-slice_fusion.1 = f32[4,7360,128]{2,1,0:T(8,128)} fusion(f32[4,7360,128]{2,1,0:T(8,128)} %bitcast_dynamic-update-slice_fusion.2, s32[]{:T(128)S(6)} %select_n.721, f16[7360,128]{1,0:T(8,128)(2,1)} %collective-permute-done.24, f32[4,7360,128]{2,1,0:T(8,128)S(1)} %bitcast.123, f32[]{:T(128)} %bitcast.30, f32[]{:T(128)} %bitcast.29), kind=kLoop, calls=%fused_computation.25 | loop fusion | flops 4710400 | bytes 9421828 | tf_op jit(solution)/shard_map/jit(dynamic_update_index_in_dim)/dynamic_update_slice | solution.py:945
  425.6 3.8 bitcast_dynamic-update-slice_fusion
  429.4 6.7 %all-to-all-done.2 = bf16[16,128,768]{2,1,0:T(8,128)(2,1)} async-done(((bf16[16,128,768]{2,1,0:T(8,128)(2,1)}), bf16[16,128,768]{2,1,0:T(8,128)(2,1)}, u32[]{:S(2)}, u32[]{:S(2)}) %all-to-all-start.2) | async-done | bytes 3145760 | tf_op jit(solution)/shard_map/all_to_all | solution.py:848
  436.1 4.3 gather_fusion.2
  (189 shorter events, 48.6 us)
Async XLA Ops:
  7.2 59.9 %all-gather.3.cloned.1.call-start = ((), (), s32[]{:S(2)}) async-start(), calls=%async_computation.3 | async-start | bytes 9420800 | tf_op jit(solution)/shard_map/all_gather | solution.py:817
  10.7 235.0 %all-gather.5.cloned.1.call-start = ((), (), s32[]{:S(2)}) async-start(), calls=%async_computation.4 | async-start | bytes 18841600 | tf_op jit(solution)/shard_map/all_gather | solution.py:830
  15.0 7.4 %copy-start = (bf16[1,1024,768]{2,1,0:T(8,128)(2,1)S(1)}, bf16[1,1024,768]{2,1,0:T(8,128)(2,1)}, u32[]{:S(2)}) copy-start(bf16[1,1024,768]{2,1,0:T(8,128)(2,1)} %param.10) | copy-start | bytes 4718596
  15.0 9.2 %copy-start.26 = (s32[64]{0:T(128)S(1)}, s32[64]{0:T(128)}, u32[]{:S(2)}) copy-start(s32[64]{0:T(128)} %param.11) | copy-start | bytes 772
  15.0 78.2 %all-to-all-start = ((bf16[16,128,768]{2,1,0:T(8,128)(2,1)}), bf16[16,128,768]{2,1,0:T(8,128)(2,1)}, u32[]{:S(2)}, u32[]{:S(2)}) async-start(bf16[16,128,768]{2,1,0:T(8,128)(2,1)} %gather_fusion), calls=%async_computation | async-start | bytes 6291456 | tf_op jit(solution)/shard_map/all_to_all | solution.py:819
  78.5 7.0 %copy-start.6 = (bf16[1536,128]{1,0:T(8,128)(2,1)}, bf16[1536,128]{1,0:T(8,128)(2,1)S(1)}, u32[]{:S(2)}) copy-start(bf16[1536,128]{1,0:T(8,128)(2,1)S(1)} %get-tuple-element.83.et_ref) | copy-start | bytes 1179652
  93.2 5.8 %copy-start.2 = (bf16[3584,768]{1,0:T(8,128)(2,1)S(1)}, bf16[3584,768]{1,0:T(8,128)(2,1)}, u32[]{:S(2)}) copy-start(bf16[3584,768]{1,0:T(8,128)(2,1)} %copy-done.1) | copy-start | bytes 16515076
  103.7 5.8 %copy-start.4 = (bf16[256,1536]{1,0:T(8,128)(2,1)S(1)}, bf16[256,1536]{1,0:T(8,128)(2,1)}, u32[]{:S(2)}) copy-start(bf16[256,1536]{1,0:T(8,128)(2,1)} %copy-done.3) | copy-start | bytes 2359300
  103.7 5.8 %copy-start.7 = (bf16[1536,128]{1,0:T(8,128)(2,1)S(1)}, bf16[1536,128]{1,0:T(8,128)(2,1)}, u32[]{:S(2)}) copy-start(bf16[1536,128]{1,0:T(8,128)(2,1)} %copy-done.6) | copy-start | bytes 1179652
  157.4 8.9 %copy-start.20 = (bf16[1,1024,768]{2,1,0:T(8,128)(2,1)}, bf16[1,1024,768]{2,1,0:T(8,128)(2,1)S(1)}, u32[]{:S(2)}) copy-start(bf16[1,1024,768]{2,1,0:T(8,128)(2,1)S(1)} %fusion.101) | copy-start | bytes 4718596
  166.3 11.8 %collective-permute-start = (f16[2,896,768]{2,1,0:T(8,128)(2,1)}, f16[2,896,768]{2,1,0:T(8,128)(2,1)}, u32[]{:S(2)}, u32[]{:S(2)}) collective-permute-start(f16[2,896,768]{2,1,0:T(8,128)(2,1)} %select_convert_fusion), channel_id=1, source_target_pairs={{0,1},{1,0},{2,3},{3,2},{4,5},{5,4},{6,7},{7,6},{8,9},{9,8},{10,11... | collective-permute-start | bytes 8257544 | tf_op jit(solution)/shard_map/ppermute | solution.py:691
  167.2 94.6 %all-to-all-start.1 = ((bf16[16,128,768]{2,1,0:T(8,128)(2,1)}), bf16[16,128,768]{2,1,0:T(8,128)(2,1)}, u32[]{:S(2)}, u32[]{:S(2)}) async-start(bf16[16,128,768]{2,1,0:T(8,128)(2,1)} %bitcast.133), calls=%async_computation.1 | async-start | bytes 6291456 | tf_op jit(solution)/shard_map/all_to_all | solution.py:848
  182.0 62.0 %collective-permute-start.1 = (f16[784,768]{1,0:T(8,128)(2,1)S(1)}, f16[784,768]{1,0:T(8,128)(2,1)S(1)}, u32[]{:S(2)}, u32[]{:S(2)}) collective-permute-start(f16[784,768]{1,0:T(8,128)(2,1)S(1)} %select_convert_fusion.2), channel_id=1, source_target_pairs={{0,2},{1,3},{2,0},{3,1},{4,6},{5,7},{6,4},{7,5},{8,10},{9,11},{10,... | collective-permute-start | bytes 3612680 | tf_op jit(solution)/shard_map/ppermute | solution.py:691
  247.0 6.7 %copy-start.10 = (bf16[2,1024,1024]{2,1,0:T(8,128)(2,1)S(1)}, bf16[2,1024,1024]{2,1,0:T(8,128)(2,1)}, u32[]{:S(2)}) copy-start(bf16[2,1024,1024]{2,1,0:T(8,128)(2,1)} %copy-done.9) | copy-start | bytes 12582916
  253.0 5.3 %collective-permute-start.2 = (f16[2,640,768]{2,1,0:T(8,128)(2,1)S(1)}, f16[2,640,768]{2,1,0:T(8,128)(2,1)S(1)}, u32[]{:S(2)}, u32[]{:S(2)}) collective-permute-start(f16[2,640,768]{2,1,0:T(8,128)(2,1)S(1)} %select_convert_fusion.1), channel_id=1, source_target_pairs={{0,1},{1,0},{2,3},{3,2},{4,5},{5,4},{6,7},{7,6},{8,9},{9,8},{10,11... | collective-permute-start | bytes 5898248 | tf_op jit(solution)/shard_map/ppermute | solution.py:691
  253.5 3.8 collective-permute-start.8
  257.2 26.5 %collective-permute-start.9 = (f32[48,768]{1,0:T(8,128)S(1)}, f32[48,768]{1,0:T(8,128)S(1)}, u32[]{:S(2)}, u32[]{:S(2)}) collective-permute-start(f32[48,768]{1,0:T(8,128)S(1)} %add.432), channel_id=1, source_target_pairs={{0,2},{1,3},{2,0},{3,1},{4,6},{5,7},{6,4},{7,5},{8,10},{9,11},{10,... | collective-permute-start | bytes 442376 | tf_op jit(solution)/shard_map/ppermute | solution.py:691
  260.7 20.4 %collective-permute-start.3 = (f16[528,768]{1,0:T(8,128)(2,1)}, f16[528,768]{1,0:T(8,128)(2,1)}, u32[]{:S(2)}, u32[]{:S(2)}) collective-permute-start(f16[528,768]{1,0:T(8,128)(2,1)} %select_convert_fusion.3), channel_id=1, source_target_pairs={{0,2},{1,3},{2,0},{3,1},{4,6},{5,7},{6,4},{7,5},{8,10},{9,11},{10,... | collective-permute-start | bytes 2433032 | tf_op jit(solution)/shard_map/ppermute | solution.py:691
  264.1 21.8 %collective-permute-start.4 = (f16[400,768]{1,0:T(8,128)(2,1)}, f16[400,768]{1,0:T(8,128)(2,1)}, u32[]{:S(2)}, u32[]{:S(2)}) collective-permute-start(f16[400,768]{1,0:T(8,128)(2,1)} %select_convert_fusion.4), channel_id=1, source_target_pairs={{0,4},{4,0},{8,12},{12,8},{16,20},{20,16},{24,28},{28,24},{1,5},{5... | collective-permute-start | bytes 1843208 | tf_op jit(solution)/shard_map/ppermute | solution.py:691
  284.2 13.0 %collective-permute-start.10 = (f16[336,768]{1,0:T(8,128)(2,1)S(1)}, f16[336,768]{1,0:T(8,128)(2,1)S(1)}, u32[]{:S(2)}, u32[]{:S(2)}) collective-permute-start(f16[336,768]{1,0:T(8,128)(2,1)S(1)} %select_convert_fusion.5), channel_id=1, source_target_pairs={{0,4},{4,0},{8,12},{12,8},{16,20},{20,16},{24,28},{28,24},{1,5},{5... | collective-permute-start | bytes 1548296 | tf_op jit(solution)/shard_map/ppermute | solution.py:691
  288.1 13.4 %collective-permute-start.5 = (f16[112,768]{1,0:T(8,128)(2,1)S(1)}, f16[112,768]{1,0:T(8,128)(2,1)S(1)}, u32[]{:S(2)}, u32[]{:S(2)}) collective-permute-start(f16[112,768]{1,0:T(8,128)(2,1)S(1)} %get-tuple-element.175), channel_id=1, source_target_pairs={{0,8},{4,12},{8,0},{12,4},{16,24},{20,28},{24,16},{28,20},{1,9},{5... | collective-permute-start | bytes 516104 | tf_op jit(solution)/shard_map/ppermute | solution.py:691
  289.6 16.2 %collective-permute-start.6 = (f16[112,768]{1,0:T(8,128)(2,1)S(1)}, f16[112,768]{1,0:T(8,128)(2,1)S(1)}, u32[]{:S(2)}, u32[]{:S(2)}) collective-permute-start(f16[112,768]{1,0:T(8,128)(2,1)S(1)} %get-tuple-element.174), channel_id=1, source_target_pairs={{0,16},{4,20},{8,24},{12,28},{16,0},{20,4},{24,8},{28,12},{1,17},{... | collective-permute-start | bytes 516104 | tf_op jit(solution)/shard_map/ppermute | solution.py:691
  292.0 13.8 %collective-permute-start.7 = (f16[112,768]{1,0:T(8,128)(2,1)S(1)}, f16[112,768]{1,0:T(8,128)(2,1)S(1)}, u32[]{:S(2)}, u32[]{:S(2)}) collective-permute-start(f16[112,768]{1,0:T(8,128)(2,1)S(1)} %get-tuple-element.173), channel_id=1, source_target_pairs={{0,24},{4,28},{8,16},{12,20},{16,8},{20,12},{24,0},{28,4},{1,25},{... | collective-permute-start | bytes 516104 | tf_op jit(solution)/shard_map/ppermute | solution.py:691
  297.5 24.2 %collective-permute-start.14 = (f16[96,768]{1,0:T(8,128)(2,1)S(1)}, f16[96,768]{1,0:T(8,128)(2,1)S(1)}, u32[]{:S(2)}, u32[]{:S(2)}) collective-permute-start(f16[96,768]{1,0:T(8,128)(2,1)S(1)} %get-tuple-element.180), channel_id=1, source_target_pairs={{0,8},{4,12},{8,0},{12,4},{16,24},{20,28},{24,16},{28,20},{1,9},{5... | collective-permute-start | bytes 442376 | tf_op jit(solution)/shard_map/ppermute | solution.py:691
  299.1 22.6 %collective-permute-start.16 = (f16[96,768]{1,0:T(8,128)(2,1)S(1)}, f16[96,768]{1,0:T(8,128)(2,1)S(1)}, u32[]{:S(2)}, u32[]{:S(2)}) collective-permute-start(f16[96,768]{1,0:T(8,128)(2,1)S(1)} %get-tuple-element.178), channel_id=1, source_target_pairs={{0,24},{4,28},{8,16},{12,20},{16,8},{20,12},{24,0},{28,4},{1,25},{... | collective-permute-start | bytes 442376 | tf_op jit(solution)/shard_map/ppermute | solution.py:691
  301.5 25.8 %collective-permute-start.15 = (f16[96,768]{1,0:T(8,128)(2,1)S(1)}, f16[96,768]{1,0:T(8,128)(2,1)S(1)}, u32[]{:S(2)}, u32[]{:S(2)}) collective-permute-start(f16[96,768]{1,0:T(8,128)(2,1)S(1)} %get-tuple-element.179), channel_id=1, source_target_pairs={{0,16},{4,20},{8,24},{12,28},{16,0},{20,4},{24,8},{28,12},{1,17},{... | collective-permute-start | bytes 442376 | tf_op jit(solution)/shard_map/ppermute | solution.py:691
  306.0 21.3 %collective-permute-start.11 = (f16[96,768]{1,0:T(8,128)(2,1)S(1)}, f16[96,768]{1,0:T(8,128)(2,1)S(1)}, u32[]{:S(2)}, u32[]{:S(2)}) collective-permute-start(f16[96,768]{1,0:T(8,128)(2,1)S(1)} %multiply_convert_fusion), channel_id=1, source_target_pairs={{0,24},{4,28},{8,16},{12,20},{16,8},{20,12},{24,0},{28,4},{1,25},{... | collective-permute-start | bytes 442376 | tf_op jit(solution)/shard_map/ppermute | solution.py:691
  308.5 23.2 %collective-permute-start.12 = (f16[96,768]{1,0:T(8,128)(2,1)S(1)}, f16[96,768]{1,0:T(8,128)(2,1)S(1)}, u32[]{:S(2)}, u32[]{:S(2)}) collective-permute-start(f16[96,768]{1,0:T(8,128)(2,1)S(1)} %multiply_convert_fusion), channel_id=1, source_target_pairs={{0,16},{4,20},{8,24},{12,28},{16,0},{20,4},{24,8},{28,12},{1,17},{... | collective-permute-start | bytes 442376 | tf_op jit(solution)/shard_map/ppermute | solution.py:691
  321.6 10.0 %collective-permute-start.13 = (f16[96,768]{1,0:T(8,128)(2,1)S(1)}, f16[96,768]{1,0:T(8,128)(2,1)S(1)}, u32[]{:S(2)}, u32[]{:S(2)}) collective-permute-start(f16[96,768]{1,0:T(8,128)(2,1)S(1)} %multiply_convert_fusion), channel_id=1, source_target_pairs={{0,8},{4,12},{8,0},{12,4},{16,24},{20,28},{24,16},{28,20},{1,9},{5... | collective-permute-start | bytes 442376 | tf_op jit(solution)/shard_map/ppermute | solution.py:691
  332.2 13.7 %collective-permute-start.17 = (f16[384,768]{1,0:T(8,128)(2,1)S(1)}, f16[384,768]{1,0:T(8,128)(2,1)S(1)}, u32[]{:S(2)}, u32[]{:S(2)}) collective-permute-start(f16[384,768]{1,0:T(8,128)(2,1)S(1)} %pad_maximum_fusion.11), channel_id=1, source_target_pairs={{0,4},{4,0},{8,12},{12,8},{16,20},{20,16},{24,28},{28,24},{1,5},{5... | collective-permute-start | bytes 1769480 | tf_op jit(solution)/shard_map/ppermute | solution.py:691
  333.0 7.6 %collective-permute-start.19 = (f16[80,768]{1,0:T(8,128)(2,1)S(1)}, f16[80,768]{1,0:T(8,128)(2,1)S(1)}, u32[]{:S(2)}, u32[]{:S(2)}) collective-permute-start(f16[80,768]{1,0:T(8,128)(2,1)S(1)} %multiply_convert_fusion.1), channel_id=1, source_target_pairs={{0,24},{4,28},{8,16},{12,20},{16,8},{20,12},{24,0},{28,4},{1,25},{... | collective-permute-start | bytes 368648 | tf_op jit(solution)/shard_map/ppermute | solution.py:691
  335.3 9.0 %collective-permute-start.20 = (f16[80,768]{1,0:T(8,128)(2,1)S(1)}, f16[80,768]{1,0:T(8,128)(2,1)S(1)}, u32[]{:S(2)}, u32[]{:S(2)}) collective-permute-start(f16[80,768]{1,0:T(8,128)(2,1)S(1)} %multiply_convert_fusion.1), channel_id=1, source_target_pairs={{0,16},{4,20},{8,24},{12,28},{16,0},{20,4},{24,8},{28,12},{1,17},{... | collective-permute-start | bytes 368648 | tf_op jit(solution)/shard_map/ppermute | solution.py:691
  335.3 9.0 %collective-permute-start.21 = (f16[80,768]{1,0:T(8,128)(2,1)S(1)}, f16[80,768]{1,0:T(8,128)(2,1)S(1)}, u32[]{:S(2)}, u32[]{:S(2)}) collective-permute-start(f16[80,768]{1,0:T(8,128)(2,1)S(1)} %multiply_convert_fusion.1), channel_id=1, source_target_pairs={{0,8},{4,12},{8,0},{12,4},{16,24},{20,28},{24,16},{28,20},{1,9},{5... | collective-permute-start | bytes 368648 | tf_op jit(solution)/shard_map/ppermute | solution.py:691
  344.6 12.1 %collective-permute-start.22 = (f16[320,768]{1,0:T(8,128)(2,1)S(1)}, f16[320,768]{1,0:T(8,128)(2,1)S(1)}, u32[]{:S(2)}, u32[]{:S(2)}) collective-permute-start(f16[320,768]{1,0:T(8,128)(2,1)S(1)} %pad_maximum_fusion.12), channel_id=1, source_target_pairs={{0,4},{4,0},{8,12},{12,8},{16,20},{20,16},{24,28},{28,24},{1,5},{5... | collective-permute-start | bytes 1474568 | tf_op jit(solution)/shard_map/ppermute | solution.py:691
  346.4 12.8 %copy-start.24 = (f32[2]{0:T(128)S(1)}, f32[2]{0:T(128)}, u32[]{:S(2)}) copy-start(f32[2]{0:T(128)} %param.16) | copy-start | bytes 28
  346.4 18.2 %collective-permute-start.18 = (f32[768,768]{1,0:T(8,128)S(1)}, f32[768,768]{1,0:T(8,128)}, u32[]{:S(2)}, u32[]{:S(2)}) collective-permute-start(f32[768,768]{1,0:T(8,128)S(1)} %convert_multiply_fusion.2.early_ref), channel_id=1, source_target_pairs={{0,1},{1,0},{2,3},{3,2},{4,5},{5,4},{6,7},{7,6},{8,9},{9,8},{10,11... | collective-permute-start | bytes 7077896 | tf_op jit(solution)/shard_map/ppermute | solution.py:691
  358.3 6.3 %collective-permute-start.23 = (f32[512,768]{1,0:T(8,128)}, f32[512,768]{1,0:T(8,128)}, u32[]{:S(2)}, u32[]{:S(2)}) collective-permute-start(f32[512,768]{1,0:T(8,128)} %convert_multiply_fusion.3.late_ref), channel_id=1, source_target_pairs={{0,1},{1,0},{2,3},{3,2},{4,5},{5,4},{6,7},{7,6},{8,9},{9,8},{10,11... | collective-permute-start | bytes 4718600 | tf_op jit(solution)/shard_map/ppermute | solution.py:691
  359.8 76.3 %all-to-all-start.2 = ((bf16[16,128,768]{2,1,0:T(8,128)(2,1)}), bf16[16,128,768]{2,1,0:T(8,128)(2,1)}, u32[]{:S(2)}, u32[]{:S(2)}) async-start(bf16[16,128,768]{2,1,0:T(8,128)(2,1)} %bitcast.134), calls=%async_computation.2 | async-start | bytes 6291456 | tf_op jit(solution)/shard_map/all_to_all | solution.py:848
  364.6 6.2 %copy-start.16 = (f32[942080]{0:T(1024)S(1)}, f32[942080]{0:T(1024)}, u32[]{:S(2)}) copy-start(f32[942080]{0:T(1024)} %param.15) | copy-start | bytes 11304964
  370.8 7.0 %copy-start.15 = (f32[7360,128]{1,0:T(8,128)S(1)}, f32[7360,128]{1,0:T(8,128)}, u32[]{:S(2)}) copy-start(f32[7360,128]{1,0:T(8,128)} %shard_map.139) | copy-start | bytes 11304964
  370.8 7.0 %copy-start.17 = (f32[942080]{0:T(1024)S(1)}, f32[942080]{0:T(1024)}, u32[]{:S(2)}) copy-start(f32[942080]{0:T(1024)} %param.15) | copy-start | bytes 11304964
  376.6 43.7 %collective-permute-start.24 = (f16[7360,128]{1,0:T(8,128)(2,1)}, f16[7360,128]{1,0:T(8,128)(2,1)}, u32[]{:S(2)}, u32[]{:S(2)}) collective-permute-start(f16[7360,128]{1,0:T(8,128)(2,1)} %divide_convert_fusion), channel_id=1, source_target_pairs={{0,2},{1,3},{2,0},{3,1},{4,6},{5,7},{6,4},{7,5},{8,10},{9,11},{10,... | collective-permute-start | bytes 5652488 | tf_op jit(solution)/shard_map/ppermute | solution.py:691
  377.6 19.0 %collective-permute-start.25 = (f16[7360,128]{1,0:T(8,128)(2,1)}, f16[7360,128]{1,0:T(8,128)(2,1)}, u32[]{:S(2)}, u32[]{:S(2)}) collective-permute-start(f16[7360,128]{1,0:T(8,128)(2,1)} %divide_convert_fusion), channel_id=1, source_target_pairs={{0,1},{1,0},{2,3},{3,2},{4,5},{5,4},{6,7},{7,6},{8,9},{9,8},{10,11... | collective-permute-start | bytes 5652488 | tf_op jit(solution)/shard_map/ppermute | solution.py:691
  377.8 13.5 %slice-start = ((s8[15073280]{0:T(1024)(128)(4,1)}), s8[2490368]{0:T(1024)(128)(4,1)S(1)}, s32[]{:S(2)}) async-start(s8[15073280]{0:T(1024)(128)(4,1)} %bitcast.119), calls=%async_computation.5 | async-start | bytes 4980736
  377.8 13.5 %slice-start.1 = ((s8[15073280]{0:T(1024)(128)(4,1)}), s8[4194304]{0:T(1024)(128)(4,1)S(1)}, s32[]{:S(2)}) async-start(s8[15073280]{0:T(1024)(128)(4,1)} %bitcast.119), calls=%async_computation.6 | async-start | bytes 8388608
  377.8 13.5 %slice-start.2 = ((s8[15073280]{0:T(1024)(128)(4,1)}), s8[4194304]{0:T(1024)(128)(4,1)S(1)}, s32[]{:S(2)}) async-start(s8[15073280]{0:T(1024)(128)(4,1)} %bitcast.119), calls=%async_computation.7 | async-start | bytes 8388608
  384.7 6.6 %slice-start.3 = ((s8[15073280]{0:T(1024)(128)(4,1)}), s8[4194304]{0:T(1024)(128)(4,1)S(1)}, s32[]{:S(2)}) async-start(s8[15073280]{0:T(1024)(128)(4,1)} %bitcast.119), calls=%async_computation.8 | async-start | bytes 8388608
  420.3 5.3 %collective-permute-start.26 = (f16[7360,128]{1,0:T(8,128)(2,1)}, f16[7360,128]{1,0:T(8,128)(2,1)S(1)}, u32[]{:S(2)}, u32[]{:S(2)}) collective-permute-start(f16[7360,128]{1,0:T(8,128)(2,1)} %collective-permute-done.24), channel_id=1, source_target_pairs={{0,1},{1,0},{2,3},{3,2},{4,5},{5,4},{6,7},{7,6},{8,9},{9,8},{10,11... | collective-permute-start | bytes 5652488 | tf_op jit(solution)/shard_map/ppermute | solution.py:691
  (15 other events, 32.1 us)
Sparse Core Ops, SparseCore 0:
  10.9 56.1 all-gather.2
  68.6 96.2 all-gather.4
